TPU v7x, 32 devices: a whole 2x2x4 slice. The times are simulated.
32 devices in a mesh: groups: 2 (over x), seq: 16 (over z, y, core).
Axes of the slice: x: 2, y: 2, z: 4, core: 2. Of those that a mesh axis runs over, the one named last changes fastest.
Arguments:
- query_in: bfloat16 [16384, 128], P(('groups', 'seq')), parts along dimension 0, may hold values from -6 to 6
- key_in: bfloat16 [16384, 128], P(('groups', 'seq')), parts along dimension 0, may hold values from -6 to 6
- value_in: bfloat16 [16384, 1024], P(('groups', 'seq')), parts along dimension 0, may hold values from -6 to 6
- conv_query: float32 [3, 128], replicated, may hold values from -3.5 to 3.5
- conv_key: float32 [3, 128], replicated, may hold values from -3.5 to 3.5
- conv_value: float32 [3, 1024], replicated, may hold values from -3.5 to 3.5
- norm_gain: float32 [1024], replicated, may hold values from 0.25 to 1.75
- grad_out: bfloat16 [16384, 1024], P(('groups', 'seq')), parts along dimension 0, may hold values from -6 to 6
Outputs:
- out_tokens: bfloat16 [16384, 1024], P(('groups', 'seq')), parts along dimension 0
- grad_query: bfloat16 [16384, 128], P(('groups', 'seq')), parts along dimension 0
- grad_key: bfloat16 [16384, 128], P(('groups', 'seq')), parts along dimension 0
- grad_value: bfloat16 [16384, 1024], P(('groups', 'seq')), parts along dimension 0
- grad_conv_query: float32 [6, 128], P('groups'), parts along dimension 0
- grad_conv_key: float32 [6, 128], P('groups'), parts along dimension 0
- grad_conv_value: float32 [6, 1024], P('groups'), parts along dimension 0
- grad_gain: float32 [2048], P('groups'), parts along dimension 0
There are 2 independent parts, one for each index of `groups`. A program takes and returns all parts, laid end to end along the dimension named above; an argument that names none is the same for every part. Nothing has to cross between parts.
All inputs are finite; a program needn't handle non-finite values.
Results may differ from a plain program's by a relative error of at most 0.0088.
Values may be sent and summed in bfloat16 or wider, within the bound.
No kernel may reach another device: no remote copies, remote signals or barrier semaphores. Data moves between devices by JAX's collectives and lax.ppermute only.
A program may use at most 192 MiB of HBM per device.

v0:
```python
from functools import reduce

import jax
import jax.numpy as jnp
from jax import lax
from jax.sharding import PartitionSpec as P

HEADS = 8
FEAT = 16
HEAD_DIM = 128
BLOCK = 512


EPSILON = 1e-06


def from_behind(block, axis, distance):
    devices = range(lax.axis_size(axis))
    route = [(i - distance, i) for i in devices if i - distance in devices]
    return lax.ppermute(block, axis, route)


def entering(value, axis, combine, identity, reverse):
    count, here = (lax.axis_size(axis), lax.axis_index(axis))
    everything = jax.tree.map(lambda part: lax.all_gather(part, axis), value)
    start = jax.tree.map(
        lambda part, zero: jnp.broadcast_to(jnp.asarray(zero, part.dtype), part.shape),
        value,
        identity,
    )

    def hop(k, before):
        at = count - 1 - k if reverse else k
        reached = at > here if reverse else at < here
        new = combine(before, jax.tree.map(lambda part: part[at], everything))
        return jax.tree.map(lambda a, b: jnp.where(reached, a, b), new, before)

    return lax.fori_loop(0, count, hop, start)


def add_states(earlier, later):
    return jax.tree.map(jnp.add, earlier, later)


def conv_apply(wide, taps, rows):
    total = jnp.zeros((rows, wide.shape[1]), jnp.float32)
    for offset in range(taps.shape[0]):
        total = total + taps[offset] * wide[offset : offset + rows]
    return total


def conv_grads(wide, taps, grad, follow):
    rows = grad.shape[0]
    margin = taps.shape[0] - 1
    grad_wide = jnp.concatenate([grad, follow], axis=0)
    grad_signal = jnp.zeros(grad.shape, jnp.float32)
    for offset in range(taps.shape[0]):
        grad_signal = (
            grad_signal + taps[offset] * grad_wide[margin - offset : margin - offset + rows]
        )
    grad_taps = jnp.stack(
        [jnp.sum(grad * wide[offset : offset + rows], axis=0) for offset in range(taps.shape[0])]
    )
    return (grad_signal, grad_taps)


def feature_maps(points):
    heads, feature, rows = points.shape
    wide = points.astype(jnp.float32)
    linear = (wide * feature ** (-0.25)).astype(jnp.bfloat16)
    square = wide[:, :, None, :] * wide[:, None, :, :] * (0.5 / feature) ** 0.5
    return (linear, square.reshape(heads, feature * feature, rows).astype(jnp.bfloat16))


def block_states(linear, square, values):
    return (
        jnp.sum(values.astype(jnp.float32), axis=0),
        jnp.einsum("hfs,shd->hfd", linear, values, preferred_element_type=jnp.float32),
        jnp.einsum("hgs,shd->hgd", square, values, preferred_element_type=jnp.float32),
    )


def carried_values(linear, square, state):
    first = state[1].astype(jnp.bfloat16)
    second = state[2].astype(jnp.bfloat16)
    return (
        state[0][None]
        + jnp.einsum("hft,hfd->thd", linear, first, preferred_element_type=jnp.float32)
        + jnp.einsum("hgt,hgd->thd", square, second, preferred_element_type=jnp.float32)
    )


def kernel_block(query_block, key_block):
    feature = query_block.shape[1]
    length = query_block.shape[2]
    sigma = jnp.einsum("hft,hfs->hts", query_block, key_block, preferred_element_type=jnp.float32)
    weight = 1.0 + sigma * feature ** (-0.5) + sigma * sigma * (0.5 / feature)
    causal = lax.broadcasted_iota(jnp.int32, (length, length), 0) >= lax.broadcasted_iota(
        jnp.int32, (length, length), 1
    )
    return (sigma, causal, jnp.where(causal[None], weight, 0.0).astype(jnp.bfloat16))


def numerator(query_block, key_block, value_block, prefix):
    sigma, causal, weights = kernel_block(query_block, key_block)
    local = jnp.einsum("hts,shd->thd", weights, value_block, preferred_element_type=jnp.float32)
    linear, square = feature_maps(query_block)
    return (local + carried_values(linear, square, prefix), linear, square)


def norm_pass(summed, gain, grad_block):
    scale = lax.rsqrt(jnp.mean(summed * summed, axis=-1, keepdims=True) + EPSILON)
    normal = summed * scale
    output = (normal * gain).astype(jnp.bfloat16)
    incoming = grad_block.astype(jnp.float32)
    upstream = incoming * gain
    grad_sum = scale * (upstream - normal * jnp.mean(normal * upstream, axis=-1, keepdims=True))
    return (output, grad_sum.astype(jnp.bfloat16), jnp.sum(incoming * normal, axis=0))


def feature_grad(point, vector, state):
    heads, feature, rows = point.shape
    first = state[1].astype(jnp.bfloat16)
    second = state[2].astype(jnp.bfloat16)
    linear_grad = jnp.einsum("nhd,hfd->hfn", vector, first, preferred_element_type=jnp.float32)
    quadratic = jnp.einsum("nhd,hgd->hgn", vector, second, preferred_element_type=jnp.float32)
    quadratic = quadratic.reshape(heads, feature, feature, rows)
    wide = point.astype(jnp.float32)
    crossed = jnp.sum(
        (quadratic + jnp.transpose(quadratic, (0, 2, 1, 3))) * wide[:, None, :, :], axis=2
    )
    return linear_grad * feature ** (-0.25) + crossed * (0.5 / feature) ** 0.5


def backward_block(query_block, key_block, value_block, prefix, grad_sum, later):
    feature = query_block.shape[1]
    sigma, causal, weights = kernel_block(query_block, key_block)
    grad_weights = jnp.einsum(
        "thd,shd->hts", grad_sum, value_block, preferred_element_type=jnp.float32
    )
    grad_sigma = jnp.where(
        causal[None], grad_weights * (feature ** (-0.5) + sigma / feature), 0.0
    ).astype(jnp.bfloat16)
    key_linear, key_square = feature_maps(key_block)
    grad_query = jnp.einsum(
        "hts,hfs->hft", grad_sigma, key_block, preferred_element_type=jnp.float32
    ) + feature_grad(query_block, grad_sum, prefix)
    grad_key = jnp.einsum(
        "hts,hft->hfs", grad_sigma, query_block, preferred_element_type=jnp.float32
    ) + feature_grad(key_block, value_block, later)
    grad_value = jnp.einsum(
        "hts,thd->shd", weights, grad_sum, preferred_element_type=jnp.float32
    ) + carried_values(key_linear, key_square, later)
    return (grad_query, grad_key, grad_value)


def heads_first(flat, rows):
    return flat.reshape(rows, HEADS, FEAT).transpose(1, 2, 0)


def shards(query_in, key_in, value_in, conv_query, conv_key, conv_value, norm_gain, grad_out):
    rows = query_in.shape[0]
    margin = conv_query.shape[0] - 1
    count = rows // BLOCK
    total_rows = rows * lax.axis_size("seq")
    rims = from_behind(
        (query_in[rows - margin :], key_in[rows - margin :], value_in[rows - margin :]), "seq", 1
    )
    query_wide = jnp.concatenate([rims[0], query_in], axis=0).astype(jnp.float32)
    key_wide = jnp.concatenate([rims[1], key_in], axis=0).astype(jnp.float32)
    value_wide = jnp.concatenate([rims[2], value_in], axis=0).astype(jnp.float32)
    query_round = heads_first(conv_apply(query_wide, conv_query, rows).astype(jnp.bfloat16), rows)
    key_round = heads_first(conv_apply(key_wide, conv_key, rows).astype(jnp.bfloat16), rows)
    value_round = (
        conv_apply(value_wide, conv_value, rows)
        .astype(jnp.bfloat16)
        .reshape(count, BLOCK, HEADS, HEAD_DIM)
    )
    gain = norm_gain.reshape(HEADS, HEAD_DIM)
    grad_rows = grad_out.reshape(count, BLOCK, HEADS, HEAD_DIM)

    def query_part():
        return query_round

    def key_part():
        return key_round

    index = 0
    linear, square = feature_maps(key_part())
    key_states = [block_states(linear, square, value_round[index])]
    device_total = reduce(add_states, key_states)
    earlier = entering(
        device_total, "seq", add_states, jax.tree.map(jnp.zeros_like, device_total), False
    )
    running = earlier
    gain_sum = jnp.zeros((HEADS, HEAD_DIM), jnp.float32)
    index = 0
    prefixes = [running]
    summed, linear, square = numerator(query_part(), key_part(), value_round[index], running)
    output, grad_sum, gain_part = norm_pass(summed, gain, grad_rows[index])
    grad_sums = [grad_sum]
    gain_sum = gain_sum + gain_part
    grad_states = [block_states(linear, square, grad_sum)]
    grad_total = reduce(add_states, grad_states)
    later = entering(grad_total, "seq", add_states, jax.tree.map(jnp.zeros_like, grad_total), True)
    results = [None] * count
    running = later
    for index in reversed(range(count)):
        results[index] = backward_block(
            query_part(), key_part(), value_round[index], prefixes[index], grad_sums[index], running
        )
        running = add_states(running, grad_states[index])
    grad_query_conv = (
        jnp.concatenate([result[0] for result in results], axis=2)
        .transpose(2, 0, 1)
        .reshape(rows, HEADS * FEAT)
    )
    grad_key_conv = (
        jnp.concatenate([result[1] for result in results], axis=2)
        .transpose(2, 0, 1)
        .reshape(rows, HEADS * FEAT)
    )
    grad_value_conv = jnp.concatenate([result[2] for result in results], axis=0).reshape(
        rows, HEADS * HEAD_DIM
    )
    follow = from_behind(
        (grad_query_conv[:margin], grad_key_conv[:margin], grad_value_conv[:margin]), "seq", -1
    )
    grad_query, taps_query = conv_grads(query_wide, conv_query, grad_query_conv, follow[0])
    grad_key, taps_key = conv_grads(key_wide, conv_key, grad_key_conv, follow[1])
    grad_value, taps_value = conv_grads(value_wide, conv_value, grad_value_conv, follow[2])
    sums = lax.psum((taps_query, taps_key, taps_value, gain_sum.reshape(HEADS * HEAD_DIM)), "seq")
    factor = total_rows ** (-0.5)
    return (
        output.reshape(rows, HEADS * HEAD_DIM),
        grad_query.astype(jnp.bfloat16),
        grad_key.astype(jnp.bfloat16),
        grad_value.astype(jnp.bfloat16),
        sums[0] * factor,
        sums[1] * factor,
        sums[2] * factor,
        sums[3] * factor,
    )


def solution(mesh):
    placed = (
        P(("groups", "seq"), None),
        P(("groups", "seq"), None),
        P(("groups", "seq"), None),
        P(),
        P(),
        P(),
        P(),
        P(("groups", "seq"), None),
    )
    return jax.shard_map(
        shards,
        mesh=mesh,
        in_specs=placed,
        out_specs=(
            P(("groups", "seq"), None),
            P(("groups", "seq"), None),
            P(("groups", "seq"), None),
            P(("groups", "seq"), None),
            P("groups", None),
            P("groups", None),
            P("groups", None),
            P("groups"),
        ),
        check_vma=False,
    )
```

profile of v0, /device:TPU:0, one launch (start us, length us, event | category | flops | bytes accessed | tf_op | source)
XLA Modules:
  0.0 556.1 jit_solution(295418018309457341)
XLA Ops:
  8.0 2.3 collective-permute-start.2
  11.1 4.5 collective-permute-start
  24.9 1.7 fusion.19
  27.9 2.5 collective-permute-start.1
  31.2 2.6 copy.59
  36.2 1.7 copy.53
  38.9 2.0 multiply_convert_fusion
  42.2 21.1 %all_gather.37 = f32[16,8,128]{2,1,0:T(8,128)} all-gather(f32[1,8,128]{2,1,0:T(8,128)S(1)} %bitcast.193), channel_id=1, replica_groups=mesh['groups'=2,'seq'=16] {'seq'}, dimensions={0}, use_global_device_ids=true | all-gather | bytes 69632 | tf_op jit(solution)/shard_map/all_gather | solution.py:25
  63.4 3.5 fusion.13
  66.9 121.4 %all-gather.12.cloned.1.call-done = f32[128,256,128]{2,1,0:T(8,128)} async-done(((f32[8,256,128]{2,1,0:T(8,128)}), f32[128,256,128]{2,1,0:T(8,128)}) %all-gather.12.cloned.1.call-update) | async-done | bytes 16777232 | tf_op jit(solution)/shard_map/all_gather | solution.py:25
  188.3 50.6 %while.38 = (s32[]{:T(128)}, f32[8,128]{1,0:T(8,128)S(1)}, f32[8,16,128]{2,1,0:T(8,128)S(1)}, f32[8,256,128]{2,1,0:T(8,128)S(1)}, s32[]{:T(128)}, /*index=5*/f32...) while((s32[]{:T(128)}, f32[8,128]{1,0:T(8,128)S(1)}, ...), condition=%wide.region_2.3_spmd.clone, body=%wide.region_1.2_spmd.clone.sunk | while | flops 838660 | bytes 3354769 | solution.py:38
  189.8 1.6 add_select_fusion.14
  193.0 1.6 add_select_fusion.14
  199.3 1.6 add_select_fusion.14
  205.6 1.6 add_select_fusion.14
  208.8 1.6 add_select_fusion.14
  212.0 1.6 add_select_fusion.14
  215.1 1.6 add_select_fusion.14
  218.3 1.6 add_select_fusion.14
  221.5 1.6 add_select_fusion.14
  227.8 1.6 add_select_fusion.14
  230.9 1.6 add_select_fusion.14
  234.1 1.6 add_select_fusion.14
  237.3 1.6 add_select_fusion.14
  238.9 2.5 fusion.46
  243.9 1.7 multiply_convert_fusion.2
  246.8 3.3 fusion.60
  250.1 2.0 fusion.44
  252.1 3.6 fusion.3
  256.0 4.6 select_convert_fusion
  267.0 6.9 %fusion.57 = f32[8,128,512]{2,1,0:T(8,128)} fusion(bf16[512,8,128]{0,2,1:T(8,128)(2,1)S(1)} %get-tuple-element.474, f32[8,512,512]{2,1,0:T(8,128)} %copy-done.4, pred[512,512]{1,0:T(8,128)(4,1)} %iota_compare_fusion), kind=kOutput, calls=%fused_computation.127 | convolution fusion | flops 551550976 | bytes 11796480 | tf_op jit(solution)/shard_map/hts,thd->shd/dot_general | solution.py:151
  273.9 22.2 %all-gather.2 = f32[128,128]{1,0:T(8,128)} all-gather(f32[8,128]{1,0:T(8,128)S(1)} %convert_reduce_fusion), channel_id=4, replica_groups=mesh['groups'=2,'seq'=16] {'seq'}, dimensions={0}, use_global_device_ids=true | all-gather | bytes 69632 | tf_op jit(solution)/shard_map/all_gather | solution.py:25
  296.1 2.3 copy.89
  298.4 1.8 copy.66
  300.2 2.3 multiply_reduce_fusion.10
  302.5 108.1 %all-gather.16.cloned.1.call-done = f32[128,256,128]{2,1,0:T(8,128)} async-done(((f32[8,256,128]{2,1,0:T(8,128)}), f32[128,256,128]{2,1,0:T(8,128)}) %all-gather.16.cloned.1.call-update) | async-done | bytes 16777232 | tf_op jit(solution)/shard_map/all_gather | solution.py:25
  410.7 50.6 %while.39 = (s32[]{:T(128)}, f32[8,128]{1,0:T(8,128)S(1)}, f32[8,16,128]{2,1,0:T(8,128)S(1)}, f32[8,256,128]{2,1,0:T(8,128)S(1)}, s32[]{:T(128)}, /*index=5*/f32...) while((s32[]{:T(128)}, f32[8,128]{1,0:T(8,128)S(1)}, ...), condition=%wide.region_8.9_spmd.clone, body=%wide.region_7.8_spmd.clone.sunk | while | flops 838664 | bytes 3354831 | solution.py:38
  412.2 1.6 add_select_fusion.17
  415.4 1.6 add_select_fusion.17
  418.6 1.6 add_select_fusion.17
  421.7 1.6 add_select_fusion.17
  431.2 1.6 add_select_fusion.17
  461.3 3.5 fusion.41
  465.8 3.6 fusion.1
  471.9 2.7 add_add_fusion
  477.6 2.9 copy.78
  481.5 4.7 multiply_reduce_fusion.3
  486.2 61.6 %all-reduce = (f32[3,128]{1,0:T(4,128)S(1)}, f32[3,128]{1,0:T(4,128)S(1)}, f32[3,1024]{1,0:T(4,128)S(1)}, f32[1024]{0:T(1024)S(1)}) all-reduce(f32[3,128]{1,0:T(4,128)S(1)} %pad_maximum_fusion.4, f32[3,128]{1,0:T(4,128)S(1)} %pad_maximum_fusion.5, ...), channel_id=1, replica_groups=mesh['groups'=2,'seq'=16] {'seq'}, use_global_device_ids=true, to_apply=%region_13.14 | all-reduce | flops 4864 | bytes 38912 | tf_op jit(solution)/shard_map/psum | solution.py:232
  (213 shorter events, 108.5 us)
Async XLA Ops:
  7.2 11.9 %copy-start.28 = (bf16[512,1024]{1,0:T(8,128)(2,1)S(1)}, bf16[512,1024]{1,0:T(8,128)(2,1)}, u32[]{:S(2)}) copy-start(bf16[512,1024]{1,0:T(8,128)(2,1)} %param.14) | copy-start | bytes 3145732
  7.2 59.7 %all-gather.10.cloned.1.call-start = ((), (), s32[]{:S(2)}) async-start(), calls=%async_computation | async-start | bytes 1114112 | tf_op jit(solution)/shard_map/all_gather | solution.py:25
  8.0 9.3 %collective-permute-start.2 = (bf16[2,128]{1,0:T(2,128)(2,1)S(1)}, bf16[2,128]{1,0:T(2,128)(2,1)S(1)}, u32[]{:S(2)}, u32[]{:S(2)}) collective-permute-start(bf16[2,128]{1,0:T(2,128)(2,1)S(1)} %slice.132), channel_id=1, source_target_pairs={{0,1},{1,2},{2,3},{3,4},{4,5},{5,6},{6,7},{7,8},{8,9},{9,10},{10,1... | collective-permute-start | bytes 1544 | tf_op jit(solution)/shard_map/ppermute | solution.py:20
  11.1 8.0 %collective-permute-start = (bf16[2,1024]{1,0:T(2,128)(2,1)S(1)}, bf16[2,1024]{1,0:T(2,128)(2,1)S(1)}, u32[]{:S(2)}, u32[]{:S(2)}) collective-permute-start(bf16[2,1024]{1,0:T(2,128)(2,1)S(1)} %slice.118), channel_id=1, source_target_pairs={{0,1},{1,2},{2,3},{3,4},{4,5},{5,6},{6,7},{7,8},{8,9},{9,10},{10,1... | collective-permute-start | bytes 12296 | tf_op jit(solution)/shard_map/ppermute | solution.py:20
  19.4 0.9 copy-start.20
  20.1 3.5 copy-start.6
  21.2 167.0 %all-gather.12.cloned.1.call-start = ((), (), s32[]{:S(2)}) async-start(), calls=%async_computation.1 | async-start | bytes 17825792 | tf_op jit(solution)/shard_map/all_gather | solution.py:25
  22.2 0.7 copy-start.16
  23.6 1.3 copy-start.10
  24.9 6.3 %copy-start.32 = (f32[3,128]{1,0:T(4,128)S(1)}, f32[3,128]{1,0:T(4,128)}, u32[]{:S(2)}) copy-start(f32[3,128]{1,0:T(4,128)} %param.15) | copy-start | bytes 4612
  26.6 275.9 %all-gather.14.cloned.1.call-start = ((), (), s32[]{:S(2)}) async-start(), calls=%async_computation.2 | async-start | bytes 1114112 | tf_op jit(solution)/shard_map/all_gather | solution.py:25
  27.9 5.9 %collective-permute-start.1 = (bf16[2,128]{1,0:T(2,128)(2,1)}, bf16[2,128]{1,0:T(2,128)(2,1)}, u32[]{:S(2)}, u32[]{:S(2)}) collective-permute-start(bf16[2,128]{1,0:T(2,128)(2,1)} %slice.125), channel_id=1, source_target_pairs={{0,1},{1,2},{2,3},{3,4},{4,5},{5,6},{6,7},{7,8},{8,9},{9,10},{10,1... | collective-permute-start | bytes 1544 | tf_op jit(solution)/shard_map/ppermute | solution.py:20
  34.7 0.7 copy-start.11
  37.9 3.0 copy-start.13
  37.9 3.0 copy-start.21
  38.9 3.3 copy-start.18
  40.9 22.5 %copy-start.7 = (bf16[512,1024]{1,0:T(8,128)(2,1)S(1)}, bf16[512,1024]{1,0:T(8,128)(2,1)}, u32[]{:S(2)}) copy-start(bf16[512,1024]{1,0:T(8,128)(2,1)} %copy-done.6) | copy-start | bytes 3145732
  40.9 22.5 %copy-start.29 = (pred[512,512]{1,0:T(8,128)(4,1)S(1)}, pred[512,512]{1,0:T(8,128)(4,1)}, u32[]{:S(2)}) copy-start(pred[512,512]{1,0:T(8,128)(4,1)} %iota_compare_fusion) | copy-start | bytes 786436
  42.2 21.2 %copy-start.4 = (f32[8,512,512]{2,1,0:T(8,128)}, f32[8,512,512]{2,1,0:T(8,128)S(1)}, u32[]{:S(2)}) copy-start(f32[8,512,512]{2,1,0:T(8,128)S(1)} %fusion.59) | copy-start | bytes 25165828
  238.9 2.6 copy-start.1
  238.9 2.6 copy-start.24
  238.9 2.6 copy-start.14
  238.9 2.7 copy-start.26
  241.6 1.6 copy-start.5
  241.6 1.6 copy-start.31
  246.5 164.1 %all-gather.16.cloned.1.call-start = ((), (), s32[]{:S(2)}) async-start(), calls=%async_computation.3 | async-start | bytes 17825792 | tf_op jit(solution)/shard_map/all_gather | solution.py:25
  250.1 2.0 copy-start.19
  252.1 3.7 copy-start.25
  252.1 3.9 copy-start.8
  252.1 3.9 copy-start.30
  256.0 4.6 copy-start.22
  260.7 2.0 copy-start.2
  262.6 0.7 copy-start.27
  265.5 34.8 %collective-permute-start.3 = (f32[2,128]{1,0:T(2,128)}, f32[2,128]{1,0:T(2,128)}, u32[]{:S(2)}, u32[]{:S(2)}) collective-permute-start(f32[2,128]{1,0:T(2,128)} %copy.65), channel_id=1, source_target_pairs={{1,0},{2,1},{3,2},{4,3},{5,4},{6,5},{7,6},{8,7},{9,8},{10,9},{11,1... | collective-permute-start | bytes 3080 | tf_op jit(solution)/shard_map/ppermute | solution.py:20
  273.9 136.8 %copy-start = (f32[8,256,128]{2,1,0:T(8,128)S(1)}, f32[8,256,128]{2,1,0:T(8,128)}, u32[]{:S(2)}) copy-start(f32[8,256,128]{2,1,0:T(8,128)} %custom-call.5) | copy-start | bytes 3145732
  461.3 3.5 copy-start.9
  464.9 1.0 copy-start.17
  465.8 4.0 copy-start.3
  465.8 4.0 copy-start.15
  469.9 2.1 copy-start.23
  470.6 10.0 %collective-permute-start.4 = (f32[2,128]{1,0:T(2,128)S(1)}, f32[2,128]{1,0:T(2,128)S(1)}, u32[]{:S(2)}, u32[]{:S(2)}) collective-permute-start(f32[2,128]{1,0:T(2,128)S(1)} %copy.73), channel_id=1, source_target_pairs={{1,0},{2,1},{3,2},{4,3},{5,4},{6,5},{7,6},{8,7},{9,8},{10,9},{11,1... | collective-permute-start | bytes 3080 | tf_op jit(solution)/shard_map/ppermute | solution.py:20
  474.7 1.3 copy-start.12
  476.3 5.2 collective-permute-start.5
Sparse Core Ops, SparseCore 0:
  21.4 38.2 all-gather.9
  62.4 125.8 all-gather.11
  246.7 36.1 all-gather.13
  284.8 125.7 all-gather.15
where the time goes:
time: 561 us; the launch traced here: 556 us
  waiting for transfers between devices  230 us (41%)
  other arithmetic  129 us (23%)
  blocking collectives  105 us (19%)
  matrix products  37.9 us (7%)
  local copies, waits for them, and re-layouts  25.8 us (5%)
  between operations  14.3 us (3%)
  starting transfers between devices  13.6 us (2%)
    all_gather x4, waiting for transfers between devices, entering(): everything = jax.tree.map(lambda part: lax.all_gather(part, axis), value)  230 us
    select_n x96, other arithmetic, hop(): return jax.tree.map(lambda a, b: jnp.where(reached, a, b), new, before)  100 us
    psum x1, blocking collectives, shards(): lax.psum((taps_query, taps_key, taps_value, gain_sum.reshape(HEADS * HEAD...  61.6 us
    all_gather x2, blocking collectives, entering(): everything = jax.tree.map(lambda part: lax.all_gather(part, axis), value)  43.4 us
    ppermute x6, starting transfers between devices, from_behind(): return lax.ppermute(block, axis, route)  13.2 us
  transfers between devices with their start and end apart: 10, of which 2 were waited for; matrix products, arithmetic and copies ran while one was open for 11% of the time, Pallas kernels for 0%

commit v1 on v0

v1 whole, which is shorter than its diff:
```python
import functools

import jax
import jax.numpy as jnp
from jax import lax
from jax.experimental import pallas as pl
from jax.experimental.pallas import tpu as pltpu
from jax.sharding import PartitionSpec as P

HEADS = 8
HALF = HEADS // 2
FEAT = 16
DIM = 128
EPSILON = 1e-06
LANES = HEADS * FEAT
WIDE = HEADS * DIM
ALL = 2 * LANES + WIDE
ROWS = 160
LIN = 128
TAIL = 144
RIM = 16
STEP = 128
F32 = jnp.float32
BF16 = jnp.bfloat16

NN = (((1,), (0,)), ((), ()))
NT = (((1,), (1,)), ((), ()))
TN = (((0,), (0,)), ((), ()))


def dot(a, b, dims):
    return lax.dot_general(a, b, dims, preferred_element_type=F32)


def head_rows(h):
    return slice(h * FEAT, (h + 1) * FEAT)


def head_lanes(h):
    return slice(h * DIM, (h + 1) * DIM)


def conv(wide_ref, taps, rows):
    margin = taps.shape[0] - 1
    total = taps[0:1] * wide_ref[RIM - margin : RIM - margin + rows]
    for o in range(1, margin + 1):
        total = total + taps[o : o + 1] * wide_ref[RIM - margin + o : RIM - margin + o + rows]
    return total


def tap_sums(grad, wide_ref, taps):
    rows = grad.shape[0]
    start = RIM - (taps - 1)
    return [
        jnp.sum(grad * wide_ref[start + o : start + o + rows], axis=0, keepdims=True)
        for o in range(taps)
    ]


def turned(x, shift):
    return x if shift % FEAT == 0 else pltpu.roll(x, shift % FEAT, 0)


def features(x):
    half = (0.5 / FEAT) ** 0.5
    pieces = [(x * turned(x, FEAT - d) * half).astype(BF16) for d in range(8)]
    pieces.append((x * FEAT ** (-0.25)).astype(BF16))
    rows = lax.broadcasted_iota(jnp.int32, (8, x.shape[1]), 0)
    one = jnp.where(rows == 0, 1.0, 0.0).astype(F32)
    pieces.append(jnp.concatenate([x[:8] * x[8:] * half, one], axis=0).astype(BF16))
    return jnp.concatenate(pieces, axis=0)


def feature_grad(x, state, vector):
    g = dot(state, vector, NT)
    crossed = 2.0 * g[0:FEAT] * x
    for d in range(1, 8):
        part = g[d * FEAT : (d + 1) * FEAT]
        crossed = crossed + part * turned(x, FEAT - d) + turned(part * x, d)
    part = g[TAIL : TAIL + 8]
    crossed = crossed + jnp.concatenate([part * x[8:], part * x[:8]], axis=0)
    return g[LIN:TAIL] * FEAT ** (-0.25) + crossed * (0.5 / FEAT) ** 0.5


def gather_state(own_ref, other_ref, state_ref):
    core = lax.rem(lax.axis_index("seq"), 2)
    rows = lax.broadcasted_iota(jnp.int32, (ROWS, DIM), 0)
    pair = ((rows >= FEAT) & (rows < LIN)) | ((rows >= TAIL) & (rows < TAIL + 8))
    weight = jnp.where(pair, 2.0, 1.0).astype(F32)
    for g in range(HALF):
        state_ref[core * HALF + g] = (own_ref[g].astype(F32) * weight).astype(BF16)
        state_ref[(1 - core) * HALF + g] = (other_ref[g].astype(F32) * weight).astype(BF16)


def hand_out(state_ref, keep_ref, send_ref):
    core = lax.rem(lax.axis_index("seq"), 2)
    keep_ref[...] = state_ref[pl.ds(core * HALF, HALF)]
    send_ref[...] = state_ref[pl.ds((1 - core) * HALF, HALF)]


def head_mask(h):
    lanes = lax.broadcasted_iota(jnp.int32, (1, LANES), 1)
    return jnp.where(lanes // FEAT == h, 1.0, 0.0).astype(F32).astype(BF16)


def key_kernel(key, value, rim, taps_k, taps_v, v_out, k_out, kt_out, fk_out, keep, send, wide, state):
    rows = key.shape[0]
    wide[0:RIM] = rim[:, LANES : 2 * LANES].astype(F32)
    wide[RIM : RIM + rows] = key[...].astype(F32)
    k = conv(wide, taps_k[...], rows).astype(BF16)
    k_out[...] = k
    kt = k.astype(F32).T
    kt_out[...] = kt.astype(BF16)
    for h in range(HEADS):
        f = features(kt[head_rows(h)])
        fk_out[h] = f
        wide[0:RIM] = rim[:, 2 * LANES + h * DIM : 2 * LANES + (h + 1) * DIM].astype(F32)
        wide[RIM : RIM + rows] = value[:, head_lanes(h)].astype(F32)
        v = conv(wide, taps_v[:, head_lanes(h)], rows).astype(BF16)
        v_out[:, head_lanes(h)] = v
        state[h] = dot(f, v, NN).astype(BF16)
    hand_out(state, keep, send)


def query_kernel(query, rim, taps_q, q_out, qt_out, fq_out, wide):
    rows = query.shape[0]
    wide[0:RIM] = rim[:, 0:LANES].astype(F32)
    wide[RIM : RIM + rows] = query[...].astype(F32)
    q = conv(wide, taps_q[...], rows).astype(BF16)
    q_out[...] = q
    qt = q.astype(F32).T
    qt_out[...] = qt.astype(BF16)
    for h in range(HEADS):
        fq_out[h] = features(qt[head_rows(h)])


def local_kernel(first, q_ref, k_ref, v_ref, out):
    rows = q_ref.shape[0]
    quarter = q_ref[...] * jnp.asarray(FEAT ** (-0.5), BF16)
    for g in range(HALF):
        qs = quarter * head_mask(first + g)
        for start in range(0, rows, STEP):
            stop = start + STEP
            t = dot(qs[start:stop], k_ref[0:stop], NT)
            w = (0.5 * t + 1.0) * t + 1.0
            at = lax.broadcasted_iota(jnp.int32, (STEP, stop), 0) + start
            w = jnp.where(at >= lax.broadcasted_iota(jnp.int32, (STEP, stop), 1), w, 0.0)
            out[start:stop, head_lanes(g)] = dot(
                w.astype(BF16), v_ref[0:stop, head_lanes(first + g)], NN
            )


def norm_kernel(low, high, fq, own, other, grad, gain, out, gs_out, keep, send, gain_out, pre, state):
    gather_state(own, other, pre)
    for h in range(HEADS):
        f = fq[h]
        local = (low if h < HALF else high)[:, head_lanes(h % HALF)]
        summed = local + dot(f, pre[h], TN)
        scale = lax.rsqrt(jnp.mean(summed * summed, axis=-1, keepdims=True) + EPSILON)
        normal = summed * scale
        weight = gain[h : h + 1]
        out[:, head_lanes(h)] = (normal * weight).astype(BF16)
        incoming = grad[:, head_lanes(h)].astype(F32)
        gain_out[h : h + 1] = jnp.sum(incoming * normal, axis=0, keepdims=True)
        upstream = incoming * weight
        gs = scale * (upstream - normal * jnp.mean(normal * upstream, axis=-1, keepdims=True))
        gs = gs.astype(BF16)
        gs_out[:, head_lanes(h)] = gs
        state[h] = dot(f, gs, NN).astype(BF16)
    hand_out(state, keep, send)


def back_kernel(first, q_ref, k_ref, qt_ref, kt_ref, v_ref, gs_ref, gv_out, gq_out, gk_out):
    rows = q_ref.shape[0]
    quarter = q_ref[...] * jnp.asarray(FEAT ** (-0.5), BF16)
    for g in range(HALF):
        h = first + g
        ks = k_ref[...] * head_mask(h)
        qt = qt_ref[head_rows(h)]
        kt = kt_ref[head_rows(h)]
        for start in range(0, rows, STEP):
            stop = start + STEP
            shape = (STEP, rows - start)
            t = dot(ks[start:stop], quarter[start:], NT)
            seen = lax.broadcasted_iota(jnp.int32, shape, 1) >= lax.broadcasted_iota(jnp.int32, shape, 0)
            w = jnp.where(seen, (0.5 * t + 1.0) * t + 1.0, 0.0).astype(BF16)
            gs = gs_ref[start:, head_lanes(h)]
            gv_out[start:stop, head_lanes(g)] = dot(w, gs, NN)
            gw = dot(v_ref[start:stop, head_lanes(h)], gs, NT)
            s = jnp.where(seen, gw * (FEAT ** (-0.5) + FEAT ** (-0.5) * t), 0.0).astype(BF16)
            part = dot(kt[:, start:stop], s, NN)
            if start == 0:
                gq_out[head_rows(g)] = part
            else:
                gq_out[head_rows(g), start:] += part
            gk_out[head_rows(g), start:stop] = dot(qt[:, start:], s, NT)


def query_grad_kernel(query, rim, qt_ref, gs_ref, own, other, low, high, taps_q, g_out, sums, wide, pre):
    rows = query.shape[0]
    gather_state(own, other, pre)
    pieces = []
    for h in range(HEADS):
        local = (low if h < HALF else high)[head_rows(h % HALF)]
        pieces.append(
            local + feature_grad(qt_ref[head_rows(h)].astype(F32), pre[h], gs_ref[:, head_lanes(h)])
        )
    grad = jnp.concatenate(pieces, axis=0).T
    g_out[...] = grad
    wide[0:RIM] = rim[:, 0:LANES].astype(F32)
    wide[RIM : RIM + rows] = query[...].astype(F32)
    for o, row in enumerate(tap_sums(grad, wide, taps_q.shape[0])):
        sums[o : o + 1] = row


def later_kernel(
    key, value, rim, kt_ref, fk, v_ref, own, other, gv_low, gv_high, gk_low, gk_high, gq, sums_q, gain_sum,
    gv_out, gk_out, head_out, sums, wide, post,
):
    rows = key.shape[0]
    taps = sums_q.shape[0]
    gather_state(own, other, post)
    pieces = []
    head_out[:, 0:LANES] = gq[...]
    sums[0:taps, 0:LANES] = sums_q[...]
    sums[taps : taps + 1, 0 : 2 * LANES] = jnp.zeros((1, 2 * LANES), F32)
    for h in range(HEADS):
        local = (gk_low if h < HALF else gk_high)[head_rows(h % HALF)]
        pieces.append(
            local + feature_grad(kt_ref[head_rows(h)].astype(F32), post[h], v_ref[:, head_lanes(h)])
        )
        local = (gv_low if h < HALF else gv_high)[:, head_lanes(h % HALF)]
        grad = local + dot(fk[h], post[h], TN)
        gv_out[:, head_lanes(h)] = grad
        place = slice(2 * LANES + h * DIM, 2 * LANES + (h + 1) * DIM)
        head_out[:, place] = grad[0:8]
        wide[0:RIM] = rim[:, place].astype(F32)
        wide[RIM : RIM + rows] = value[:, head_lanes(h)].astype(F32)
        for o, row in enumerate(tap_sums(grad, wide, taps)):
            sums[o : o + 1, place] = row
        sums[taps : taps + 1, place] = gain_sum[h : h + 1]
    grad = jnp.concatenate(pieces, axis=0).T
    gk_out[...] = grad
    head_out[:, LANES : 2 * LANES] = grad[0:8]
    wide[0:RIM] = rim[:, LANES : 2 * LANES].astype(F32)
    wide[RIM : RIM + rows] = key[...].astype(F32)
    for o, row in enumerate(tap_sums(grad, wide, taps)):
        sums[o : o + 1, LANES : 2 * LANES] = row


def signal_kernel(gq, gk, gv, follow, taps_q, taps_k, taps_v, q_out, k_out, v_out, wide):
    rows = gq.shape[0]
    count = taps_q.shape[0]

    def one(grad, place, taps):
        wide[0:rows] = grad
        wide[rows : rows + 8] = follow[:, place]
        total = taps[0:1] * wide[count - 1 : count - 1 + rows]
        for o in range(1, count):
            total = total + taps[o : o + 1] * wide[count - 1 - o : count - 1 - o + rows]
        return total.astype(BF16)

    q_out[...] = one(gq[...], slice(0, LANES), taps_q[...])
    k_out[...] = one(gk[...], slice(LANES, 2 * LANES), taps_k[...])
    for h in range(HEADS):
        place = slice(2 * LANES + h * DIM, 2 * LANES + (h + 1) * DIM)
        v_out[:, head_lanes(h)] = one(gv[:, head_lanes(h)], place, taps_v[:, head_lanes(h)])


def call(kernel, outs, scratch, args, flops, limit=24):
    size = lambda a: a.size * a.dtype.itemsize
    moved = sum(size(a) for a in args) + sum(size(o) for o in outs)
    return pl.pallas_call(
        kernel,
        out_shape=outs,
        scratch_shapes=scratch,
        compiler_params=pltpu.CompilerParams(vmem_limit_bytes=limit * 2**20),
        cost_estimate=pl.CostEstimate(flops=flops, bytes_accessed=moved, transcendentals=0),
    )(*args)


def exchange(x, distance):
    count = lax.axis_size("seq")
    return lax.ppermute(x, "seq", [(i, i ^ distance) for i in range(count)])


def beyond(keep, send, reverse):
    count, here = lax.axis_size("seq"), lax.axis_index("seq")

    def mine(bit):
        on = (here & bit) == 0 if reverse else (here & bit) != 0
        return jnp.where(on, 1.0, 0.0).astype(F32)

    near = exchange(send, 1)
    a, b = keep.astype(F32), near.astype(F32)
    total = a + b
    before = jnp.zeros_like(total)
    bit = 2
    while bit < count:
        got = exchange(total.astype(BF16), bit).astype(F32)
        before = before + mine(bit) * got
        total = total + got
        bit *= 2
    own = (before + mine(1) * b).astype(BF16)
    give = (before + (1.0 - mine(1)) * a).astype(BF16)
    return own, exchange(give, 1)


def shards(query_in, key_in, value_in, conv_query, conv_key, conv_value, norm_gain, grad_out):
    rows = query_in.shape[0]
    taps = conv_query.shape[0]
    count = lax.axis_size("seq")
    total_rows = rows * count
    st = jax.ShapeDtypeStruct
    half_state = st((HALF, ROWS, DIM), BF16)
    full_state = pltpu.VMEM((HEADS, ROWS, DIM), BF16)
    wide = pltpu.VMEM((RIM + rows, DIM), F32)
    gain = norm_gain.reshape(HEADS, DIM)
    state_flops = 2 * HEADS * ROWS * DIM * rows
    square_flops = 2 * HALF * rows * rows * DIM

    ends = jnp.concatenate([a[rows - RIM :] for a in (query_in, key_in, value_in)], axis=1)
    rim = lax.ppermute(ends, "seq", [(i, i + 1) for i in range(count - 1)])

    v, k, kt, fk, keep, send = call(
        key_kernel,
        [st((rows, WIDE), BF16), st((rows, LANES), BF16), st((LANES, rows), BF16), st((HEADS, ROWS, rows), BF16),
         half_state, half_state],
        [wide, full_state],
        (key_in, value_in, rim, conv_key, conv_value),
        state_flops,
    )
    q, qt, fq = call(
        query_kernel,
        [st((rows, LANES), BF16), st((LANES, rows), BF16), st((HEADS, ROWS, rows), BF16)],
        [wide],
        (query_in, rim, conv_query),
        state_flops,
    )
    local = [
        call(functools.partial(local_kernel, first), [st((rows, HALF * DIM), F32)], [], (q, k, v), 2 * square_flops)[0]
        for first in (0, HALF)
    ]
    own, other = beyond(keep, send, False)
    output, gs, keep, send, gain_sum = call(
        norm_kernel,
        [st((rows, WIDE), BF16), st((rows, WIDE), BF16), half_state, half_state, st((HEADS, DIM), F32)],
        [full_state, full_state],
        (*local, fq, own, other, grad_out, gain),
        2 * state_flops,
    )
    back = [
        call(
            functools.partial(back_kernel, first),
            [st((rows, HALF * DIM), F32), st((HALF * FEAT, rows), F32), st((HALF * FEAT, rows), F32)],
            [],
            (q, k, qt, kt, v, gs),
            4 * square_flops,
        )
        for first in (0, HALF)
    ]
    gq, sums_q = call(
        query_grad_kernel,
        [st((rows, LANES), F32), st((taps, LANES), F32)],
        [wide, full_state],
        (query_in, rim, qt, gs, own, other, back[0][1], back[1][1], conv_query),
        state_flops,
    )
    own, other = beyond(keep, send, True)
    gv, gk, heads, sums = call(
        later_kernel,
        [st((rows, WIDE), F32), st((rows, LANES), F32), st((8, ALL), F32), st((taps + 1, ALL), F32)],
        [wide, full_state],
        (key_in, value_in, rim, kt, fk, v, own, other, back[0][0], back[1][0], back[0][2], back[1][2],
         gq[0:8], sums_q, gain_sum),
        2 * state_flops,
    )
    follow = lax.ppermute(heads, "seq", [(i + 1, i) for i in range(count - 1)])
    bit = 1
    while bit < count:
        sums = sums + exchange(sums, bit)
        bit *= 2
    grad_query, grad_key, grad_value = call(
        signal_kernel,
        [st((rows, LANES), BF16), st((rows, LANES), BF16), st((rows, WIDE), BF16)],
        [pltpu.VMEM((rows + 8, DIM), F32)],
        (gq, gk, gv, follow, conv_query, conv_key, conv_value),
        state_flops,
    )
    sums = sums * total_rows ** (-0.5)
    return (
        output,
        grad_query,
        grad_key,
        grad_value,
        sums[0:taps, 0:LANES],
        sums[0:taps, LANES : 2 * LANES],
        sums[0:taps, 2 * LANES :],
        sums[taps, 2 * LANES :],
    )


def solution(mesh):
    rows = P(("groups", "seq"), None)
    return jax.shard_map(
        shards,
        mesh=mesh,
        in_specs=(rows, rows, rows, P(), P(), P(), P(), rows),
        out_specs=(rows, rows, rows, rows, P("groups", None), P("groups", None), P("groups", None), P("groups")),
        check_vma=False,
    )
```

time: 561 us -> 107 us (0.19)
  waiting for transfers between devices: 230 us -> 41.5 us
  other arithmetic: 129 us -> 3.63 us
  blocking collectives: 105 us -> 0 us
  matrix products: 37.9 us -> 0 us
  Pallas kernels: 0 us -> 26.8 us
  local copies, waits for them, and re-layouts: 25.8 us -> 10.6 us
  between operations: 14.3 us -> 0.85 us
  starting transfers between devices: 13.6 us -> 23.1 us
    all_gather x4 -> x0, waiting for transfers between devices: 230 us -> none  [entering(): everything = jax.tree.map(lambda part: lax.all_gather(part, axis), value)]
    select_n x96 -> x0, other arithmetic: 100 us -> none  [hop(): return jax.tree.map(lambda a, b: jnp.where(reached, a, b), new, before)]
    psum x1 -> x0, blocking collectives: 61.6 us -> none  [shards(): lax.psum((taps_query, taps_key, taps_value, gain_sum.reshape(HEADS * HEAD...]
    all_gather x2 -> x0, blocking collectives: 43.4 us -> none  [entering(): everything = jax.tree.map(lambda part: lax.all_gather(part, axis), value)]
    ppermute x6 -> x16, waiting for transfers between devices: 0.02 us -> 41.5 us  [the longest x14 40.7 us: exchange(): return lax.ppermute(x, 'seq', [(i, i ^ distance) for i in range(count)])]
    dot_general x18 -> x0, matrix products: 37.9 us -> none  [the longest x1 6.94 us: backward_block(): jnp.einsum('hts,thd->shd', weights, grad_sum, preferred_element_type=jnp....]
    pallas_call x0 -> x10, Pallas kernels: none -> 26.8 us  [call(): pl.pallas_call(kernel, out_shape=outs, scratch_shapes=scratch, compiler_p...]
    reduce_sum x8 -> x0, other arithmetic: 16.7 us -> none  [the longest x3 7.82 us: conv_grads(): jnp.sum(grad * wide[offset:offset + rows], axis=0)]
  transfers between devices with their start and end apart: 10 -> 16, of which waited for: 2 -> 13; matrix products, arithmetic and copies ran while one was open for 11% -> 0% of each run, Pallas kernels for 0% -> 18%
where the time goes in v1:
time: 107 us
  waiting for transfers between devices  41.5 us (39%)
  Pallas kernels  26.8 us (25%)
  starting transfers between devices  23.1 us (22%)
  local copies, waits for them, and re-layouts  10.6 us (10%)
  other arithmetic  3.63 us (3%)
    ppermute x14, waiting for transfers between devices, exchange(): return lax.ppermute(x, 'seq', [(i, i ^ distance) for i in range(count)])  40.7 us
    pallas_call x10, Pallas kernels, call(): pl.pallas_call(kernel, out_shape=outs, scratch_shapes=scratch, compiler_p...  26.8 us
    ppermute x14, starting transfers between devices, exchange(): return lax.ppermute(x, 'seq', [(i, i ^ distance) for i in range(count)])  19.5 us
    unnamed x38, local copies, waits for them, and re-layouts  6.7 us
    convert_element_type x2, other arithmetic, beyond(): give = (before + (1.0 - mine(1)) * a).astype(BF16)  2.52 us
    ppermute x1, starting transfers between devices, shards(): rim = lax.ppermute(ends, 'seq', [(i, i + 1) for i in range(count - 1)])  2.35 us
  transfers between devices with their start and end apart: 16, of which 13 were waited for; matrix products, arithmetic and copies ran while one was open for 0% of the time, Pallas kernels for 18%

profile of v1, /device:TPU:0, one launch (start us, length us, event | category | flops | bytes accessed | tf_op | source)
XLA Modules:
  0.0 106.5 jit_solution(3994298851553440926)
XLA Ops:
  0.6 0.8 slice.26
  1.4 0.7 slice.24
  2.1 0.7 slice.25
  2.8 2.3 %collective-permute-start = (bf16[16,1280]{1,0:T(8,128)(2,1)S(1)}, bf16[16,1280]{1,0:T(8,128)(2,1)S(1)}, u32[]{:S(2)}, u32[]{:S(2)}) collective-permute-start(bf16[16,1280]{1,0:T(8,128)(2,1)S(1)} %pad_maximum_fusion), channel_id=1, source_target_pairs={{0,1},{1,2},{2,3},{3,4},{4,5},{5,6},{6,7},{7,8},{8,9},{9,10},{10,1... | collective-permute-start | bytes 122888 | tf_op jit(solution)/shard_map/ppermute | solution.py:323
  5.1 0.9 collective-permute-done.rim
  6.0 1.2 %copy-done = bf16[512,1024]{1,0:T(8,128)(2,1)S(1)} copy-done((bf16[512,1024]{1,0:T(8,128)(2,1)S(1)}, bf16[512,1024]{1,0:T(8,128)(2,1)}, u32[]{:S(2)}) %copy-start) | copy-done | bytes 1048600
  7.2 0.9 copy-done.6
  8.1 0.7 copy-done.9
  8.8 0.7 copy-done.12
  9.5 1.5 %shard_map.144 = (bf16[512,1024]{1,0:T(8,128)(2,1)S(1)}, bf16[512,128]{1,0:T(8,128)(2,1)S(1)}, bf16[128,512]{1,0:T(8,128)(2,1)S(1)}, bf16[8,160,512]{2,1,0:T(8,1...) custom-call(bf16[512,128]{1,0:T(8,128)(2,1)S(1)} %copy-done.6, ...), custom_call_target="tpu_custom_call" | custom-call | flops 167772160 | bytes 4183552 | tf_op jit(solution)/shard_map/pallas_call | solution.py:273
  11.0 2.9 %collective-permute-start.1 = (bf16[4,160,128]{2,1,0:T(8,128)(2,1)S(1)}, bf16[4,160,128]{2,1,0:T(8,128)(2,1)S(1)}, u32[]{:S(2)}, u32[]{:S(2)}) collective-permute-start(bf16[4,160,128]{2,1,0:T(8,128)(2,1)S(1)} %get-tuple-element.42), channel_id=1, source_target_pairs={{0,1},{1,0},{2,3},{3,2},{4,5},{5,4},{6,7},{7,6},{8,9},{9,8},{10,11... | collective-permute-start | bytes 491528 | tf_op jit(solution)/shard_map/ppermute | solution.py:284
  13.9 1.0 collective-permute-done.1
  15.0 2.6 %collective-permute-start.2 = (bf16[4,160,128]{2,1,0:T(8,128)(2,1)S(1)}, bf16[4,160,128]{2,1,0:T(8,128)(2,1)S(1)}, u32[]{:S(2)}, u32[]{:S(2)}) collective-permute-start(bf16[4,160,128]{2,1,0:T(8,128)(2,1)S(1)} %fusion.14), channel_id=1, source_target_pairs={{0,2},{1,3},{2,0},{3,1},{4,6},{5,7},{6,4},{7,5},{8,10},{9,11},{10,... | collective-permute-start | bytes 491528 | tf_op jit(solution)/shard_map/ppermute | solution.py:284
  17.7 4.5 %collective-permute-done.2 = bf16[4,160,128]{2,1,0:T(8,128)(2,1)S(1)} collective-permute-done((bf16[4,160,128]{2,1,0:T(8,128)(2,1)S(1)}, bf16[4,160,128]{2,1,0:T(8,128)(2,1)S(1)}, u32[]{:S(2)}, u32[]{:S(2)}) %collective-permute-start.2) | collective-permute-done | bytes 163872 | tf_op jit(solution)/shard_map/ppermute | solution.py:284
  22.2 2.8 %collective-permute-start.3 = (bf16[4,160,128]{2,1,0:T(8,128)(2,1)S(1)}, bf16[4,160,128]{2,1,0:T(8,128)(2,1)S(1)}, u32[]{:S(2)}, u32[]{:S(2)}) collective-permute-start(bf16[4,160,128]{2,1,0:T(8,128)(2,1)S(1)} %fusion.16), channel_id=1, source_target_pairs={{0,4},{1,5},{2,6},{3,7},{4,0},{5,1},{6,2},{7,3},{8,12},{9,13},{10,... | collective-permute-start | bytes 491528 | tf_op jit(solution)/shard_map/ppermute | solution.py:284
  25.0 3.7 %collective-permute-done.3 = bf16[4,160,128]{2,1,0:T(8,128)(2,1)S(1)} collective-permute-done((bf16[4,160,128]{2,1,0:T(8,128)(2,1)S(1)}, bf16[4,160,128]{2,1,0:T(8,128)(2,1)S(1)}, u32[]{:S(2)}, u32[]{:S(2)}) %collective-permute-start.3) | collective-permute-done | bytes 163872 | tf_op jit(solution)/shard_map/ppermute | solution.py:284
  28.7 0.7 copy-done.17
  29.4 2.8 %collective-permute-start.4 = (bf16[4,160,128]{2,1,0:T(8,128)(2,1)S(1)}, bf16[4,160,128]{2,1,0:T(8,128)(2,1)}, u32[]{:S(2)}, u32[]{:S(2)}) collective-permute-start(bf16[4,160,128]{2,1,0:T(8,128)(2,1)S(1)} %fusion.6), channel_id=1, source_target_pairs={{0,8},{1,9},{2,10},{3,11},{4,12},{5,13},{6,14},{7,15},{8,0},{9,1},... | collective-permute-start | bytes 491528 | tf_op jit(solution)/shard_map/ppermute | solution.py:284
  32.2 6.6 %collective-permute-done.4 = bf16[4,160,128]{2,1,0:T(8,128)(2,1)} collective-permute-done((bf16[4,160,128]{2,1,0:T(8,128)(2,1)S(1)}, bf16[4,160,128]{2,1,0:T(8,128)(2,1)}, u32[]{:S(2)}, u32[]{:S(2)}) %collective-permute-start.4) | collective-permute-done | bytes 163872 | tf_op jit(solution)/shard_map/ppermute | solution.py:284
  38.8 1.2 %fusion.1 = (bf16[4,160,128]{2,1,0:T(8,128)(2,1)S(1)}, bf16[4,160,128]{2,1,0:T(8,128)(2,1)S(1)}) fusion(bf16[4,160,128]{2,1,0:T(8,128)(2,1)S(1)} %get-tuple-element.41, f32[]{:T(128)S(6)} %sub.6, bf16[4,160,128]{2,1,0:T(8,128)(2,1)} %collective-permute-done.4, f32[]{:T(128)S(6)} %select_n.29, bf16[4,160,128]{2,1,0:T(8,128)(2,1)} %copy-done.17, ...), kind=kLoop, calls=%fused_computation.15 | loop fusion | flops 1310720 | bytes 1146900 | tf_op jit(solution)/shard_map/convert_element_type | solution.py:305
  40.6 2.3 %shard_map.146.high = f32[512,512]{1,0:T(8,128)S(1)} custom-call(bf16[512,128]{1,0:T(8,128)(2,1)S(1)} %get-tuple-element.37.q_ref, bf16[512,128]{1,0:T(8,128)(2,1)S(1)} %get-tuple-element.38.k_ref, bf16[512,1024]{1,0:T(8,128)(2,1)S(1)} %get-tuple-element.39.v_ref), custom_call_target="tpu_custom_call" | custom-call | flops 536870912 | bytes 2359296 | tf_op jit(solution)/shard_map/pallas_call | solution.py:273
  42.9 2.3 %shard_map.145.low = f32[512,512]{1,0:T(8,128)S(1)} custom-call(bf16[512,128]{1,0:T(8,128)(2,1)S(1)} %get-tuple-element.37.q_ref, bf16[512,128]{1,0:T(8,128)(2,1)S(1)} %get-tuple-element.38.k_ref, bf16[512,1024]{1,0:T(8,128)(2,1)S(1)} %get-tuple-element.39.v_ref), custom_call_target="tpu_custom_call" | custom-call | flops 536870912 | bytes 2359296 | tf_op jit(solution)/shard_map/pallas_call | solution.py:273
  45.3 4.6 %shard_map.147 = (bf16[512,1024]{1,0:T(8,128)(2,1)}, bf16[512,1024]{1,0:T(8,128)(2,1)S(1)}, bf16[4,160,128]{2,1,0:T(8,128)(2,1)S(1)}, bf16[4,160,128]{2,1,0:T(8,128)(2,1)S(1)}, f32[8,128]{1,0:T(8,128)S(1)}) custom-call(f32[512,512]{1,0:T(8,128)S(1)} %shard_map.145.low, f32[512,512]{1,0:T(8,128)S(1)} %shard_map.146.high, ...), custom_call_target="tpu_custom_call" | custom-call | flops 335544320 | bytes 7217152 | tf_op jit(solution)/shard_map/pallas_call | solution.py:273
  49.9 1.0 copy-done.2
  51.3 1.0 collective-permute-done.6
  52.4 0.6 collective-permute-start.7
  53.0 6.0 %collective-permute-done.7 = bf16[4,160,128]{2,1,0:T(8,128)(2,1)S(1)} collective-permute-done((bf16[4,160,128]{2,1,0:T(8,128)(2,1)S(1)}, bf16[4,160,128]{2,1,0:T(8,128)(2,1)S(1)}, u32[]{:S(2)}, u32[]{:S(2)}) %collective-permute-start.7) | collective-permute-done | bytes 163872 | tf_op jit(solution)/shard_map/ppermute | solution.py:284
  59.5 5.2 %collective-permute-done.8 = bf16[4,160,128]{2,1,0:T(8,128)(2,1)S(1)} collective-permute-done((bf16[4,160,128]{2,1,0:T(8,128)(2,1)S(1)}, bf16[4,160,128]{2,1,0:T(8,128)(2,1)S(1)}, u32[]{:S(2)}, u32[]{:S(2)}) %collective-permute-start.8) | collective-permute-done | bytes 163872 | tf_op jit(solution)/shard_map/ppermute | solution.py:284
  64.7 0.8 fusion.13
  65.5 2.2 %collective-permute-start.9 = (bf16[4,160,128]{2,1,0:T(8,128)(2,1)}, bf16[4,160,128]{2,1,0:T(8,128)(2,1)}, u32[]{:S(2)}, u32[]{:S(2)}) collective-permute-start(bf16[4,160,128]{2,1,0:T(8,128)(2,1)} %fusion.13), channel_id=1, source_target_pairs={{0,8},{1,9},{2,10},{3,11},{4,12},{5,13},{6,14},{7,15},{8,0},{9,1},... | collective-permute-start | bytes 491528 | tf_op jit(solution)/shard_map/ppermute | solution.py:284
  67.7 7.3 %collective-permute-done.9 = bf16[4,160,128]{2,1,0:T(8,128)(2,1)} collective-permute-done((bf16[4,160,128]{2,1,0:T(8,128)(2,1)}, bf16[4,160,128]{2,1,0:T(8,128)(2,1)}, u32[]{:S(2)}, u32[]{:S(2)}) %collective-permute-start.9) | collective-permute-done | bytes 163872 | tf_op jit(solution)/shard_map/ppermute | solution.py:284
  75.0 1.3 %fusion.8 = (bf16[4,160,128]{2,1,0:T(8,128)(2,1)S(1)}, bf16[4,160,128]{2,1,0:T(8,128)(2,1)S(1)}) fusion(bf16[4,160,128]{2,1,0:T(8,128)(2,1)S(1)} %get-tuple-element.51, f32[]{:T(128)S(6)} %sub.7, bf16[4,160,128]{2,1,0:T(8,128)(2,1)} %collective-permute-done.9, f32[]{:T(128)S(6)} %select_n.33, bf16[4,160,128]{2,1,0:T(8,128)(2,1)} %copy-done.18, ...), kind=kLoop, calls=%fused_computation.22 | loop fusion | flops 1310720 | bytes 1146900 | tf_op jit(solution)/shard_map/convert_element_type | solution.py:305
  76.4 1.2 %copy-done.3 = bf16[512,1024]{1,0:T(8,128)(2,1)S(1)} copy-done((bf16[512,1024]{1,0:T(8,128)(2,1)S(1)}, bf16[512,1024]{1,0:T(8,128)(2,1)}, u32[]{:S(2)}) %copy-start.3) | copy-done | bytes 1048600
  77.6 5.1 %shard_map.149 = (f32[512,512]{1,0:T(8,128)S(1)}, f32[64,512]{1,0:T(8,128)S(1)}, f32[64,512]{1,0:T(8,128)S(1)}) custom-call(bf16[512,128]{1,0:T(8,128)(2,1)S(1)} %get-tuple-element.37.q_ref, bf16[512,128]{1,0:T(8,128)(2,1)S(1)} %get-tuple-element.38.k_ref, bf16[128,512]{1,0:T(8,128)(2,1)S(1)} %get-tuple-element.44.qt_ref, ...), custom_call_target="tpu_custom_call" | custom-call | flops 1073741824 | bytes 3932160 | tf_op jit(solution)/shard_map/pallas_call | solution.py:273
  82.7 5.0 %shard_map.148 = (f32[512,512]{1,0:T(8,128)S(1)}, f32[64,512]{1,0:T(8,128)S(1)}, f32[64,512]{1,0:T(8,128)S(1)}) custom-call(bf16[512,128]{1,0:T(8,128)(2,1)S(1)} %get-tuple-element.37.q_ref, bf16[512,128]{1,0:T(8,128)(2,1)S(1)} %get-tuple-element.38.k_ref, bf16[128,512]{1,0:T(8,128)(2,1)S(1)} %get-tuple-element.44.qt_ref, ...), custom_call_target="tpu_custom_call" | custom-call | flops 1073741824 | bytes 3932160 | tf_op jit(solution)/shard_map/pallas_call | solution.py:273
  87.7 0.9 shard_map.150
  88.9 2.0 %shard_map.151 = (f32[512,1024]{1,0:T(8,128)S(1)}, f32[512,128]{1,0:T(8,128)S(1)}, f32[8,1280]{1,0:T(8,128)S(1)}, f32[4,1280]{1,0:T(4,128)S(1)}) custom-call(bf16[512,128]{1,0:T(8,128)(2,1)S(1)} %copy-done.7, bf16[512,1024]{1,0:T(8,128)(2,1)S(1)} %copy-done.1, bf16[16,1280]{1,0:T(8,128)(2,1)S(1)} %collective-permute-done.rim, ...), custom_call_target="tpu_custom_call" | custom-call | flops 335544320 | bytes 8828416 | tf_op jit(solution)/shard_map/pallas_call | solution.py:273
  90.9 0.6 collective-permute-start.12
  91.5 0.8 collective-permute-done.12
  92.8 1.3 %collective-permute-start.11 = (f32[8,1280]{1,0:T(8,128)S(1)}, f32[8,1280]{1,0:T(8,128)S(1)}, u32[]{:S(2)}, u32[]{:S(2)}) collective-permute-start(f32[8,1280]{1,0:T(8,128)S(1)} %get-tuple-element.61), channel_id=1, source_target_pairs={{1,0},{2,1},{3,2},{4,3},{5,4},{6,5},{7,6},{8,7},{9,8},{10,9},{11,1... | collective-permute-start | bytes 122888 | tf_op jit(solution)/shard_map/ppermute | solution.py:378
  94.1 2.0 %collective-permute-done.13 = f32[4,1280]{1,0:T(4,128)S(1)} collective-permute-done((f32[4,1280]{1,0:T(4,128)S(1)}, f32[4,1280]{1,0:T(4,128)S(1)}, u32[]{:S(2)}, u32[]{:S(2)}) %collective-permute-start.13) | collective-permute-done | bytes 20512 | tf_op jit(solution)/shard_map/ppermute | solution.py:284
  96.1 1.4 %collective-permute-start.14 = (f32[4,1280]{1,0:T(4,128)S(1)}, f32[4,1280]{1,0:T(4,128)S(1)}, u32[]{:S(2)}, u32[]{:S(2)}) collective-permute-start(f32[4,1280]{1,0:T(4,128)S(1)} %add.69), channel_id=1, source_target_pairs={{0,4},{1,5},{2,6},{3,7},{4,0},{5,1},{6,2},{7,3},{8,12},{9,13},{10,... | collective-permute-start | bytes 61448 | tf_op jit(solution)/shard_map/ppermute | solution.py:284
  97.6 2.4 %collective-permute-done.14 = f32[4,1280]{1,0:T(4,128)S(1)} collective-permute-done((f32[4,1280]{1,0:T(4,128)S(1)}, f32[4,1280]{1,0:T(4,128)S(1)}, u32[]{:S(2)}, u32[]{:S(2)}) %collective-permute-start.14) | collective-permute-done | bytes 20512 | tf_op jit(solution)/shard_map/ppermute | solution.py:284
  100.0 2.0 %collective-permute-start.15 = (f32[4,1280]{1,0:T(4,128)S(1)}, f32[4,1280]{1,0:T(4,128)S(1)}, u32[]{:S(2)}, u32[]{:S(2)}) collective-permute-start(f32[4,1280]{1,0:T(4,128)S(1)} %add.70), channel_id=1, source_target_pairs={{0,8},{1,9},{2,10},{3,11},{4,12},{5,13},{6,14},{7,15},{8,0},{9,1},... | collective-permute-start | bytes 61448 | tf_op jit(solution)/shard_map/ppermute | solution.py:284
  101.9 2.6 %shard_map.152 = (bf16[512,128]{1,0:T(8,128)(2,1)}, bf16[512,128]{1,0:T(8,128)(2,1)}, bf16[512,1024]{1,0:T(8,128)(2,1)}) custom-call(f32[512,128]{1,0:T(8,128)S(1)} %get-tuple-element.49.gq, f32[512,128]{1,0:T(8,128)S(1)} %get-tuple-element.59.gk, f32[512,1024]{1,0:T(8,128)S(1)} %get-tuple-element.60.gv, f32[8,1280]{1,0:T(8,128)S(1)} %collective-permute-done.11.follow, ...), custom_call_target="tpu_custom_call" | custom-call | flops 167772160 | bytes 3988480 | tf_op jit(solution)/shard_map/pallas_call | solution.py:273
  104.7 0.6 slice.34
  105.3 0.6 fusion.18
  105.9 0.6 slice.35
  (52 shorter events, 2.9 us)
Async XLA Ops:
  2.8 3.2 %collective-permute-start = (bf16[16,1280]{1,0:T(8,128)(2,1)S(1)}, bf16[16,1280]{1,0:T(8,128)(2,1)S(1)}, u32[]{:S(2)}, u32[]{:S(2)}) collective-permute-start(bf16[16,1280]{1,0:T(8,128)(2,1)S(1)} %pad_maximum_fusion), channel_id=1, source_target_pairs={{0,1},{1,2},{2,3},{3,4},{4,5},{5,6},{6,7},{7,8},{8,9},{9,10},{10,1... | collective-permute-start | bytes 122888 | tf_op jit(solution)/shard_map/ppermute | solution.py:323
  6.0 1.2 %copy-start = (bf16[512,1024]{1,0:T(8,128)(2,1)S(1)}, bf16[512,1024]{1,0:T(8,128)(2,1)}, u32[]{:S(2)}) copy-start(bf16[512,1024]{1,0:T(8,128)(2,1)} %value.3) | copy-start | bytes 3145732
  7.2 0.9 copy-start.6
  8.1 0.7 copy-start.9
  8.8 0.7 copy-start.12
  11.0 4.0 %collective-permute-start.1 = (bf16[4,160,128]{2,1,0:T(8,128)(2,1)S(1)}, bf16[4,160,128]{2,1,0:T(8,128)(2,1)S(1)}, u32[]{:S(2)}, u32[]{:S(2)}) collective-permute-start(bf16[4,160,128]{2,1,0:T(8,128)(2,1)S(1)} %get-tuple-element.42), channel_id=1, source_target_pairs={{0,1},{1,0},{2,3},{3,2},{4,5},{5,4},{6,7},{7,6},{8,9},{9,8},{10,11... | collective-permute-start | bytes 491528 | tf_op jit(solution)/shard_map/ppermute | solution.py:284
  15.0 25.1 %copy-start.8 = (bf16[512,128]{1,0:T(8,128)(2,1)S(1)}, bf16[512,128]{1,0:T(8,128)(2,1)}, u32[]{:S(2)}) copy-start(bf16[512,128]{1,0:T(8,128)(2,1)} %query.3) | copy-start | bytes 393220
  15.0 25.1 %copy-start.11 = (f32[3,128]{1,0:T(4,128)S(1)}, f32[3,128]{1,0:T(4,128)}, u32[]{:S(2)}) copy-start(f32[3,128]{1,0:T(4,128)} %taps_q.5) | copy-start | bytes 4612
  15.0 7.2 %collective-permute-start.2 = (bf16[4,160,128]{2,1,0:T(8,128)(2,1)S(1)}, bf16[4,160,128]{2,1,0:T(8,128)(2,1)S(1)}, u32[]{:S(2)}, u32[]{:S(2)}) collective-permute-start(bf16[4,160,128]{2,1,0:T(8,128)(2,1)S(1)} %fusion.14), channel_id=1, source_target_pairs={{0,2},{1,3},{2,0},{3,1},{4,6},{5,7},{6,4},{7,5},{8,10},{9,11},{10,... | collective-permute-start | bytes 491528 | tf_op jit(solution)/shard_map/ppermute | solution.py:284
  22.2 6.4 %collective-permute-start.3 = (bf16[4,160,128]{2,1,0:T(8,128)(2,1)S(1)}, bf16[4,160,128]{2,1,0:T(8,128)(2,1)S(1)}, u32[]{:S(2)}, u32[]{:S(2)}) collective-permute-start(bf16[4,160,128]{2,1,0:T(8,128)(2,1)S(1)} %fusion.16), channel_id=1, source_target_pairs={{0,4},{1,5},{2,6},{3,7},{4,0},{5,1},{6,2},{7,3},{8,12},{9,13},{10,... | collective-permute-start | bytes 491528 | tf_op jit(solution)/shard_map/ppermute | solution.py:284
  28.7 0.7 copy-start.17
  29.4 9.4 %collective-permute-start.4 = (bf16[4,160,128]{2,1,0:T(8,128)(2,1)S(1)}, bf16[4,160,128]{2,1,0:T(8,128)(2,1)}, u32[]{:S(2)}, u32[]{:S(2)}) collective-permute-start(bf16[4,160,128]{2,1,0:T(8,128)(2,1)S(1)} %fusion.6), channel_id=1, source_target_pairs={{0,8},{1,9},{2,10},{3,11},{4,12},{5,13},{6,14},{7,15},{8,0},{9,1},... | collective-permute-start | bytes 491528 | tf_op jit(solution)/shard_map/ppermute | solution.py:284
  40.0 5.2 %collective-permute-start.5 = (bf16[4,160,128]{2,1,0:T(8,128)(2,1)S(1)}, bf16[4,160,128]{2,1,0:T(8,128)(2,1)S(1)}, u32[]{:S(2)}, u32[]{:S(2)}) collective-permute-start(bf16[4,160,128]{2,1,0:T(8,128)(2,1)S(1)} %get-tuple-element.68), channel_id=1, source_target_pairs={{0,1},{1,0},{2,3},{3,2},{4,5},{5,4},{6,7},{7,6},{8,9},{9,8},{10,11... | collective-permute-start | bytes 491528 | tf_op jit(solution)/shard_map/ppermute | solution.py:284
  42.9 2.4 %copy-start.5 = (bf16[512,1024]{1,0:T(8,128)(2,1)S(1)}, bf16[512,1024]{1,0:T(8,128)(2,1)}, u32[]{:S(2)}) copy-start(bf16[512,1024]{1,0:T(8,128)(2,1)} %grad.1) | copy-start | bytes 3145732
  42.9 2.4 %copy-start.14 = (f32[1024]{0:T(1024)S(1)}, f32[1024]{0:T(1024)}, u32[]{:S(2)}) copy-start(f32[1024]{0:T(1024)} %param.14) | copy-start | bytes 12292
  49.9 1.0 copy-start.2
  50.8 1.5 %collective-permute-start.6 = (bf16[4,160,128]{2,1,0:T(8,128)(2,1)S(1)}, bf16[4,160,128]{2,1,0:T(8,128)(2,1)S(1)}, u32[]{:S(2)}, u32[]{:S(2)}) collective-permute-start(bf16[4,160,128]{2,1,0:T(8,128)(2,1)S(1)} %get-tuple-element.52), channel_id=1, source_target_pairs={{0,1},{1,0},{2,3},{3,2},{4,5},{5,4},{6,7},{7,6},{8,9},{9,8},{10,11... | collective-permute-start | bytes 491528 | tf_op jit(solution)/shard_map/ppermute | solution.py:284
  52.3 12.4 %copy-start.15 = (bf16[4,160,128]{2,1,0:T(8,128)(2,1)}, bf16[4,160,128]{2,1,0:T(8,128)(2,1)S(1)}, u32[]{:S(2)}) copy-start(bf16[4,160,128]{2,1,0:T(8,128)(2,1)S(1)} %collective-permute-done.6) | copy-start | bytes 491524
  52.4 6.5 %collective-permute-start.7 = (bf16[4,160,128]{2,1,0:T(8,128)(2,1)S(1)}, bf16[4,160,128]{2,1,0:T(8,128)(2,1)S(1)}, u32[]{:S(2)}, u32[]{:S(2)}) collective-permute-start(bf16[4,160,128]{2,1,0:T(8,128)(2,1)S(1)} %fusion.15), channel_id=1, source_target_pairs={{0,2},{1,3},{2,0},{3,1},{4,6},{5,7},{6,4},{7,5},{8,10},{9,11},{10,... | collective-permute-start | bytes 491528 | tf_op jit(solution)/shard_map/ppermute | solution.py:284
  58.9 6.6 %copy-start.16 = (bf16[4,160,128]{2,1,0:T(8,128)(2,1)}, bf16[4,160,128]{2,1,0:T(8,128)(2,1)S(1)}, u32[]{:S(2)}) copy-start(bf16[4,160,128]{2,1,0:T(8,128)(2,1)S(1)} %collective-permute-done.7) | copy-start | bytes 491524
  59.0 5.7 %collective-permute-start.8 = (bf16[4,160,128]{2,1,0:T(8,128)(2,1)S(1)}, bf16[4,160,128]{2,1,0:T(8,128)(2,1)S(1)}, u32[]{:S(2)}, u32[]{:S(2)}) collective-permute-start(bf16[4,160,128]{2,1,0:T(8,128)(2,1)S(1)} %fusion.17), channel_id=1, source_target_pairs={{0,4},{1,5},{2,6},{3,7},{4,0},{5,1},{6,2},{7,3},{8,12},{9,13},{10,... | collective-permute-start | bytes 491528 | tf_op jit(solution)/shard_map/ppermute | solution.py:284
  64.7 0.8 copy-start.18
  65.5 9.5 %collective-permute-start.9 = (bf16[4,160,128]{2,1,0:T(8,128)(2,1)}, bf16[4,160,128]{2,1,0:T(8,128)(2,1)}, u32[]{:S(2)}, u32[]{:S(2)}) collective-permute-start(bf16[4,160,128]{2,1,0:T(8,128)(2,1)} %fusion.13), channel_id=1, source_target_pairs={{0,8},{1,9},{2,10},{3,11},{4,12},{5,13},{6,14},{7,15},{8,0},{9,1},... | collective-permute-start | bytes 491528 | tf_op jit(solution)/shard_map/ppermute | solution.py:284
  76.3 12.3 %collective-permute-start.10 = (bf16[4,160,128]{2,1,0:T(8,128)(2,1)S(1)}, bf16[4,160,128]{2,1,0:T(8,128)(2,1)S(1)}, u32[]{:S(2)}, u32[]{:S(2)}) collective-permute-start(bf16[4,160,128]{2,1,0:T(8,128)(2,1)S(1)} %get-tuple-element.66), channel_id=1, source_target_pairs={{0,1},{1,0},{2,3},{3,2},{4,5},{5,4},{6,7},{7,6},{8,9},{9,8},{10,11... | collective-permute-start | bytes 491528 | tf_op jit(solution)/shard_map/ppermute | solution.py:284
  76.4 1.2 %copy-start.3 = (bf16[512,1024]{1,0:T(8,128)(2,1)S(1)}, bf16[512,1024]{1,0:T(8,128)(2,1)}, u32[]{:S(2)}) copy-start(bf16[512,1024]{1,0:T(8,128)(2,1)} %copy-done.2) | copy-start | bytes 3145732
  82.7 5.0 %copy-start.4 = (bf16[512,1024]{1,0:T(8,128)(2,1)S(1)}, bf16[512,1024]{1,0:T(8,128)(2,1)}, u32[]{:S(2)}) copy-start(bf16[512,1024]{1,0:T(8,128)(2,1)} %copy-done.2) | copy-start | bytes 3145732
  87.7 1.2 %copy-start.1 = (bf16[512,1024]{1,0:T(8,128)(2,1)S(1)}, bf16[512,1024]{1,0:T(8,128)(2,1)}, u32[]{:S(2)}) copy-start(bf16[512,1024]{1,0:T(8,128)(2,1)} %value.3) | copy-start | bytes 3145732
  87.7 1.2 %copy-start.7 = (bf16[512,128]{1,0:T(8,128)(2,1)S(1)}, bf16[512,128]{1,0:T(8,128)(2,1)}, u32[]{:S(2)}) copy-start(bf16[512,128]{1,0:T(8,128)(2,1)} %key.3) | copy-start | bytes 393220
  88.9 13.0 %copy-start.10 = (f32[3,1024]{1,0:T(4,128)S(1)}, f32[3,1024]{1,0:T(4,128)}, u32[]{:S(2)}) copy-start(f32[3,1024]{1,0:T(4,128)} %taps_v.3) | copy-start | bytes 36868
  88.9 13.0 %copy-start.13 = (f32[3,128]{1,0:T(4,128)S(1)}, f32[3,128]{1,0:T(4,128)}, u32[]{:S(2)}) copy-start(f32[3,128]{1,0:T(4,128)} %taps_k.3) | copy-start | bytes 4612
  90.9 1.4 %collective-permute-start.12 = (f32[4,1280]{1,0:T(4,128)S(1)}, f32[4,1280]{1,0:T(4,128)S(1)}, u32[]{:S(2)}, u32[]{:S(2)}) collective-permute-start(f32[4,1280]{1,0:T(4,128)S(1)} %get-tuple-element.65), channel_id=1, source_target_pairs={{0,1},{1,0},{2,3},{3,2},{4,5},{5,4},{6,7},{7,6},{8,9},{9,8},{10,11... | collective-permute-start | bytes 61448 | tf_op jit(solution)/shard_map/ppermute | solution.py:284
  92.3 3.8 %collective-permute-start.13 = (f32[4,1280]{1,0:T(4,128)S(1)}, f32[4,1280]{1,0:T(4,128)S(1)}, u32[]{:S(2)}, u32[]{:S(2)}) collective-permute-start(f32[4,1280]{1,0:T(4,128)S(1)} %add.68), channel_id=1, source_target_pairs={{0,2},{1,3},{2,0},{3,1},{4,6},{5,7},{6,4},{7,5},{8,10},{9,11},{10,... | collective-permute-start | bytes 61448 | tf_op jit(solution)/shard_map/ppermute | solution.py:284
  92.8 9.1 %collective-permute-start.11 = (f32[8,1280]{1,0:T(8,128)S(1)}, f32[8,1280]{1,0:T(8,128)S(1)}, u32[]{:S(2)}, u32[]{:S(2)}) collective-permute-start(f32[8,1280]{1,0:T(8,128)S(1)} %get-tuple-element.61), channel_id=1, source_target_pairs={{1,0},{2,1},{3,2},{4,3},{5,4},{6,5},{7,6},{8,7},{9,8},{10,9},{11,1... | collective-permute-start | bytes 122888 | tf_op jit(solution)/shard_map/ppermute | solution.py:378
  96.1 3.8 %collective-permute-start.14 = (f32[4,1280]{1,0:T(4,128)S(1)}, f32[4,1280]{1,0:T(4,128)S(1)}, u32[]{:S(2)}, u32[]{:S(2)}) collective-permute-start(f32[4,1280]{1,0:T(4,128)S(1)} %add.69), channel_id=1, source_target_pairs={{0,4},{1,5},{2,6},{3,7},{4,0},{5,1},{6,2},{7,3},{8,12},{9,13},{10,... | collective-permute-start | bytes 61448 | tf_op jit(solution)/shard_map/ppermute | solution.py:284
  100.0 4.7 %collective-permute-start.15 = (f32[4,1280]{1,0:T(4,128)S(1)}, f32[4,1280]{1,0:T(4,128)S(1)}, u32[]{:S(2)}, u32[]{:S(2)}) collective-permute-start(f32[4,1280]{1,0:T(4,128)S(1)} %add.70), channel_id=1, source_target_pairs={{0,8},{1,9},{2,10},{3,11},{4,12},{5,13},{6,14},{7,15},{8,0},{9,1},... | collective-permute-start | bytes 61448 | tf_op jit(solution)/shard_map/ppermute | solution.py:284

commit v2 on v1

--- a/solution.py
+++ b/solution.py
@@ -9,6 +9,7 @@
 
 HEADS = 8
 HALF = HEADS // 2
+PART = HEADS // 4
 FEAT = 16
 DIM = 128
 EPSILON = 1e-06
@@ -103,8 +104,27 @@
     return jnp.where(lanes // FEAT == h, 1.0, 0.0).astype(F32).astype(BF16)
 
 
-def key_kernel(key, value, rim, taps_k, taps_v, v_out, k_out, kt_out, fk_out, keep, send, wide, state):
+def end_kernel(query, key, value, out, sems):
+    start = query.shape[0] - RIM
+    copies = [
+        pltpu.make_async_copy(ref.at[pl.ds(start, RIM)], out.at[:, pl.ds(lane, ref.shape[1])], sems.at[i])
+        for i, (ref, lane) in enumerate(((query, 0), (key, LANES), (value, 2 * LANES)))
+    ]
+    for copy in copies:
+        copy.start()
+    for copy in copies:
+        copy.wait()
+
+
+def key_kernel(
+    key_far, value_far, rim, taps_k, taps_v, v_out, k_out, kt_out, fk_out, keep, send, wide, state, key, value, sems
+):
     rows = key.shape[0]
+    key_copy = pltpu.make_async_copy(key_far, key, sems.at[0])
+    value_copy = pltpu.make_async_copy(value_far, value, sems.at[1])
+    key_copy.start()
+    value_copy.start()
+    key_copy.wait()
     wide[0:RIM] = rim[:, LANES : 2 * LANES].astype(F32)
     wide[RIM : RIM + rows] = key[...].astype(F32)
     k = conv(wide, taps_k[...], rows).astype(BF16)
@@ -112,8 +132,10 @@
     kt = k.astype(F32).T
     kt_out[...] = kt.astype(BF16)
     for h in range(HEADS):
-        f = features(kt[head_rows(h)])
-        fk_out[h] = f
+        fk_out[h] = features(kt[head_rows(h)])
+    value_copy.wait()
+    for h in range(HEADS):
+        f = fk_out[h]
         wide[0:RIM] = rim[:, 2 * LANES + h * DIM : 2 * LANES + (h + 1) * DIM].astype(F32)
         wide[RIM : RIM + rows] = value[:, head_lanes(h)].astype(F32)
         v = conv(wide, taps_v[:, head_lanes(h)], rows).astype(BF16)
@@ -173,7 +195,7 @@
 def back_kernel(first, q_ref, k_ref, qt_ref, kt_ref, v_ref, gs_ref, gv_out, gq_out, gk_out):
     rows = q_ref.shape[0]
     quarter = q_ref[...] * jnp.asarray(FEAT ** (-0.5), BF16)
-    for g in range(HALF):
+    for g in range(PART):
         h = first + g
         ks = k_ref[...] * head_mask(h)
         qt = qt_ref[head_rows(h)]
@@ -196,12 +218,13 @@
             gk_out[head_rows(g), start:stop] = dot(qt[:, start:], s, NT)
 
 
-def query_grad_kernel(query, rim, qt_ref, gs_ref, own, other, low, high, taps_q, g_out, sums, wide, pre):
+def query_grad_kernel(query, rim, qt_ref, gs_ref, own, other, l0, l1, l2, l3, taps_q, g_out, sums, wide, pre):
     rows = query.shape[0]
+    locals_ = (l0, l1, l2, l3)
     gather_state(own, other, pre)
     pieces = []
     for h in range(HEADS):
-        local = (low if h < HALF else high)[head_rows(h % HALF)]
+        local = locals_[h // PART][head_rows(h % PART)]
         pieces.append(
             local + feature_grad(qt_ref[head_rows(h)].astype(F32), pre[h], gs_ref[:, head_lanes(h)])
         )
@@ -214,22 +237,23 @@
 
 
 def later_kernel(
-    key, value, rim, kt_ref, fk, v_ref, own, other, gv_low, gv_high, gk_low, gk_high, gq, sums_q, gain_sum,
+    key, value, rim, kt_ref, fk, v_ref, own, other, v0, v1, v2, v3, k0, k1, k2, k3, gq, sums_q, gain_sum,
     gv_out, gk_out, head_out, sums, wide, post,
 ):
     rows = key.shape[0]
     taps = sums_q.shape[0]
+    value_parts, key_parts = (v0, v1, v2, v3), (k0, k1, k2, k3)
     gather_state(own, other, post)
     pieces = []
-    head_out[:, 0:LANES] = gq[...]
+    head_out[:, 0:LANES] = gq[0:8]
     sums[0:taps, 0:LANES] = sums_q[...]
     sums[taps : taps + 1, 0 : 2 * LANES] = jnp.zeros((1, 2 * LANES), F32)
     for h in range(HEADS):
-        local = (gk_low if h < HALF else gk_high)[head_rows(h % HALF)]
+        local = key_parts[h // PART][head_rows(h % PART)]
         pieces.append(
             local + feature_grad(kt_ref[head_rows(h)].astype(F32), post[h], v_ref[:, head_lanes(h)])
         )
-        local = (gv_low if h < HALF else gv_high)[:, head_lanes(h % HALF)]
+        local = value_parts[h // PART][:, head_lanes(h % PART)]
         grad = local + dot(fk[h], post[h], TN)
         gv_out[:, head_lanes(h)] = grad
         place = slice(2 * LANES + h * DIM, 2 * LANES + (h + 1) * DIM)
@@ -267,15 +291,33 @@
         v_out[:, head_lanes(h)] = one(gv[:, head_lanes(h)], place, taps_v[:, head_lanes(h)])
 
 
-def call(kernel, outs, scratch, args, flops, limit=24):
+def finish_kernel(factor, sums, got, q_out, k_out, v_out, gain_out):
+    taps = q_out.shape[0]
+    total = (sums[...] + got[...]) * factor
+    q_out[...] = total[0:taps, 0:LANES]
+    k_out[...] = total[0:taps, LANES : 2 * LANES]
+    v_out[...] = total[0:taps, 2 * LANES :]
+    gain_out[...] = total[taps : taps + 1, 2 * LANES :]
+
+
+def far(x):
+    return pltpu.with_memory_space_constraint(x, pltpu.HBM)
+
+
+def held(*xs):
+    return [pltpu.with_memory_space_constraint(x, pltpu.VMEM) for x in xs]
+
+
+def call(kernel, outs, scratch, args, flops, limit=16, loose=(), **specs):
     size = lambda a: a.size * a.dtype.itemsize
     moved = sum(size(a) for a in args) + sum(size(o) for o in outs)
     return pl.pallas_call(
         kernel,
-        out_shape=outs,
+        out_shape=[o if i in loose else pltpu.VMEM(o.shape, o.dtype) for i, o in enumerate(outs)],
         scratch_shapes=scratch,
         compiler_params=pltpu.CompilerParams(vmem_limit_bytes=limit * 2**20),
         cost_estimate=pl.CostEstimate(flops=flops, bytes_accessed=moved, transcendentals=0),
+        **specs,
     )(*args)
 
 
@@ -284,26 +326,87 @@
     return lax.ppermute(x, "seq", [(i, i ^ distance) for i in range(count)])
 
 
-def beyond(keep, send, reverse):
-    count, here = lax.axis_size("seq"), lax.axis_index("seq")
-
-    def mine(bit):
-        on = (here & bit) == 0 if reverse else (here & bit) != 0
-        return jnp.where(on, 1.0, 0.0).astype(F32)
+def tie(x, *others):
+    return lax.optimization_barrier((x, *others))[0]
+
+
+def on_side(bit, reverse):
+    set_ = lax.rem(lax.div(lax.axis_index("seq"), bit), 2)
+    return set_ == (0 if reverse else 1)
+
+
+def chosen(flag, x):
+    return jnp.where(flag, x, jnp.zeros_like(x))
+
+
+def pair_kernel(keep, near, part, their):
+    upper = lax.rem(lax.div(lax.axis_index("seq"), 2), 2)
+
+    def half(which):
+        place = pl.ds(which * PART, PART)
+        return keep[place].astype(F32) + near[place].astype(F32)
+
+    part[...] = half(upper)
+    their[...] = half(1 - upper).astype(BF16)
+
+
+def step_kernel(total, got, new, send):
+    both = total[...] + got[...].astype(F32)
+    new[...] = both
+    send[...] = both.astype(BF16)
+
+
+def part_kernel(reverse, part, got_y, *rest):
+    *gots, own, give = rest
+    before = jnp.zeros(part.shape, F32)
+    for i, got in enumerate(gots):
+        before = before + chosen(on_side(4 << i, reverse), got[...].astype(F32))
+    own[...] = before + chosen(on_side(2, reverse), got_y[...].astype(F32))
+    give[...] = (before + chosen(jnp.logical_not(on_side(2, reverse)), part[...])).astype(BF16)
+
+
+def merge_kernel(reverse, own_part, other_part, keep, near, own, give):
+    upper = lax.rem(lax.div(lax.axis_index("seq"), 2), 2)
+    side = on_side(1, reverse)
+    for part, which in ((own_part, upper), (other_part, 1 - upper)):
+        place = pl.ds(which * PART, PART)
+        before = part[...].astype(F32)
+        own[place] = (before + chosen(side, near[place].astype(F32))).astype(BF16)
+        give[place] = (before + chosen(jnp.logical_not(side), keep[place].astype(F32))).astype(BF16)
+
+
+def beyond(keep, send, reverse, works):
+    count = lax.axis_size("seq")
+    works = list(works)
+    st = jax.ShapeDtypeStruct
+    whole, part_shape = keep.shape, (PART, *keep.shape[1:])
+    wide, narrow = st(part_shape, F32), st(part_shape, BF16)
+    cost = 4 * keep.size
+
+    def under(x):
+        return tie(x, works.pop(0)()) if works else x
 
     near = exchange(send, 1)
-    a, b = keep.astype(F32), near.astype(F32)
-    total = a + b
-    before = jnp.zeros_like(total)
-    bit = 2
+    part, their = call(pair_kernel, [wide, narrow], [], (keep, near), cost)
+    got_y = exchange(their, 2)
+    total, gots, got = part, [], got_y
+    bit = 4
     while bit < count:
-        got = exchange(total.astype(BF16), bit).astype(F32)
-        before = before + mine(bit) * got
-        total = total + got
+        total, send = call(step_kernel, [wide, narrow], [], (total, got), cost)
+        got = exchange(under(send), bit)
+        gots.append(got)
         bit *= 2
-    own = (before + mine(1) * b).astype(BF16)
-    give = (before + (1.0 - mine(1)) * a).astype(BF16)
-    return own, exchange(give, 1)
+    own_part, give_part = call(
+        functools.partial(part_kernel, reverse), [wide, narrow], [], (part, got_y, *gots), cost
+    )
+    other_part = exchange(under(give_part), 2)
+    own, give = call(
+        functools.partial(merge_kernel, reverse), [st(whole, BF16)] * 2, [], (own_part, other_part, keep, near), cost
+    )
+    other = exchange(under(give), 1)
+    while works:
+        other = under(other)
+    return own, other
 
 
 def shards(query_in, key_in, value_in, conv_query, conv_key, conv_value, norm_gain, grad_out):
@@ -319,84 +422,133 @@
     state_flops = 2 * HEADS * ROWS * DIM * rows
     square_flops = 2 * HALF * rows * rows * DIM
 
-    ends = jnp.concatenate([a[rows - RIM :] for a in (query_in, key_in, value_in)], axis=1)
+    apart = pl.BlockSpec(memory_space=pltpu.HBM)
+    near = pl.BlockSpec(memory_space=pltpu.VMEM)
+    ends = call(
+        end_kernel,
+        [st((RIM, ALL), BF16)],
+        [pltpu.SemaphoreType.DMA((3,))],
+        (far(query_in), far(key_in), far(value_in)),
+        rows,
+        in_specs=[apart] * 3,
+    )[0]
     rim = lax.ppermute(ends, "seq", [(i, i + 1) for i in range(count - 1)])
 
     v, k, kt, fk, keep, send = call(
         key_kernel,
         [st((rows, WIDE), BF16), st((rows, LANES), BF16), st((LANES, rows), BF16), st((HEADS, ROWS, rows), BF16),
          half_state, half_state],
-        [wide, full_state],
-        (key_in, value_in, rim, conv_key, conv_value),
+        [wide, full_state, pltpu.VMEM((rows, LANES), BF16), pltpu.VMEM((rows, WIDE), BF16),
+         pltpu.SemaphoreType.DMA((2,))],
+        (far(key_in), far(value_in), rim, conv_key, conv_value),
         state_flops,
-    )
-    q, qt, fq = call(
-        query_kernel,
-        [st((rows, LANES), BF16), st((LANES, rows), BF16), st((HEADS, ROWS, rows), BF16)],
-        [wide],
-        (query_in, rim, conv_query),
-        state_flops,
-    )
-    local = [
-        call(functools.partial(local_kernel, first), [st((rows, HALF * DIM), F32)], [], (q, k, v), 2 * square_flops)[0]
-        for first in (0, HALF)
-    ]
-    own, other = beyond(keep, send, False)
+        in_specs=[apart, apart, near, near, near],
+    )
+
+    made = {}
+
+    def query_work():
+        made["q"] = call(
+            query_kernel,
+            [st((rows, LANES), BF16), st((LANES, rows), BF16), st((HEADS, ROWS, rows), BF16)],
+            [wide],
+            (query_in, rim, conv_query),
+            state_flops,
+        )
+        return local_work(0)()
+
+    def local_work(first):
+        def work():
+            made["local", first] = call(
+                functools.partial(local_kernel, first),
+                [st((rows, HALF * DIM), F32)],
+                [],
+                held(made["q"][0], k, v),
+                2 * HALF * rows * rows * DIM,
+            )[0]
+            return made["local", first]
+
+        return work
+
+    own, other = beyond(keep, send, False, [query_work, local_work(HALF)])
+    q, qt, fq = made["q"]
     output, gs, keep, send, gain_sum = call(
         norm_kernel,
         [st((rows, WIDE), BF16), st((rows, WIDE), BF16), half_state, half_state, st((HEADS, DIM), F32)],
         [full_state, full_state],
-        (*local, fq, own, other, grad_out, gain),
+        (*held(made["local", 0], made["local", HALF], fq), own, other, grad_out, gain),
         2 * state_flops,
-    )
-    back = [
-        call(
-            functools.partial(back_kernel, first),
-            [st((rows, HALF * DIM), F32), st((HALF * FEAT, rows), F32), st((HALF * FEAT, rows), F32)],
-            [],
-            (q, k, qt, kt, v, gs),
-            4 * square_flops,
+        loose=(0,),
+    )
+    back = []
+
+    def back_work():
+        back.append(
+            call(
+                functools.partial(back_kernel, len(back) * PART),
+                [st((rows, PART * DIM), F32), st((PART * FEAT, rows), F32), st((PART * FEAT, rows), F32)],
+                [],
+                held(q, k, qt, kt, v, gs),
+                4 * PART * rows * rows * DIM,
+            )
         )
-        for first in (0, HALF)
-    ]
-    gq, sums_q = call(
-        query_grad_kernel,
-        [st((rows, LANES), F32), st((taps, LANES), F32)],
-        [wide, full_state],
-        (query_in, rim, qt, gs, own, other, back[0][1], back[1][1], conv_query),
-        state_flops,
-    )
-    own, other = beyond(keep, send, True)
+        return back[-1][0]
+
+    def query_grad_work():
+        made["gq"] = call(
+            query_grad_kernel,
+            [st((rows, LANES), F32), st((taps, LANES), F32)],
+            [wide, full_state],
+            (query_in, rim, *held(qt, gs), before[0], before[1], *held(*[b[1] for b in back]), conv_query),
+            state_flops,
+        )
+        return made["gq"][0]
+
+    before = (own, other)
+    own, other = beyond(keep, send, True, [back_work] * 4 + [query_grad_work])
+    gq, sums_q = made["gq"]
     gv, gk, heads, sums = call(
         later_kernel,
         [st((rows, WIDE), F32), st((rows, LANES), F32), st((8, ALL), F32), st((taps + 1, ALL), F32)],
         [wide, full_state],
-        (key_in, value_in, rim, kt, fk, v, own, other, back[0][0], back[1][0], back[0][2], back[1][2],
-         gq[0:8], sums_q, gain_sum),
+        (key_in, value_in, rim, *held(kt, fk, v), own, other,
+         *held(*[b[0] for b in back], *[b[2] for b in back], gq, sums_q, gain_sum)),
         2 * state_flops,
     )
     follow = lax.ppermute(heads, "seq", [(i + 1, i) for i in range(count - 1)])
-    bit = 1
+    got = exchange(sums, 1)
+    bit = 2
     while bit < count:
-        sums = sums + exchange(sums, bit)
+        sums = sums + got
+        if bit == count // 2:
+            grad_query, grad_key, grad_value = call(
+                signal_kernel,
+                [st((rows, LANES), BF16), st((rows, LANES), BF16), st((rows, WIDE), BF16)],
+                [pltpu.VMEM((rows + 8, DIM), F32)],
+                (*held(gq, gk, gv), follow, conv_query, conv_key, conv_value),
+                state_flops,
+                loose=(0, 1, 2),
+            )
+            sums = tie(sums, grad_value)
+        got = exchange(sums, bit)
         bit *= 2
-    grad_query, grad_key, grad_value = call(
-        signal_kernel,
-        [st((rows, LANES), BF16), st((rows, LANES), BF16), st((rows, WIDE), BF16)],
-        [pltpu.VMEM((rows + 8, DIM), F32)],
-        (gq, gk, gv, follow, conv_query, conv_key, conv_value),
-        state_flops,
-    )
-    sums = sums * total_rows ** (-0.5)
+    taps_query, taps_key, taps_value, taps_gain = call(
+        functools.partial(finish_kernel, total_rows ** (-0.5)),
+        [st((taps, LANES), F32), st((taps, LANES), F32), st((taps, WIDE), F32), st((1, WIDE), F32)],
+        [],
+        (sums, got),
+        rows,
+        loose=(0, 1, 2, 3),
+    )
     return (
         output,
         grad_query,
         grad_key,
         grad_value,
-        sums[0:taps, 0:LANES],
-        sums[0:taps, LANES : 2 * LANES],
-        sums[0:taps, 2 * LANES :],
-        sums[taps, 2 * LANES :],
+        taps_query,
+        taps_key,
+        taps_value,
+        taps_gain.reshape(WIDE),
     )
 
 

time: 107 us -> 81 us (0.76)
  waiting for transfers between devices: 41.5 us -> 17.1 us
  local copies, waits for them, and re-layouts: 10.6 us -> 0.04 us
  starting transfers between devices: 23.1 us -> 31.4 us
  Pallas kernels: 26.8 us -> 31.3 us
  other arithmetic: 3.63 us -> 0.02 us
    ppermute x14 -> x16, waiting for transfers between devices: 40.7 us -> 16.3 us  [exchange(): return lax.ppermute(x, 'seq', [(i, i ^ distance) for i in range(count)])]
    ppermute x14 -> x16, starting transfers between devices: 19.5 us -> 27.8 us  [exchange(): return lax.ppermute(x, 'seq', [(i, i ^ distance) for i in range(count)])]
    unnamed x38 -> x16, local copies, waits for them, and re-layouts: 6.7 us -> 0.04 us
    pallas_call x10 -> x24, Pallas kernels: 26.8 us -> 31.3 us  [call(): pl.pallas_call(kernel, out_shape=[o if i in loose else pltpu.VMEM(o.shape...]
    slice x7 -> x0, local copies, waits for them, and re-layouts: 3.93 us -> none  [the longest x3 2.14 us: shards(): a[rows - RIM:]]
    convert_element_type x8 -> x0, other arithmetic: 3.59 us -> none  [the longest x2 2.52 us: beyond(): give = (before + (1.0 - mine(1)) * a).astype(BF16)]
  transfers between devices with their start and end apart: 16 -> 18, of which waited for: 13 -> 12; matrix products, arithmetic and copies ran while one was open for 0% -> 0% of each run, Pallas kernels for 18% -> 23%
where the time goes in v2:
time: 81 us; the launch traced here: 80.8 us
  starting transfers between devices  31.4 us (39%)
  Pallas kernels  31.3 us (39%)
  waiting for transfers between devices  17.1 us (21%)
  between operations  0.85 us (1%)
    pallas_call x24, Pallas kernels, call(): pl.pallas_call(kernel, out_shape=[o if i in loose else pltpu.VMEM(o.shape...  31.3 us
    ppermute x16, starting transfers between devices, exchange(): return lax.ppermute(x, 'seq', [(i, i ^ distance) for i in range(count)])  27.8 us
    ppermute x16, waiting for transfers between devices, exchange(): return lax.ppermute(x, 'seq', [(i, i ^ distance) for i in range(count)])  16.3 us
    ppermute x1, starting transfers between devices, shards(): rim = lax.ppermute(ends, 'seq', [(i, i + 1) for i in range(count - 1)])  2.36 us
  transfers between devices with their start and end apart: 18, of which 12 were waited for; matrix products, arithmetic and copies ran while one was open for 0% of the time, Pallas kernels for 23%

profile of v2, /device:TPU:0, one launch (start us, length us, event | category | flops | bytes accessed | tf_op | source)
XLA Modules:
  0.0 80.8 jit_solution(15514374386390468142)
XLA Ops:
  0.7 0.9 %shard_map.143 = bf16[16,1280]{1,0:T(8,128)(2,1)S(1)} custom-call(bf16[512,128]{1,0:T(8,128)(2,1)} %query.5, bf16[512,128]{1,0:T(8,128)(2,1)} %key.3, bf16[512,1024]{1,0:T(8,128)(2,1)} %value.3), custom_call_target="tpu_custom_call" | custom-call | flops 512 | bytes 1351680 | tf_op jit(solution)/shard_map/pallas_call | solution.py:314
  1.6 2.4 %collective-permute-start = (bf16[16,1280]{1,0:T(8,128)(2,1)S(1)}, bf16[16,1280]{1,0:T(8,128)(2,1)S(1)}, u32[]{:S(2)}, u32[]{:S(2)}) collective-permute-start(bf16[16,1280]{1,0:T(8,128)(2,1)S(1)} %shard_map.143), channel_id=1, source_target_pairs={{0,1},{1,2},{2,3},{3,4},{4,5},{5,6},{6,7},{7,8},{8,9},{9,10},{10,1... | collective-permute-start | bytes 122888 | tf_op jit(solution)/shard_map/ppermute | solution.py:435
  3.9 0.9 %collective-permute-done.rim = bf16[16,1280]{1,0:T(8,128)(2,1)S(1)} collective-permute-done((bf16[16,1280]{1,0:T(8,128)(2,1)S(1)}, bf16[16,1280]{1,0:T(8,128)(2,1)S(1)}, u32[]{:S(2)}, u32[]{:S(2)}) %collective-permute-start) | collective-permute-done | bytes 40992 | tf_op jit(solution)/shard_map/ppermute | solution.py:435
  4.8 2.5 %shard_map.145 = (bf16[512,1024]{1,0:T(8,128)(2,1)S(1)}, bf16[512,128]{1,0:T(8,128)(2,1)S(1)}, bf16[128,512]{1,0:T(8,128)(2,1)S(1)}, bf16[8,160,512]{2,1,0:T(8,1...) custom-call(bf16[512,128]{1,0:T(8,128)(2,1)} %key.3, bf16[512,1024]{1,0:T(8,128)(2,1)} %value.3, ...), custom_call_target="tpu_custom_call" | custom-call | flops 167772160 | bytes 4183552 | tf_op jit(solution)/shard_map/pallas_call | solution.py:314
  7.3 2.9 %collective-permute-start.1 = (bf16[4,160,128]{2,1,0:T(8,128)(2,1)S(1)}, bf16[4,160,128]{2,1,0:T(8,128)(2,1)S(1)}, u32[]{:S(2)}, u32[]{:S(2)}) collective-permute-start(bf16[4,160,128]{2,1,0:T(8,128)(2,1)S(1)} %get-tuple-element.78), channel_id=1, source_target_pairs={{0,1},{1,0},{2,3},{3,2},{4,5},{5,4},{6,7},{7,6},{8,9},{9,8},{10,11... | collective-permute-start | bytes 491528 | tf_op jit(solution)/shard_map/ppermute | solution.py:326
  10.2 1.0 %collective-permute-done.1.near = bf16[4,160,128]{2,1,0:T(8,128)(2,1)S(1)} collective-permute-done((bf16[4,160,128]{2,1,0:T(8,128)(2,1)S(1)}, bf16[4,160,128]{2,1,0:T(8,128)(2,1)S(1)}, u32[]{:S(2)}, u32[]{:S(2)}) %collective-permute-start.1) | collective-permute-done | bytes 163872 | tf_op jit(solution)/shard_map/ppermute | solution.py:326
  11.3 2.6 %collective-permute-start.2 = (bf16[2,160,128]{2,1,0:T(8,128)(2,1)S(1)}, bf16[2,160,128]{2,1,0:T(8,128)(2,1)S(1)}, u32[]{:S(2)}, u32[]{:S(2)}) collective-permute-start(bf16[2,160,128]{2,1,0:T(8,128)(2,1)S(1)} %get-tuple-element.80), channel_id=1, source_target_pairs={{0,2},{1,3},{2,0},{3,1},{4,6},{5,7},{6,4},{7,5},{8,10},{9,11},{10,... | collective-permute-start | bytes 245768 | tf_op jit(solution)/shard_map/ppermute | solution.py:326
  14.0 0.5 shard_map.144
  14.4 2.3 %shard_map.146.low = f32[512,512]{1,0:T(8,128)S(1)} custom-call(bf16[512,128]{1,0:T(8,128)(2,1)S(1)} %get-tuple-element.73.q_ref, bf16[512,128]{1,0:T(8,128)(2,1)S(1)} %get-tuple-element.74.k_ref, bf16[512,1024]{1,0:T(8,128)(2,1)S(1)} %get-tuple-element.75.v_ref), custom_call_target="tpu_custom_call" | custom-call | flops 268435456 | bytes 2359296 | tf_op jit(solution)/shard_map/pallas_call | solution.py:314
  16.8 2.7 %collective-permute-start.3 = (bf16[2,160,128]{2,1,0:T(8,128)(2,1)S(1)}, bf16[2,160,128]{2,1,0:T(8,128)(2,1)S(1)}, u32[]{:S(2)}, u32[]{:S(2)}) collective-permute-start(bf16[2,160,128]{2,1,0:T(8,128)(2,1)S(1)} %get-tuple-element.82), channel_id=1, source_target_pairs={{0,4},{1,5},{2,6},{3,7},{4,0},{5,1},{6,2},{7,3},{8,12},{9,13},{10,... | collective-permute-start | bytes 245768 | tf_op jit(solution)/shard_map/ppermute | solution.py:326
  19.5 2.3 %shard_map.147.high = f32[512,512]{1,0:T(8,128)S(1)} custom-call(bf16[512,128]{1,0:T(8,128)(2,1)S(1)} %get-tuple-element.73.q_ref, bf16[512,128]{1,0:T(8,128)(2,1)S(1)} %get-tuple-element.74.k_ref, bf16[512,1024]{1,0:T(8,128)(2,1)S(1)} %get-tuple-element.75.v_ref), custom_call_target="tpu_custom_call" | custom-call | flops 268435456 | bytes 2359296 | tf_op jit(solution)/shard_map/pallas_call | solution.py:314
  21.8 0.1 collective-permute-done.3.got.rest_0_
  21.9 0.7 shard_map.150
  22.6 3.0 %collective-permute-start.4 = (bf16[2,160,128]{2,1,0:T(8,128)(2,1)S(1)}, bf16[2,160,128]{2,1,0:T(8,128)(2,1)S(1)}, u32[]{:S(2)}, u32[]{:S(2)}) collective-permute-start(bf16[2,160,128]{2,1,0:T(8,128)(2,1)S(1)} %get-tuple-element.85), channel_id=1, source_target_pairs={{0,8},{1,9},{2,10},{3,11},{4,12},{5,13},{6,14},{7,15},{8,0},{9,1},... | collective-permute-start | bytes 245768 | tf_op jit(solution)/shard_map/ppermute | solution.py:326
  25.7 2.4 %collective-permute-done.4.rest_1_ = bf16[2,160,128]{2,1,0:T(8,128)(2,1)S(1)} collective-permute-done((bf16[2,160,128]{2,1,0:T(8,128)(2,1)S(1)}, bf16[2,160,128]{2,1,0:T(8,128)(2,1)S(1)}, u32[]{:S(2)}, u32[]{:S(2)}) %collective-permute-start.4) | collective-permute-done | bytes 81952 | tf_op jit(solution)/shard_map/ppermute | solution.py:326
  28.1 1.0 %collective-permute-start.5 = (bf16[2,160,128]{2,1,0:T(8,128)(2,1)S(1)}, bf16[2,160,128]{2,1,0:T(8,128)(2,1)S(1)}, u32[]{:S(2)}, u32[]{:S(2)}) collective-permute-start(bf16[2,160,128]{2,1,0:T(8,128)(2,1)S(1)} %get-tuple-element.87), channel_id=1, source_target_pairs={{0,2},{1,3},{2,0},{3,1},{4,6},{5,7},{6,4},{7,5},{8,10},{9,11},{10,... | collective-permute-start | bytes 245768 | tf_op jit(solution)/shard_map/ppermute | solution.py:326
  29.2 3.5 %collective-permute-done.5.other_part = bf16[2,160,128]{2,1,0:T(8,128)(2,1)S(1)} collective-permute-done((bf16[2,160,128]{2,1,0:T(8,128)(2,1)S(1)}, bf16[2,160,128]{2,1,0:T(8,128)(2,1)S(1)}, u32[]{:S(2)}, u32[]{:S(2)}) %collective-permute-start.5) | collective-permute-done | bytes 81952 | tf_op jit(solution)/shard_map/ppermute | solution.py:326
  32.7 0.1 shard_map.152
  32.8 0.1 collective-permute-start.6
  32.8 1.4 %collective-permute-done.6.other = bf16[4,160,128]{2,1,0:T(8,128)(2,1)S(1)} collective-permute-done((bf16[4,160,128]{2,1,0:T(8,128)(2,1)S(1)}, bf16[4,160,128]{2,1,0:T(8,128)(2,1)S(1)}, u32[]{:S(2)}, u32[]{:S(2)}) %collective-permute-start.6) | collective-permute-done | bytes 163872 | tf_op jit(solution)/shard_map/ppermute | solution.py:326
  34.2 4.5 %shard_map.153 = (bf16[512,1024]{1,0:T(8,128)(2,1)}, bf16[512,1024]{1,0:T(8,128)(2,1)S(1)}, bf16[4,160,128]{2,1,0:T(8,128)(2,1)S(1)}, bf16[4,160,128]{2,1,0:T(8,128)(2,1)S(1)}, f32[8,128]{1,0:T(8,128)S(1)}) custom-call(f32[512,512]{1,0:T(8,128)S(1)} %shard_map.146.low, f32[512,512]{1,0:T(8,128)S(1)} %shard_map.147.high, ...), custom_call_target="tpu_custom_call" | custom-call | flops 335544320 | bytes 7217152 | tf_op jit(solution)/shard_map/pallas_call | solution.py:314
  38.7 0.1 collective-permute-start.7
  38.9 1.2 %collective-permute-done.7.near = bf16[4,160,128]{2,1,0:T(8,128)(2,1)S(1)} collective-permute-done((bf16[4,160,128]{2,1,0:T(8,128)(2,1)S(1)}, bf16[4,160,128]{2,1,0:T(8,128)(2,1)S(1)}, u32[]{:S(2)}, u32[]{:S(2)}) %collective-permute-start.7) | collective-permute-done | bytes 163872 | tf_op jit(solution)/shard_map/ppermute | solution.py:326
  40.2 1.0 %collective-permute-start.8 = (bf16[2,160,128]{2,1,0:T(8,128)(2,1)S(1)}, bf16[2,160,128]{2,1,0:T(8,128)(2,1)S(1)}, u32[]{:S(2)}, u32[]{:S(2)}) collective-permute-start(bf16[2,160,128]{2,1,0:T(8,128)(2,1)S(1)} %get-tuple-element.103), channel_id=1, source_target_pairs={{0,2},{1,3},{2,0},{3,1},{4,6},{5,7},{6,4},{7,5},{8,10},{9,11},{10,... | collective-permute-start | bytes 245768 | tf_op jit(solution)/shard_map/ppermute | solution.py:326
  41.2 2.5 %shard_map.154 = (f32[512,256]{1,0:T(8,128)S(1)}, f32[32,512]{1,0:T(8,128)S(1)}, f32[32,512]{1,0:T(8,128)S(1)}) custom-call(bf16[512,128]{1,0:T(8,128)(2,1)S(1)} %get-tuple-element.73.q_ref, bf16[512,128]{1,0:T(8,128)(2,1)S(1)} %get-tuple-element.74.k_ref, bf16[128,512]{1,0:T(8,128)(2,1)S(1)} %get-tuple-element.91.qt_ref, ...), custom_call_target="tpu_custom_call" | custom-call | flops 268435456 | bytes 3276800 | tf_op jit(solution)/shard_map/pallas_call | solution.py:314
  43.7 1.0 %collective-permute-done.8.got.got_y = bf16[2,160,128]{2,1,0:T(8,128)(2,1)S(1)} collective-permute-done((bf16[2,160,128]{2,1,0:T(8,128)(2,1)S(1)}, bf16[2,160,128]{2,1,0:T(8,128)(2,1)S(1)}, u32[]{:S(2)}, u32[]{:S(2)}) %collective-permute-start.8) | collective-permute-done | bytes 81952 | tf_op jit(solution)/shard_map/ppermute | solution.py:326
  44.8 2.0 %collective-permute-start.9 = (bf16[2,160,128]{2,1,0:T(8,128)(2,1)S(1)}, bf16[2,160,128]{2,1,0:T(8,128)(2,1)S(1)}, u32[]{:S(2)}, u32[]{:S(2)}) collective-permute-start(bf16[2,160,128]{2,1,0:T(8,128)(2,1)S(1)} %get-tuple-element.106), channel_id=1, source_target_pairs={{0,4},{1,5},{2,6},{3,7},{4,0},{5,1},{6,2},{7,3},{8,12},{9,13},{10,... | collective-permute-start | bytes 245768 | tf_op jit(solution)/shard_map/ppermute | solution.py:326
  46.7 2.7 %shard_map.155 = (f32[512,256]{1,0:T(8,128)S(1)}, f32[32,512]{1,0:T(8,128)S(1)}, f32[32,512]{1,0:T(8,128)S(1)}) custom-call(bf16[512,128]{1,0:T(8,128)(2,1)S(1)} %get-tuple-element.73.q_ref, bf16[512,128]{1,0:T(8,128)(2,1)S(1)} %get-tuple-element.74.k_ref, bf16[128,512]{1,0:T(8,128)(2,1)S(1)} %get-tuple-element.91.qt_ref, ...), custom_call_target="tpu_custom_call" | custom-call | flops 268435456 | bytes 3276800 | tf_op jit(solution)/shard_map/pallas_call | solution.py:314
  49.4 0.7 shard_map.161
  50.1 3.4 %collective-permute-start.10 = (bf16[2,160,128]{2,1,0:T(8,128)(2,1)S(1)}, bf16[2,160,128]{2,1,0:T(8,128)(2,1)S(1)}, u32[]{:S(2)}, u32[]{:S(2)}) collective-permute-start(bf16[2,160,128]{2,1,0:T(8,128)(2,1)S(1)} %get-tuple-element.110), channel_id=1, source_target_pairs={{0,8},{1,9},{2,10},{3,11},{4,12},{5,13},{6,14},{7,15},{8,0},{9,1},... | collective-permute-start | bytes 245768 | tf_op jit(solution)/shard_map/ppermute | solution.py:326
  53.5 2.5 %shard_map.156 = (f32[512,256]{1,0:T(8,128)S(1)}, f32[32,512]{1,0:T(8,128)S(1)}, f32[32,512]{1,0:T(8,128)S(1)}) custom-call(bf16[512,128]{1,0:T(8,128)(2,1)S(1)} %get-tuple-element.73.q_ref, bf16[512,128]{1,0:T(8,128)(2,1)S(1)} %get-tuple-element.74.k_ref, bf16[128,512]{1,0:T(8,128)(2,1)S(1)} %get-tuple-element.91.qt_ref, ...), custom_call_target="tpu_custom_call" | custom-call | flops 268435456 | bytes 3276800 | tf_op jit(solution)/shard_map/pallas_call | solution.py:314
  56.0 0.1 shard_map.162
  56.1 0.7 collective-permute-start.11
  56.8 2.5 %shard_map.157 = (f32[512,256]{1,0:T(8,128)S(1)}, f32[32,512]{1,0:T(8,128)S(1)}, f32[32,512]{1,0:T(8,128)S(1)}) custom-call(bf16[512,128]{1,0:T(8,128)(2,1)S(1)} %get-tuple-element.73.q_ref, bf16[512,128]{1,0:T(8,128)(2,1)S(1)} %get-tuple-element.74.k_ref, bf16[128,512]{1,0:T(8,128)(2,1)S(1)} %get-tuple-element.91.qt_ref, ...), custom_call_target="tpu_custom_call" | custom-call | flops 268435456 | bytes 3276800 | tf_op jit(solution)/shard_map/pallas_call | solution.py:314
  59.3 1.3 %collective-permute-done.11.other_part = bf16[2,160,128]{2,1,0:T(8,128)(2,1)S(1)} collective-permute-done((bf16[2,160,128]{2,1,0:T(8,128)(2,1)S(1)}, bf16[2,160,128]{2,1,0:T(8,128)(2,1)S(1)}, u32[]{:S(2)}, u32[]{:S(2)}) %collective-permute-start.11) | collective-permute-done | bytes 81952 | tf_op jit(solution)/shard_map/ppermute | solution.py:326
  60.6 0.1 shard_map.163
  60.8 0.9 %shard_map.158 = (f32[512,128]{1,0:T(8,128)S(1)}, f32[3,128]{1,0:T(4,128)S(1)}) custom-call(bf16[512,128]{1,0:T(8,128)(2,1)S(1)} %copy-done.3, bf16[16,1280]{1,0:T(8,128)(2,1)S(1)} %collective-permute-done.rim, bf16[128,512]{1,0:T(8,128)(2,1)S(1)} %get-tuple-element.91.qt_ref, bf16[512,1024]{1,0:T(8,128)(2,1)S(1)} %get-tuple-element.92.gs_ref, ...), custom_call_target="tpu_custom_call" | custom-call | flops 167772160 | bytes 2206720 | tf_op jit(solution)/shard_map/pallas_call | solution.py:314
  61.7 0.5 collective-permute-done.12.other
  62.2 2.1 %shard_map.164 = (f32[512,1024]{1,0:T(8,128)S(1)}, f32[512,128]{1,0:T(8,128)S(1)}, f32[8,1280]{1,0:T(8,128)S(1)}, f32[4,1280]{1,0:T(4,128)S(1)}) custom-call(bf16[512,128]{1,0:T(8,128)(2,1)S(1)} %copy-done.1, bf16[512,1024]{1,0:T(8,128)(2,1)S(1)} %copy-done, bf16[16,1280]{1,0:T(8,128)(2,1)S(1)} %collective-permute-done.rim, ...), custom_call_target="tpu_custom_call" | custom-call | flops 335544320 | bytes 9086464 | tf_op jit(solution)/shard_map/pallas_call | solution.py:314
  64.3 0.2 collective-permute-start.14
  64.5 1.3 %collective-permute-start.13 = (f32[8,1280]{1,0:T(8,128)S(1)}, f32[8,1280]{1,0:T(8,128)S(1)}, u32[]{:S(2)}, u32[]{:S(2)}) collective-permute-start(f32[8,1280]{1,0:T(8,128)S(1)} %get-tuple-element.128), channel_id=1, source_target_pairs={{1,0},{2,1},{3,2},{4,3},{5,4},{6,5},{7,6},{8,7},{9,8},{10,9},{11,1... | collective-permute-start | bytes 122888 | tf_op jit(solution)/shard_map/ppermute | solution.py:518
  65.8 2.7 %collective-permute-start.15 = (f32[4,1280]{1,0:T(4,128)S(1)}, f32[4,1280]{1,0:T(4,128)S(1)}, u32[]{:S(2)}, u32[]{:S(2)}) collective-permute-start(f32[4,1280]{1,0:T(4,128)S(1)} %add.9), channel_id=1, source_target_pairs={{0,2},{1,3},{2,0},{3,1},{4,6},{5,7},{6,4},{7,5},{8,10},{9,11},{10,... | collective-permute-start | bytes 61448 | tf_op jit(solution)/shard_map/ppermute | solution.py:326
  68.5 2.1 %collective-permute-done.15 = f32[4,1280]{1,0:T(4,128)S(1)} collective-permute-done((f32[4,1280]{1,0:T(4,128)S(1)}, f32[4,1280]{1,0:T(4,128)S(1)}, u32[]{:S(2)}, u32[]{:S(2)}) %collective-permute-start.15) | collective-permute-done | bytes 20512 | tf_op jit(solution)/shard_map/ppermute | solution.py:326
  70.6 1.8 %collective-permute-start.16 = (f32[4,1280]{1,0:T(4,128)S(1)}, f32[4,1280]{1,0:T(4,128)S(1)}, u32[]{:S(2)}, u32[]{:S(2)}) collective-permute-start(f32[4,1280]{1,0:T(4,128)S(1)} %add.10), channel_id=1, source_target_pairs={{0,4},{1,5},{2,6},{3,7},{4,0},{5,1},{6,2},{7,3},{8,12},{9,13},{10,... | collective-permute-start | bytes 61448 | tf_op jit(solution)/shard_map/ppermute | solution.py:326
  72.4 2.6 %shard_map.165 = (bf16[512,128]{1,0:T(8,128)(2,1)}, bf16[512,128]{1,0:T(8,128)(2,1)}, bf16[512,1024]{1,0:T(8,128)(2,1)}) custom-call(f32[512,128]{1,0:T(8,128)S(1)} %get-tuple-element.98.gq, f32[512,128]{1,0:T(8,128)S(1)} %get-tuple-element.126.gk, f32[512,1024]{1,0:T(8,128)S(1)} %get-tuple-element.127.gv, f32[8,1280]{1,0:T(8,128)S(1)} %collective-permute-done.13.follow, ...), custom_call_target="tpu_custom_call" | custom-call | flops 167772160 | bytes 3988480 | tf_op jit(solution)/shard_map/pallas_call | solution.py:314
  74.9 3.4 %collective-permute-start.17 = (f32[4,1280]{1,0:T(4,128)S(1)}, f32[4,1280]{1,0:T(4,128)S(1)}, u32[]{:S(2)}, u32[]{:S(2)}) collective-permute-start(f32[4,1280]{1,0:T(4,128)S(1)} %add.11.sums), channel_id=1, source_target_pairs={{0,8},{1,9},{2,10},{3,11},{4,12},{5,13},{6,14},{7,15},{8,0},{9,1},... | collective-permute-start | bytes 61448 | tf_op jit(solution)/shard_map/ppermute | solution.py:326
  78.4 1.8 %collective-permute-done.17.got = f32[4,1280]{1,0:T(4,128)S(1)} collective-permute-done((f32[4,1280]{1,0:T(4,128)S(1)}, f32[4,1280]{1,0:T(4,128)S(1)}, u32[]{:S(2)}, u32[]{:S(2)}) %collective-permute-start.17) | collective-permute-done | bytes 20512 | tf_op jit(solution)/shard_map/ppermute | solution.py:326
  80.1 0.6 shard_map.166
  (31 shorter events, 0.3 us)
Async XLA Ops:
  0.6 13.3 %copy-start.3 = (bf16[512,128]{1,0:T(8,128)(2,1)S(1)}, bf16[512,128]{1,0:T(8,128)(2,1)}, u32[]{:S(2)}) copy-start(bf16[512,128]{1,0:T(8,128)(2,1)} %query.5) | copy-start | bytes 393220
  0.6 4.1 %copy-start.4 = (f32[3,1024]{1,0:T(4,128)S(1)}, f32[3,1024]{1,0:T(4,128)}, u32[]{:S(2)}) copy-start(f32[3,1024]{1,0:T(4,128)} %taps_v.3) | copy-start | bytes 36868
  0.7 4.1 %copy-start.6 = (f32[3,128]{1,0:T(4,128)S(1)}, f32[3,128]{1,0:T(4,128)}, u32[]{:S(2)}) copy-start(f32[3,128]{1,0:T(4,128)} %taps_k.3) | copy-start | bytes 4612
  0.7 13.3 %copy-start.5 = (f32[3,128]{1,0:T(4,128)S(1)}, f32[3,128]{1,0:T(4,128)}, u32[]{:S(2)}) copy-start(f32[3,128]{1,0:T(4,128)} %taps_q.5) | copy-start | bytes 4612
  1.6 3.2 %collective-permute-start = (bf16[16,1280]{1,0:T(8,128)(2,1)S(1)}, bf16[16,1280]{1,0:T(8,128)(2,1)S(1)}, u32[]{:S(2)}, u32[]{:S(2)}) collective-permute-start(bf16[16,1280]{1,0:T(8,128)(2,1)S(1)} %shard_map.143), channel_id=1, source_target_pairs={{0,1},{1,2},{2,3},{3,4},{4,5},{5,6},{6,7},{7,8},{8,9},{9,10},{10,1... | collective-permute-start | bytes 122888 | tf_op jit(solution)/shard_map/ppermute | solution.py:435
  7.3 4.0 %collective-permute-start.1 = (bf16[4,160,128]{2,1,0:T(8,128)(2,1)S(1)}, bf16[4,160,128]{2,1,0:T(8,128)(2,1)S(1)}, u32[]{:S(2)}, u32[]{:S(2)}) collective-permute-start(bf16[4,160,128]{2,1,0:T(8,128)(2,1)S(1)} %get-tuple-element.78), channel_id=1, source_target_pairs={{0,1},{1,0},{2,3},{3,2},{4,5},{5,4},{6,7},{7,6},{8,9},{9,8},{10,11... | collective-permute-start | bytes 491528 | tf_op jit(solution)/shard_map/ppermute | solution.py:326
  11.3 5.4 %collective-permute-start.2 = (bf16[2,160,128]{2,1,0:T(8,128)(2,1)S(1)}, bf16[2,160,128]{2,1,0:T(8,128)(2,1)S(1)}, u32[]{:S(2)}, u32[]{:S(2)}) collective-permute-start(bf16[2,160,128]{2,1,0:T(8,128)(2,1)S(1)} %get-tuple-element.80), channel_id=1, source_target_pairs={{0,2},{1,3},{2,0},{3,1},{4,6},{5,7},{6,4},{7,5},{8,10},{9,11},{10,... | collective-permute-start | bytes 245768 | tf_op jit(solution)/shard_map/ppermute | solution.py:326
  16.8 17.4 %copy-start.2 = (bf16[512,1024]{1,0:T(8,128)(2,1)S(1)}, bf16[512,1024]{1,0:T(8,128)(2,1)}, u32[]{:S(2)}) copy-start(bf16[512,1024]{1,0:T(8,128)(2,1)} %grad.1) | copy-start | bytes 3145732
  16.8 17.4 %copy-start.7 = (f32[1024]{0:T(1024)S(1)}, f32[1024]{0:T(1024)}, u32[]{:S(2)}) copy-start(f32[1024]{0:T(1024)} %param.14) | copy-start | bytes 12292
  16.8 5.1 %collective-permute-start.3 = (bf16[2,160,128]{2,1,0:T(8,128)(2,1)S(1)}, bf16[2,160,128]{2,1,0:T(8,128)(2,1)S(1)}, u32[]{:S(2)}, u32[]{:S(2)}) collective-permute-start(bf16[2,160,128]{2,1,0:T(8,128)(2,1)S(1)} %get-tuple-element.82), channel_id=1, source_target_pairs={{0,4},{1,5},{2,6},{3,7},{4,0},{5,1},{6,2},{7,3},{8,12},{9,13},{10,... | collective-permute-start | bytes 245768 | tf_op jit(solution)/shard_map/ppermute | solution.py:326
  22.6 5.5 %collective-permute-start.4 = (bf16[2,160,128]{2,1,0:T(8,128)(2,1)S(1)}, bf16[2,160,128]{2,1,0:T(8,128)(2,1)S(1)}, u32[]{:S(2)}, u32[]{:S(2)}) collective-permute-start(bf16[2,160,128]{2,1,0:T(8,128)(2,1)S(1)} %get-tuple-element.85), channel_id=1, source_target_pairs={{0,8},{1,9},{2,10},{3,11},{4,12},{5,13},{6,14},{7,15},{8,0},{9,1},... | collective-permute-start | bytes 245768 | tf_op jit(solution)/shard_map/ppermute | solution.py:326
  28.1 4.5 %collective-permute-start.5 = (bf16[2,160,128]{2,1,0:T(8,128)(2,1)S(1)}, bf16[2,160,128]{2,1,0:T(8,128)(2,1)S(1)}, u32[]{:S(2)}, u32[]{:S(2)}) collective-permute-start(bf16[2,160,128]{2,1,0:T(8,128)(2,1)S(1)} %get-tuple-element.87), channel_id=1, source_target_pairs={{0,2},{1,3},{2,0},{3,1},{4,6},{5,7},{6,4},{7,5},{8,10},{9,11},{10,... | collective-permute-start | bytes 245768 | tf_op jit(solution)/shard_map/ppermute | solution.py:326
  32.8 1.5 %collective-permute-start.6 = (bf16[4,160,128]{2,1,0:T(8,128)(2,1)S(1)}, bf16[4,160,128]{2,1,0:T(8,128)(2,1)S(1)}, u32[]{:S(2)}, u32[]{:S(2)}) collective-permute-start(bf16[4,160,128]{2,1,0:T(8,128)(2,1)S(1)} %get-tuple-element.89), channel_id=1, source_target_pairs={{0,1},{1,0},{2,3},{3,2},{4,5},{5,4},{6,7},{7,6},{8,9},{9,8},{10,11... | collective-permute-start | bytes 491528 | tf_op jit(solution)/shard_map/ppermute | solution.py:326
  38.7 1.4 %collective-permute-start.7 = (bf16[4,160,128]{2,1,0:T(8,128)(2,1)S(1)}, bf16[4,160,128]{2,1,0:T(8,128)(2,1)S(1)}, u32[]{:S(2)}, u32[]{:S(2)}) collective-permute-start(bf16[4,160,128]{2,1,0:T(8,128)(2,1)S(1)} %get-tuple-element.101), channel_id=1, source_target_pairs={{0,1},{1,0},{2,3},{3,2},{4,5},{5,4},{6,7},{7,6},{8,9},{9,8},{10,11... | collective-permute-start | bytes 491528 | tf_op jit(solution)/shard_map/ppermute | solution.py:326
  40.2 4.6 %collective-permute-start.8 = (bf16[2,160,128]{2,1,0:T(8,128)(2,1)S(1)}, bf16[2,160,128]{2,1,0:T(8,128)(2,1)S(1)}, u32[]{:S(2)}, u32[]{:S(2)}) collective-permute-start(bf16[2,160,128]{2,1,0:T(8,128)(2,1)S(1)} %get-tuple-element.103), channel_id=1, source_target_pairs={{0,2},{1,3},{2,0},{3,1},{4,6},{5,7},{6,4},{7,5},{8,10},{9,11},{10,... | collective-permute-start | bytes 245768 | tf_op jit(solution)/shard_map/ppermute | solution.py:326
  44.8 4.7 %collective-permute-start.9 = (bf16[2,160,128]{2,1,0:T(8,128)(2,1)S(1)}, bf16[2,160,128]{2,1,0:T(8,128)(2,1)S(1)}, u32[]{:S(2)}, u32[]{:S(2)}) collective-permute-start(bf16[2,160,128]{2,1,0:T(8,128)(2,1)S(1)} %get-tuple-element.106), channel_id=1, source_target_pairs={{0,4},{1,5},{2,6},{3,7},{4,0},{5,1},{6,2},{7,3},{8,12},{9,13},{10,... | collective-permute-start | bytes 245768 | tf_op jit(solution)/shard_map/ppermute | solution.py:326
  50.1 5.9 %collective-permute-start.10 = (bf16[2,160,128]{2,1,0:T(8,128)(2,1)S(1)}, bf16[2,160,128]{2,1,0:T(8,128)(2,1)S(1)}, u32[]{:S(2)}, u32[]{:S(2)}) collective-permute-start(bf16[2,160,128]{2,1,0:T(8,128)(2,1)S(1)} %get-tuple-element.110), channel_id=1, source_target_pairs={{0,8},{1,9},{2,10},{3,11},{4,12},{5,13},{6,14},{7,15},{8,0},{9,1},... | collective-permute-start | bytes 245768 | tf_op jit(solution)/shard_map/ppermute | solution.py:326
  56.1 4.5 %collective-permute-start.11 = (bf16[2,160,128]{2,1,0:T(8,128)(2,1)S(1)}, bf16[2,160,128]{2,1,0:T(8,128)(2,1)S(1)}, u32[]{:S(2)}, u32[]{:S(2)}) collective-permute-start(bf16[2,160,128]{2,1,0:T(8,128)(2,1)S(1)} %get-tuple-element.114), channel_id=1, source_target_pairs={{0,2},{1,3},{2,0},{3,1},{4,6},{5,7},{6,4},{7,5},{8,10},{9,11},{10,... | collective-permute-start | bytes 245768 | tf_op jit(solution)/shard_map/ppermute | solution.py:326
  59.3 2.9 %copy-start = (bf16[512,1024]{1,0:T(8,128)(2,1)S(1)}, bf16[512,1024]{1,0:T(8,128)(2,1)}, u32[]{:S(2)}) copy-start(bf16[512,1024]{1,0:T(8,128)(2,1)} %value.3) | copy-start | bytes 3145732
  59.3 2.9 %copy-start.1 = (bf16[512,128]{1,0:T(8,128)(2,1)S(1)}, bf16[512,128]{1,0:T(8,128)(2,1)}, u32[]{:S(2)}) copy-start(bf16[512,128]{1,0:T(8,128)(2,1)} %key.3) | copy-start | bytes 393220
  60.7 1.5 %collective-permute-start.12 = (bf16[4,160,128]{2,1,0:T(8,128)(2,1)S(1)}, bf16[4,160,128]{2,1,0:T(8,128)(2,1)S(1)}, u32[]{:S(2)}, u32[]{:S(2)}) collective-permute-start(bf16[4,160,128]{2,1,0:T(8,128)(2,1)S(1)} %get-tuple-element.118), channel_id=1, source_target_pairs={{0,1},{1,0},{2,3},{3,2},{4,5},{5,4},{6,7},{7,6},{8,9},{9,8},{10,11... | collective-permute-start | bytes 491528 | tf_op jit(solution)/shard_map/ppermute | solution.py:326
  64.3 1.5 %collective-permute-start.14 = (f32[4,1280]{1,0:T(4,128)S(1)}, f32[4,1280]{1,0:T(4,128)S(1)}, u32[]{:S(2)}, u32[]{:S(2)}) collective-permute-start(f32[4,1280]{1,0:T(4,128)S(1)} %get-tuple-element.132), channel_id=1, source_target_pairs={{0,1},{1,0},{2,3},{3,2},{4,5},{5,4},{6,7},{7,6},{8,9},{9,8},{10,11... | collective-permute-start | bytes 61448 | tf_op jit(solution)/shard_map/ppermute | solution.py:326
  64.5 7.9 %collective-permute-start.13 = (f32[8,1280]{1,0:T(8,128)S(1)}, f32[8,1280]{1,0:T(8,128)S(1)}, u32[]{:S(2)}, u32[]{:S(2)}) collective-permute-start(f32[8,1280]{1,0:T(8,128)S(1)} %get-tuple-element.128), channel_id=1, source_target_pairs={{1,0},{2,1},{3,2},{4,3},{5,4},{6,5},{7,6},{8,7},{9,8},{10,9},{11,1... | collective-permute-start | bytes 122888 | tf_op jit(solution)/shard_map/ppermute | solution.py:518
  65.8 4.8 %collective-permute-start.15 = (f32[4,1280]{1,0:T(4,128)S(1)}, f32[4,1280]{1,0:T(4,128)S(1)}, u32[]{:S(2)}, u32[]{:S(2)}) collective-permute-start(f32[4,1280]{1,0:T(4,128)S(1)} %add.9), channel_id=1, source_target_pairs={{0,2},{1,3},{2,0},{3,1},{4,6},{5,7},{6,4},{7,5},{8,10},{9,11},{10,... | collective-permute-start | bytes 61448 | tf_op jit(solution)/shard_map/ppermute | solution.py:326
  70.6 4.4 %collective-permute-start.16 = (f32[4,1280]{1,0:T(4,128)S(1)}, f32[4,1280]{1,0:T(4,128)S(1)}, u32[]{:S(2)}, u32[]{:S(2)}) collective-permute-start(f32[4,1280]{1,0:T(4,128)S(1)} %add.10), channel_id=1, source_target_pairs={{0,4},{1,5},{2,6},{3,7},{4,0},{5,1},{6,2},{7,3},{8,12},{9,13},{10,... | collective-permute-start | bytes 61448 | tf_op jit(solution)/shard_map/ppermute | solution.py:326
  74.9 5.2 %collective-permute-start.17 = (f32[4,1280]{1,0:T(4,128)S(1)}, f32[4,1280]{1,0:T(4,128)S(1)}, u32[]{:S(2)}, u32[]{:S(2)}) collective-permute-start(f32[4,1280]{1,0:T(4,128)S(1)} %add.11.sums), channel_id=1, source_target_pairs={{0,8},{1,9},{2,10},{3,11},{4,12},{5,13},{6,14},{7,15},{8,0},{9,1},... | collective-permute-start | bytes 61448 | tf_op jit(solution)/shard_map/ppermute | solution.py:326

commit v3 on v2

v3 whole, which is shorter than its diff:
```python
import functools

import jax
import jax.numpy as jnp
from jax import lax
from jax.experimental import pallas as pl
from jax.experimental.pallas import tpu as pltpu
from jax.sharding import PartitionSpec as P

HEADS = 8
HALF = HEADS // 2
PART = HEADS // 4
FEAT = 16
DIM = 128
EPSILON = 1e-06
LANES = HEADS * FEAT
WIDE = HEADS * DIM
ALL = 2 * LANES + WIDE
ROWS = 160
LIN = 128
TAIL = 144
RIM = 16
STEP = 128
F32 = jnp.float32
BF16 = jnp.bfloat16

NN = (((1,), (0,)), ((), ()))
NT = (((1,), (1,)), ((), ()))
TN = (((0,), (0,)), ((), ()))


def dot(a, b, dims):
    return lax.dot_general(a, b, dims, preferred_element_type=F32)


def head_rows(h):
    return slice(h * FEAT, (h + 1) * FEAT)


def head_lanes(h):
    return slice(h * DIM, (h + 1) * DIM)


def conv(wide_ref, taps, rows):
    margin = taps.shape[0] - 1
    total = taps[0:1] * wide_ref[RIM - margin : RIM - margin + rows]
    for o in range(1, margin + 1):
        total = total + taps[o : o + 1] * wide_ref[RIM - margin + o : RIM - margin + o + rows]
    return total


def tap_sums(grad, wide_ref, taps):
    rows = grad.shape[0]
    start = RIM - (taps - 1)
    return [
        jnp.sum(grad * wide_ref[start + o : start + o + rows], axis=0, keepdims=True)
        for o in range(taps)
    ]


def turned(x, shift):
    return x if shift % FEAT == 0 else pltpu.roll(x, shift % FEAT, 0)


def features(x):
    half = (0.5 / FEAT) ** 0.5
    pieces = [(x * turned(x, FEAT - d) * half).astype(BF16) for d in range(8)]
    pieces.append((x * FEAT ** (-0.25)).astype(BF16))
    rows = lax.broadcasted_iota(jnp.int32, (8, x.shape[1]), 0)
    one = jnp.where(rows == 0, 1.0, 0.0).astype(F32)
    pieces.append(jnp.concatenate([x[:8] * x[8:] * half, one], axis=0).astype(BF16))
    return jnp.concatenate(pieces, axis=0)


def feature_grad(x, state, vector):
    g = dot(state, vector, NT)
    crossed = 2.0 * g[0:FEAT] * x
    for d in range(1, 8):
        part = g[d * FEAT : (d + 1) * FEAT]
        crossed = crossed + part * turned(x, FEAT - d) + turned(part * x, d)
    part = g[TAIL : TAIL + 8]
    crossed = crossed + jnp.concatenate([part * x[8:], part * x[:8]], axis=0)
    return g[LIN:TAIL] * FEAT ** (-0.25) + crossed * (0.5 / FEAT) ** 0.5


def half_index(own):
    core = lax.rem(lax.axis_index("seq"), 2)
    return core if own else 1 - core


def rows_of(half, g):
    return pl.ds(pl.multiple_of((half * HALF + g) * FEAT, FEAT), FEAT)


def lanes_of(half, g, start=0):
    return pl.ds(pl.multiple_of(start + (half * HALF + g) * DIM, DIM), DIM)


def doubled(state_ref, out_ref):
    rows = lax.broadcasted_iota(jnp.int32, (ROWS, DIM), 0)
    pair = ((rows >= FEAT) & (rows < LIN)) | ((rows >= TAIL) & (rows < TAIL + 8))
    weight = jnp.where(pair, 2.0, 1.0).astype(F32)
    for g in range(HALF):
        out_ref[g] = (state_ref[g].astype(F32) * weight).astype(BF16)


def head_mask(h):
    lanes = lax.broadcasted_iota(jnp.int32, (1, LANES), 1)
    return jnp.where(lanes // FEAT == h, 1.0, 0.0).astype(F32).astype(BF16)


def fill(wide, rim, rest):
    wide[0:RIM] = rim.astype(F32)
    wide[RIM : RIM + rest.shape[0]] = rest.astype(F32)


def end_kernel(query, key, value, out, sems):
    start = query.shape[0] - RIM
    copies = [
        pltpu.make_async_copy(ref.at[pl.ds(start, RIM)], out.at[:, pl.ds(lane, ref.shape[1])], sems.at[i])
        for i, (ref, lane) in enumerate(((query, 0), (key, LANES), (value, 2 * LANES)))
    ]
    for copy in copies:
        copy.start()
    for copy in copies:
        copy.wait()


def value_states(half, kt, value, rim, taps_v, v_out, f_out, state_out, wide):
    rows = value.shape[0]
    for g in range(HALF):
        f_out[g] = features(kt[rows_of(half, g)].astype(F32))
    for g in range(HALF):
        fill(wide, rim[:, lanes_of(half, g, 2 * LANES)], value[:, lanes_of(half, g)])
        v_out[:, head_lanes(g)] = conv(wide, taps_v[:, lanes_of(half, g)], rows).astype(BF16)
    for g in range(HALF):
        state_out[g] = dot(f_out[g], v_out[:, head_lanes(g)], NN).astype(BF16)


def first_key_kernel(key, value, rim, taps_k, taps_v, k_out, kt_out, v_out, f_out, state_out, wide):
    rows = key.shape[0]
    fill(wide, rim[:, LANES : 2 * LANES], key[...])
    k = conv(wide, taps_k[...], rows).astype(BF16)
    k_out[...] = k
    kt_out[...] = k.astype(F32).T.astype(BF16)
    value_states(half_index(False), kt_out, value, rim, taps_v, v_out, f_out, state_out, wide)


def second_key_kernel(kt, value, rim, taps_v, v_out, f_out, state_out, wide):
    value_states(half_index(True), kt, value, rim, taps_v, v_out, f_out, state_out, wide)


def query_kernel(query, rim, taps_q, q_out, qt_out, fq_out, wide):
    rows = query.shape[0]
    fill(wide, rim[:, 0:LANES], query[...])
    q = conv(wide, taps_q[...], rows).astype(BF16)
    q_out[...] = q
    qt = q.astype(F32).T
    qt_out[...] = qt.astype(BF16)
    for h in range(HEADS):
        fq_out[h] = features(qt[head_rows(h)])


def local_kernel(own, q_ref, k_ref, v_ref, out):
    rows = q_ref.shape[0]
    half = half_index(own)
    quarter = q_ref[...] * jnp.asarray(FEAT ** (-0.5), BF16)
    for g in range(HALF):
        qs = quarter * head_mask(half * HALF + g)
        for start in range(0, rows, STEP):
            stop = start + STEP
            t = dot(qs[start:stop], k_ref[0:stop], NT)
            w = (0.5 * t + 1.0) * t + 1.0
            at = lax.broadcasted_iota(jnp.int32, (STEP, stop), 0) + start
            w = jnp.where(at >= lax.broadcasted_iota(jnp.int32, (STEP, stop), 1), w, 0.0)
            out[start:stop, head_lanes(g)] = dot(w.astype(BF16), v_ref[0:stop, head_lanes(g)], NN)


def norm_kernel(own, local, fq, prefix, grad, gain, out, gs_out, state_out, gain_out, pre, summed_ref):
    half = half_index(own)
    doubled(prefix, pre)
    for g in range(HALF):
        place = head_lanes(g)
        summed_ref[:, place] = local[:, place] + dot(fq[half * HALF + g], pre[g], TN)
    for g in range(HALF):
        place = head_lanes(g)
        summed = summed_ref[:, place]
        scale = lax.rsqrt(jnp.mean(summed * summed, axis=-1, keepdims=True) + EPSILON)
        normal = summed * scale
        weight = gain[pl.ds(half * HALF + g, 1)]
        out[:, place] = (normal * weight).astype(BF16)
        incoming = grad[:, lanes_of(half, g)].astype(F32)
        gain_out[g : g + 1] = jnp.sum(incoming * normal, axis=0, keepdims=True)
        upstream = incoming * weight
        gs = scale * (upstream - normal * jnp.mean(normal * upstream, axis=-1, keepdims=True))
        gs = gs.astype(BF16)
        gs_out[:, place] = gs
        state_out[g] = dot(fq[half * HALF + g], gs, NN).astype(BF16)


def back_kernel(own, part, q_ref, k_ref, qt_ref, kt_ref, v_ref, gs_ref, gv_out, gq_out, gk_out):
    rows = q_ref.shape[0]
    half = half_index(own)
    quarter = q_ref[...] * jnp.asarray(FEAT ** (-0.5), BF16)
    for i in range(PART):
        g = part * PART + i
        ks = k_ref[...] * head_mask(half * HALF + g)
        qt = qt_ref[rows_of(half, g)]
        kt = kt_ref[rows_of(half, g)]
        for start in range(0, rows, STEP):
            stop = start + STEP
            shape = (STEP, rows - start)
            t = dot(ks[start:stop], quarter[start:], NT)
            seen = lax.broadcasted_iota(jnp.int32, shape, 1) >= lax.broadcasted_iota(jnp.int32, shape, 0)
            w = jnp.where(seen, (0.5 * t + 1.0) * t + 1.0, 0.0).astype(BF16)
            gs = gs_ref[start:, head_lanes(g)]
            gv_out[start:stop, head_lanes(i)] = dot(w, gs, NN)
            gw = dot(v_ref[start:stop, head_lanes(g)], gs, NT)
            s = jnp.where(seen, gw * (FEAT ** (-0.5) + FEAT ** (-0.5) * t), 0.0).astype(BF16)
            part_q = dot(kt[:, start:stop], s, NN)
            if start == 0:
                gq_out[head_rows(i)] = part_q
            else:
                gq_out[head_rows(i), start:] += part_q
            gk_out[head_rows(i), start:stop] = dot(qt[:, start:], s, NT)


def query_grad_kernel(
    query, rim, qt_ref, gs_a, gs_b, pre_a, pre_b, a0, a1, b0, b1, taps_q, g_out, sums, wide, pre, turned_grad
):
    for own, gs, prefix, locals_ in ((True, gs_a, pre_a, (a0, a1)), (False, gs_b, pre_b, (b0, b1))):
        half = half_index(own)
        doubled(prefix, pre)
        for g in range(HALF):
            x = qt_ref[rows_of(half, g)].astype(F32)
            turned_grad[rows_of(half, g)] = locals_[g // PART][head_rows(g % PART)] + feature_grad(
                x, pre[g], gs[:, head_lanes(g)]
            )
    grad = turned_grad[...].T
    g_out[...] = grad
    fill(wide, rim[:, 0:LANES], query[...])
    for o, row in enumerate(tap_sums(grad, wide, taps_q.shape[0])):
        sums[o : o + 1] = row


def later_half(half, value, rim, kt, fk, v, state, locals_v, locals_k, gv_out, gk_put, sums_put, wide, post, taps):
    doubled(state, post)
    for g in range(HALF):
        local = locals_v[g // PART][:, head_lanes(g % PART)]
        gv_out[:, head_lanes(g)] = local + dot(fk[g], post[g], TN)
    for g in range(HALF):
        local = locals_k[g // PART][head_rows(g % PART)]
        x = kt[rows_of(half, g)].astype(F32)
        gk_put(g, local + feature_grad(x, post[g], v[:, head_lanes(g)]))
    for g in range(HALF):
        fill(wide, rim[:, lanes_of(half, g, 2 * LANES)], value[:, lanes_of(half, g)])
        for o, row in enumerate(tap_sums(gv_out[:, head_lanes(g)], wide, taps)):
            sums_put(o, g, row)


def first_later_kernel(value, rim, kt, fk, v, state, v0, v1, k0, k1, gv_out, gk_out, sums, wide, post):
    def gk_put(g, x):
        gk_out[head_rows(g)] = x

    def sums_put(o, g, row):
        sums[o : o + 1, head_lanes(g)] = row

    later_half(
        half_index(False), value, rim, kt, fk, v, state, (v0, v1), (k0, k1), gv_out, gk_put, sums_put, wide, post,
        sums.shape[0],
    )


def second_later_kernel(
    key, value, rim, kt, fk, v, state, v0, v1, k0, k1, gv_b, gk_b, sums_b, gq, sums_q, gain_a, gain_b,
    gv_out, gk_out, head_out, sums, wide, post, turned_grad,
):
    taps = sums_q.shape[0]
    rows = key.shape[0]
    half_a, half_b = half_index(True), half_index(False)

    def gk_put(g, x):
        turned_grad[rows_of(half_a, g)] = x

    def sums_put(o, g, row):
        sums[o : o + 1, lanes_of(half_a, g, 2 * LANES)] = row

    turned_grad[pl.ds(pl.multiple_of(half_b * HALF * FEAT, HALF * FEAT), HALF * FEAT)] = gk_b[...]
    later_half(
        half_a, value, rim, kt, fk, v, state, (v0, v1), (k0, k1), gv_out, gk_put, sums_put, wide, post, taps
    )
    grad = turned_grad[...].T
    gk_out[...] = grad
    fill(wide, rim[:, LANES : 2 * LANES], key[...])
    for o, row in enumerate(tap_sums(grad, wide, taps)):
        sums[o : o + 1, LANES : 2 * LANES] = row
    sums[0:taps, 0:LANES] = sums_q[...]
    sums[taps : taps + 1, 0 : 2 * LANES] = jnp.zeros((1, 2 * LANES), F32)
    head_out[:, 0:LANES] = gq[0:8]
    head_out[:, LANES : 2 * LANES] = grad[0:8]
    for g in range(HALF):
        sums[0:taps, lanes_of(half_b, g, 2 * LANES)] = sums_b[:, head_lanes(g)]
        for half, gain, gv in ((half_a, gain_a, gv_out), (half_b, gain_b, gv_b)):
            sums[taps : taps + 1, lanes_of(half, g, 2 * LANES)] = gain[g : g + 1]
            head_out[:, lanes_of(half, g, 2 * LANES)] = gv[0:8, head_lanes(g)]


def signal_kernel(
    gq, gk, gv_a, gv_b, follow, out_a, out_b, taps_q, taps_k, taps_v, q_out, k_out, v_out, out, wide
):
    rows = gq.shape[0]
    count = taps_q.shape[0]

    def one(grad, after, taps):
        wide[0:rows] = grad
        wide[rows : rows + 8] = after
        total = taps[0:1] * wide[count - 1 : count - 1 + rows]
        for o in range(1, count):
            total = total + taps[o : o + 1] * wide[count - 1 - o : count - 1 - o + rows]
        return total.astype(BF16)

    q_out[...] = one(gq[...], follow[:, 0:LANES], taps_q[...])
    k_out[...] = one(gk[...], follow[:, LANES : 2 * LANES], taps_k[...])
    for own, gv, tokens in ((True, gv_a, out_a), (False, gv_b, out_b)):
        half = half_index(own)
        for g in range(HALF):
            place = lanes_of(half, g)
            out[:, place] = tokens[:, head_lanes(g)]
            v_out[:, place] = one(gv[:, head_lanes(g)], follow[:, lanes_of(half, g, 2 * LANES)], taps_v[:, place])


def finish_kernel(factor, *refs):
    *terms, q_out, k_out, v_out, gain_out = refs
    taps = q_out.shape[0]
    total = terms[0][...]
    for term in terms[1:]:
        total = total + term[...]
    total = total * factor
    q_out[...] = total[0:taps, 0:LANES]
    k_out[...] = total[0:taps, LANES : 2 * LANES]
    v_out[...] = total[0:taps, 2 * LANES :]
    gain_out[...] = total[taps : taps + 1, 2 * LANES :]


def far(x):
    return pltpu.with_memory_space_constraint(x, pltpu.HBM)


def held(*xs):
    return [pltpu.with_memory_space_constraint(x, pltpu.VMEM) for x in xs]


def call(kernel, outs, scratch, args, flops, limit=16, loose=(), **specs):
    size = lambda a: a.size * a.dtype.itemsize
    moved = sum(size(a) for a in args) + sum(size(o) for o in outs)
    return pl.pallas_call(
        kernel,
        out_shape=[o if i in loose else pltpu.VMEM(o.shape, o.dtype) for i, o in enumerate(outs)],
        scratch_shapes=scratch,
        compiler_params=pltpu.CompilerParams(vmem_limit_bytes=limit * 2**20),
        cost_estimate=pl.CostEstimate(flops=flops, bytes_accessed=moved, transcendentals=0),
        **specs,
    )(*args)


def exchange(x, distance):
    count = lax.axis_size("seq")
    return lax.ppermute(x, "seq", [(i, i ^ distance) for i in range(count)])


def tie(x, *others):
    return lax.optimization_barrier((x, *others))[0]


def on_side(bit, reverse):
    set_ = lax.rem(lax.div(lax.axis_index("seq"), bit), 2)
    return set_ == (0 if reverse else 1)


def chosen(flag, x):
    return jnp.where(flag, x, jnp.zeros_like(x))


def pair_kernel(keep, near, part, their):
    upper = lax.rem(lax.div(lax.axis_index("seq"), 2), 2)

    def half(which):
        place = pl.ds(which * PART, PART)
        return keep[place].astype(F32) + near[place].astype(F32)

    part[...] = half(upper)
    their[...] = half(1 - upper).astype(BF16)


def step_kernel(part, *refs):
    *gots, send = refs
    total = part[...]
    for got in gots:
        total = total + got[...].astype(F32)
    send[...] = total.astype(BF16)


def part_kernel(reverse, part, got_y, *rest):
    *gots, own, give = rest
    before = jnp.zeros(part.shape, F32)
    for i, got in enumerate(gots):
        before = before + chosen(on_side(4 << i, reverse), got[...].astype(F32))
    own[...] = before + chosen(on_side(2, reverse), got_y[...].astype(F32))
    give[...] = (before + chosen(jnp.logical_not(on_side(2, reverse)), part[...])).astype(BF16)


def merge_kernel(reverse, own_part, other_part, keep, near, own, give):
    upper = lax.rem(lax.div(lax.axis_index("seq"), 2), 2)
    side = on_side(1, reverse)
    for part, which in ((own_part, upper), (other_part, 1 - upper)):
        place = pl.ds(which * PART, PART)
        before = part[...].astype(F32)
        own[place] = (before + chosen(side, near[place].astype(F32))).astype(BF16)
        give[place] = (before + chosen(jnp.logical_not(side), keep[place].astype(F32))).astype(BF16)


def beyond(keep, send, reverse, works, last):
    count = lax.axis_size("seq")
    works = list(works)
    st = jax.ShapeDtypeStruct
    whole, part_shape = keep.shape, (PART, *keep.shape[1:])
    wide, narrow = st(part_shape, F32), st(part_shape, BF16)
    cost = 4 * keep.size

    def under(x):
        return tie(x, works.pop(0)()) if works else x

    near = exchange(send, 1)
    part, their = call(pair_kernel, [wide, narrow], [], (keep, near), cost)
    got_y = exchange(their, 2)
    gots = []
    bit = 4
    while bit < count:
        send = call(step_kernel, [narrow], [], (part, got_y, *gots), cost)[0]
        gots.append(exchange(under(send), bit))
        bit *= 2
    own_part, give_part = call(
        functools.partial(part_kernel, reverse), [wide, narrow], [], (part, got_y, *gots), cost
    )
    other_part = exchange(under(give_part), 2)
    own, give = call(
        functools.partial(merge_kernel, reverse), [st(whole, BF16)] * 2, [], (own_part, other_part, keep, near), cost
    )
    other = exchange(under(give), 1)
    return own, tie(other, last(own))


def shards(query_in, key_in, value_in, conv_query, conv_key, conv_value, norm_gain, grad_out):
    rows = query_in.shape[0]
    taps = conv_query.shape[0]
    count = lax.axis_size("seq")
    total_rows = rows * count
    st = jax.ShapeDtypeStruct
    half_width = HALF * DIM
    half_state, half_wide = st((HALF, ROWS, DIM), BF16), st((rows, half_width), F32)
    half_narrow, half_features = st((rows, half_width), BF16), st((HALF, ROWS, rows), BF16)
    flat, turned_flat = st((rows, LANES), F32), st((LANES, rows), BF16)
    state_scratch = pltpu.VMEM((HALF, ROWS, DIM), BF16)
    wide = pltpu.VMEM((RIM + rows, DIM), F32)
    gain = norm_gain.reshape(HEADS, DIM)
    state_flops = HEADS * ROWS * DIM * rows
    square_flops = 2 * HALF * rows * rows * DIM

    apart = pl.BlockSpec(memory_space=pltpu.HBM)
    ends = call(
        end_kernel,
        [st((RIM, ALL), BF16)],
        [pltpu.SemaphoreType.DMA((3,))],
        (far(query_in), far(key_in), far(value_in)),
        rows,
        in_specs=[apart] * 3,
    )[0]
    rim = lax.ppermute(ends, "seq", [(i, i + 1) for i in range(count - 1)])

    k, kt, v_b, fk_b, state_b = call(
        first_key_kernel,
        [st((rows, LANES), BF16), turned_flat, half_narrow, half_features, half_state],
        [wide],
        (key_in, value_in, rim, conv_key, conv_value),
        state_flops,
    )
    v_a, fk_a, state_a = call(
        second_key_kernel,
        [half_narrow, half_features, half_state],
        [wide],
        (*held(kt), value_in, rim, conv_value),
        state_flops,
    )
    made = {}

    def local_work(own, v):
        def work():
            if "q" not in made:
                made["q"] = call(
                    query_kernel,
                    [st((rows, LANES), BF16), turned_flat, st((HEADS, ROWS, rows), BF16)],
                    [wide],
                    (query_in, rim, conv_query),
                    state_flops,
                )
            made[own] = call(
                functools.partial(local_kernel, own),
                [half_wide],
                [],
                held(made["q"][0], k, v),
                2 * square_flops,
            )[0]
            return made[own]

        return work

    def norm(own, prefix):
        return call(
            functools.partial(norm_kernel, own),
            [half_narrow, half_narrow, half_state, st((HALF, DIM), F32)],
            [state_scratch, pltpu.VMEM((rows, half_width), F32)],
            (*held(made[own], made["q"][2]), prefix, grad_out, gain),
            2 * state_flops,
        )

    def first_norm(prefix):
        made["norm"] = norm(True, prefix)
        return made["norm"][0]

    pre_a, pre_b = beyond(
        state_a, state_b, False, [local_work(True, v_a), local_work(False, v_b)], first_norm
    )
    q, qt, fq = made["q"]
    out_a, gs_a, state_a, gain_a = made["norm"]
    out_b, gs_b, state_b, gain_b = norm(False, pre_b)
    back = []

    def back_work(own, part, v, gs):
        def work():
            back.append(
                call(
                    functools.partial(back_kernel, own, part),
                    [st((rows, PART * DIM), F32), st((PART * FEAT, rows), F32), st((PART * FEAT, rows), F32)],
                    [],
                    held(q, k, qt, kt, v, gs),
                    2 * square_flops,
                )
            )
            return back[-1][0]

        return work

    def last_work():
        work = back_work(False, 1, v_b, gs_b)()
        made["gq"] = call(
            query_grad_kernel,
            [flat, st((taps, LANES), F32)],
            [wide, state_scratch, pltpu.VMEM((LANES, rows), F32)],
            (query_in, rim, *held(qt, gs_a, gs_b), pre_a, pre_b, *held(*[b[1] for b in back]), conv_query),
            state_flops,
        )
        return made["gq"][0]

    def first_later(state):
        made["later"] = call(
            first_later_kernel,
            [half_wide, st((HALF * FEAT, rows), F32), st((taps, half_width), F32)],
            [wide, state_scratch],
            (value_in, rim, *held(kt, fk_b, v_b), state, *held(back[2][0], back[3][0], back[2][2], back[3][2])),
            2 * state_flops,
        )
        return made["later"][0]

    works = [back_work(True, 0, v_a, gs_a), back_work(True, 1, v_a, gs_a), back_work(False, 0, v_b, gs_b), last_work]
    _, post_a = beyond(state_b, state_a, True, works, first_later)
    gv_b, gk_b, sums_b = made["later"]
    gq, sums_q = made["gq"]
    gv_a, gk, heads, sums = call(
        second_later_kernel,
        [half_wide, flat, st((8, ALL), F32), st((taps + 1, ALL), F32)],
        [wide, state_scratch, pltpu.VMEM((LANES, rows), F32)],
        (key_in, value_in, rim, *held(kt, fk_a, v_a), post_a,
         *held(back[0][0], back[1][0], back[0][2], back[1][2], gv_b, gk_b, sums_b, gq, sums_q, gain_a, gain_b)),
        2 * state_flops,
    )
    follow = lax.ppermute(heads, "seq", [(i + 1, i) for i in range(count - 1)])
    bit = 4
    while bit < count:
        group = (bit, 2 * bit, 3 * bit) if 2 * bit < count else (bit,)
        for got in [exchange(sums, distance) for distance in group]:
            sums = sums + got
        bit *= len(group) + 1
    grad_query, grad_key, grad_value, output = call(
        signal_kernel,
        [st((rows, LANES), BF16), st((rows, LANES), BF16), st((rows, WIDE), BF16), st((rows, WIDE), BF16)],
        [pltpu.VMEM((rows + 8, DIM), F32)],
        (*held(gq, gk, gv_a, gv_b), follow, *held(out_a, out_b), conv_query, conv_key, conv_value),
        2 * state_flops,
        loose=(0, 1, 2, 3),
    )
    taps_query, taps_key, taps_value, taps_gain = call(
        functools.partial(finish_kernel, total_rows ** (-0.5)),
        [st((taps, LANES), F32), st((taps, LANES), F32), st((taps, WIDE), F32), st((1, WIDE), F32)],
        [],
        (tie(sums, grad_value), *[exchange(sums, distance) for distance in (1, 2, 3)]),
        rows,
        loose=(0, 1, 2, 3),
    )
    return (
        output,
        grad_query,
        grad_key,
        grad_value,
        taps_query,
        taps_key,
        taps_value,
        taps_gain.reshape(WIDE),
    )


def solution(mesh):
    rows = P(("groups", "seq"), None)
    return jax.shard_map(
        shards,
        mesh=mesh,
        in_specs=(rows, rows, rows, P(), P(), P(), P(), rows),
        out_specs=(rows, rows, rows, rows, P("groups", None), P("groups", None), P("groups", None), P("groups")),
        check_vma=False,
    )
```

time: 81 us -> 71.5 us (0.88)
  waiting for transfers between devices: 17.1 us -> 11.5 us
  Pallas kernels: 31.3 us -> 27.8 us
    ppermute x16 -> x18, waiting for transfers between devices: 16.3 us -> 10.7 us  [exchange(): return lax.ppermute(x, 'seq', [(i, i ^ distance) for i in range(count)])]
    pallas_call x24 -> x27, Pallas kernels: 31.3 us -> 27.8 us  [call(): pl.pallas_call(kernel, out_shape=[o if i in loose else pltpu.VMEM(o.shape...]
    ppermute x16 -> x18, starting transfers between devices: 27.8 us -> 27.2 us  [exchange(): return lax.ppermute(x, 'seq', [(i, i ^ distance) for i in range(count)])]
  transfers between devices with their start and end apart: 18 -> 20, of which waited for: 12 -> 9; matrix products, arithmetic and copies ran while one was open for 0% -> 0% of each run, Pallas kernels for 23% -> 33%
where the time goes in v3:
time: 71.5 us; the launch traced here: 71.3 us
  starting transfers between devices  31 us (43%)
  Pallas kernels  27.8 us (39%)
  waiting for transfers between devices  11.5 us (16%)
  between operations  0.89 us (1%)
    pallas_call x27, Pallas kernels, call(): pl.pallas_call(kernel, out_shape=[o if i in loose else pltpu.VMEM(o.shape...  27.8 us
    ppermute x18, starting transfers between devices, exchange(): return lax.ppermute(x, 'seq', [(i, i ^ distance) for i in range(count)])  27.2 us
    ppermute x18, waiting for transfers between devices, exchange(): return lax.ppermute(x, 'seq', [(i, i ^ distance) for i in range(count)])  10.7 us
    ppermute x1, starting transfers between devices, shards(): rim = lax.ppermute(ends, 'seq', [(i, i + 1) for i in range(count - 1)])  2.49 us
  transfers between devices with their start and end apart: 20, of which 9 were waited for; matrix products, arithmetic and copies ran while one was open for 0% of the time, Pallas kernels for 33%

profile of v3, /device:TPU:0, one launch (start us, length us, event | category | flops | bytes accessed | tf_op | source)
XLA Modules:
  0.0 71.3 jit_solution(14195396557354324143)
XLA Ops:
  0.7 0.9 %shard_map.143 = bf16[16,1280]{1,0:T(8,128)(2,1)S(1)} custom-call(bf16[512,128]{1,0:T(8,128)(2,1)} %query.5, bf16[512,128]{1,0:T(8,128)(2,1)} %key.5, bf16[512,1024]{1,0:T(8,128)(2,1)} %value.9), custom_call_target="tpu_custom_call" | custom-call | flops 512 | bytes 1351680 | tf_op jit(solution)/shard_map/pallas_call | solution.py:356
  1.6 2.5 %collective-permute-start = (bf16[16,1280]{1,0:T(8,128)(2,1)S(1)}, bf16[16,1280]{1,0:T(8,128)(2,1)S(1)}, u32[]{:S(2)}, u32[]{:S(2)}) collective-permute-start(bf16[16,1280]{1,0:T(8,128)(2,1)S(1)} %shard_map.143), channel_id=1, source_target_pairs={{0,1},{1,2},{2,3},{3,4},{4,5},{5,6},{6,7},{7,8},{8,9},{9,10},{10,1... | collective-permute-start | bytes 122888 | tf_op jit(solution)/shard_map/ppermute | solution.py:478
  4.1 0.9 %collective-permute-done.rim = bf16[16,1280]{1,0:T(8,128)(2,1)S(1)} collective-permute-done((bf16[16,1280]{1,0:T(8,128)(2,1)S(1)}, bf16[16,1280]{1,0:T(8,128)(2,1)S(1)}, u32[]{:S(2)}, u32[]{:S(2)}) %collective-permute-start) | collective-permute-done | bytes 40992 | tf_op jit(solution)/shard_map/ppermute | solution.py:478
  5.0 0.9 %shard_map.145 = (bf16[512,128]{1,0:T(8,128)(2,1)S(1)}, bf16[128,512]{1,0:T(8,128)(2,1)S(1)}, bf16[512,512]{1,0:T(8,128)(2,1)S(1)}, bf16[4,160,512]{2,1,0:T(8,128)(2,1)S(1)}, bf16[4,160,128]{2,1,0:T(8,128)(2,1)S(1)}) custom-call(bf16[512,128]{1,0:T(8,128)(2,1)S(1)} %copy-done.2, bf16[512,1024]{1,0:T(8,128)(2,1)S(1)} %copy-done, ...), custom_call_target="tpu_custom_call" | custom-call | flops 83886080 | bytes 2840064 | tf_op jit(solution)/shard_map/pallas_call | solution.py:356
  5.9 2.9 %collective-permute-start.1 = (bf16[4,160,128]{2,1,0:T(8,128)(2,1)S(1)}, bf16[4,160,128]{2,1,0:T(8,128)(2,1)S(1)}, u32[]{:S(2)}, u32[]{:S(2)}) collective-permute-start(bf16[4,160,128]{2,1,0:T(8,128)(2,1)S(1)} %get-tuple-element.84), channel_id=1, source_target_pairs={{0,1},{1,0},{2,3},{3,2},{4,5},{5,4},{6,7},{7,6},{8,9},{9,8},{10,11... | collective-permute-start | bytes 491528 | tf_op jit(solution)/shard_map/ppermute | solution.py:368
  8.8 0.8 %shard_map.146 = (bf16[512,512]{1,0:T(8,128)(2,1)S(1)}, bf16[4,160,512]{2,1,0:T(8,128)(2,1)S(1)}, bf16[4,160,128]{2,1,0:T(8,128)(2,1)S(1)}) custom-call(bf16[128,512]{1,0:T(8,128)(2,1)S(1)} %get-tuple-element.80.kt.kt_ref, bf16[512,1024]{1,0:T(8,128)(2,1)S(1)} %copy-done, bf16[16,1280]{1,0:T(8,128)(2,1)S(1)} %collective-permute-done.rim, f32[3,1024]{1,0:T(4,128)S(1)} %copy-done.4), custom_call_target="tpu_custom_call" | custom-call | flops 83886080 | bytes 2576384 | tf_op jit(solution)/shard_map/pallas_call | solution.py:356
  9.6 0.3 collective-permute-done.1.near
  9.9 2.6 %collective-permute-start.2 = (bf16[2,160,128]{2,1,0:T(8,128)(2,1)S(1)}, bf16[2,160,128]{2,1,0:T(8,128)(2,1)S(1)}, u32[]{:S(2)}, u32[]{:S(2)}) collective-permute-start(bf16[2,160,128]{2,1,0:T(8,128)(2,1)S(1)} %get-tuple-element.86), channel_id=1, source_target_pairs={{0,2},{1,3},{2,0},{3,1},{4,6},{5,7},{6,4},{7,5},{8,10},{9,11},{10,... | collective-permute-start | bytes 245768 | tf_op jit(solution)/shard_map/ppermute | solution.py:368
  12.5 0.5 shard_map.144
  13.0 2.3 %shard_map.147.local = f32[512,512]{1,0:T(8,128)S(1)} custom-call(bf16[512,128]{1,0:T(8,128)(2,1)S(1)} %get-tuple-element.78.q_ref, bf16[512,128]{1,0:T(8,128)(2,1)S(1)} %get-tuple-element.79.k_ref, bf16[512,512]{1,0:T(8,128)(2,1)S(1)} %get-tuple-element.81.v_ref.v), custom_call_target="tpu_custom_call" | custom-call | flops 536870912 | bytes 1835008 | tf_op jit(solution)/shard_map/pallas_call | solution.py:356
  15.3 2.7 %collective-permute-start.3 = (bf16[2,160,128]{2,1,0:T(8,128)(2,1)S(1)}, bf16[2,160,128]{2,1,0:T(8,128)(2,1)S(1)}, u32[]{:S(2)}, u32[]{:S(2)}) collective-permute-start(bf16[2,160,128]{2,1,0:T(8,128)(2,1)S(1)} %shard_map.149), channel_id=1, source_target_pairs={{0,4},{1,5},{2,6},{3,7},{4,0},{5,1},{6,2},{7,3},{8,12},{9,13},{10,... | collective-permute-start | bytes 245768 | tf_op jit(solution)/shard_map/ppermute | solution.py:368
  18.1 2.3 %shard_map.151.local = f32[512,512]{1,0:T(8,128)S(1)} custom-call(bf16[512,128]{1,0:T(8,128)(2,1)S(1)} %get-tuple-element.78.q_ref, bf16[512,128]{1,0:T(8,128)(2,1)S(1)} %get-tuple-element.79.k_ref, bf16[512,512]{1,0:T(8,128)(2,1)S(1)} %get-tuple-element.88.v_ref.v), custom_call_target="tpu_custom_call" | custom-call | flops 536870912 | bytes 1835008 | tf_op jit(solution)/shard_map/pallas_call | solution.py:356
  20.4 0.1 collective-permute-done.3.refs_1_.rest_0_
  20.5 3.1 %collective-permute-start.4 = (bf16[2,160,128]{2,1,0:T(8,128)(2,1)S(1)}, bf16[2,160,128]{2,1,0:T(8,128)(2,1)S(1)}, u32[]{:S(2)}, u32[]{:S(2)}) collective-permute-start(bf16[2,160,128]{2,1,0:T(8,128)(2,1)S(1)} %shard_map.150), channel_id=1, source_target_pairs={{0,8},{1,9},{2,10},{3,11},{4,12},{5,13},{6,14},{7,15},{8,0},{9,1},... | collective-permute-start | bytes 245768 | tf_op jit(solution)/shard_map/ppermute | solution.py:368
  23.6 2.4 %collective-permute-done.4.rest_1_ = bf16[2,160,128]{2,1,0:T(8,128)(2,1)S(1)} collective-permute-done((bf16[2,160,128]{2,1,0:T(8,128)(2,1)S(1)}, bf16[2,160,128]{2,1,0:T(8,128)(2,1)S(1)}, u32[]{:S(2)}, u32[]{:S(2)}) %collective-permute-start.4) | collective-permute-done | bytes 81952 | tf_op jit(solution)/shard_map/ppermute | solution.py:368
  26.0 0.1 shard_map.152
  26.1 1.0 %collective-permute-start.5 = (bf16[2,160,128]{2,1,0:T(8,128)(2,1)S(1)}, bf16[2,160,128]{2,1,0:T(8,128)(2,1)S(1)}, u32[]{:S(2)}, u32[]{:S(2)}) collective-permute-start(bf16[2,160,128]{2,1,0:T(8,128)(2,1)S(1)} %get-tuple-element.91), channel_id=1, source_target_pairs={{0,2},{1,3},{2,0},{3,1},{4,6},{5,7},{6,4},{7,5},{8,10},{9,11},{10,... | collective-permute-start | bytes 245768 | tf_op jit(solution)/shard_map/ppermute | solution.py:368
  27.1 3.5 %collective-permute-done.5.other_part = bf16[2,160,128]{2,1,0:T(8,128)(2,1)S(1)} collective-permute-done((bf16[2,160,128]{2,1,0:T(8,128)(2,1)S(1)}, bf16[2,160,128]{2,1,0:T(8,128)(2,1)S(1)}, u32[]{:S(2)}, u32[]{:S(2)}) %collective-permute-start.5) | collective-permute-done | bytes 81952 | tf_op jit(solution)/shard_map/ppermute | solution.py:368
  30.6 0.1 shard_map.153
  30.7 0.1 collective-permute-start.6
  30.8 1.4 %shard_map.154 = (bf16[512,512]{1,0:T(8,128)(2,1)S(1)}, bf16[512,512]{1,0:T(8,128)(2,1)S(1)}, bf16[4,160,128]{2,1,0:T(8,128)(2,1)S(1)}, f32[4,128]{1,0:T(4,128)S(1)}) custom-call(f32[512,512]{1,0:T(8,128)S(1)} %shard_map.147.local, bf16[8,160,512]{2,1,0:T(8,128)(2,1)S(1)} %get-tuple-element.82.fq, bf16[4,160,128]{2,1,0:T(8,128)(2,1)S(1)} %get-tuple-element.92.prefix.pre_a, ...), custom_call_target="tpu_custom_call" | custom-call | flops 167772160 | bytes 4790272 | tf_op jit(solution)/shard_map/pallas_call | solution.py:356
  32.2 0.5 collective-permute-start.7
  32.7 1.4 %shard_map.155 = (bf16[512,512]{1,0:T(8,128)(2,1)S(1)}, bf16[512,512]{1,0:T(8,128)(2,1)S(1)}, bf16[4,160,128]{2,1,0:T(8,128)(2,1)S(1)}, f32[4,128]{1,0:T(4,128)S(1)}) custom-call(f32[512,512]{1,0:T(8,128)S(1)} %shard_map.151.local, bf16[8,160,512]{2,1,0:T(8,128)(2,1)S(1)} %get-tuple-element.82.fq, ...), custom_call_target="tpu_custom_call" | custom-call | flops 167772160 | bytes 4790272 | tf_op jit(solution)/shard_map/pallas_call | solution.py:356
  34.1 1.0 %collective-permute-start.8 = (bf16[2,160,128]{2,1,0:T(8,128)(2,1)S(1)}, bf16[2,160,128]{2,1,0:T(8,128)(2,1)S(1)}, u32[]{:S(2)}, u32[]{:S(2)}) collective-permute-start(bf16[2,160,128]{2,1,0:T(8,128)(2,1)S(1)} %get-tuple-element.107), channel_id=1, source_target_pairs={{0,2},{1,3},{2,0},{3,1},{4,6},{5,7},{6,4},{7,5},{8,10},{9,11},{10,... | collective-permute-start | bytes 245768 | tf_op jit(solution)/shard_map/ppermute | solution.py:368
  35.2 2.5 %shard_map.156 = (f32[512,256]{1,0:T(8,128)S(1)}, f32[32,512]{1,0:T(8,128)S(1)}, f32[32,512]{1,0:T(8,128)S(1)}) custom-call(bf16[512,128]{1,0:T(8,128)(2,1)S(1)} %get-tuple-element.78.q_ref, bf16[512,128]{1,0:T(8,128)(2,1)S(1)} %get-tuple-element.79.k_ref, bf16[128,512]{1,0:T(8,128)(2,1)S(1)} %get-tuple-element.77.qt_ref, ...), custom_call_target="tpu_custom_call" | custom-call | flops 536870912 | bytes 2228224 | tf_op jit(solution)/shard_map/pallas_call | solution.py:356
  37.7 1.0 %collective-permute-done.8.refs_0_.got_y = bf16[2,160,128]{2,1,0:T(8,128)(2,1)S(1)} collective-permute-done((bf16[2,160,128]{2,1,0:T(8,128)(2,1)S(1)}, bf16[2,160,128]{2,1,0:T(8,128)(2,1)S(1)}, u32[]{:S(2)}, u32[]{:S(2)}) %collective-permute-start.8) | collective-permute-done | bytes 81952 | tf_op jit(solution)/shard_map/ppermute | solution.py:368
  38.7 2.0 %collective-permute-start.9 = (bf16[2,160,128]{2,1,0:T(8,128)(2,1)S(1)}, bf16[2,160,128]{2,1,0:T(8,128)(2,1)S(1)}, u32[]{:S(2)}, u32[]{:S(2)}) collective-permute-start(bf16[2,160,128]{2,1,0:T(8,128)(2,1)S(1)} %shard_map.162), channel_id=1, source_target_pairs={{0,4},{1,5},{2,6},{3,7},{4,0},{5,1},{6,2},{7,3},{8,12},{9,13},{10,... | collective-permute-start | bytes 245768 | tf_op jit(solution)/shard_map/ppermute | solution.py:368
  40.7 2.5 %shard_map.157 = (f32[512,256]{1,0:T(8,128)S(1)}, f32[32,512]{1,0:T(8,128)S(1)}, f32[32,512]{1,0:T(8,128)S(1)}) custom-call(bf16[512,128]{1,0:T(8,128)(2,1)S(1)} %get-tuple-element.78.q_ref, bf16[512,128]{1,0:T(8,128)(2,1)S(1)} %get-tuple-element.79.k_ref, bf16[128,512]{1,0:T(8,128)(2,1)S(1)} %get-tuple-element.77.qt_ref, ...), custom_call_target="tpu_custom_call" | custom-call | flops 536870912 | bytes 2228224 | tf_op jit(solution)/shard_map/pallas_call | solution.py:356
  43.2 3.4 %collective-permute-start.10 = (bf16[2,160,128]{2,1,0:T(8,128)(2,1)S(1)}, bf16[2,160,128]{2,1,0:T(8,128)(2,1)S(1)}, u32[]{:S(2)}, u32[]{:S(2)}) collective-permute-start(bf16[2,160,128]{2,1,0:T(8,128)(2,1)S(1)} %shard_map.163), channel_id=1, source_target_pairs={{0,8},{1,9},{2,10},{3,11},{4,12},{5,13},{6,14},{7,15},{8,0},{9,1},... | collective-permute-start | bytes 245768 | tf_op jit(solution)/shard_map/ppermute | solution.py:368
  46.6 2.7 %shard_map.158 = (f32[512,256]{1,0:T(8,128)S(1)}, f32[32,512]{1,0:T(8,128)S(1)}, f32[32,512]{1,0:T(8,128)S(1)}) custom-call(bf16[512,128]{1,0:T(8,128)(2,1)S(1)} %get-tuple-element.78.q_ref, bf16[512,128]{1,0:T(8,128)(2,1)S(1)} %get-tuple-element.79.k_ref, bf16[128,512]{1,0:T(8,128)(2,1)S(1)} %get-tuple-element.77.qt_ref, ...), custom_call_target="tpu_custom_call" | custom-call | flops 536870912 | bytes 2228224 | tf_op jit(solution)/shard_map/pallas_call | solution.py:356
  49.3 0.1 shard_map.164
  49.4 0.7 collective-permute-start.11
  50.1 2.5 %shard_map.159 = (f32[512,256]{1,0:T(8,128)S(1)}, f32[32,512]{1,0:T(8,128)S(1)}, f32[32,512]{1,0:T(8,128)S(1)}) custom-call(bf16[512,128]{1,0:T(8,128)(2,1)S(1)} %get-tuple-element.78.q_ref, bf16[512,128]{1,0:T(8,128)(2,1)S(1)} %get-tuple-element.79.k_ref, bf16[128,512]{1,0:T(8,128)(2,1)S(1)} %get-tuple-element.77.qt_ref, ...), custom_call_target="tpu_custom_call" | custom-call | flops 536870912 | bytes 2228224 | tf_op jit(solution)/shard_map/pallas_call | solution.py:356
  52.6 0.9 %shard_map.160 = (f32[512,128]{1,0:T(8,128)S(1)}, f32[3,128]{1,0:T(4,128)S(1)}) custom-call(bf16[512,128]{1,0:T(8,128)(2,1)S(1)} %copy-done.3, bf16[16,1280]{1,0:T(8,128)(2,1)S(1)} %collective-permute-done.rim, bf16[128,512]{1,0:T(8,128)(2,1)S(1)} %get-tuple-element.77.qt_ref, bf16[512,512]{1,0:T(8,128)(2,1)S(1)} %get-tuple-element.93.gs_ref.gs_a, ...), custom_call_target="tpu_custom_call" | custom-call | flops 83886080 | bytes 2206720 | tf_op jit(solution)/shard_map/pallas_call | solution.py:356
  53.5 0.4 collective-permute-done.11.other_part
  53.9 0.1 shard_map.165
  54.0 0.1 collective-permute-start.12
  54.1 1.1 %shard_map.166 = (f32[512,512]{1,0:T(8,128)S(1)}, f32[64,512]{1,0:T(8,128)S(1)}, f32[3,512]{1,0:T(4,128)S(1)}) custom-call(bf16[512,1024]{1,0:T(8,128)(2,1)S(1)} %copy-done, bf16[16,1280]{1,0:T(8,128)(2,1)S(1)} %collective-permute-done.rim, bf16[128,512]{1,0:T(8,128)(2,1)S(1)} %get-tuple-element.80.kt.kt_ref, ...), custom_call_target="tpu_custom_call" | custom-call | flops 167772160 | bytes 4929536 | tf_op jit(solution)/shard_map/pallas_call | solution.py:356
  55.2 0.3 collective-permute-done.12.state
  55.5 1.1 %shard_map.167 = (f32[512,512]{1,0:T(8,128)S(1)}, f32[512,128]{1,0:T(8,128)S(1)}, f32[8,1280]{1,0:T(8,128)S(1)}, f32[4,1280]{1,0:T(4,128)S(1)}) custom-call(bf16[512,128]{1,0:T(8,128)(2,1)S(1)} %copy-done.2, bf16[512,1024]{1,0:T(8,128)(2,1)S(1)} %copy-done, bf16[16,1280]{1,0:T(8,128)(2,1)S(1)} %collective-permute-done.rim, ...), custom_call_target="tpu_custom_call" | custom-call | flops 167772160 | bytes 6700544 | tf_op jit(solution)/shard_map/pallas_call | solution.py:356
  56.6 4.5 %collective-permute-start.16 = (f32[4,1280]{1,0:T(4,128)S(1)}, f32[4,1280]{1,0:T(4,128)S(1)}, u32[]{:S(2)}, u32[]{:S(2)}) collective-permute-start(f32[4,1280]{1,0:T(4,128)S(1)} %get-tuple-element.140), channel_id=1, source_target_pairs={{0,12},{1,13},{2,14},{3,15},{4,8},{5,9},{6,10},{7,11},{8,4},{9,5},... | collective-permute-start | bytes 61448 | tf_op jit(solution)/shard_map/ppermute | solution.py:368
  61.1 0.6 collective-permute-start.14
  61.7 1.3 %collective-permute-start.13 = (f32[8,1280]{1,0:T(8,128)S(1)}, f32[8,1280]{1,0:T(8,128)S(1)}, u32[]{:S(2)}, u32[]{:S(2)}) collective-permute-start(f32[8,1280]{1,0:T(8,128)S(1)} %get-tuple-element.134), channel_id=1, source_target_pairs={{1,0},{2,1},{3,2},{4,3},{5,4},{6,5},{7,6},{8,7},{9,8},{10,9},{11,1... | collective-permute-start | bytes 122888 | tf_op jit(solution)/shard_map/ppermute | solution.py:586
  63.0 2.7 %collective-permute-done.15 = f32[4,1280]{1,0:T(4,128)S(1)} collective-permute-done((f32[4,1280]{1,0:T(4,128)S(1)}, f32[4,1280]{1,0:T(4,128)S(1)}, u32[]{:S(2)}, u32[]{:S(2)}) %collective-permute-start.15) | collective-permute-done | bytes 20512 | tf_op jit(solution)/shard_map/ppermute | solution.py:368
  65.9 1.1 %collective-permute-start.18 = (f32[4,1280]{1,0:T(4,128)S(1)}, f32[4,1280]{1,0:T(4,128)S(1)}, u32[]{:S(2)}, u32[]{:S(2)}) collective-permute-start(f32[4,1280]{1,0:T(4,128)S(1)} %add_add_fusion.refs_0_), channel_id=1, source_target_pairs={{0,2},{1,3},{2,0},{3,1},{4,6},{5,7},{6,4},{7,5},{8,10},{9,11},{10,... | collective-permute-start | bytes 61448 | tf_op jit(solution)/shard_map/ppermute | solution.py:368
  67.0 0.7 %collective-permute-start.19 = (f32[4,1280]{1,0:T(4,128)S(1)}, f32[4,1280]{1,0:T(4,128)S(1)}, u32[]{:S(2)}, u32[]{:S(2)}) collective-permute-start(f32[4,1280]{1,0:T(4,128)S(1)} %add_add_fusion.refs_0_), channel_id=1, source_target_pairs={{0,3},{1,2},{2,1},{3,0},{4,7},{5,6},{6,5},{7,4},{8,11},{9,10},{10,... | collective-permute-start | bytes 61448 | tf_op jit(solution)/shard_map/ppermute | solution.py:368
  67.7 2.9 %shard_map.168 = (bf16[512,128]{1,0:T(8,128)(2,1)}, bf16[512,128]{1,0:T(8,128)(2,1)}, bf16[512,1024]{1,0:T(8,128)(2,1)}, bf16[512,1024]{1,0:T(8,128)(2,1)}) custom-call(f32[512,128]{1,0:T(8,128)S(1)} %get-tuple-element.102.gq, f32[512,128]{1,0:T(8,128)S(1)} %get-tuple-element.132.gk, f32[512,512]{1,0:T(8,128)S(1)} %get-tuple-element.133.gv_a, ...), custom_call_target="tpu_custom_call" | custom-call | flops 167772160 | bytes 6085632 | tf_op jit(solution)/shard_map/pallas_call | solution.py:356
  70.7 0.6 shard_map.169
  (36 shorter events, 0.4 us)
Async XLA Ops:
  0.6 4.3 %copy-start.2 = (bf16[512,128]{1,0:T(8,128)(2,1)S(1)}, bf16[512,128]{1,0:T(8,128)(2,1)}, u32[]{:S(2)}) copy-start(bf16[512,128]{1,0:T(8,128)(2,1)} %key.5) | copy-start | bytes 393220
  0.6 4.3 %copy-start = (bf16[512,1024]{1,0:T(8,128)(2,1)S(1)}, bf16[512,1024]{1,0:T(8,128)(2,1)}, u32[]{:S(2)}) copy-start(bf16[512,1024]{1,0:T(8,128)(2,1)} %value.9) | copy-start | bytes 3145732
  0.7 4.3 %copy-start.7 = (f32[3,128]{1,0:T(4,128)S(1)}, f32[3,128]{1,0:T(4,128)}, u32[]{:S(2)}) copy-start(f32[3,128]{1,0:T(4,128)} %taps_k.3) | copy-start | bytes 4612
  0.7 4.3 %copy-start.4 = (f32[3,1024]{1,0:T(4,128)S(1)}, f32[3,1024]{1,0:T(4,128)}, u32[]{:S(2)}) copy-start(f32[3,1024]{1,0:T(4,128)} %taps_v.5) | copy-start | bytes 36868
  1.6 10.9 %copy-start.3 = (bf16[512,128]{1,0:T(8,128)(2,1)S(1)}, bf16[512,128]{1,0:T(8,128)(2,1)}, u32[]{:S(2)}) copy-start(bf16[512,128]{1,0:T(8,128)(2,1)} %query.5) | copy-start | bytes 393220
  1.6 10.9 %copy-start.6 = (f32[3,128]{1,0:T(4,128)S(1)}, f32[3,128]{1,0:T(4,128)}, u32[]{:S(2)}) copy-start(f32[3,128]{1,0:T(4,128)} %taps_q.5) | copy-start | bytes 4612
  1.6 3.3 %collective-permute-start = (bf16[16,1280]{1,0:T(8,128)(2,1)S(1)}, bf16[16,1280]{1,0:T(8,128)(2,1)S(1)}, u32[]{:S(2)}, u32[]{:S(2)}) collective-permute-start(bf16[16,1280]{1,0:T(8,128)(2,1)S(1)} %shard_map.143), channel_id=1, source_target_pairs={{0,1},{1,2},{2,3},{3,4},{4,5},{5,6},{6,7},{7,8},{8,9},{9,10},{10,1... | collective-permute-start | bytes 122888 | tf_op jit(solution)/shard_map/ppermute | solution.py:478
  5.9 4.0 %collective-permute-start.1 = (bf16[4,160,128]{2,1,0:T(8,128)(2,1)S(1)}, bf16[4,160,128]{2,1,0:T(8,128)(2,1)S(1)}, u32[]{:S(2)}, u32[]{:S(2)}) collective-permute-start(bf16[4,160,128]{2,1,0:T(8,128)(2,1)S(1)} %get-tuple-element.84), channel_id=1, source_target_pairs={{0,1},{1,0},{2,3},{3,2},{4,5},{5,4},{6,7},{7,6},{8,9},{9,8},{10,11... | collective-permute-start | bytes 491528 | tf_op jit(solution)/shard_map/ppermute | solution.py:368
  9.9 5.4 %collective-permute-start.2 = (bf16[2,160,128]{2,1,0:T(8,128)(2,1)S(1)}, bf16[2,160,128]{2,1,0:T(8,128)(2,1)S(1)}, u32[]{:S(2)}, u32[]{:S(2)}) collective-permute-start(bf16[2,160,128]{2,1,0:T(8,128)(2,1)S(1)} %get-tuple-element.86), channel_id=1, source_target_pairs={{0,2},{1,3},{2,0},{3,1},{4,6},{5,7},{6,4},{7,5},{8,10},{9,11},{10,... | collective-permute-start | bytes 245768 | tf_op jit(solution)/shard_map/ppermute | solution.py:368
  15.3 5.1 %collective-permute-start.3 = (bf16[2,160,128]{2,1,0:T(8,128)(2,1)S(1)}, bf16[2,160,128]{2,1,0:T(8,128)(2,1)S(1)}, u32[]{:S(2)}, u32[]{:S(2)}) collective-permute-start(bf16[2,160,128]{2,1,0:T(8,128)(2,1)S(1)} %shard_map.149), channel_id=1, source_target_pairs={{0,4},{1,5},{2,6},{3,7},{4,0},{5,1},{6,2},{7,3},{8,12},{9,13},{10,... | collective-permute-start | bytes 245768 | tf_op jit(solution)/shard_map/ppermute | solution.py:368
  18.1 12.7 %copy-start.1 = (bf16[512,1024]{1,0:T(8,128)(2,1)S(1)}, bf16[512,1024]{1,0:T(8,128)(2,1)}, u32[]{:S(2)}) copy-start(bf16[512,1024]{1,0:T(8,128)(2,1)} %grad.3) | copy-start | bytes 3145732
  18.1 12.7 %copy-start.5 = (f32[1024]{0:T(1024)S(1)}, f32[1024]{0:T(1024)}, u32[]{:S(2)}) copy-start(f32[1024]{0:T(1024)} %param.14) | copy-start | bytes 12292
  20.5 5.5 %collective-permute-start.4 = (bf16[2,160,128]{2,1,0:T(8,128)(2,1)S(1)}, bf16[2,160,128]{2,1,0:T(8,128)(2,1)S(1)}, u32[]{:S(2)}, u32[]{:S(2)}) collective-permute-start(bf16[2,160,128]{2,1,0:T(8,128)(2,1)S(1)} %shard_map.150), channel_id=1, source_target_pairs={{0,8},{1,9},{2,10},{3,11},{4,12},{5,13},{6,14},{7,15},{8,0},{9,1},... | collective-permute-start | bytes 245768 | tf_op jit(solution)/shard_map/ppermute | solution.py:368
  26.1 4.5 %collective-permute-start.5 = (bf16[2,160,128]{2,1,0:T(8,128)(2,1)S(1)}, bf16[2,160,128]{2,1,0:T(8,128)(2,1)S(1)}, u32[]{:S(2)}, u32[]{:S(2)}) collective-permute-start(bf16[2,160,128]{2,1,0:T(8,128)(2,1)S(1)} %get-tuple-element.91), channel_id=1, source_target_pairs={{0,2},{1,3},{2,0},{3,1},{4,6},{5,7},{6,4},{7,5},{8,10},{9,11},{10,... | collective-permute-start | bytes 245768 | tf_op jit(solution)/shard_map/ppermute | solution.py:368
  30.7 2.0 %collective-permute-start.6 = (bf16[4,160,128]{2,1,0:T(8,128)(2,1)S(1)}, bf16[4,160,128]{2,1,0:T(8,128)(2,1)S(1)}, u32[]{:S(2)}, u32[]{:S(2)}) collective-permute-start(bf16[4,160,128]{2,1,0:T(8,128)(2,1)S(1)} %get-tuple-element.94), channel_id=1, source_target_pairs={{0,1},{1,0},{2,3},{3,2},{4,5},{5,4},{6,7},{7,6},{8,9},{9,8},{10,11... | collective-permute-start | bytes 491528 | tf_op jit(solution)/shard_map/ppermute | solution.py:368
  32.2 1.9 %collective-permute-start.7 = (bf16[4,160,128]{2,1,0:T(8,128)(2,1)S(1)}, bf16[4,160,128]{2,1,0:T(8,128)(2,1)S(1)}, u32[]{:S(2)}, u32[]{:S(2)}) collective-permute-start(bf16[4,160,128]{2,1,0:T(8,128)(2,1)S(1)} %get-tuple-element.105), channel_id=1, source_target_pairs={{0,1},{1,0},{2,3},{3,2},{4,5},{5,4},{6,7},{7,6},{8,9},{9,8},{10,11... | collective-permute-start | bytes 491528 | tf_op jit(solution)/shard_map/ppermute | solution.py:368
  34.1 4.5 %collective-permute-start.8 = (bf16[2,160,128]{2,1,0:T(8,128)(2,1)S(1)}, bf16[2,160,128]{2,1,0:T(8,128)(2,1)S(1)}, u32[]{:S(2)}, u32[]{:S(2)}) collective-permute-start(bf16[2,160,128]{2,1,0:T(8,128)(2,1)S(1)} %get-tuple-element.107), channel_id=1, source_target_pairs={{0,2},{1,3},{2,0},{3,1},{4,6},{5,7},{6,4},{7,5},{8,10},{9,11},{10,... | collective-permute-start | bytes 245768 | tf_op jit(solution)/shard_map/ppermute | solution.py:368
  38.7 4.5 %collective-permute-start.9 = (bf16[2,160,128]{2,1,0:T(8,128)(2,1)S(1)}, bf16[2,160,128]{2,1,0:T(8,128)(2,1)S(1)}, u32[]{:S(2)}, u32[]{:S(2)}) collective-permute-start(bf16[2,160,128]{2,1,0:T(8,128)(2,1)S(1)} %shard_map.162), channel_id=1, source_target_pairs={{0,4},{1,5},{2,6},{3,7},{4,0},{5,1},{6,2},{7,3},{8,12},{9,13},{10,... | collective-permute-start | bytes 245768 | tf_op jit(solution)/shard_map/ppermute | solution.py:368
  43.2 6.1 %collective-permute-start.10 = (bf16[2,160,128]{2,1,0:T(8,128)(2,1)S(1)}, bf16[2,160,128]{2,1,0:T(8,128)(2,1)S(1)}, u32[]{:S(2)}, u32[]{:S(2)}) collective-permute-start(bf16[2,160,128]{2,1,0:T(8,128)(2,1)S(1)} %shard_map.163), channel_id=1, source_target_pairs={{0,8},{1,9},{2,10},{3,11},{4,12},{5,13},{6,14},{7,15},{8,0},{9,1},... | collective-permute-start | bytes 245768 | tf_op jit(solution)/shard_map/ppermute | solution.py:368
  49.4 4.5 %collective-permute-start.11 = (bf16[2,160,128]{2,1,0:T(8,128)(2,1)S(1)}, bf16[2,160,128]{2,1,0:T(8,128)(2,1)S(1)}, u32[]{:S(2)}, u32[]{:S(2)}) collective-permute-start(bf16[2,160,128]{2,1,0:T(8,128)(2,1)S(1)} %get-tuple-element.115), channel_id=1, source_target_pairs={{0,2},{1,3},{2,0},{3,1},{4,6},{5,7},{6,4},{7,5},{8,10},{9,11},{10,... | collective-permute-start | bytes 245768 | tf_op jit(solution)/shard_map/ppermute | solution.py:368
  54.0 1.5 %collective-permute-start.12 = (bf16[4,160,128]{2,1,0:T(8,128)(2,1)S(1)}, bf16[4,160,128]{2,1,0:T(8,128)(2,1)S(1)}, u32[]{:S(2)}, u32[]{:S(2)}) collective-permute-start(bf16[4,160,128]{2,1,0:T(8,128)(2,1)S(1)} %get-tuple-element.117), channel_id=1, source_target_pairs={{0,1},{1,0},{2,3},{3,2},{4,5},{5,4},{6,7},{7,6},{8,9},{9,8},{10,11... | collective-permute-start | bytes 491528 | tf_op jit(solution)/shard_map/ppermute | solution.py:368
  56.6 6.4 %collective-permute-start.16 = (f32[4,1280]{1,0:T(4,128)S(1)}, f32[4,1280]{1,0:T(4,128)S(1)}, u32[]{:S(2)}, u32[]{:S(2)}) collective-permute-start(f32[4,1280]{1,0:T(4,128)S(1)} %get-tuple-element.140), channel_id=1, source_target_pairs={{0,12},{1,13},{2,14},{3,15},{4,8},{5,9},{6,10},{7,11},{8,4},{9,5},... | collective-permute-start | bytes 61448 | tf_op jit(solution)/shard_map/ppermute | solution.py:368
  61.1 4.7 %collective-permute-start.15 = (f32[4,1280]{1,0:T(4,128)S(1)}, f32[4,1280]{1,0:T(4,128)S(1)}, u32[]{:S(2)}, u32[]{:S(2)}) collective-permute-start(f32[4,1280]{1,0:T(4,128)S(1)} %get-tuple-element.140), channel_id=1, source_target_pairs={{0,8},{1,9},{2,10},{3,11},{4,12},{5,13},{6,14},{7,15},{8,0},{9,1},... | collective-permute-start | bytes 61448 | tf_op jit(solution)/shard_map/ppermute | solution.py:368
  61.1 4.7 %collective-permute-start.14 = (f32[4,1280]{1,0:T(4,128)S(1)}, f32[4,1280]{1,0:T(4,128)S(1)}, u32[]{:S(2)}, u32[]{:S(2)}) collective-permute-start(f32[4,1280]{1,0:T(4,128)S(1)} %get-tuple-element.140), channel_id=1, source_target_pairs={{0,4},{1,5},{2,6},{3,7},{4,0},{5,1},{6,2},{7,3},{8,12},{9,13},{10,... | collective-permute-start | bytes 61448 | tf_op jit(solution)/shard_map/ppermute | solution.py:368
  61.7 6.0 %collective-permute-start.13 = (f32[8,1280]{1,0:T(8,128)S(1)}, f32[8,1280]{1,0:T(8,128)S(1)}, u32[]{:S(2)}, u32[]{:S(2)}) collective-permute-start(f32[8,1280]{1,0:T(8,128)S(1)} %get-tuple-element.134), channel_id=1, source_target_pairs={{1,0},{2,1},{3,2},{4,3},{5,4},{6,5},{7,6},{8,7},{9,8},{10,9},{11,1... | collective-permute-start | bytes 122888 | tf_op jit(solution)/shard_map/ppermute | solution.py:586
  65.8 4.9 %collective-permute-start.17 = (f32[4,1280]{1,0:T(4,128)S(1)}, f32[4,1280]{1,0:T(4,128)S(1)}, u32[]{:S(2)}, u32[]{:S(2)}) collective-permute-start(f32[4,1280]{1,0:T(4,128)S(1)} %add_add_fusion.refs_0_), channel_id=1, source_target_pairs={{0,1},{1,0},{2,3},{3,2},{4,5},{5,4},{6,7},{7,6},{8,9},{9,8},{10,11... | collective-permute-start | bytes 61448 | tf_op jit(solution)/shard_map/ppermute | solution.py:368
  65.9 4.8 %collective-permute-start.18 = (f32[4,1280]{1,0:T(4,128)S(1)}, f32[4,1280]{1,0:T(4,128)S(1)}, u32[]{:S(2)}, u32[]{:S(2)}) collective-permute-start(f32[4,1280]{1,0:T(4,128)S(1)} %add_add_fusion.refs_0_), channel_id=1, source_target_pairs={{0,2},{1,3},{2,0},{3,1},{4,6},{5,7},{6,4},{7,5},{8,10},{9,11},{10,... | collective-permute-start | bytes 61448 | tf_op jit(solution)/shard_map/ppermute | solution.py:368
  67.0 3.7 %collective-permute-start.19 = (f32[4,1280]{1,0:T(4,128)S(1)}, f32[4,1280]{1,0:T(4,128)S(1)}, u32[]{:S(2)}, u32[]{:S(2)}) collective-permute-start(f32[4,1280]{1,0:T(4,128)S(1)} %add_add_fusion.refs_0_), channel_id=1, source_target_pairs={{0,3},{1,2},{2,1},{3,0},{4,7},{5,6},{6,5},{7,4},{8,11},{9,10},{10,... | collective-permute-start | bytes 61448 | tf_op jit(solution)/shard_map/ppermute | solution.py:368

commit v4 on v3

--- a/solution.py
+++ b/solution.py
@@ -84,8 +84,12 @@
 
 
 def half_index(own):
-    core = lax.rem(lax.axis_index("seq"), 2)
-    return core if own else 1 - core
+    here, parity, bit = lax.axis_index("seq"), 0, 1
+    while bit < lax.axis_size("seq"):
+        parity = parity + lax.rem(lax.div(here, bit), 2)
+        bit *= 2
+    parity = lax.rem(parity, 2)
+    return parity if own else 1 - parity
 
 
 def rows_of(half, g):
@@ -305,11 +309,24 @@
             head_out[:, lanes_of(half, g, 2 * LANES)] = gv[0:8, head_lanes(g)]
 
 
+def token_kernel(out_a, out_b, out, sems):
+    copies = []
+    for i, (own, tokens) in enumerate(((True, out_a), (False, out_b))):
+        width = tokens.shape[1]
+        place = pl.ds(pl.multiple_of(half_index(own) * width, width), width)
+        copies.append(pltpu.make_async_copy(tokens, out.at[:, place], sems.at[i]))
+    for copy in copies:
+        copy.start()
+    for copy in copies:
+        copy.wait()
+
+
 def signal_kernel(
-    gq, gk, gv_a, gv_b, follow, out_a, out_b, taps_q, taps_k, taps_v, q_out, k_out, v_out, out, wide
+    gq, gk, gv_a, gv_b, follow, taps_q, taps_k, taps_v, q_out, k_out, v_out, wide, q_part, k_part, v_part, sems
 ):
     rows = gq.shape[0]
     count = taps_q.shape[0]
+    copies = []
 
     def one(grad, after, taps):
         wide[0:rows] = grad
@@ -319,14 +336,24 @@
             total = total + taps[o : o + 1] * wide[count - 1 - o : count - 1 - o + rows]
         return total.astype(BF16)
 
-    q_out[...] = one(gq[...], follow[:, 0:LANES], taps_q[...])
-    k_out[...] = one(gk[...], follow[:, LANES : 2 * LANES], taps_k[...])
-    for own, gv, tokens in ((True, gv_a, out_a), (False, gv_b, out_b)):
+    def move(part, out):
+        copies.append(pltpu.make_async_copy(part, out, sems.at[len(copies)]))
+        copies[-1].start()
+
+    for i, (own, gv) in enumerate(((True, gv_a), (False, gv_b))):
         half = half_index(own)
         for g in range(HALF):
             place = lanes_of(half, g)
-            out[:, place] = tokens[:, head_lanes(g)]
-            v_out[:, place] = one(gv[:, head_lanes(g)], follow[:, lanes_of(half, g, 2 * LANES)], taps_v[:, place])
+            slot = i * HALF + g
+            after = follow[:, lanes_of(half, g, 2 * LANES)]
+            v_part[slot] = one(gv[:, head_lanes(g)], after, taps_v[:, place])
+            move(v_part.at[slot], v_out.at[:, place])
+    q_part[...] = one(gq[...], follow[:, 0:LANES], taps_q[...])
+    move(q_part, q_out)
+    k_part[...] = one(gk[...], follow[:, LANES : 2 * LANES], taps_k[...])
+    move(k_part, k_out)
+    for copy in copies:
+        copy.wait()
 
 
 def finish_kernel(factor, *refs):
@@ -428,21 +455,21 @@
     cost = 4 * keep.size
 
     def under(x):
-        return tie(x, works.pop(0)()) if works else x
+        return tie(x, *works.pop(0)()) if works else x
 
     near = exchange(send, 1)
     part, their = call(pair_kernel, [wide, narrow], [], (keep, near), cost)
-    got_y = exchange(their, 2)
+    got_y = exchange(their, 3)
     gots = []
     bit = 4
     while bit < count:
         send = call(step_kernel, [narrow], [], (part, got_y, *gots), cost)[0]
-        gots.append(exchange(under(send), bit))
+        gots.append(exchange(under(send), bit + 1))
         bit *= 2
     own_part, give_part = call(
         functools.partial(part_kernel, reverse), [wide, narrow], [], (part, got_y, *gots), cost
     )
-    other_part = exchange(under(give_part), 2)
+    other_part = exchange(under(give_part), 3)
     own, give = call(
         functools.partial(merge_kernel, reverse), [st(whole, BF16)] * 2, [], (own_part, other_part, keep, near), cost
     )
@@ -510,7 +537,7 @@
                 held(made["q"][0], k, v),
                 2 * square_flops,
             )[0]
-            return made[own]
+            return (made[own],)
 
         return work
 
@@ -534,6 +561,18 @@
     out_a, gs_a, state_a, gain_a = made["norm"]
     out_b, gs_b, state_b, gain_b = norm(False, pre_b)
     back = []
+
+    def first_back():
+        made["out"] = call(
+            token_kernel,
+            [st((rows, WIDE), BF16)],
+            [pltpu.SemaphoreType.DMA((2,))],
+            held(out_a, out_b),
+            rows,
+            loose=(0,),
+            out_specs=[apart],
+        )[0]
+        return (*back_work(True, 0, v_a, gs_a)(), made["out"])
 
     def back_work(own, part, v, gs):
         def work():
@@ -546,12 +585,12 @@
                     2 * square_flops,
                 )
             )
-            return back[-1][0]
+            return (back[-1][0],)
 
         return work
 
     def last_work():
-        work = back_work(False, 1, v_b, gs_b)()
+        work = back_work(False, 1, v_b, gs_b)()[0]
         made["gq"] = call(
             query_grad_kernel,
             [flat, st((taps, LANES), F32)],
@@ -559,7 +598,7 @@
             (query_in, rim, *held(qt, gs_a, gs_b), pre_a, pre_b, *held(*[b[1] for b in back]), conv_query),
             state_flops,
         )
-        return made["gq"][0]
+        return (work, made["gq"][0])
 
     def first_later(state):
         made["later"] = call(
@@ -571,7 +610,7 @@
         )
         return made["later"][0]
 
-    works = [back_work(True, 0, v_a, gs_a), back_work(True, 1, v_a, gs_a), back_work(False, 0, v_b, gs_b), last_work]
+    works = [first_back, back_work(True, 1, v_a, gs_a), back_work(False, 0, v_b, gs_b), last_work]
     _, post_a = beyond(state_b, state_a, True, works, first_later)
     gv_b, gk_b, sums_b = made["later"]
     gq, sums_q = made["gq"]
@@ -586,17 +625,20 @@
     follow = lax.ppermute(heads, "seq", [(i + 1, i) for i in range(count - 1)])
     bit = 4
     while bit < count:
-        group = (bit, 2 * bit, 3 * bit) if 2 * bit < count else (bit,)
+        group = (bit + 1, 2 * bit + 1, 3 * bit) if 2 * bit < count else (bit + 1,)
         for got in [exchange(sums, distance) for distance in group]:
             sums = sums + got
         bit *= len(group) + 1
-    grad_query, grad_key, grad_value, output = call(
+    flat_narrow = st((rows, LANES), BF16)
+    grad_query, grad_key, grad_value = call(
         signal_kernel,
-        [st((rows, LANES), BF16), st((rows, LANES), BF16), st((rows, WIDE), BF16), st((rows, WIDE), BF16)],
-        [pltpu.VMEM((rows + 8, DIM), F32)],
-        (*held(gq, gk, gv_a, gv_b), follow, *held(out_a, out_b), conv_query, conv_key, conv_value),
+        [flat_narrow, flat_narrow, st((rows, WIDE), BF16)],
+        [pltpu.VMEM((rows + 8, DIM), F32), pltpu.VMEM((rows, LANES), BF16), pltpu.VMEM((rows, LANES), BF16),
+         pltpu.VMEM((HEADS, rows, DIM), BF16), pltpu.SemaphoreType.DMA((HEADS + 2,))],
+        (*held(gq, gk, gv_a, gv_b), follow, conv_query, conv_key, conv_value),
         2 * state_flops,
-        loose=(0, 1, 2, 3),
+        loose=(0, 1, 2),
+        out_specs=[apart] * 3,
     )
     taps_query, taps_key, taps_value, taps_gain = call(
         functools.partial(finish_kernel, total_rows ** (-0.5)),
@@ -607,7 +649,7 @@
         loose=(0, 1, 2, 3),
     )
     return (
-        output,
+        made["out"],
         grad_query,
         grad_key,
         grad_value,

time: 71.5 us -> 72.8 us (1.018)
  starting transfers between devices: 31 us -> 33.4 us
  waiting for transfers between devices: 11.5 us -> 10.1 us
    ppermute x18, starting transfers between devices: 27.2 us -> 29.7 us  [exchange(): return lax.ppermute(x, 'seq', [(i, i ^ distance) for i in range(count)])]
    ppermute x18, waiting for transfers between devices: 10.7 us -> 9.27 us  [exchange(): return lax.ppermute(x, 'seq', [(i, i ^ distance) for i in range(count)])]
    pallas_call x27 -> x28, Pallas kernels: 27.8 us -> 28.1 us  [call(): pl.pallas_call(kernel, out_shape=[o if i in loose else pltpu.VMEM(o.shape...]
  transfers between devices with their start and end apart: 20 -> 20, of which waited for: 9 -> 10; matrix products, arithmetic and copies ran while one was open for 0% -> 0% of each run, Pallas kernels for 33% -> 33%
where the time goes in v4:
time: 72.8 us; the launch traced here: 72.6 us
  starting transfers between devices  33.4 us (46%)
  Pallas kernels  28.1 us (39%)
  waiting for transfers between devices  10.1 us (14%)
  between operations  0.9 us (1%)
    ppermute x18, starting transfers between devices, exchange(): return lax.ppermute(x, 'seq', [(i, i ^ distance) for i in range(count)])  29.7 us
    pallas_call x28, Pallas kernels, call(): pl.pallas_call(kernel, out_shape=[o if i in loose else pltpu.VMEM(o.shape...  28.1 us
    ppermute x18, waiting for transfers between devices, exchange(): return lax.ppermute(x, 'seq', [(i, i ^ distance) for i in range(count)])  9.27 us
    ppermute x1, starting transfers between devices, shards(): rim = lax.ppermute(ends, 'seq', [(i, i + 1) for i in range(count - 1)])  2.49 us
  transfers between devices with their start and end apart: 20, of which 10 were waited for; matrix products, arithmetic and copies ran while one was open for 0% of the time, Pallas kernels for 33%

profile of v4, /device:TPU:0, one launch (start us, length us, event | category | flops | bytes accessed | tf_op | source)
XLA Modules:
  0.0 72.6 jit_solution(11869770782617903068)
XLA Ops:
  0.7 0.9 %shard_map.143 = bf16[16,1280]{1,0:T(8,128)(2,1)S(1)} custom-call(bf16[512,128]{1,0:T(8,128)(2,1)} %query.5, bf16[512,128]{1,0:T(8,128)(2,1)} %key.5, bf16[512,1024]{1,0:T(8,128)(2,1)} %value.9), custom_call_target="tpu_custom_call" | custom-call | flops 512 | bytes 1351680 | tf_op jit(solution)/shard_map/pallas_call | solution.py:383
  1.6 2.5 %collective-permute-start = (bf16[16,1280]{1,0:T(8,128)(2,1)S(1)}, bf16[16,1280]{1,0:T(8,128)(2,1)S(1)}, u32[]{:S(2)}, u32[]{:S(2)}) collective-permute-start(bf16[16,1280]{1,0:T(8,128)(2,1)S(1)} %shard_map.143), channel_id=1, source_target_pairs={{0,1},{1,2},{2,3},{3,4},{4,5},{5,6},{6,7},{7,8},{8,9},{9,10},{10,1... | collective-permute-start | bytes 122888 | tf_op jit(solution)/shard_map/ppermute | solution.py:505
  4.1 0.9 %collective-permute-done.rim = bf16[16,1280]{1,0:T(8,128)(2,1)S(1)} collective-permute-done((bf16[16,1280]{1,0:T(8,128)(2,1)S(1)}, bf16[16,1280]{1,0:T(8,128)(2,1)S(1)}, u32[]{:S(2)}, u32[]{:S(2)}) %collective-permute-start) | collective-permute-done | bytes 40992 | tf_op jit(solution)/shard_map/ppermute | solution.py:505
  5.0 0.9 %shard_map.145 = (bf16[512,128]{1,0:T(8,128)(2,1)S(1)}, bf16[128,512]{1,0:T(8,128)(2,1)S(1)}, bf16[512,512]{1,0:T(8,128)(2,1)S(1)}, bf16[4,160,512]{2,1,0:T(8,128)(2,1)S(1)}, bf16[4,160,128]{2,1,0:T(8,128)(2,1)S(1)}) custom-call(bf16[512,128]{1,0:T(8,128)(2,1)S(1)} %copy-done.2, bf16[512,1024]{1,0:T(8,128)(2,1)S(1)} %copy-done, ...), custom_call_target="tpu_custom_call" | custom-call | flops 83886080 | bytes 2840064 | tf_op jit(solution)/shard_map/pallas_call | solution.py:383
  5.9 2.9 %collective-permute-start.1 = (bf16[4,160,128]{2,1,0:T(8,128)(2,1)S(1)}, bf16[4,160,128]{2,1,0:T(8,128)(2,1)S(1)}, u32[]{:S(2)}, u32[]{:S(2)}) collective-permute-start(bf16[4,160,128]{2,1,0:T(8,128)(2,1)S(1)} %get-tuple-element.82), channel_id=1, source_target_pairs={{0,1},{1,0},{2,3},{3,2},{4,5},{5,4},{6,7},{7,6},{8,9},{9,8},{10,11... | collective-permute-start | bytes 491528 | tf_op jit(solution)/shard_map/ppermute | solution.py:395
  8.8 0.8 %shard_map.146 = (bf16[512,512]{1,0:T(8,128)(2,1)S(1)}, bf16[4,160,512]{2,1,0:T(8,128)(2,1)S(1)}, bf16[4,160,128]{2,1,0:T(8,128)(2,1)S(1)}) custom-call(bf16[128,512]{1,0:T(8,128)(2,1)S(1)} %get-tuple-element.78.kt.kt_ref, bf16[512,1024]{1,0:T(8,128)(2,1)S(1)} %copy-done, bf16[16,1280]{1,0:T(8,128)(2,1)S(1)} %collective-permute-done.rim, f32[3,1024]{1,0:T(4,128)S(1)} %copy-done.4), custom_call_target="tpu_custom_call" | custom-call | flops 83886080 | bytes 2576384 | tf_op jit(solution)/shard_map/pallas_call | solution.py:383
  9.6 0.3 collective-permute-done.1.near
  9.9 2.4 %collective-permute-start.2 = (bf16[2,160,128]{2,1,0:T(8,128)(2,1)S(1)}, bf16[2,160,128]{2,1,0:T(8,128)(2,1)S(1)}, u32[]{:S(2)}, u32[]{:S(2)}) collective-permute-start(bf16[2,160,128]{2,1,0:T(8,128)(2,1)S(1)} %get-tuple-element.84), channel_id=1, source_target_pairs={{0,3},{1,2},{2,1},{3,0},{4,7},{5,6},{6,5},{7,4},{8,11},{9,10},{10,... | collective-permute-start | bytes 245768 | tf_op jit(solution)/shard_map/ppermute | solution.py:395
  12.3 0.5 shard_map.144
  12.7 2.3 %shard_map.147.local = f32[512,512]{1,0:T(8,128)S(1)} custom-call(bf16[512,128]{1,0:T(8,128)(2,1)S(1)} %get-tuple-element.76.q_ref, bf16[512,128]{1,0:T(8,128)(2,1)S(1)} %get-tuple-element.77.k_ref, bf16[512,512]{1,0:T(8,128)(2,1)S(1)} %get-tuple-element.79.v_ref.v), custom_call_target="tpu_custom_call" | custom-call | flops 536870912 | bytes 1835008 | tf_op jit(solution)/shard_map/pallas_call | solution.py:383
  15.1 2.6 %collective-permute-start.3 = (bf16[2,160,128]{2,1,0:T(8,128)(2,1)S(1)}, bf16[2,160,128]{2,1,0:T(8,128)(2,1)S(1)}, u32[]{:S(2)}, u32[]{:S(2)}) collective-permute-start(bf16[2,160,128]{2,1,0:T(8,128)(2,1)S(1)} %shard_map.149), channel_id=1, source_target_pairs={{0,5},{1,4},{2,7},{3,6},{4,1},{5,0},{6,3},{7,2},{8,13},{9,12},{10,... | collective-permute-start | bytes 245768 | tf_op jit(solution)/shard_map/ppermute | solution.py:395
  17.7 2.3 %shard_map.151.local = f32[512,512]{1,0:T(8,128)S(1)} custom-call(bf16[512,128]{1,0:T(8,128)(2,1)S(1)} %get-tuple-element.76.q_ref, bf16[512,128]{1,0:T(8,128)(2,1)S(1)} %get-tuple-element.77.k_ref, bf16[512,512]{1,0:T(8,128)(2,1)S(1)} %get-tuple-element.86.v_ref.v), custom_call_target="tpu_custom_call" | custom-call | flops 536870912 | bytes 1835008 | tf_op jit(solution)/shard_map/pallas_call | solution.py:383
  20.1 0.2 collective-permute-done.3.refs_1_.rest_0_
  20.3 3.0 %collective-permute-start.4 = (bf16[2,160,128]{2,1,0:T(8,128)(2,1)S(1)}, bf16[2,160,128]{2,1,0:T(8,128)(2,1)S(1)}, u32[]{:S(2)}, u32[]{:S(2)}) collective-permute-start(bf16[2,160,128]{2,1,0:T(8,128)(2,1)S(1)} %shard_map.150), channel_id=1, source_target_pairs={{0,9},{1,8},{2,11},{3,10},{4,13},{5,12},{6,15},{7,14},{8,1},{9,0},... | collective-permute-start | bytes 245768 | tf_op jit(solution)/shard_map/ppermute | solution.py:395
  23.3 2.5 %collective-permute-done.4.rest_1_ = bf16[2,160,128]{2,1,0:T(8,128)(2,1)S(1)} collective-permute-done((bf16[2,160,128]{2,1,0:T(8,128)(2,1)S(1)}, bf16[2,160,128]{2,1,0:T(8,128)(2,1)S(1)}, u32[]{:S(2)}, u32[]{:S(2)}) %collective-permute-start.4) | collective-permute-done | bytes 81952 | tf_op jit(solution)/shard_map/ppermute | solution.py:395
  25.9 2.6 %collective-permute-start.5 = (bf16[2,160,128]{2,1,0:T(8,128)(2,1)S(1)}, bf16[2,160,128]{2,1,0:T(8,128)(2,1)S(1)}, u32[]{:S(2)}, u32[]{:S(2)}) collective-permute-start(bf16[2,160,128]{2,1,0:T(8,128)(2,1)S(1)} %get-tuple-element.89), channel_id=1, source_target_pairs={{0,3},{1,2},{2,1},{3,0},{4,7},{5,6},{6,5},{7,4},{8,11},{9,10},{10,... | collective-permute-start | bytes 245768 | tf_op jit(solution)/shard_map/ppermute | solution.py:395
  28.5 2.5 %collective-permute-done.5.other_part = bf16[2,160,128]{2,1,0:T(8,128)(2,1)S(1)} collective-permute-done((bf16[2,160,128]{2,1,0:T(8,128)(2,1)S(1)}, bf16[2,160,128]{2,1,0:T(8,128)(2,1)S(1)}, u32[]{:S(2)}, u32[]{:S(2)}) %collective-permute-start.5) | collective-permute-done | bytes 81952 | tf_op jit(solution)/shard_map/ppermute | solution.py:395
  31.0 0.1 shard_map.153
  31.1 0.9 %collective-permute-start.6 = (bf16[4,160,128]{2,1,0:T(8,128)(2,1)S(1)}, bf16[4,160,128]{2,1,0:T(8,128)(2,1)S(1)}, u32[]{:S(2)}, u32[]{:S(2)}) collective-permute-start(bf16[4,160,128]{2,1,0:T(8,128)(2,1)S(1)} %get-tuple-element.92), channel_id=1, source_target_pairs={{0,1},{1,0},{2,3},{3,2},{4,5},{5,4},{6,7},{7,6},{8,9},{9,8},{10,11... | collective-permute-start | bytes 491528 | tf_op jit(solution)/shard_map/ppermute | solution.py:395
  32.0 1.4 %shard_map.154 = (bf16[512,512]{1,0:T(8,128)(2,1)S(1)}, bf16[512,512]{1,0:T(8,128)(2,1)S(1)}, bf16[4,160,128]{2,1,0:T(8,128)(2,1)S(1)}, f32[4,128]{1,0:T(4,128)S(1)}) custom-call(f32[512,512]{1,0:T(8,128)S(1)} %shard_map.147.local, bf16[8,160,512]{2,1,0:T(8,128)(2,1)S(1)} %get-tuple-element.80.fq, bf16[4,160,128]{2,1,0:T(8,128)(2,1)S(1)} %get-tuple-element.90.prefix.pre_a, ...), custom_call_target="tpu_custom_call" | custom-call | flops 167772160 | bytes 4790272 | tf_op jit(solution)/shard_map/pallas_call | solution.py:383
  33.4 0.1 collective-permute-start.7
  33.5 1.4 %shard_map.155 = (bf16[512,512]{1,0:T(8,128)(2,1)S(1)}, bf16[512,512]{1,0:T(8,128)(2,1)S(1)}, bf16[4,160,128]{2,1,0:T(8,128)(2,1)S(1)}, f32[4,128]{1,0:T(4,128)S(1)}) custom-call(f32[512,512]{1,0:T(8,128)S(1)} %shard_map.151.local, bf16[8,160,512]{2,1,0:T(8,128)(2,1)S(1)} %get-tuple-element.80.fq, ...), custom_call_target="tpu_custom_call" | custom-call | flops 167772160 | bytes 4790272 | tf_op jit(solution)/shard_map/pallas_call | solution.py:383
  34.9 1.6 %collective-permute-start.8 = (bf16[2,160,128]{2,1,0:T(8,128)(2,1)S(1)}, bf16[2,160,128]{2,1,0:T(8,128)(2,1)S(1)}, u32[]{:S(2)}, u32[]{:S(2)}) collective-permute-start(bf16[2,160,128]{2,1,0:T(8,128)(2,1)S(1)} %get-tuple-element.107), channel_id=1, source_target_pairs={{0,3},{1,2},{2,1},{3,0},{4,7},{5,6},{6,5},{7,4},{8,11},{9,10},{10,... | collective-permute-start | bytes 245768 | tf_op jit(solution)/shard_map/ppermute | solution.py:395
  36.6 2.5 %shard_map.157 = (f32[512,256]{1,0:T(8,128)S(1)}, f32[32,512]{1,0:T(8,128)S(1)}, f32[32,512]{1,0:T(8,128)S(1)}) custom-call(bf16[512,128]{1,0:T(8,128)(2,1)S(1)} %get-tuple-element.76.q_ref, bf16[512,128]{1,0:T(8,128)(2,1)S(1)} %get-tuple-element.77.k_ref, bf16[128,512]{1,0:T(8,128)(2,1)S(1)} %get-tuple-element.95.qt_ref, ...), custom_call_target="tpu_custom_call" | custom-call | flops 536870912 | bytes 2228224 | tf_op jit(solution)/shard_map/pallas_call | solution.py:383
  39.1 1.0 %shard_map.156 = bf16[512,1024]{1,0:T(8,128)(2,1)} custom-call(bf16[512,512]{1,0:T(8,128)(2,1)S(1)} %get-tuple-element.91.out_a, bf16[512,512]{1,0:T(8,128)(2,1)S(1)} %get-tuple-element.94.out_b), custom_call_target="tpu_custom_call" | custom-call | flops 512 | bytes 2097152 | tf_op jit(solution)/shard_map/pallas_call | solution.py:383
  40.1 1.4 %collective-permute-start.9 = (bf16[2,160,128]{2,1,0:T(8,128)(2,1)S(1)}, bf16[2,160,128]{2,1,0:T(8,128)(2,1)S(1)}, u32[]{:S(2)}, u32[]{:S(2)}) collective-permute-start(bf16[2,160,128]{2,1,0:T(8,128)(2,1)S(1)} %shard_map.163), channel_id=1, source_target_pairs={{0,5},{1,4},{2,7},{3,6},{4,1},{5,0},{6,3},{7,2},{8,13},{9,12},{10,... | collective-permute-start | bytes 245768 | tf_op jit(solution)/shard_map/ppermute | solution.py:395
  41.6 2.5 %shard_map.158 = (f32[512,256]{1,0:T(8,128)S(1)}, f32[32,512]{1,0:T(8,128)S(1)}, f32[32,512]{1,0:T(8,128)S(1)}) custom-call(bf16[512,128]{1,0:T(8,128)(2,1)S(1)} %get-tuple-element.76.q_ref, bf16[512,128]{1,0:T(8,128)(2,1)S(1)} %get-tuple-element.77.k_ref, bf16[128,512]{1,0:T(8,128)(2,1)S(1)} %get-tuple-element.95.qt_ref, ...), custom_call_target="tpu_custom_call" | custom-call | flops 536870912 | bytes 2228224 | tf_op jit(solution)/shard_map/pallas_call | solution.py:383
  44.1 0.4 collective-permute-done.9.refs_1_.rest_0_
  44.5 2.9 %collective-permute-start.10 = (bf16[2,160,128]{2,1,0:T(8,128)(2,1)S(1)}, bf16[2,160,128]{2,1,0:T(8,128)(2,1)S(1)}, u32[]{:S(2)}, u32[]{:S(2)}) collective-permute-start(bf16[2,160,128]{2,1,0:T(8,128)(2,1)S(1)} %shard_map.164), channel_id=1, source_target_pairs={{0,9},{1,8},{2,11},{3,10},{4,13},{5,12},{6,15},{7,14},{8,1},{9,0},... | collective-permute-start | bytes 245768 | tf_op jit(solution)/shard_map/ppermute | solution.py:395
  47.4 2.7 %shard_map.159 = (f32[512,256]{1,0:T(8,128)S(1)}, f32[32,512]{1,0:T(8,128)S(1)}, f32[32,512]{1,0:T(8,128)S(1)}) custom-call(bf16[512,128]{1,0:T(8,128)(2,1)S(1)} %get-tuple-element.76.q_ref, bf16[512,128]{1,0:T(8,128)(2,1)S(1)} %get-tuple-element.77.k_ref, bf16[128,512]{1,0:T(8,128)(2,1)S(1)} %get-tuple-element.95.qt_ref, ...), custom_call_target="tpu_custom_call" | custom-call | flops 536870912 | bytes 2228224 | tf_op jit(solution)/shard_map/pallas_call | solution.py:383
  50.2 2.6 %collective-permute-start.11 = (bf16[2,160,128]{2,1,0:T(8,128)(2,1)S(1)}, bf16[2,160,128]{2,1,0:T(8,128)(2,1)S(1)}, u32[]{:S(2)}, u32[]{:S(2)}) collective-permute-start(bf16[2,160,128]{2,1,0:T(8,128)(2,1)S(1)} %get-tuple-element.115), channel_id=1, source_target_pairs={{0,3},{1,2},{2,1},{3,0},{4,7},{5,6},{6,5},{7,4},{8,11},{9,10},{10,... | collective-permute-start | bytes 245768 | tf_op jit(solution)/shard_map/ppermute | solution.py:395
  52.8 2.5 %shard_map.160 = (f32[512,256]{1,0:T(8,128)S(1)}, f32[32,512]{1,0:T(8,128)S(1)}, f32[32,512]{1,0:T(8,128)S(1)}) custom-call(bf16[512,128]{1,0:T(8,128)(2,1)S(1)} %get-tuple-element.76.q_ref, bf16[512,128]{1,0:T(8,128)(2,1)S(1)} %get-tuple-element.77.k_ref, bf16[128,512]{1,0:T(8,128)(2,1)S(1)} %get-tuple-element.95.qt_ref, ...), custom_call_target="tpu_custom_call" | custom-call | flops 536870912 | bytes 2228224 | tf_op jit(solution)/shard_map/pallas_call | solution.py:383
  55.3 0.9 %shard_map.161 = (f32[512,128]{1,0:T(8,128)S(1)}, f32[3,128]{1,0:T(4,128)S(1)}) custom-call(bf16[512,128]{1,0:T(8,128)(2,1)S(1)} %copy-done.3, bf16[16,1280]{1,0:T(8,128)(2,1)S(1)} %collective-permute-done.rim, bf16[128,512]{1,0:T(8,128)(2,1)S(1)} %get-tuple-element.95.qt_ref, bf16[512,512]{1,0:T(8,128)(2,1)S(1)} %get-tuple-element.96.gs_ref.gs_a, ...), custom_call_target="tpu_custom_call" | custom-call | flops 83886080 | bytes 2206720 | tf_op jit(solution)/shard_map/pallas_call | solution.py:383
  56.2 0.1 shard_map.166
  56.4 1.1 %shard_map.167 = (f32[512,512]{1,0:T(8,128)S(1)}, f32[64,512]{1,0:T(8,128)S(1)}, f32[3,512]{1,0:T(4,128)S(1)}) custom-call(bf16[512,1024]{1,0:T(8,128)(2,1)S(1)} %copy-done, bf16[16,1280]{1,0:T(8,128)(2,1)S(1)} %collective-permute-done.rim, bf16[128,512]{1,0:T(8,128)(2,1)S(1)} %get-tuple-element.78.kt.kt_ref, ...), custom_call_target="tpu_custom_call" | custom-call | flops 167772160 | bytes 4929536 | tf_op jit(solution)/shard_map/pallas_call | solution.py:383
  57.5 0.3 collective-permute-done.12.state
  57.8 1.1 %shard_map.168 = (f32[512,512]{1,0:T(8,128)S(1)}, f32[512,128]{1,0:T(8,128)S(1)}, f32[8,1280]{1,0:T(8,128)S(1)}, f32[4,1280]{1,0:T(4,128)S(1)}) custom-call(bf16[512,128]{1,0:T(8,128)(2,1)S(1)} %copy-done.2, bf16[512,1024]{1,0:T(8,128)(2,1)S(1)} %copy-done, bf16[16,1280]{1,0:T(8,128)(2,1)S(1)} %collective-permute-done.rim, ...), custom_call_target="tpu_custom_call" | custom-call | flops 167772160 | bytes 6700544 | tf_op jit(solution)/shard_map/pallas_call | solution.py:383
  58.9 4.2 %collective-permute-start.16 = (f32[4,1280]{1,0:T(4,128)S(1)}, f32[4,1280]{1,0:T(4,128)S(1)}, u32[]{:S(2)}, u32[]{:S(2)}) collective-permute-start(f32[4,1280]{1,0:T(4,128)S(1)} %get-tuple-element.138), channel_id=1, source_target_pairs={{0,12},{1,13},{2,14},{3,15},{4,8},{5,9},{6,10},{7,11},{8,4},{9,5},... | collective-permute-start | bytes 61448 | tf_op jit(solution)/shard_map/ppermute | solution.py:395
  63.1 0.4 collective-permute-start.14
  63.5 1.3 %collective-permute-start.13 = (f32[8,1280]{1,0:T(8,128)S(1)}, f32[8,1280]{1,0:T(8,128)S(1)}, u32[]{:S(2)}, u32[]{:S(2)}) collective-permute-start(f32[8,1280]{1,0:T(8,128)S(1)} %get-tuple-element.134), channel_id=1, source_target_pairs={{1,0},{2,1},{3,2},{4,3},{5,4},{6,5},{7,6},{8,7},{9,8},{10,9},{11,1... | collective-permute-start | bytes 122888 | tf_op jit(solution)/shard_map/ppermute | solution.py:625
  64.8 0.2 collective-permute-done.16
  65.0 2.3 %collective-permute-done.15 = f32[4,1280]{1,0:T(4,128)S(1)} collective-permute-done((f32[4,1280]{1,0:T(4,128)S(1)}, f32[4,1280]{1,0:T(4,128)S(1)}, u32[]{:S(2)}, u32[]{:S(2)}) %collective-permute-start.15) | collective-permute-done | bytes 20512 | tf_op jit(solution)/shard_map/ppermute | solution.py:395
  67.3 0.2 collective-permute-start.17
  67.4 1.3 %collective-permute-start.18 = (f32[4,1280]{1,0:T(4,128)S(1)}, f32[4,1280]{1,0:T(4,128)S(1)}, u32[]{:S(2)}, u32[]{:S(2)}) collective-permute-start(f32[4,1280]{1,0:T(4,128)S(1)} %add_add_fusion.refs_0_), channel_id=1, source_target_pairs={{0,2},{1,3},{2,0},{3,1},{4,6},{5,7},{6,4},{7,5},{8,10},{9,11},{10,... | collective-permute-start | bytes 61448 | tf_op jit(solution)/shard_map/ppermute | solution.py:395
  68.8 0.4 collective-permute-start.19
  69.2 2.2 %shard_map.169 = (bf16[512,128]{1,0:T(8,128)(2,1)}, bf16[512,128]{1,0:T(8,128)(2,1)}, bf16[512,1024]{1,0:T(8,128)(2,1)}) custom-call(f32[512,128]{1,0:T(8,128)S(1)} %get-tuple-element.102.gq, f32[512,128]{1,0:T(8,128)S(1)} %get-tuple-element.132.gk, f32[512,512]{1,0:T(8,128)S(1)} %get-tuple-element.133.gv_a, f32[512,512]{1,0:T(8,128)S(1)} %get-tuple-element.123.gv_b, ...), custom_call_target="tpu_custom_call" | custom-call | flops 167772160 | bytes 3988480 | tf_op jit(solution)/shard_map/pallas_call | solution.py:383
  71.4 0.6 collective-permute-done.19.refs_3_
  72.0 0.6 shard_map.170
  (37 shorter events, 0.5 us)
Async XLA Ops:
  0.6 4.3 %copy-start.2 = (bf16[512,128]{1,0:T(8,128)(2,1)S(1)}, bf16[512,128]{1,0:T(8,128)(2,1)}, u32[]{:S(2)}) copy-start(bf16[512,128]{1,0:T(8,128)(2,1)} %key.5) | copy-start | bytes 393220
  0.6 4.3 %copy-start = (bf16[512,1024]{1,0:T(8,128)(2,1)S(1)}, bf16[512,1024]{1,0:T(8,128)(2,1)}, u32[]{:S(2)}) copy-start(bf16[512,1024]{1,0:T(8,128)(2,1)} %value.9) | copy-start | bytes 3145732
  0.7 4.3 %copy-start.7 = (f32[3,128]{1,0:T(4,128)S(1)}, f32[3,128]{1,0:T(4,128)}, u32[]{:S(2)}) copy-start(f32[3,128]{1,0:T(4,128)} %taps_k.3) | copy-start | bytes 4612
  0.7 4.3 %copy-start.4 = (f32[3,1024]{1,0:T(4,128)S(1)}, f32[3,1024]{1,0:T(4,128)}, u32[]{:S(2)}) copy-start(f32[3,1024]{1,0:T(4,128)} %taps_v.5) | copy-start | bytes 36868
  1.6 10.7 %copy-start.3 = (bf16[512,128]{1,0:T(8,128)(2,1)S(1)}, bf16[512,128]{1,0:T(8,128)(2,1)}, u32[]{:S(2)}) copy-start(bf16[512,128]{1,0:T(8,128)(2,1)} %query.5) | copy-start | bytes 393220
  1.6 10.7 %copy-start.6 = (f32[3,128]{1,0:T(4,128)S(1)}, f32[3,128]{1,0:T(4,128)}, u32[]{:S(2)}) copy-start(f32[3,128]{1,0:T(4,128)} %taps_q.5) | copy-start | bytes 4612
  1.6 3.3 %collective-permute-start = (bf16[16,1280]{1,0:T(8,128)(2,1)S(1)}, bf16[16,1280]{1,0:T(8,128)(2,1)S(1)}, u32[]{:S(2)}, u32[]{:S(2)}) collective-permute-start(bf16[16,1280]{1,0:T(8,128)(2,1)S(1)} %shard_map.143), channel_id=1, source_target_pairs={{0,1},{1,2},{2,3},{3,4},{4,5},{5,6},{6,7},{7,8},{8,9},{9,10},{10,1... | collective-permute-start | bytes 122888 | tf_op jit(solution)/shard_map/ppermute | solution.py:505
  5.9 4.0 %collective-permute-start.1 = (bf16[4,160,128]{2,1,0:T(8,128)(2,1)S(1)}, bf16[4,160,128]{2,1,0:T(8,128)(2,1)S(1)}, u32[]{:S(2)}, u32[]{:S(2)}) collective-permute-start(bf16[4,160,128]{2,1,0:T(8,128)(2,1)S(1)} %get-tuple-element.82), channel_id=1, source_target_pairs={{0,1},{1,0},{2,3},{3,2},{4,5},{5,4},{6,7},{7,6},{8,9},{9,8},{10,11... | collective-permute-start | bytes 491528 | tf_op jit(solution)/shard_map/ppermute | solution.py:395
  9.9 5.2 %collective-permute-start.2 = (bf16[2,160,128]{2,1,0:T(8,128)(2,1)S(1)}, bf16[2,160,128]{2,1,0:T(8,128)(2,1)S(1)}, u32[]{:S(2)}, u32[]{:S(2)}) collective-permute-start(bf16[2,160,128]{2,1,0:T(8,128)(2,1)S(1)} %get-tuple-element.84), channel_id=1, source_target_pairs={{0,3},{1,2},{2,1},{3,0},{4,7},{5,6},{6,5},{7,4},{8,11},{9,10},{10,... | collective-permute-start | bytes 245768 | tf_op jit(solution)/shard_map/ppermute | solution.py:395
  15.1 5.2 %collective-permute-start.3 = (bf16[2,160,128]{2,1,0:T(8,128)(2,1)S(1)}, bf16[2,160,128]{2,1,0:T(8,128)(2,1)S(1)}, u32[]{:S(2)}, u32[]{:S(2)}) collective-permute-start(bf16[2,160,128]{2,1,0:T(8,128)(2,1)S(1)} %shard_map.149), channel_id=1, source_target_pairs={{0,5},{1,4},{2,7},{3,6},{4,1},{5,0},{6,3},{7,2},{8,13},{9,12},{10,... | collective-permute-start | bytes 245768 | tf_op jit(solution)/shard_map/ppermute | solution.py:395
  17.7 14.3 %copy-start.1 = (bf16[512,1024]{1,0:T(8,128)(2,1)S(1)}, bf16[512,1024]{1,0:T(8,128)(2,1)}, u32[]{:S(2)}) copy-start(bf16[512,1024]{1,0:T(8,128)(2,1)} %grad.3) | copy-start | bytes 3145732
  17.7 14.3 %copy-start.5 = (f32[1024]{0:T(1024)S(1)}, f32[1024]{0:T(1024)}, u32[]{:S(2)}) copy-start(f32[1024]{0:T(1024)} %param.14) | copy-start | bytes 12292
  20.3 5.5 %collective-permute-start.4 = (bf16[2,160,128]{2,1,0:T(8,128)(2,1)S(1)}, bf16[2,160,128]{2,1,0:T(8,128)(2,1)S(1)}, u32[]{:S(2)}, u32[]{:S(2)}) collective-permute-start(bf16[2,160,128]{2,1,0:T(8,128)(2,1)S(1)} %shard_map.150), channel_id=1, source_target_pairs={{0,9},{1,8},{2,11},{3,10},{4,13},{5,12},{6,15},{7,14},{8,1},{9,0},... | collective-permute-start | bytes 245768 | tf_op jit(solution)/shard_map/ppermute | solution.py:395
  25.9 5.1 %collective-permute-start.5 = (bf16[2,160,128]{2,1,0:T(8,128)(2,1)S(1)}, bf16[2,160,128]{2,1,0:T(8,128)(2,1)S(1)}, u32[]{:S(2)}, u32[]{:S(2)}) collective-permute-start(bf16[2,160,128]{2,1,0:T(8,128)(2,1)S(1)} %get-tuple-element.89), channel_id=1, source_target_pairs={{0,3},{1,2},{2,1},{3,0},{4,7},{5,6},{6,5},{7,4},{8,11},{9,10},{10,... | collective-permute-start | bytes 245768 | tf_op jit(solution)/shard_map/ppermute | solution.py:395
  31.1 2.4 %collective-permute-start.6 = (bf16[4,160,128]{2,1,0:T(8,128)(2,1)S(1)}, bf16[4,160,128]{2,1,0:T(8,128)(2,1)S(1)}, u32[]{:S(2)}, u32[]{:S(2)}) collective-permute-start(bf16[4,160,128]{2,1,0:T(8,128)(2,1)S(1)} %get-tuple-element.92), channel_id=1, source_target_pairs={{0,1},{1,0},{2,3},{3,2},{4,5},{5,4},{6,7},{7,6},{8,9},{9,8},{10,11... | collective-permute-start | bytes 491528 | tf_op jit(solution)/shard_map/ppermute | solution.py:395
  33.4 1.5 %collective-permute-start.7 = (bf16[4,160,128]{2,1,0:T(8,128)(2,1)S(1)}, bf16[4,160,128]{2,1,0:T(8,128)(2,1)S(1)}, u32[]{:S(2)}, u32[]{:S(2)}) collective-permute-start(bf16[4,160,128]{2,1,0:T(8,128)(2,1)S(1)} %get-tuple-element.105), channel_id=1, source_target_pairs={{0,1},{1,0},{2,3},{3,2},{4,5},{5,4},{6,7},{7,6},{8,9},{9,8},{10,11... | collective-permute-start | bytes 491528 | tf_op jit(solution)/shard_map/ppermute | solution.py:395
  34.9 5.2 %collective-permute-start.8 = (bf16[2,160,128]{2,1,0:T(8,128)(2,1)S(1)}, bf16[2,160,128]{2,1,0:T(8,128)(2,1)S(1)}, u32[]{:S(2)}, u32[]{:S(2)}) collective-permute-start(bf16[2,160,128]{2,1,0:T(8,128)(2,1)S(1)} %get-tuple-element.107), channel_id=1, source_target_pairs={{0,3},{1,2},{2,1},{3,0},{4,7},{5,6},{6,5},{7,4},{8,11},{9,10},{10,... | collective-permute-start | bytes 245768 | tf_op jit(solution)/shard_map/ppermute | solution.py:395
  40.1 4.4 %collective-permute-start.9 = (bf16[2,160,128]{2,1,0:T(8,128)(2,1)S(1)}, bf16[2,160,128]{2,1,0:T(8,128)(2,1)S(1)}, u32[]{:S(2)}, u32[]{:S(2)}) collective-permute-start(bf16[2,160,128]{2,1,0:T(8,128)(2,1)S(1)} %shard_map.163), channel_id=1, source_target_pairs={{0,5},{1,4},{2,7},{3,6},{4,1},{5,0},{6,3},{7,2},{8,13},{9,12},{10,... | collective-permute-start | bytes 245768 | tf_op jit(solution)/shard_map/ppermute | solution.py:395
  44.5 5.6 %collective-permute-start.10 = (bf16[2,160,128]{2,1,0:T(8,128)(2,1)S(1)}, bf16[2,160,128]{2,1,0:T(8,128)(2,1)S(1)}, u32[]{:S(2)}, u32[]{:S(2)}) collective-permute-start(bf16[2,160,128]{2,1,0:T(8,128)(2,1)S(1)} %shard_map.164), channel_id=1, source_target_pairs={{0,9},{1,8},{2,11},{3,10},{4,13},{5,12},{6,15},{7,14},{8,1},{9,0},... | collective-permute-start | bytes 245768 | tf_op jit(solution)/shard_map/ppermute | solution.py:395
  50.2 6.0 %collective-permute-start.11 = (bf16[2,160,128]{2,1,0:T(8,128)(2,1)S(1)}, bf16[2,160,128]{2,1,0:T(8,128)(2,1)S(1)}, u32[]{:S(2)}, u32[]{:S(2)}) collective-permute-start(bf16[2,160,128]{2,1,0:T(8,128)(2,1)S(1)} %get-tuple-element.115), channel_id=1, source_target_pairs={{0,3},{1,2},{2,1},{3,0},{4,7},{5,6},{6,5},{7,4},{8,11},{9,10},{10,... | collective-permute-start | bytes 245768 | tf_op jit(solution)/shard_map/ppermute | solution.py:395
  56.4 1.5 %collective-permute-start.12 = (bf16[4,160,128]{2,1,0:T(8,128)(2,1)S(1)}, bf16[4,160,128]{2,1,0:T(8,128)(2,1)S(1)}, u32[]{:S(2)}, u32[]{:S(2)}) collective-permute-start(bf16[4,160,128]{2,1,0:T(8,128)(2,1)S(1)} %get-tuple-element.118), channel_id=1, source_target_pairs={{0,1},{1,0},{2,3},{3,2},{4,5},{5,4},{6,7},{7,6},{8,9},{9,8},{10,11... | collective-permute-start | bytes 491528 | tf_op jit(solution)/shard_map/ppermute | solution.py:395
  58.9 6.0 %collective-permute-start.16 = (f32[4,1280]{1,0:T(4,128)S(1)}, f32[4,1280]{1,0:T(4,128)S(1)}, u32[]{:S(2)}, u32[]{:S(2)}) collective-permute-start(f32[4,1280]{1,0:T(4,128)S(1)} %get-tuple-element.138), channel_id=1, source_target_pairs={{0,12},{1,13},{2,14},{3,15},{4,8},{5,9},{6,10},{7,11},{8,4},{9,5},... | collective-permute-start | bytes 61448 | tf_op jit(solution)/shard_map/ppermute | solution.py:395
  63.1 4.1 %collective-permute-start.15 = (f32[4,1280]{1,0:T(4,128)S(1)}, f32[4,1280]{1,0:T(4,128)S(1)}, u32[]{:S(2)}, u32[]{:S(2)}) collective-permute-start(f32[4,1280]{1,0:T(4,128)S(1)} %get-tuple-element.138), channel_id=1, source_target_pairs={{0,9},{1,8},{2,11},{3,10},{4,13},{5,12},{6,15},{7,14},{8,1},{9,0},... | collective-permute-start | bytes 61448 | tf_op jit(solution)/shard_map/ppermute | solution.py:395
  63.1 4.1 %collective-permute-start.14 = (f32[4,1280]{1,0:T(4,128)S(1)}, f32[4,1280]{1,0:T(4,128)S(1)}, u32[]{:S(2)}, u32[]{:S(2)}) collective-permute-start(f32[4,1280]{1,0:T(4,128)S(1)} %get-tuple-element.138), channel_id=1, source_target_pairs={{0,5},{1,4},{2,7},{3,6},{4,1},{5,0},{6,3},{7,2},{8,13},{9,12},{10,... | collective-permute-start | bytes 61448 | tf_op jit(solution)/shard_map/ppermute | solution.py:395
  63.5 5.7 %collective-permute-start.13 = (f32[8,1280]{1,0:T(8,128)S(1)}, f32[8,1280]{1,0:T(8,128)S(1)}, u32[]{:S(2)}, u32[]{:S(2)}) collective-permute-start(f32[8,1280]{1,0:T(8,128)S(1)} %get-tuple-element.134), channel_id=1, source_target_pairs={{1,0},{2,1},{3,2},{4,3},{5,4},{6,5},{7,6},{8,7},{9,8},{10,9},{11,1... | collective-permute-start | bytes 122888 | tf_op jit(solution)/shard_map/ppermute | solution.py:625
  67.3 4.1 %collective-permute-start.17 = (f32[4,1280]{1,0:T(4,128)S(1)}, f32[4,1280]{1,0:T(4,128)S(1)}, u32[]{:S(2)}, u32[]{:S(2)}) collective-permute-start(f32[4,1280]{1,0:T(4,128)S(1)} %add_add_fusion.refs_0_), channel_id=1, source_target_pairs={{0,1},{1,0},{2,3},{3,2},{4,5},{5,4},{6,7},{7,6},{8,9},{9,8},{10,11... | collective-permute-start | bytes 61448 | tf_op jit(solution)/shard_map/ppermute | solution.py:395
  67.4 3.9 %collective-permute-start.18 = (f32[4,1280]{1,0:T(4,128)S(1)}, f32[4,1280]{1,0:T(4,128)S(1)}, u32[]{:S(2)}, u32[]{:S(2)}) collective-permute-start(f32[4,1280]{1,0:T(4,128)S(1)} %add_add_fusion.refs_0_), channel_id=1, source_target_pairs={{0,2},{1,3},{2,0},{3,1},{4,6},{5,7},{6,4},{7,5},{8,10},{9,11},{10,... | collective-permute-start | bytes 61448 | tf_op jit(solution)/shard_map/ppermute | solution.py:395
  68.8 3.2 %collective-permute-start.19 = (f32[4,1280]{1,0:T(4,128)S(1)}, f32[4,1280]{1,0:T(4,128)S(1)}, u32[]{:S(2)}, u32[]{:S(2)}) collective-permute-start(f32[4,1280]{1,0:T(4,128)S(1)} %add_add_fusion.refs_0_), channel_id=1, source_target_pairs={{0,3},{1,2},{2,1},{3,0},{4,7},{5,6},{6,5},{7,4},{8,11},{9,10},{10,... | collective-permute-start | bytes 61448 | tf_op jit(solution)/shard_map/ppermute | solution.py:395

commit v5 on v3

--- a/solution.py
+++ b/solution.py
@@ -176,9 +176,13 @@
             out[start:stop, head_lanes(g)] = dot(w.astype(BF16), v_ref[0:stop, head_lanes(g)], NN)
 
 
-def norm_kernel(own, local, fq, prefix, grad, gain, out, gs_out, state_out, gain_out, pre, summed_ref):
+def norm_kernel(own, local, fq, prefix, grad, gain, *refs):
+    *others, out, gs_out, state_out, gain_out, pre, summed_ref = refs
     half = half_index(own)
     doubled(prefix, pre)
+    for other in others:
+        for g in range(HALF):
+            out[:, lanes_of(1 - half, g)] = other[:, head_lanes(g)]
     for g in range(HALF):
         place = head_lanes(g)
         summed_ref[:, place] = local[:, place] + dot(fq[half * HALF + g], pre[g], TN)
@@ -188,7 +192,7 @@
         scale = lax.rsqrt(jnp.mean(summed * summed, axis=-1, keepdims=True) + EPSILON)
         normal = summed * scale
         weight = gain[pl.ds(half * HALF + g, 1)]
-        out[:, place] = (normal * weight).astype(BF16)
+        out[:, place if own else lanes_of(half, g)] = (normal * weight).astype(BF16)
         incoming = grad[:, lanes_of(half, g)].astype(F32)
         gain_out[g : g + 1] = jnp.sum(incoming * normal, axis=0, keepdims=True)
         upstream = incoming * weight
@@ -196,6 +200,13 @@
         gs = gs.astype(BF16)
         gs_out[:, place] = gs
         state_out[g] = dot(fq[half * HALF + g], gs, NN).astype(BF16)
+
+
+def first_back_kernel(q_ref, k_ref, qt_ref, kt_ref, v_ref, gs_ref, tokens, gv_out, gq_out, gk_out, out, sem):
+    copy = pltpu.make_async_copy(tokens, out, sem)
+    copy.start()
+    back_kernel(True, 0, q_ref, k_ref, qt_ref, kt_ref, v_ref, gs_ref, gv_out, gq_out, gk_out)
+    copy.wait()
 
 
 def back_kernel(own, part, q_ref, k_ref, qt_ref, kt_ref, v_ref, gs_ref, gv_out, gq_out, gk_out):
@@ -273,7 +284,7 @@
 
 def second_later_kernel(
     key, value, rim, kt, fk, v, state, v0, v1, k0, k1, gv_b, gk_b, sums_b, gq, sums_q, gain_a, gain_b,
-    gv_out, gk_out, head_out, sums, wide, post, turned_grad,
+    gv_out, gk_out, sums, wide, post, turned_grad,
 ):
     taps = sums_q.shape[0]
     rows = key.shape[0]
@@ -296,50 +307,121 @@
         sums[o : o + 1, LANES : 2 * LANES] = row
     sums[0:taps, 0:LANES] = sums_q[...]
     sums[taps : taps + 1, 0 : 2 * LANES] = jnp.zeros((1, 2 * LANES), F32)
-    head_out[:, 0:LANES] = gq[0:8]
-    head_out[:, LANES : 2 * LANES] = grad[0:8]
+    heads = slice(taps + 1, 2 * taps)
+    sums[heads, 0:LANES] = gq[0 : taps - 1]
+    sums[heads, LANES : 2 * LANES] = grad[0 : taps - 1]
+    sums[2 * taps :] = jnp.zeros((sums.shape[0] - 2 * taps, ALL), F32)
     for g in range(HALF):
         sums[0:taps, lanes_of(half_b, g, 2 * LANES)] = sums_b[:, head_lanes(g)]
         for half, gain, gv in ((half_a, gain_a, gv_out), (half_b, gain_b, gv_b)):
             sums[taps : taps + 1, lanes_of(half, g, 2 * LANES)] = gain[g : g + 1]
-            head_out[:, lanes_of(half, g, 2 * LANES)] = gv[0:8, head_lanes(g)]
+            sums[heads, lanes_of(half, g, 2 * LANES)] = gv[0 : taps - 1, head_lanes(g)]
+
+
+def signal_rows(wide, taps, rows):
+    count = taps.shape[0]
+    total = taps[0:1] * wide[count - 1 : count - 1 + rows]
+    for o in range(1, count):
+        total = total + taps[o : o + 1] * wide[count - 1 - o : count - 1 - o + rows]
+    return total.astype(BF16)
 
 
 def signal_kernel(
-    gq, gk, gv_a, gv_b, follow, out_a, out_b, taps_q, taps_k, taps_v, q_out, k_out, v_out, out, wide
+    gq, gk, gv_a, gv_b, taps_q, taps_k, taps_v, q_out, k_out, v_out, wide, q_part, k_part, v_part, sems
 ):
     rows = gq.shape[0]
-    count = taps_q.shape[0]
-
-    def one(grad, after, taps):
+    copies = []
+    wide[rows:] = jnp.zeros((wide.shape[0] - rows, DIM), F32)
+
+    def one(grad, taps):
         wide[0:rows] = grad
-        wide[rows : rows + 8] = after
-        total = taps[0:1] * wide[count - 1 : count - 1 + rows]
-        for o in range(1, count):
-            total = total + taps[o : o + 1] * wide[count - 1 - o : count - 1 - o + rows]
-        return total.astype(BF16)
-
-    q_out[...] = one(gq[...], follow[:, 0:LANES], taps_q[...])
-    k_out[...] = one(gk[...], follow[:, LANES : 2 * LANES], taps_k[...])
-    for own, gv, tokens in ((True, gv_a, out_a), (False, gv_b, out_b)):
+        return signal_rows(wide, taps, rows)
+
+    def move(part, out):
+        copies.append(pltpu.make_async_copy(part, out, sems.at[len(copies)]))
+        copies[-1].start()
+
+    for i, (own, gv) in enumerate(((True, gv_a), (False, gv_b))):
         half = half_index(own)
         for g in range(HALF):
             place = lanes_of(half, g)
-            out[:, place] = tokens[:, head_lanes(g)]
-            v_out[:, place] = one(gv[:, head_lanes(g)], follow[:, lanes_of(half, g, 2 * LANES)], taps_v[:, place])
-
-
-def finish_kernel(factor, *refs):
-    *terms, q_out, k_out, v_out, gain_out = refs
-    taps = q_out.shape[0]
-    total = terms[0][...]
-    for term in terms[1:]:
-        total = total + term[...]
-    total = total * factor
-    q_out[...] = total[0:taps, 0:LANES]
-    k_out[...] = total[0:taps, LANES : 2 * LANES]
-    v_out[...] = total[0:taps, 2 * LANES :]
-    gain_out[...] = total[taps : taps + 1, 2 * LANES :]
+            slot = i * HALF + g
+            v_part[slot] = one(gv[:, head_lanes(g)], taps_v[:, place])
+            move(v_part.at[slot], v_out.at[:, place])
+    q_part[...] = one(gq[...], taps_q[...])
+    move(q_part, q_out)
+    k_part[...] = one(gk[...], taps_k[...])
+    move(k_part, k_out)
+    for copy in copies:
+        copy.wait()
+
+
+def digit(bit, radix):
+    return lax.rem(lax.div(lax.axis_index("seq"), bit), radix)
+
+
+def combine_kernel(bit, radix, taps, final, with_own, with_next, *refs):
+    *gots, own_out, next_out = refs
+    sums, heads = slice(0, taps + 1), slice(taps + 1, 2 * taps)
+    here = digit(bit, radix)
+    total = with_own[sums]
+    for got in gots:
+        total = total + got[sums]
+    passed = with_next[heads]
+    open_ = lax.rem(lax.div(lax.axis_index("seq"), 4), max(bit // 4, 1)) == bit // 4 - 1 if bit > 4 else None
+    taken = passed
+    for d in range(radix):
+        source = d ^ (d + 1) if d + 1 < radix else d
+        taken = jnp.where(here == d, gots[source - 1][heads], taken)
+    passed = taken if open_ is None else jnp.where(open_, taken, passed)
+    if final:
+        passed = jnp.where(digit(1, 4) == 0, passed, with_own[heads])
+    rest = jnp.zeros((own_out.shape[0] - 2 * taps, ALL), F32)
+    for ref, rows in ((own_out, with_own[heads]), (next_out, passed)):
+        ref[sums] = total
+        ref[heads] = rows
+        ref[2 * taps :] = rest
+
+
+def finish_kernel(
+    factor, last, sums, got_1, got_2, got_3, gq, gk, gv_a, gv_b, taps_q, taps_k, taps_v, q_in, k_in, v_in,
+    q_out, k_out, v_out, q_sums, k_sums, v_sums, gain_sums, wide, q_part, k_part, v_part, sems,
+):
+    taps = q_sums.shape[0]
+    here = lax.axis_index("seq")
+    heads = slice(taps + 1, 2 * taps)
+    margin = taps - 1
+    start = gq.shape[0] - RIM
+    wide[RIM:] = jnp.zeros((wide.shape[0] - RIM, DIM), F32)
+    even = lax.rem(here, 2) == 0
+
+    def one(grad, place, taps_ref):
+        follow = jnp.where(even, got_1[heads, place], got_3[heads, place])
+        wide[0:RIM] = grad
+        wide[RIM : RIM + margin] = jnp.where(here == last, jnp.zeros_like(follow), follow)
+        return signal_rows(wide, taps_ref, RIM)
+
+    q_part[...] = one(gq[start:], slice(0, LANES), taps_q[...])
+    k_part[...] = one(gk[start:], slice(LANES, 2 * LANES), taps_k[...])
+    for own, gv in ((True, gv_a), (False, gv_b)):
+        half = half_index(own)
+        for g in range(HALF):
+            place = lanes_of(half, g)
+            v_part[:, place] = one(gv[start:, head_lanes(g)], lanes_of(half, g, 2 * LANES), taps_v[:, place])
+    copies = [
+        pltpu.make_async_copy(part, out.at[pl.ds(start, RIM)], sems.at[i])
+        for i, (part, out) in enumerate(((q_part, q_out), (k_part, k_out), (v_part, v_out)))
+    ]
+    for copy in copies:
+        copy.start()
+    rows = slice(0, taps + 1)
+    total = (sums[rows] + got_1[rows] + got_2[rows] + got_3[rows]) * factor
+    q_sums[...] = total[0:taps, 0:LANES]
+    k_sums[...] = total[0:taps, LANES : 2 * LANES]
+    v_sums[...] = total[0:taps, 2 * LANES :]
+    gain_sums[...] = total[taps : taps + 1, 2 * LANES :]
+    for copy in copies:
+        copy.wait()
 
 
 def far(x):
@@ -428,7 +510,7 @@
     cost = 4 * keep.size
 
     def under(x):
-        return tie(x, works.pop(0)()) if works else x
+        return tie(x, *works.pop(0)()) if works else x
 
     near = exchange(send, 1)
     part, their = call(pair_kernel, [wide, narrow], [], (keep, near), cost)
@@ -467,6 +549,7 @@
     square_flops = 2 * HALF * rows * rows * DIM
 
     apart = pl.BlockSpec(memory_space=pltpu.HBM)
+    near = pl.BlockSpec(memory_space=pltpu.VMEM)
     ends = call(
         end_kernel,
         [st((RIM, ALL), BF16)],
@@ -510,16 +593,16 @@
                 held(made["q"][0], k, v),
                 2 * square_flops,
             )[0]
-            return made[own]
+            return (made[own],)
 
         return work
 
-    def norm(own, prefix):
+    def norm(own, prefix, *others):
         return call(
             functools.partial(norm_kernel, own),
-            [half_narrow, half_narrow, half_state, st((HALF, DIM), F32)],
+            [half_narrow if own else st((rows, WIDE), BF16), half_narrow, half_state, st((HALF, DIM), F32)],
             [state_scratch, pltpu.VMEM((rows, half_width), F32)],
-            (*held(made[own], made["q"][2]), prefix, grad_out, gain),
+            (*held(made[own], made["q"][2]), prefix, grad_out, gain, *held(*others)),
             2 * state_flops,
         )
 
@@ -532,8 +615,22 @@
     )
     q, qt, fq = made["q"]
     out_a, gs_a, state_a, gain_a = made["norm"]
-    out_b, gs_b, state_b, gain_b = norm(False, pre_b)
+    tokens, gs_b, state_b, gain_b = norm(False, pre_b, out_a)
     back = []
+
+    def first_back():
+        *parts, made["out"] = call(
+            first_back_kernel,
+            [st((rows, PART * DIM), F32), st((PART * FEAT, rows), F32), st((PART * FEAT, rows), F32),
+             st((rows, WIDE), BF16)],
+            [pltpu.SemaphoreType.DMA],
+            held(q, k, qt, kt, v_a, gs_a, tokens),
+            2 * square_flops,
+            loose=(3,),
+            out_specs=[near] * 3 + [apart],
+        )
+        back.append(parts)
+        return (parts[0],)
 
     def back_work(own, part, v, gs):
         def work():
@@ -546,12 +643,12 @@
                     2 * square_flops,
                 )
             )
-            return back[-1][0]
+            return (back[-1][0],)
 
         return work
 
     def last_work():
-        work = back_work(False, 1, v_b, gs_b)()
+        work = back_work(False, 1, v_b, gs_b)()[0]
         made["gq"] = call(
             query_grad_kernel,
             [flat, st((taps, LANES), F32)],
@@ -559,7 +656,7 @@
             (query_in, rim, *held(qt, gs_a, gs_b), pre_a, pre_b, *held(*[b[1] for b in back]), conv_query),
             state_flops,
         )
-        return made["gq"][0]
+        return (work, made["gq"][0])
 
     def first_later(state):
         made["later"] = call(
@@ -571,43 +668,58 @@
         )
         return made["later"][0]
 
-    works = [back_work(True, 0, v_a, gs_a), back_work(True, 1, v_a, gs_a), back_work(False, 0, v_b, gs_b), last_work]
+    works = [first_back, back_work(True, 1, v_a, gs_a), back_work(False, 0, v_b, gs_b), last_work]
     _, post_a = beyond(state_b, state_a, True, works, first_later)
     gv_b, gk_b, sums_b = made["later"]
     gq, sums_q = made["gq"]
-    gv_a, gk, heads, sums = call(
+    pack = st((-(-2 * taps // 8) * 8, ALL), F32)
+    gv_a, gk, sums = call(
         second_later_kernel,
-        [half_wide, flat, st((8, ALL), F32), st((taps + 1, ALL), F32)],
+        [half_wide, flat, pack],
         [wide, state_scratch, pltpu.VMEM((LANES, rows), F32)],
         (key_in, value_in, rim, *held(kt, fk_a, v_a), post_a,
          *held(back[0][0], back[1][0], back[0][2], back[1][2], gv_b, gk_b, sums_b, gq, sums_q, gain_a, gain_b)),
         2 * state_flops,
     )
-    follow = lax.ppermute(heads, "seq", [(i + 1, i) for i in range(count - 1)])
-    bit = 4
+    sums_next, bit = sums, 4
     while bit < count:
-        group = (bit, 2 * bit, 3 * bit) if 2 * bit < count else (bit,)
-        for got in [exchange(sums, distance) for distance in group]:
-            sums = sums + got
-        bit *= len(group) + 1
-    grad_query, grad_key, grad_value, output = call(
+        radix = 4 if 4 * bit <= count else 2
+        gots = [exchange(sums_next, bit * j) for j in range(1, radix)]
+        sums, sums_next = call(
+            functools.partial(combine_kernel, bit, radix, taps, bit * radix == count),
+            [pack, pack],
+            [],
+            (sums, sums_next, *gots),
+            rows,
+        )
+        bit *= radix
+    flat_narrow, wide_narrow = st((rows, LANES), BF16), st((rows, WIDE), BF16)
+    grads = call(
         signal_kernel,
-        [st((rows, LANES), BF16), st((rows, LANES), BF16), st((rows, WIDE), BF16), st((rows, WIDE), BF16)],
-        [pltpu.VMEM((rows + 8, DIM), F32)],
-        (*held(gq, gk, gv_a, gv_b), follow, *held(out_a, out_b), conv_query, conv_key, conv_value),
+        [flat_narrow, flat_narrow, wide_narrow],
+        [pltpu.VMEM((rows + 8, DIM), F32), pltpu.VMEM((rows, LANES), BF16), pltpu.VMEM((rows, LANES), BF16),
+         pltpu.VMEM((HEADS, rows, DIM), BF16), pltpu.SemaphoreType.DMA((HEADS + 2,))],
+        (*held(gq, gk, gv_a, gv_b), conv_query, conv_key, conv_value),
         2 * state_flops,
-        loose=(0, 1, 2, 3),
-    )
-    taps_query, taps_key, taps_value, taps_gain = call(
-        functools.partial(finish_kernel, total_rows ** (-0.5)),
-        [st((taps, LANES), F32), st((taps, LANES), F32), st((taps, WIDE), F32), st((1, WIDE), F32)],
-        [],
-        (tie(sums, grad_value), *[exchange(sums, distance) for distance in (1, 2, 3)]),
+        loose=(0, 1, 2),
+        out_specs=[apart] * 3,
+    )
+    gots = [exchange(sums_next if j == 3 else sums, j) for j in range(1, 4)]
+    grad_query, grad_key, grad_value, taps_query, taps_key, taps_value, taps_gain = call(
+        functools.partial(finish_kernel, total_rows ** (-0.5), count - 1),
+        [flat_narrow, flat_narrow, wide_narrow,
+         st((taps, LANES), F32), st((taps, LANES), F32), st((taps, WIDE), F32), st((1, WIDE), F32)],
+        [pltpu.VMEM((RIM + 8, DIM), F32), pltpu.VMEM((RIM, LANES), BF16), pltpu.VMEM((RIM, LANES), BF16),
+         pltpu.VMEM((RIM, WIDE), BF16), pltpu.SemaphoreType.DMA((3,))],
+        (sums, *gots, *held(gq, gk, gv_a, gv_b), conv_query, conv_key, conv_value, *[far(g) for g in grads]),
         rows,
-        loose=(0, 1, 2, 3),
+        loose=range(7),
+        in_specs=[near] * 11 + [apart] * 3,
+        out_specs=[apart] * 3 + [near] * 4,
+        input_output_aliases={11: 0, 12: 1, 13: 2},
     )
     return (
-        output,
+        made["out"],
         grad_query,
         grad_key,
         grad_value,

time: 71.5 us -> 74 us (1.035)
  waiting for transfers between devices: 11.5 us -> 14.1 us
  starting transfers between devices: 31 us -> 30 us
  Pallas kernels: 27.8 us -> 28.6 us
    ppermute x18, waiting for transfers between devices: 10.7 us -> 13.3 us  [exchange(): return lax.ppermute(x, 'seq', [(i, i ^ distance) for i in range(count)])]
    ppermute x1 -> x0, starting transfers between devices: 1.28 us -> none  [shards(): follow = lax.ppermute(heads, 'seq', [(i + 1, i) for i in range(count - 1)])]
    pallas_call x27 -> x28, Pallas kernels: 27.8 us -> 28.6 us  [call(): pl.pallas_call(kernel, out_shape=[o if i in loose else pltpu.VMEM(o.shape...]
  transfers between devices with their start and end apart: 20 -> 19, of which waited for: 9 -> 11; matrix products, arithmetic and copies ran while one was open for 0% -> 0% of each run, Pallas kernels for 33% -> 32%
where the time goes in v5:
time: 74 us; the launch traced here: 73.8 us
  starting transfers between devices  30 us (41%)
  Pallas kernels  28.6 us (39%)
  waiting for transfers between devices  14.1 us (19%)
  between operations  1.07 us (1%)
    pallas_call x28, Pallas kernels, call(): pl.pallas_call(kernel, out_shape=[o if i in loose else pltpu.VMEM(o.shape...  28.6 us
    ppermute x18, starting transfers between devices, exchange(): return lax.ppermute(x, 'seq', [(i, i ^ distance) for i in range(count)])  27.5 us
    ppermute x18, waiting for transfers between devices, exchange(): return lax.ppermute(x, 'seq', [(i, i ^ distance) for i in range(count)])  13.3 us
    ppermute x1, starting transfers between devices, shards(): rim = lax.ppermute(ends, 'seq', [(i, i + 1) for i in range(count - 1)])  2.49 us
  transfers between devices with their start and end apart: 19, of which 11 were waited for; matrix products, arithmetic and copies ran while one was open for 0% of the time, Pallas kernels for 32%

profile of v5, /device:TPU:0, one launch (start us, length us, event | category | flops | bytes accessed | tf_op | source)
XLA Modules:
  0.0 73.8 jit_solution(7763848136369783120)
XLA Ops:
  0.7 0.9 %shard_map.143 = bf16[16,1280]{1,0:T(8,128)(2,1)S(1)} custom-call(bf16[512,128]{1,0:T(8,128)(2,1)} %query.5, bf16[512,128]{1,0:T(8,128)(2,1)} %key.5, bf16[512,1024]{1,0:T(8,128)(2,1)} %value.9), custom_call_target="tpu_custom_call" | custom-call | flops 512 | bytes 1351680 | tf_op jit(solution)/shard_map/pallas_call | solution.py:438
  1.6 2.5 %collective-permute-start = (bf16[16,1280]{1,0:T(8,128)(2,1)S(1)}, bf16[16,1280]{1,0:T(8,128)(2,1)S(1)}, u32[]{:S(2)}, u32[]{:S(2)}) collective-permute-start(bf16[16,1280]{1,0:T(8,128)(2,1)S(1)} %shard_map.143), channel_id=1, source_target_pairs={{0,1},{1,2},{2,3},{3,4},{4,5},{5,6},{6,7},{7,8},{8,9},{9,10},{10,1... | collective-permute-start | bytes 122888 | tf_op jit(solution)/shard_map/ppermute | solution.py:561
  4.1 0.9 %collective-permute-done.rim = bf16[16,1280]{1,0:T(8,128)(2,1)S(1)} collective-permute-done((bf16[16,1280]{1,0:T(8,128)(2,1)S(1)}, bf16[16,1280]{1,0:T(8,128)(2,1)S(1)}, u32[]{:S(2)}, u32[]{:S(2)}) %collective-permute-start) | collective-permute-done | bytes 40992 | tf_op jit(solution)/shard_map/ppermute | solution.py:561
  5.0 0.9 %shard_map.145 = (bf16[512,128]{1,0:T(8,128)(2,1)S(1)}, bf16[128,512]{1,0:T(8,128)(2,1)S(1)}, bf16[512,512]{1,0:T(8,128)(2,1)S(1)}, bf16[4,160,512]{2,1,0:T(8,128)(2,1)S(1)}, bf16[4,160,128]{2,1,0:T(8,128)(2,1)S(1)}) custom-call(bf16[512,128]{1,0:T(8,128)(2,1)S(1)} %copy-done.2, bf16[512,1024]{1,0:T(8,128)(2,1)S(1)} %copy-done, ...), custom_call_target="tpu_custom_call" | custom-call | flops 83886080 | bytes 2840064 | tf_op jit(solution)/shard_map/pallas_call | solution.py:438
  5.9 2.9 %collective-permute-start.1 = (bf16[4,160,128]{2,1,0:T(8,128)(2,1)S(1)}, bf16[4,160,128]{2,1,0:T(8,128)(2,1)S(1)}, u32[]{:S(2)}, u32[]{:S(2)}) collective-permute-start(bf16[4,160,128]{2,1,0:T(8,128)(2,1)S(1)} %get-tuple-element.87), channel_id=1, source_target_pairs={{0,1},{1,0},{2,3},{3,2},{4,5},{5,4},{6,7},{7,6},{8,9},{9,8},{10,11... | collective-permute-start | bytes 491528 | tf_op jit(solution)/shard_map/ppermute | solution.py:450
  8.8 0.8 %shard_map.146 = (bf16[512,512]{1,0:T(8,128)(2,1)S(1)}, bf16[4,160,512]{2,1,0:T(8,128)(2,1)S(1)}, bf16[4,160,128]{2,1,0:T(8,128)(2,1)S(1)}) custom-call(bf16[128,512]{1,0:T(8,128)(2,1)S(1)} %get-tuple-element.83.kt.kt_ref, bf16[512,1024]{1,0:T(8,128)(2,1)S(1)} %copy-done, bf16[16,1280]{1,0:T(8,128)(2,1)S(1)} %collective-permute-done.rim, f32[3,1024]{1,0:T(4,128)S(1)} %copy-done.4), custom_call_target="tpu_custom_call" | custom-call | flops 83886080 | bytes 2576384 | tf_op jit(solution)/shard_map/pallas_call | solution.py:438
  9.6 0.2 collective-permute-done.1.near
  9.9 2.6 %collective-permute-start.2 = (bf16[2,160,128]{2,1,0:T(8,128)(2,1)S(1)}, bf16[2,160,128]{2,1,0:T(8,128)(2,1)S(1)}, u32[]{:S(2)}, u32[]{:S(2)}) collective-permute-start(bf16[2,160,128]{2,1,0:T(8,128)(2,1)S(1)} %get-tuple-element.89), channel_id=1, source_target_pairs={{0,2},{1,3},{2,0},{3,1},{4,6},{5,7},{6,4},{7,5},{8,10},{9,11},{10,... | collective-permute-start | bytes 245768 | tf_op jit(solution)/shard_map/ppermute | solution.py:450
  12.5 0.5 shard_map.144
  13.0 2.3 %shard_map.147.local = f32[512,512]{1,0:T(8,128)S(1)} custom-call(bf16[512,128]{1,0:T(8,128)(2,1)S(1)} %get-tuple-element.80.q_ref, bf16[512,128]{1,0:T(8,128)(2,1)S(1)} %get-tuple-element.81.k_ref, bf16[512,512]{1,0:T(8,128)(2,1)S(1)} %get-tuple-element.84.v_ref.v), custom_call_target="tpu_custom_call" | custom-call | flops 536870912 | bytes 1835008 | tf_op jit(solution)/shard_map/pallas_call | solution.py:438
  15.4 2.7 %collective-permute-start.3 = (bf16[2,160,128]{2,1,0:T(8,128)(2,1)S(1)}, bf16[2,160,128]{2,1,0:T(8,128)(2,1)S(1)}, u32[]{:S(2)}, u32[]{:S(2)}) collective-permute-start(bf16[2,160,128]{2,1,0:T(8,128)(2,1)S(1)} %shard_map.149), channel_id=1, source_target_pairs={{0,4},{1,5},{2,6},{3,7},{4,0},{5,1},{6,2},{7,3},{8,12},{9,13},{10,... | collective-permute-start | bytes 245768 | tf_op jit(solution)/shard_map/ppermute | solution.py:450
  18.1 2.3 %shard_map.151.local = f32[512,512]{1,0:T(8,128)S(1)} custom-call(bf16[512,128]{1,0:T(8,128)(2,1)S(1)} %get-tuple-element.80.q_ref, bf16[512,128]{1,0:T(8,128)(2,1)S(1)} %get-tuple-element.81.k_ref, bf16[512,512]{1,0:T(8,128)(2,1)S(1)} %get-tuple-element.91.v_ref.v), custom_call_target="tpu_custom_call" | custom-call | flops 536870912 | bytes 1835008 | tf_op jit(solution)/shard_map/pallas_call | solution.py:438
  20.4 0.1 collective-permute-done.3.refs_1_.rest_0_
  20.5 3.1 %collective-permute-start.4 = (bf16[2,160,128]{2,1,0:T(8,128)(2,1)S(1)}, bf16[2,160,128]{2,1,0:T(8,128)(2,1)S(1)}, u32[]{:S(2)}, u32[]{:S(2)}) collective-permute-start(bf16[2,160,128]{2,1,0:T(8,128)(2,1)S(1)} %shard_map.150), channel_id=1, source_target_pairs={{0,8},{1,9},{2,10},{3,11},{4,12},{5,13},{6,14},{7,15},{8,0},{9,1},... | collective-permute-start | bytes 245768 | tf_op jit(solution)/shard_map/ppermute | solution.py:450
  23.6 2.4 %collective-permute-done.4.rest_1_ = bf16[2,160,128]{2,1,0:T(8,128)(2,1)S(1)} collective-permute-done((bf16[2,160,128]{2,1,0:T(8,128)(2,1)S(1)}, bf16[2,160,128]{2,1,0:T(8,128)(2,1)S(1)}, u32[]{:S(2)}, u32[]{:S(2)}) %collective-permute-start.4) | collective-permute-done | bytes 81952 | tf_op jit(solution)/shard_map/ppermute | solution.py:450
  26.1 1.0 %collective-permute-start.5 = (bf16[2,160,128]{2,1,0:T(8,128)(2,1)S(1)}, bf16[2,160,128]{2,1,0:T(8,128)(2,1)S(1)}, u32[]{:S(2)}, u32[]{:S(2)}) collective-permute-start(bf16[2,160,128]{2,1,0:T(8,128)(2,1)S(1)} %get-tuple-element.94), channel_id=1, source_target_pairs={{0,2},{1,3},{2,0},{3,1},{4,6},{5,7},{6,4},{7,5},{8,10},{9,11},{10,... | collective-permute-start | bytes 245768 | tf_op jit(solution)/shard_map/ppermute | solution.py:450
  27.1 3.5 %collective-permute-done.5.other_part = bf16[2,160,128]{2,1,0:T(8,128)(2,1)S(1)} collective-permute-done((bf16[2,160,128]{2,1,0:T(8,128)(2,1)S(1)}, bf16[2,160,128]{2,1,0:T(8,128)(2,1)S(1)}, u32[]{:S(2)}, u32[]{:S(2)}) %collective-permute-start.5) | collective-permute-done | bytes 81952 | tf_op jit(solution)/shard_map/ppermute | solution.py:450
  30.6 0.1 shard_map.153
  30.7 0.1 collective-permute-start.6
  30.8 1.4 %shard_map.154 = (bf16[512,512]{1,0:T(8,128)(2,1)S(1)}, bf16[512,512]{1,0:T(8,128)(2,1)S(1)}, bf16[4,160,128]{2,1,0:T(8,128)(2,1)S(1)}, f32[4,128]{1,0:T(4,128)S(1)}) custom-call(f32[512,512]{1,0:T(8,128)S(1)} %shard_map.147.local, bf16[8,160,512]{2,1,0:T(8,128)(2,1)S(1)} %get-tuple-element.85.fq, bf16[4,160,128]{2,1,0:T(8,128)(2,1)S(1)} %get-tuple-element.95.prefix.pre_a, ...), custom_call_target="tpu_custom_call" | custom-call | flops 167772160 | bytes 4790272 | tf_op jit(solution)/shard_map/pallas_call | solution.py:438
  32.2 0.5 collective-permute-start.7
  32.7 1.5 %shard_map.155 = (bf16[512,1024]{1,0:T(8,128)(2,1)S(1)}, bf16[512,512]{1,0:T(8,128)(2,1)S(1)}, bf16[4,160,128]{2,1,0:T(8,128)(2,1)S(1)}, f32[4,128]{1,0:T(4,128)S(1)}) custom-call(f32[512,512]{1,0:T(8,128)S(1)} %shard_map.151.local, bf16[8,160,512]{2,1,0:T(8,128)(2,1)S(1)} %get-tuple-element.85.fq, ...), custom_call_target="tpu_custom_call" | custom-call | flops 167772160 | bytes 5838848 | tf_op jit(solution)/shard_map/pallas_call | solution.py:438
  34.3 1.0 %collective-permute-start.8 = (bf16[2,160,128]{2,1,0:T(8,128)(2,1)S(1)}, bf16[2,160,128]{2,1,0:T(8,128)(2,1)S(1)}, u32[]{:S(2)}, u32[]{:S(2)}) collective-permute-start(bf16[2,160,128]{2,1,0:T(8,128)(2,1)S(1)} %get-tuple-element.106), channel_id=1, source_target_pairs={{0,2},{1,3},{2,0},{3,1},{4,6},{5,7},{6,4},{7,5},{8,10},{9,11},{10,... | collective-permute-start | bytes 245768 | tf_op jit(solution)/shard_map/ppermute | solution.py:450
  35.3 3.1 %shard_map.156 = (f32[512,256]{1,0:T(8,128)S(1)}, f32[32,512]{1,0:T(8,128)S(1)}, f32[32,512]{1,0:T(8,128)S(1)}, bf16[512,1024]{1,0:T(8,128)(2,1)}) custom-call(bf16[512,128]{1,0:T(8,128)(2,1)S(1)} %get-tuple-element.80.q_ref, bf16[512,128]{1,0:T(8,128)(2,1)S(1)} %get-tuple-element.81.k_ref, bf16[128,512]{1,0:T(8,128)(2,1)S(1)} %get-tuple-element.82.qt_ref, ...), custom_call_target="tpu_custom_call" | custom-call | flops 536870912 | bytes 4325376 | tf_op jit(solution)/shard_map/pallas_call | solution.py:438
  38.4 0.3 collective-permute-done.8.refs_0_.got_y
  38.8 2.0 %collective-permute-start.9 = (bf16[2,160,128]{2,1,0:T(8,128)(2,1)S(1)}, bf16[2,160,128]{2,1,0:T(8,128)(2,1)S(1)}, u32[]{:S(2)}, u32[]{:S(2)}) collective-permute-start(bf16[2,160,128]{2,1,0:T(8,128)(2,1)S(1)} %shard_map.158), channel_id=1, source_target_pairs={{0,4},{1,5},{2,6},{3,7},{4,0},{5,1},{6,2},{7,3},{8,12},{9,13},{10,... | collective-permute-start | bytes 245768 | tf_op jit(solution)/shard_map/ppermute | solution.py:450
  40.8 2.5 %shard_map.160 = (f32[512,256]{1,0:T(8,128)S(1)}, f32[32,512]{1,0:T(8,128)S(1)}, f32[32,512]{1,0:T(8,128)S(1)}) custom-call(bf16[512,128]{1,0:T(8,128)(2,1)S(1)} %get-tuple-element.80.q_ref, bf16[512,128]{1,0:T(8,128)(2,1)S(1)} %get-tuple-element.81.k_ref, bf16[128,512]{1,0:T(8,128)(2,1)S(1)} %get-tuple-element.82.qt_ref, ...), custom_call_target="tpu_custom_call" | custom-call | flops 536870912 | bytes 2228224 | tf_op jit(solution)/shard_map/pallas_call | solution.py:438
  43.4 3.4 %collective-permute-start.10 = (bf16[2,160,128]{2,1,0:T(8,128)(2,1)S(1)}, bf16[2,160,128]{2,1,0:T(8,128)(2,1)S(1)}, u32[]{:S(2)}, u32[]{:S(2)}) collective-permute-start(bf16[2,160,128]{2,1,0:T(8,128)(2,1)S(1)} %shard_map.159), channel_id=1, source_target_pairs={{0,8},{1,9},{2,10},{3,11},{4,12},{5,13},{6,14},{7,15},{8,0},{9,1},... | collective-permute-start | bytes 245768 | tf_op jit(solution)/shard_map/ppermute | solution.py:450
  46.8 2.7 %shard_map.162 = (f32[512,256]{1,0:T(8,128)S(1)}, f32[32,512]{1,0:T(8,128)S(1)}, f32[32,512]{1,0:T(8,128)S(1)}) custom-call(bf16[512,128]{1,0:T(8,128)(2,1)S(1)} %get-tuple-element.80.q_ref, bf16[512,128]{1,0:T(8,128)(2,1)S(1)} %get-tuple-element.81.k_ref, bf16[128,512]{1,0:T(8,128)(2,1)S(1)} %get-tuple-element.82.qt_ref, ...), custom_call_target="tpu_custom_call" | custom-call | flops 536870912 | bytes 2228224 | tf_op jit(solution)/shard_map/pallas_call | solution.py:438
  49.5 0.1 shard_map.161
  49.6 1.1 %collective-permute-start.11 = (bf16[2,160,128]{2,1,0:T(8,128)(2,1)S(1)}, bf16[2,160,128]{2,1,0:T(8,128)(2,1)S(1)}, u32[]{:S(2)}, u32[]{:S(2)}) collective-permute-start(bf16[2,160,128]{2,1,0:T(8,128)(2,1)S(1)} %get-tuple-element.115), channel_id=1, source_target_pairs={{0,2},{1,3},{2,0},{3,1},{4,6},{5,7},{6,4},{7,5},{8,10},{9,11},{10,... | collective-permute-start | bytes 245768 | tf_op jit(solution)/shard_map/ppermute | solution.py:450
  50.7 2.5 %shard_map.164 = (f32[512,256]{1,0:T(8,128)S(1)}, f32[32,512]{1,0:T(8,128)S(1)}, f32[32,512]{1,0:T(8,128)S(1)}) custom-call(bf16[512,128]{1,0:T(8,128)(2,1)S(1)} %get-tuple-element.80.q_ref, bf16[512,128]{1,0:T(8,128)(2,1)S(1)} %get-tuple-element.81.k_ref, bf16[128,512]{1,0:T(8,128)(2,1)S(1)} %get-tuple-element.82.qt_ref, ...), custom_call_target="tpu_custom_call" | custom-call | flops 536870912 | bytes 2228224 | tf_op jit(solution)/shard_map/pallas_call | solution.py:438
  53.2 0.9 %shard_map.165 = (f32[512,128]{1,0:T(8,128)S(1)}, f32[3,128]{1,0:T(4,128)S(1)}) custom-call(bf16[512,128]{1,0:T(8,128)(2,1)S(1)} %copy-done.3, bf16[16,1280]{1,0:T(8,128)(2,1)S(1)} %collective-permute-done.rim, bf16[128,512]{1,0:T(8,128)(2,1)S(1)} %get-tuple-element.82.qt_ref, bf16[512,512]{1,0:T(8,128)(2,1)S(1)} %get-tuple-element.96.gs_ref.gs_a, ...), custom_call_target="tpu_custom_call" | custom-call | flops 83886080 | bytes 2206720 | tf_op jit(solution)/shard_map/pallas_call | solution.py:438
  54.1 0.1 shard_map.163
  54.2 0.1 collective-permute-start.12
  54.3 1.1 %shard_map.166 = (f32[512,512]{1,0:T(8,128)S(1)}, f32[64,512]{1,0:T(8,128)S(1)}, f32[3,512]{1,0:T(4,128)S(1)}) custom-call(bf16[512,1024]{1,0:T(8,128)(2,1)S(1)} %copy-done, bf16[16,1280]{1,0:T(8,128)(2,1)S(1)} %collective-permute-done.rim, bf16[128,512]{1,0:T(8,128)(2,1)S(1)} %get-tuple-element.83.kt.kt_ref, ...), custom_call_target="tpu_custom_call" | custom-call | flops 167772160 | bytes 4929536 | tf_op jit(solution)/shard_map/pallas_call | solution.py:438
  55.4 0.2 collective-permute-done.12.state
  55.7 1.1 %shard_map.167 = (f32[512,512]{1,0:T(8,128)S(1)}, f32[512,128]{1,0:T(8,128)S(1)}, f32[8,1280]{1,0:T(8,128)S(1)}) custom-call(bf16[512,128]{1,0:T(8,128)(2,1)S(1)} %copy-done.2, bf16[512,1024]{1,0:T(8,128)(2,1)S(1)} %copy-done, bf16[16,1280]{1,0:T(8,128)(2,1)S(1)} %collective-permute-done.rim, bf16[128,512]{1,0:T(8,128)(2,1)S(1)} %get-tuple-element.83.kt.kt_ref, ...), custom_call_target="tpu_custom_call" | custom-call | flops 167772160 | bytes 6680064 | tf_op jit(solution)/shard_map/pallas_call | solution.py:438
  56.8 1.9 %collective-permute-start.13 = (f32[8,1280]{1,0:T(8,128)S(1)}, f32[8,1280]{1,0:T(8,128)S(1)}, u32[]{:S(2)}, u32[]{:S(2)}) collective-permute-start(f32[8,1280]{1,0:T(8,128)S(1)} %get-tuple-element.137.with_own.with_next), channel_id=1, source_target_pairs={{0,4},{1,5},{2,6},{3,7},{4,0},{5,1},{6,2},{7,3},{8,12},{9,13},{10,... | collective-permute-start | bytes 122888 | tf_op jit(solution)/shard_map/ppermute | solution.py:450
  58.7 3.1 %collective-permute-start.14 = (f32[8,1280]{1,0:T(8,128)S(1)}, f32[8,1280]{1,0:T(8,128)S(1)}, u32[]{:S(2)}, u32[]{:S(2)}) collective-permute-start(f32[8,1280]{1,0:T(8,128)S(1)} %get-tuple-element.137.with_own.with_next), channel_id=1, source_target_pairs={{0,8},{1,9},{2,10},{3,11},{4,12},{5,13},{6,14},{7,15},{8,0},{9,1},... | collective-permute-start | bytes 122888 | tf_op jit(solution)/shard_map/ppermute | solution.py:450
  61.8 2.8 %collective-permute-done.14.refs_1_ = f32[8,1280]{1,0:T(8,128)S(1)} collective-permute-done((f32[8,1280]{1,0:T(8,128)S(1)}, f32[8,1280]{1,0:T(8,128)S(1)}, u32[]{:S(2)}, u32[]{:S(2)}) %collective-permute-start.14) | collective-permute-done | bytes 40992 | tf_op jit(solution)/shard_map/ppermute | solution.py:450
  64.7 2.9 %collective-permute-done.15.refs_2_ = f32[8,1280]{1,0:T(8,128)S(1)} collective-permute-done((f32[8,1280]{1,0:T(8,128)S(1)}, f32[8,1280]{1,0:T(8,128)S(1)}, u32[]{:S(2)}, u32[]{:S(2)}) %collective-permute-start.15) | collective-permute-done | bytes 40992 | tf_op jit(solution)/shard_map/ppermute | solution.py:450
  67.6 0.1 collective-permute-start.16
  67.7 1.1 %collective-permute-start.17 = (f32[8,1280]{1,0:T(8,128)S(1)}, f32[8,1280]{1,0:T(8,128)S(1)}, u32[]{:S(2)}, u32[]{:S(2)}) collective-permute-start(f32[8,1280]{1,0:T(8,128)S(1)} %get-tuple-element.138.sums), channel_id=1, source_target_pairs={{0,2},{1,3},{2,0},{3,1},{4,6},{5,7},{6,4},{7,5},{8,10},{9,11},{10,... | collective-permute-start | bytes 122888 | tf_op jit(solution)/shard_map/ppermute | solution.py:450
  68.8 0.8 %collective-permute-start.18 = (f32[8,1280]{1,0:T(8,128)S(1)}, f32[8,1280]{1,0:T(8,128)S(1)}, u32[]{:S(2)}, u32[]{:S(2)}) collective-permute-start(f32[8,1280]{1,0:T(8,128)S(1)} %get-tuple-element.139), channel_id=1, source_target_pairs={{0,3},{1,2},{2,1},{3,0},{4,7},{5,6},{6,5},{7,4},{8,11},{9,10},{10,... | collective-permute-start | bytes 122888 | tf_op jit(solution)/shard_map/ppermute | solution.py:450
  69.6 2.1 %shard_map.169 = (bf16[512,128]{1,0:T(8,128)(2,1)}, bf16[512,128]{1,0:T(8,128)(2,1)}, bf16[512,1024]{1,0:T(8,128)(2,1)}) custom-call(f32[512,128]{1,0:T(8,128)S(1)} %get-tuple-element.122.gq, f32[512,128]{1,0:T(8,128)S(1)} %get-tuple-element.140.gk, f32[512,512]{1,0:T(8,128)S(1)} %get-tuple-element.141.gv_a, f32[512,512]{1,0:T(8,128)S(1)} %get-tuple-element.128.gv_b, ...), custom_call_target="tpu_custom_call" | custom-call | flops 167772160 | bytes 3947520 | tf_op jit(solution)/shard_map/pallas_call | solution.py:438
  71.8 0.5 collective-permute-done.18.got_3
  72.3 1.3 %shard_map.170 = (bf16[512,128]{1,0:T(8,128)(2,1)}, bf16[512,128]{1,0:T(8,128)(2,1)}, bf16[512,1024]{1,0:T(8,128)(2,1)}, f32[3,128]{1,0:T(4,128)}, f32[3,128]{1,...) custom-call(f32[8,1280]{1,0:T(8,128)S(1)} %get-tuple-element.138.sum, ...), custom_call_target="tpu_custom_call", output_to_operand_aliasing={{0}: (11, {}), {1}: (12, {}), {2}: (13, {})} | custom-call | flops 512 | bytes 5441536 | tf_op jit(solution)/shard_map/pallas_call | solution.py:438
  (34 shorter events, 0.4 us)
Async XLA Ops:
  0.6 4.3 %copy-start.2 = (bf16[512,128]{1,0:T(8,128)(2,1)S(1)}, bf16[512,128]{1,0:T(8,128)(2,1)}, u32[]{:S(2)}) copy-start(bf16[512,128]{1,0:T(8,128)(2,1)} %key.5) | copy-start | bytes 393220
  0.6 4.3 %copy-start = (bf16[512,1024]{1,0:T(8,128)(2,1)S(1)}, bf16[512,1024]{1,0:T(8,128)(2,1)}, u32[]{:S(2)}) copy-start(bf16[512,1024]{1,0:T(8,128)(2,1)} %value.9) | copy-start | bytes 3145732
  0.7 4.3 %copy-start.6 = (f32[3,128]{1,0:T(4,128)S(1)}, f32[3,128]{1,0:T(4,128)}, u32[]{:S(2)}) copy-start(f32[3,128]{1,0:T(4,128)} %taps_k.5) | copy-start | bytes 4612
  0.7 4.3 %copy-start.4 = (f32[3,1024]{1,0:T(4,128)S(1)}, f32[3,1024]{1,0:T(4,128)}, u32[]{:S(2)}) copy-start(f32[3,1024]{1,0:T(4,128)} %taps_v.7) | copy-start | bytes 36868
  1.6 10.9 %copy-start.3 = (bf16[512,128]{1,0:T(8,128)(2,1)S(1)}, bf16[512,128]{1,0:T(8,128)(2,1)}, u32[]{:S(2)}) copy-start(bf16[512,128]{1,0:T(8,128)(2,1)} %query.5) | copy-start | bytes 393220
  1.6 10.9 %copy-start.5 = (f32[3,128]{1,0:T(4,128)S(1)}, f32[3,128]{1,0:T(4,128)}, u32[]{:S(2)}) copy-start(f32[3,128]{1,0:T(4,128)} %taps_q.7) | copy-start | bytes 4612
  1.6 3.3 %collective-permute-start = (bf16[16,1280]{1,0:T(8,128)(2,1)S(1)}, bf16[16,1280]{1,0:T(8,128)(2,1)S(1)}, u32[]{:S(2)}, u32[]{:S(2)}) collective-permute-start(bf16[16,1280]{1,0:T(8,128)(2,1)S(1)} %shard_map.143), channel_id=1, source_target_pairs={{0,1},{1,2},{2,3},{3,4},{4,5},{5,6},{6,7},{7,8},{8,9},{9,10},{10,1... | collective-permute-start | bytes 122888 | tf_op jit(solution)/shard_map/ppermute | solution.py:561
  5.9 4.0 %collective-permute-start.1 = (bf16[4,160,128]{2,1,0:T(8,128)(2,1)S(1)}, bf16[4,160,128]{2,1,0:T(8,128)(2,1)S(1)}, u32[]{:S(2)}, u32[]{:S(2)}) collective-permute-start(bf16[4,160,128]{2,1,0:T(8,128)(2,1)S(1)} %get-tuple-element.87), channel_id=1, source_target_pairs={{0,1},{1,0},{2,3},{3,2},{4,5},{5,4},{6,7},{7,6},{8,9},{9,8},{10,11... | collective-permute-start | bytes 491528 | tf_op jit(solution)/shard_map/ppermute | solution.py:450
  9.9 5.4 %collective-permute-start.2 = (bf16[2,160,128]{2,1,0:T(8,128)(2,1)S(1)}, bf16[2,160,128]{2,1,0:T(8,128)(2,1)S(1)}, u32[]{:S(2)}, u32[]{:S(2)}) collective-permute-start(bf16[2,160,128]{2,1,0:T(8,128)(2,1)S(1)} %get-tuple-element.89), channel_id=1, source_target_pairs={{0,2},{1,3},{2,0},{3,1},{4,6},{5,7},{6,4},{7,5},{8,10},{9,11},{10,... | collective-permute-start | bytes 245768 | tf_op jit(solution)/shard_map/ppermute | solution.py:450
  15.4 5.1 %collective-permute-start.3 = (bf16[2,160,128]{2,1,0:T(8,128)(2,1)S(1)}, bf16[2,160,128]{2,1,0:T(8,128)(2,1)S(1)}, u32[]{:S(2)}, u32[]{:S(2)}) collective-permute-start(bf16[2,160,128]{2,1,0:T(8,128)(2,1)S(1)} %shard_map.149), channel_id=1, source_target_pairs={{0,4},{1,5},{2,6},{3,7},{4,0},{5,1},{6,2},{7,3},{8,12},{9,13},{10,... | collective-permute-start | bytes 245768 | tf_op jit(solution)/shard_map/ppermute | solution.py:450
  18.1 12.7 %copy-start.1 = (bf16[512,1024]{1,0:T(8,128)(2,1)S(1)}, bf16[512,1024]{1,0:T(8,128)(2,1)}, u32[]{:S(2)}) copy-start(bf16[512,1024]{1,0:T(8,128)(2,1)} %grad.3) | copy-start | bytes 3145732
  18.1 12.7 %copy-start.7 = (f32[1024]{0:T(1024)S(1)}, f32[1024]{0:T(1024)}, u32[]{:S(2)}) copy-start(f32[1024]{0:T(1024)} %param.14) | copy-start | bytes 12292
  20.5 5.5 %collective-permute-start.4 = (bf16[2,160,128]{2,1,0:T(8,128)(2,1)S(1)}, bf16[2,160,128]{2,1,0:T(8,128)(2,1)S(1)}, u32[]{:S(2)}, u32[]{:S(2)}) collective-permute-start(bf16[2,160,128]{2,1,0:T(8,128)(2,1)S(1)} %shard_map.150), channel_id=1, source_target_pairs={{0,8},{1,9},{2,10},{3,11},{4,12},{5,13},{6,14},{7,15},{8,0},{9,1},... | collective-permute-start | bytes 245768 | tf_op jit(solution)/shard_map/ppermute | solution.py:450
  26.1 4.5 %collective-permute-start.5 = (bf16[2,160,128]{2,1,0:T(8,128)(2,1)S(1)}, bf16[2,160,128]{2,1,0:T(8,128)(2,1)S(1)}, u32[]{:S(2)}, u32[]{:S(2)}) collective-permute-start(bf16[2,160,128]{2,1,0:T(8,128)(2,1)S(1)} %get-tuple-element.94), channel_id=1, source_target_pairs={{0,2},{1,3},{2,0},{3,1},{4,6},{5,7},{6,4},{7,5},{8,10},{9,11},{10,... | collective-permute-start | bytes 245768 | tf_op jit(solution)/shard_map/ppermute | solution.py:450
  30.7 2.0 %collective-permute-start.6 = (bf16[4,160,128]{2,1,0:T(8,128)(2,1)S(1)}, bf16[4,160,128]{2,1,0:T(8,128)(2,1)S(1)}, u32[]{:S(2)}, u32[]{:S(2)}) collective-permute-start(bf16[4,160,128]{2,1,0:T(8,128)(2,1)S(1)} %get-tuple-element.97), channel_id=1, source_target_pairs={{0,1},{1,0},{2,3},{3,2},{4,5},{5,4},{6,7},{7,6},{8,9},{9,8},{10,11... | collective-permute-start | bytes 491528 | tf_op jit(solution)/shard_map/ppermute | solution.py:450
  32.2 2.0 %collective-permute-start.7 = (bf16[4,160,128]{2,1,0:T(8,128)(2,1)S(1)}, bf16[4,160,128]{2,1,0:T(8,128)(2,1)S(1)}, u32[]{:S(2)}, u32[]{:S(2)}) collective-permute-start(bf16[4,160,128]{2,1,0:T(8,128)(2,1)S(1)} %get-tuple-element.104), channel_id=1, source_target_pairs={{0,1},{1,0},{2,3},{3,2},{4,5},{5,4},{6,7},{7,6},{8,9},{9,8},{10,11... | collective-permute-start | bytes 491528 | tf_op jit(solution)/shard_map/ppermute | solution.py:450
  34.3 4.5 %collective-permute-start.8 = (bf16[2,160,128]{2,1,0:T(8,128)(2,1)S(1)}, bf16[2,160,128]{2,1,0:T(8,128)(2,1)S(1)}, u32[]{:S(2)}, u32[]{:S(2)}) collective-permute-start(bf16[2,160,128]{2,1,0:T(8,128)(2,1)S(1)} %get-tuple-element.106), channel_id=1, source_target_pairs={{0,2},{1,3},{2,0},{3,1},{4,6},{5,7},{6,4},{7,5},{8,10},{9,11},{10,... | collective-permute-start | bytes 245768 | tf_op jit(solution)/shard_map/ppermute | solution.py:450
  38.8 4.5 %collective-permute-start.9 = (bf16[2,160,128]{2,1,0:T(8,128)(2,1)S(1)}, bf16[2,160,128]{2,1,0:T(8,128)(2,1)S(1)}, u32[]{:S(2)}, u32[]{:S(2)}) collective-permute-start(bf16[2,160,128]{2,1,0:T(8,128)(2,1)S(1)} %shard_map.158), channel_id=1, source_target_pairs={{0,4},{1,5},{2,6},{3,7},{4,0},{5,1},{6,2},{7,3},{8,12},{9,13},{10,... | collective-permute-start | bytes 245768 | tf_op jit(solution)/shard_map/ppermute | solution.py:450
  43.4 6.1 %collective-permute-start.10 = (bf16[2,160,128]{2,1,0:T(8,128)(2,1)S(1)}, bf16[2,160,128]{2,1,0:T(8,128)(2,1)S(1)}, u32[]{:S(2)}, u32[]{:S(2)}) collective-permute-start(bf16[2,160,128]{2,1,0:T(8,128)(2,1)S(1)} %shard_map.159), channel_id=1, source_target_pairs={{0,8},{1,9},{2,10},{3,11},{4,12},{5,13},{6,14},{7,15},{8,0},{9,1},... | collective-permute-start | bytes 245768 | tf_op jit(solution)/shard_map/ppermute | solution.py:450
  49.6 4.5 %collective-permute-start.11 = (bf16[2,160,128]{2,1,0:T(8,128)(2,1)S(1)}, bf16[2,160,128]{2,1,0:T(8,128)(2,1)S(1)}, u32[]{:S(2)}, u32[]{:S(2)}) collective-permute-start(bf16[2,160,128]{2,1,0:T(8,128)(2,1)S(1)} %get-tuple-element.115), channel_id=1, source_target_pairs={{0,2},{1,3},{2,0},{3,1},{4,6},{5,7},{6,4},{7,5},{8,10},{9,11},{10,... | collective-permute-start | bytes 245768 | tf_op jit(solution)/shard_map/ppermute | solution.py:450
  54.2 1.5 %collective-permute-start.12 = (bf16[4,160,128]{2,1,0:T(8,128)(2,1)S(1)}, bf16[4,160,128]{2,1,0:T(8,128)(2,1)S(1)}, u32[]{:S(2)}, u32[]{:S(2)}) collective-permute-start(bf16[4,160,128]{2,1,0:T(8,128)(2,1)S(1)} %get-tuple-element.123), channel_id=1, source_target_pairs={{0,1},{1,0},{2,3},{3,2},{4,5},{5,4},{6,7},{7,6},{8,9},{9,8},{10,11... | collective-permute-start | bytes 491528 | tf_op jit(solution)/shard_map/ppermute | solution.py:450
  56.8 5.0 %collective-permute-start.13 = (f32[8,1280]{1,0:T(8,128)S(1)}, f32[8,1280]{1,0:T(8,128)S(1)}, u32[]{:S(2)}, u32[]{:S(2)}) collective-permute-start(f32[8,1280]{1,0:T(8,128)S(1)} %get-tuple-element.137.with_own.with_next), channel_id=1, source_target_pairs={{0,4},{1,5},{2,6},{3,7},{4,0},{5,1},{6,2},{7,3},{8,12},{9,13},{10,... | collective-permute-start | bytes 122888 | tf_op jit(solution)/shard_map/ppermute | solution.py:450
  58.7 5.9 %collective-permute-start.14 = (f32[8,1280]{1,0:T(8,128)S(1)}, f32[8,1280]{1,0:T(8,128)S(1)}, u32[]{:S(2)}, u32[]{:S(2)}) collective-permute-start(f32[8,1280]{1,0:T(8,128)S(1)} %get-tuple-element.137.with_own.with_next), channel_id=1, source_target_pairs={{0,8},{1,9},{2,10},{3,11},{4,12},{5,13},{6,14},{7,15},{8,0},{9,1},... | collective-permute-start | bytes 122888 | tf_op jit(solution)/shard_map/ppermute | solution.py:450
  61.8 5.8 %collective-permute-start.15 = (f32[8,1280]{1,0:T(8,128)S(1)}, f32[8,1280]{1,0:T(8,128)S(1)}, u32[]{:S(2)}, u32[]{:S(2)}) collective-permute-start(f32[8,1280]{1,0:T(8,128)S(1)} %get-tuple-element.137.with_own.with_next), channel_id=1, source_target_pairs={{0,12},{1,13},{2,14},{3,15},{4,8},{5,9},{6,10},{7,11},{8,4},{9,5},... | collective-permute-start | bytes 122888 | tf_op jit(solution)/shard_map/ppermute | solution.py:450
  67.6 4.1 %collective-permute-start.16 = (f32[8,1280]{1,0:T(8,128)S(1)}, f32[8,1280]{1,0:T(8,128)S(1)}, u32[]{:S(2)}, u32[]{:S(2)}) collective-permute-start(f32[8,1280]{1,0:T(8,128)S(1)} %get-tuple-element.138.sums), channel_id=1, source_target_pairs={{0,1},{1,0},{2,3},{3,2},{4,5},{5,4},{6,7},{7,6},{8,9},{9,8},{10,11... | collective-permute-start | bytes 122888 | tf_op jit(solution)/shard_map/ppermute | solution.py:450
  67.7 4.1 %collective-permute-start.17 = (f32[8,1280]{1,0:T(8,128)S(1)}, f32[8,1280]{1,0:T(8,128)S(1)}, u32[]{:S(2)}, u32[]{:S(2)}) collective-permute-start(f32[8,1280]{1,0:T(8,128)S(1)} %get-tuple-element.138.sums), channel_id=1, source_target_pairs={{0,2},{1,3},{2,0},{3,1},{4,6},{5,7},{6,4},{7,5},{8,10},{9,11},{10,... | collective-permute-start | bytes 122888 | tf_op jit(solution)/shard_map/ppermute | solution.py:450
  68.8 3.5 %collective-permute-start.18 = (f32[8,1280]{1,0:T(8,128)S(1)}, f32[8,1280]{1,0:T(8,128)S(1)}, u32[]{:S(2)}, u32[]{:S(2)}) collective-permute-start(f32[8,1280]{1,0:T(8,128)S(1)} %get-tuple-element.139), channel_id=1, source_target_pairs={{0,3},{1,2},{2,1},{3,0},{4,7},{5,6},{6,5},{7,4},{8,11},{9,10},{10,... | collective-permute-start | bytes 122888 | tf_op jit(solution)/shard_map/ppermute | solution.py:450

commit v6 on v4

--- a/solution.py
+++ b/solution.py
@@ -84,12 +84,8 @@
 
 
 def half_index(own):
-    here, parity, bit = lax.axis_index("seq"), 0, 1
-    while bit < lax.axis_size("seq"):
-        parity = parity + lax.rem(lax.div(here, bit), 2)
-        bit *= 2
-    parity = lax.rem(parity, 2)
-    return parity if own else 1 - parity
+    core = lax.rem(lax.axis_index("seq"), 2)
+    return core if own else 1 - core
 
 
 def rows_of(half, g):
@@ -180,9 +176,13 @@
             out[start:stop, head_lanes(g)] = dot(w.astype(BF16), v_ref[0:stop, head_lanes(g)], NN)
 
 
-def norm_kernel(own, local, fq, prefix, grad, gain, out, gs_out, state_out, gain_out, pre, summed_ref):
+def norm_kernel(own, local, fq, prefix, grad, gain, *refs):
+    *others, out, gs_out, state_out, gain_out, pre, summed_ref = refs
     half = half_index(own)
     doubled(prefix, pre)
+    for other in others:
+        for g in range(HALF):
+            out[:, lanes_of(1 - half, g)] = other[:, head_lanes(g)]
     for g in range(HALF):
         place = head_lanes(g)
         summed_ref[:, place] = local[:, place] + dot(fq[half * HALF + g], pre[g], TN)
@@ -192,7 +192,7 @@
         scale = lax.rsqrt(jnp.mean(summed * summed, axis=-1, keepdims=True) + EPSILON)
         normal = summed * scale
         weight = gain[pl.ds(half * HALF + g, 1)]
-        out[:, place] = (normal * weight).astype(BF16)
+        out[:, place if own else lanes_of(half, g)] = (normal * weight).astype(BF16)
         incoming = grad[:, lanes_of(half, g)].astype(F32)
         gain_out[g : g + 1] = jnp.sum(incoming * normal, axis=0, keepdims=True)
         upstream = incoming * weight
@@ -200,6 +200,13 @@
         gs = gs.astype(BF16)
         gs_out[:, place] = gs
         state_out[g] = dot(fq[half * HALF + g], gs, NN).astype(BF16)
+
+
+def first_back_kernel(q_ref, k_ref, qt_ref, kt_ref, v_ref, gs_ref, tokens, gv_out, gq_out, gk_out, out, sem):
+    copy = pltpu.make_async_copy(tokens, out, sem)
+    copy.start()
+    back_kernel(True, 0, q_ref, k_ref, qt_ref, kt_ref, v_ref, gs_ref, gv_out, gq_out, gk_out)
+    copy.wait()
 
 
 def back_kernel(own, part, q_ref, k_ref, qt_ref, kt_ref, v_ref, gs_ref, gv_out, gq_out, gk_out):
@@ -309,18 +316,6 @@
             head_out[:, lanes_of(half, g, 2 * LANES)] = gv[0:8, head_lanes(g)]
 
 
-def token_kernel(out_a, out_b, out, sems):
-    copies = []
-    for i, (own, tokens) in enumerate(((True, out_a), (False, out_b))):
-        width = tokens.shape[1]
-        place = pl.ds(pl.multiple_of(half_index(own) * width, width), width)
-        copies.append(pltpu.make_async_copy(tokens, out.at[:, place], sems.at[i]))
-    for copy in copies:
-        copy.start()
-    for copy in copies:
-        copy.wait()
-
-
 def signal_kernel(
     gq, gk, gv_a, gv_b, follow, taps_q, taps_k, taps_v, q_out, k_out, v_out, wide, q_part, k_part, v_part, sems
 ):
@@ -459,17 +454,17 @@
 
     near = exchange(send, 1)
     part, their = call(pair_kernel, [wide, narrow], [], (keep, near), cost)
-    got_y = exchange(their, 3)
+    got_y = exchange(their, 2)
     gots = []
     bit = 4
     while bit < count:
         send = call(step_kernel, [narrow], [], (part, got_y, *gots), cost)[0]
-        gots.append(exchange(under(send), bit + 1))
+        gots.append(exchange(under(send), bit))
         bit *= 2
     own_part, give_part = call(
         functools.partial(part_kernel, reverse), [wide, narrow], [], (part, got_y, *gots), cost
     )
-    other_part = exchange(under(give_part), 3)
+    other_part = exchange(under(give_part), 2)
     own, give = call(
         functools.partial(merge_kernel, reverse), [st(whole, BF16)] * 2, [], (own_part, other_part, keep, near), cost
     )
@@ -494,6 +489,7 @@
     square_flops = 2 * HALF * rows * rows * DIM
 
     apart = pl.BlockSpec(memory_space=pltpu.HBM)
+    near = pl.BlockSpec(memory_space=pltpu.VMEM)
     ends = call(
         end_kernel,
         [st((RIM, ALL), BF16)],
@@ -541,12 +537,12 @@
 
         return work
 
-    def norm(own, prefix):
+    def norm(own, prefix, *others):
         return call(
             functools.partial(norm_kernel, own),
-            [half_narrow, half_narrow, half_state, st((HALF, DIM), F32)],
+            [half_narrow if own else st((rows, WIDE), BF16), half_narrow, half_state, st((HALF, DIM), F32)],
             [state_scratch, pltpu.VMEM((rows, half_width), F32)],
-            (*held(made[own], made["q"][2]), prefix, grad_out, gain),
+            (*held(made[own], made["q"][2]), prefix, grad_out, gain, *held(*others)),
             2 * state_flops,
         )
 
@@ -559,20 +555,22 @@
     )
     q, qt, fq = made["q"]
     out_a, gs_a, state_a, gain_a = made["norm"]
-    out_b, gs_b, state_b, gain_b = norm(False, pre_b)
+    tokens, gs_b, state_b, gain_b = norm(False, pre_b, out_a)
     back = []
 
     def first_back():
-        made["out"] = call(
-            token_kernel,
-            [st((rows, WIDE), BF16)],
-            [pltpu.SemaphoreType.DMA((2,))],
-            held(out_a, out_b),
-            rows,
-            loose=(0,),
-            out_specs=[apart],
-        )[0]
-        return (*back_work(True, 0, v_a, gs_a)(), made["out"])
+        *parts, made["out"] = call(
+            first_back_kernel,
+            [st((rows, PART * DIM), F32), st((PART * FEAT, rows), F32), st((PART * FEAT, rows), F32),
+             st((rows, WIDE), BF16)],
+            [pltpu.SemaphoreType.DMA],
+            held(q, k, qt, kt, v_a, gs_a, tokens),
+            2 * square_flops,
+            loose=(3,),
+            out_specs=[near] * 3 + [apart],
+        )
+        back.append(parts)
+        return (parts[0],)
 
     def back_work(own, part, v, gs):
         def work():
@@ -625,7 +623,7 @@
     follow = lax.ppermute(heads, "seq", [(i + 1, i) for i in range(count - 1)])
     bit = 4
     while bit < count:
-        group = (bit + 1, 2 * bit + 1, 3 * bit) if 2 * bit < count else (bit + 1,)
+        group = (bit, 2 * bit, 3 * bit) if 2 * bit < count else (bit,)
         for got in [exchange(sums, distance) for distance in group]:
             sums = sums + got
         bit *= len(group) + 1

time: 72.8 us -> 71 us (0.975)
  starting transfers between devices: 33.4 us -> 31.4 us
    ppermute x18, starting transfers between devices: 29.7 us -> 27.6 us  [exchange(): return lax.ppermute(x, 'seq', [(i, i ^ distance) for i in range(count)])]
    pallas_call x28 -> x27, Pallas kernels: 28.1 us -> 27.7 us  [call(): pl.pallas_call(kernel, out_shape=[o if i in loose else pltpu.VMEM(o.shape...]
  transfers between devices with their start and end apart: 20 -> 20, of which waited for: 10 -> 9; matrix products, arithmetic and copies ran while one was open for 0% -> 0% of each run, Pallas kernels for 33% -> 33%
where the time goes in v6:
time: 71 us; the launch traced here: 70.9 us
  starting transfers between devices  31.4 us (44%)
  Pallas kernels  27.7 us (39%)
  waiting for transfers between devices  10.8 us (15%)
  between operations  0.93 us (1%)
    pallas_call x27, Pallas kernels, call(): pl.pallas_call(kernel, out_shape=[o if i in loose else pltpu.VMEM(o.shape...  27.7 us
    ppermute x18, starting transfers between devices, exchange(): return lax.ppermute(x, 'seq', [(i, i ^ distance) for i in range(count)])  27.6 us
    ppermute x18, waiting for transfers between devices, exchange(): return lax.ppermute(x, 'seq', [(i, i ^ distance) for i in range(count)])  9.95 us
    ppermute x1, starting transfers between devices, shards(): rim = lax.ppermute(ends, 'seq', [(i, i + 1) for i in range(count - 1)])  2.49 us
  transfers between devices with their start and end apart: 20, of which 9 were waited for; matrix products, arithmetic and copies ran while one was open for 0% of the time, Pallas kernels for 33%

profile of v6, /device:TPU:0, one launch (start us, length us, event | category | flops | bytes accessed | tf_op | source)
XLA Modules:
  0.0 70.9 jit_solution(6994058034884600814)
XLA Ops:
  0.7 0.9 %shard_map.143 = bf16[16,1280]{1,0:T(8,128)(2,1)S(1)} custom-call(bf16[512,128]{1,0:T(8,128)(2,1)} %query.5, bf16[512,128]{1,0:T(8,128)(2,1)} %key.5, bf16[512,1024]{1,0:T(8,128)(2,1)} %value.9), custom_call_target="tpu_custom_call" | custom-call | flops 512 | bytes 1351680 | tf_op jit(solution)/shard_map/pallas_call | solution.py:378
  1.6 2.5 %collective-permute-start = (bf16[16,1280]{1,0:T(8,128)(2,1)S(1)}, bf16[16,1280]{1,0:T(8,128)(2,1)S(1)}, u32[]{:S(2)}, u32[]{:S(2)}) collective-permute-start(bf16[16,1280]{1,0:T(8,128)(2,1)S(1)} %shard_map.143), channel_id=1, source_target_pairs={{0,1},{1,2},{2,3},{3,4},{4,5},{5,6},{6,7},{7,8},{8,9},{9,10},{10,1... | collective-permute-start | bytes 122888 | tf_op jit(solution)/shard_map/ppermute | solution.py:501
  4.1 0.9 %collective-permute-done.rim = bf16[16,1280]{1,0:T(8,128)(2,1)S(1)} collective-permute-done((bf16[16,1280]{1,0:T(8,128)(2,1)S(1)}, bf16[16,1280]{1,0:T(8,128)(2,1)S(1)}, u32[]{:S(2)}, u32[]{:S(2)}) %collective-permute-start) | collective-permute-done | bytes 40992 | tf_op jit(solution)/shard_map/ppermute | solution.py:501
  5.0 0.9 %shard_map.145 = (bf16[512,128]{1,0:T(8,128)(2,1)S(1)}, bf16[128,512]{1,0:T(8,128)(2,1)S(1)}, bf16[512,512]{1,0:T(8,128)(2,1)S(1)}, bf16[4,160,512]{2,1,0:T(8,128)(2,1)S(1)}, bf16[4,160,128]{2,1,0:T(8,128)(2,1)S(1)}) custom-call(bf16[512,128]{1,0:T(8,128)(2,1)S(1)} %copy-done.2, bf16[512,1024]{1,0:T(8,128)(2,1)S(1)} %copy-done, ...), custom_call_target="tpu_custom_call" | custom-call | flops 83886080 | bytes 2840064 | tf_op jit(solution)/shard_map/pallas_call | solution.py:378
  5.9 2.9 %collective-permute-start.1 = (bf16[4,160,128]{2,1,0:T(8,128)(2,1)S(1)}, bf16[4,160,128]{2,1,0:T(8,128)(2,1)S(1)}, u32[]{:S(2)}, u32[]{:S(2)}) collective-permute-start(bf16[4,160,128]{2,1,0:T(8,128)(2,1)S(1)} %get-tuple-element.84), channel_id=1, source_target_pairs={{0,1},{1,0},{2,3},{3,2},{4,5},{5,4},{6,7},{7,6},{8,9},{9,8},{10,11... | collective-permute-start | bytes 491528 | tf_op jit(solution)/shard_map/ppermute | solution.py:390
  8.8 0.8 %shard_map.146 = (bf16[512,512]{1,0:T(8,128)(2,1)S(1)}, bf16[4,160,512]{2,1,0:T(8,128)(2,1)S(1)}, bf16[4,160,128]{2,1,0:T(8,128)(2,1)S(1)}) custom-call(bf16[128,512]{1,0:T(8,128)(2,1)S(1)} %get-tuple-element.80.kt.kt_ref, bf16[512,1024]{1,0:T(8,128)(2,1)S(1)} %copy-done, bf16[16,1280]{1,0:T(8,128)(2,1)S(1)} %collective-permute-done.rim, f32[3,1024]{1,0:T(4,128)S(1)} %copy-done.4), custom_call_target="tpu_custom_call" | custom-call | flops 83886080 | bytes 2576384 | tf_op jit(solution)/shard_map/pallas_call | solution.py:378
  9.6 0.3 collective-permute-done.1.near
  9.9 2.6 %collective-permute-start.2 = (bf16[2,160,128]{2,1,0:T(8,128)(2,1)S(1)}, bf16[2,160,128]{2,1,0:T(8,128)(2,1)S(1)}, u32[]{:S(2)}, u32[]{:S(2)}) collective-permute-start(bf16[2,160,128]{2,1,0:T(8,128)(2,1)S(1)} %get-tuple-element.86), channel_id=1, source_target_pairs={{0,2},{1,3},{2,0},{3,1},{4,6},{5,7},{6,4},{7,5},{8,10},{9,11},{10,... | collective-permute-start | bytes 245768 | tf_op jit(solution)/shard_map/ppermute | solution.py:390
  12.5 0.5 shard_map.144
  13.0 2.3 %shard_map.147.local = f32[512,512]{1,0:T(8,128)S(1)} custom-call(bf16[512,128]{1,0:T(8,128)(2,1)S(1)} %get-tuple-element.77.q_ref, bf16[512,128]{1,0:T(8,128)(2,1)S(1)} %get-tuple-element.78.k_ref, bf16[512,512]{1,0:T(8,128)(2,1)S(1)} %get-tuple-element.81.v_ref.v), custom_call_target="tpu_custom_call" | custom-call | flops 536870912 | bytes 1835008 | tf_op jit(solution)/shard_map/pallas_call | solution.py:378
  15.3 2.7 %collective-permute-start.3 = (bf16[2,160,128]{2,1,0:T(8,128)(2,1)S(1)}, bf16[2,160,128]{2,1,0:T(8,128)(2,1)S(1)}, u32[]{:S(2)}, u32[]{:S(2)}) collective-permute-start(bf16[2,160,128]{2,1,0:T(8,128)(2,1)S(1)} %shard_map.149), channel_id=1, source_target_pairs={{0,4},{1,5},{2,6},{3,7},{4,0},{5,1},{6,2},{7,3},{8,12},{9,13},{10,... | collective-permute-start | bytes 245768 | tf_op jit(solution)/shard_map/ppermute | solution.py:390
  18.1 2.3 %shard_map.151.local = f32[512,512]{1,0:T(8,128)S(1)} custom-call(bf16[512,128]{1,0:T(8,128)(2,1)S(1)} %get-tuple-element.77.q_ref, bf16[512,128]{1,0:T(8,128)(2,1)S(1)} %get-tuple-element.78.k_ref, bf16[512,512]{1,0:T(8,128)(2,1)S(1)} %get-tuple-element.88.v_ref.v), custom_call_target="tpu_custom_call" | custom-call | flops 536870912 | bytes 1835008 | tf_op jit(solution)/shard_map/pallas_call | solution.py:378
  20.4 0.1 collective-permute-done.3.refs_1_.rest_0_
  20.5 3.1 %collective-permute-start.4 = (bf16[2,160,128]{2,1,0:T(8,128)(2,1)S(1)}, bf16[2,160,128]{2,1,0:T(8,128)(2,1)S(1)}, u32[]{:S(2)}, u32[]{:S(2)}) collective-permute-start(bf16[2,160,128]{2,1,0:T(8,128)(2,1)S(1)} %shard_map.150), channel_id=1, source_target_pairs={{0,8},{1,9},{2,10},{3,11},{4,12},{5,13},{6,14},{7,15},{8,0},{9,1},... | collective-permute-start | bytes 245768 | tf_op jit(solution)/shard_map/ppermute | solution.py:390
  23.6 2.4 %collective-permute-done.4.rest_1_ = bf16[2,160,128]{2,1,0:T(8,128)(2,1)S(1)} collective-permute-done((bf16[2,160,128]{2,1,0:T(8,128)(2,1)S(1)}, bf16[2,160,128]{2,1,0:T(8,128)(2,1)S(1)}, u32[]{:S(2)}, u32[]{:S(2)}) %collective-permute-start.4) | collective-permute-done | bytes 81952 | tf_op jit(solution)/shard_map/ppermute | solution.py:390
  26.1 1.0 %collective-permute-start.5 = (bf16[2,160,128]{2,1,0:T(8,128)(2,1)S(1)}, bf16[2,160,128]{2,1,0:T(8,128)(2,1)S(1)}, u32[]{:S(2)}, u32[]{:S(2)}) collective-permute-start(bf16[2,160,128]{2,1,0:T(8,128)(2,1)S(1)} %get-tuple-element.91), channel_id=1, source_target_pairs={{0,2},{1,3},{2,0},{3,1},{4,6},{5,7},{6,4},{7,5},{8,10},{9,11},{10,... | collective-permute-start | bytes 245768 | tf_op jit(solution)/shard_map/ppermute | solution.py:390
  27.1 3.5 %collective-permute-done.5.other_part = bf16[2,160,128]{2,1,0:T(8,128)(2,1)S(1)} collective-permute-done((bf16[2,160,128]{2,1,0:T(8,128)(2,1)S(1)}, bf16[2,160,128]{2,1,0:T(8,128)(2,1)S(1)}, u32[]{:S(2)}, u32[]{:S(2)}) %collective-permute-start.5) | collective-permute-done | bytes 81952 | tf_op jit(solution)/shard_map/ppermute | solution.py:390
  30.6 0.1 shard_map.153
  30.7 0.1 collective-permute-start.6
  30.8 1.4 %shard_map.154 = (bf16[512,512]{1,0:T(8,128)(2,1)S(1)}, bf16[512,512]{1,0:T(8,128)(2,1)S(1)}, bf16[4,160,128]{2,1,0:T(8,128)(2,1)S(1)}, f32[4,128]{1,0:T(4,128)S(1)}) custom-call(f32[512,512]{1,0:T(8,128)S(1)} %shard_map.147.local, bf16[8,160,512]{2,1,0:T(8,128)(2,1)S(1)} %get-tuple-element.82.fq, bf16[4,160,128]{2,1,0:T(8,128)(2,1)S(1)} %get-tuple-element.92.prefix.pre_a, ...), custom_call_target="tpu_custom_call" | custom-call | flops 167772160 | bytes 4790272 | tf_op jit(solution)/shard_map/pallas_call | solution.py:378
  32.2 0.5 collective-permute-start.7
  32.7 1.5 %shard_map.155 = (bf16[512,1024]{1,0:T(8,128)(2,1)S(1)}, bf16[512,512]{1,0:T(8,128)(2,1)S(1)}, bf16[4,160,128]{2,1,0:T(8,128)(2,1)S(1)}, f32[4,128]{1,0:T(4,128)S(1)}) custom-call(f32[512,512]{1,0:T(8,128)S(1)} %shard_map.151.local, bf16[8,160,512]{2,1,0:T(8,128)(2,1)S(1)} %get-tuple-element.82.fq, ...), custom_call_target="tpu_custom_call" | custom-call | flops 167772160 | bytes 5838848 | tf_op jit(solution)/shard_map/pallas_call | solution.py:378
  34.2 1.0 %collective-permute-start.8 = (bf16[2,160,128]{2,1,0:T(8,128)(2,1)S(1)}, bf16[2,160,128]{2,1,0:T(8,128)(2,1)S(1)}, u32[]{:S(2)}, u32[]{:S(2)}) collective-permute-start(bf16[2,160,128]{2,1,0:T(8,128)(2,1)S(1)} %get-tuple-element.109), channel_id=1, source_target_pairs={{0,2},{1,3},{2,0},{3,1},{4,6},{5,7},{6,4},{7,5},{8,10},{9,11},{10,... | collective-permute-start | bytes 245768 | tf_op jit(solution)/shard_map/ppermute | solution.py:390
  35.2 3.1 %shard_map.156 = (f32[512,256]{1,0:T(8,128)S(1)}, f32[32,512]{1,0:T(8,128)S(1)}, f32[32,512]{1,0:T(8,128)S(1)}, bf16[512,1024]{1,0:T(8,128)(2,1)}) custom-call(bf16[512,128]{1,0:T(8,128)(2,1)S(1)} %get-tuple-element.77.q_ref, bf16[512,128]{1,0:T(8,128)(2,1)S(1)} %get-tuple-element.78.k_ref, bf16[128,512]{1,0:T(8,128)(2,1)S(1)} %get-tuple-element.79.qt_ref, ...), custom_call_target="tpu_custom_call" | custom-call | flops 536870912 | bytes 4325376 | tf_op jit(solution)/shard_map/pallas_call | solution.py:378
  38.4 0.4 collective-permute-done.8.refs_0_.got_y
  38.8 2.0 %collective-permute-start.9 = (bf16[2,160,128]{2,1,0:T(8,128)(2,1)S(1)}, bf16[2,160,128]{2,1,0:T(8,128)(2,1)S(1)}, u32[]{:S(2)}, u32[]{:S(2)}) collective-permute-start(bf16[2,160,128]{2,1,0:T(8,128)(2,1)S(1)} %shard_map.162), channel_id=1, source_target_pairs={{0,4},{1,5},{2,6},{3,7},{4,0},{5,1},{6,2},{7,3},{8,12},{9,13},{10,... | collective-permute-start | bytes 245768 | tf_op jit(solution)/shard_map/ppermute | solution.py:390
  40.7 2.5 %shard_map.157 = (f32[512,256]{1,0:T(8,128)S(1)}, f32[32,512]{1,0:T(8,128)S(1)}, f32[32,512]{1,0:T(8,128)S(1)}) custom-call(bf16[512,128]{1,0:T(8,128)(2,1)S(1)} %get-tuple-element.77.q_ref, bf16[512,128]{1,0:T(8,128)(2,1)S(1)} %get-tuple-element.78.k_ref, bf16[128,512]{1,0:T(8,128)(2,1)S(1)} %get-tuple-element.79.qt_ref, ...), custom_call_target="tpu_custom_call" | custom-call | flops 536870912 | bytes 2228224 | tf_op jit(solution)/shard_map/pallas_call | solution.py:378
  43.3 3.4 %collective-permute-start.10 = (bf16[2,160,128]{2,1,0:T(8,128)(2,1)S(1)}, bf16[2,160,128]{2,1,0:T(8,128)(2,1)S(1)}, u32[]{:S(2)}, u32[]{:S(2)}) collective-permute-start(bf16[2,160,128]{2,1,0:T(8,128)(2,1)S(1)} %shard_map.163), channel_id=1, source_target_pairs={{0,8},{1,9},{2,10},{3,11},{4,12},{5,13},{6,14},{7,15},{8,0},{9,1},... | collective-permute-start | bytes 245768 | tf_op jit(solution)/shard_map/ppermute | solution.py:390
  46.7 2.7 %shard_map.158 = (f32[512,256]{1,0:T(8,128)S(1)}, f32[32,512]{1,0:T(8,128)S(1)}, f32[32,512]{1,0:T(8,128)S(1)}) custom-call(bf16[512,128]{1,0:T(8,128)(2,1)S(1)} %get-tuple-element.77.q_ref, bf16[512,128]{1,0:T(8,128)(2,1)S(1)} %get-tuple-element.78.k_ref, bf16[128,512]{1,0:T(8,128)(2,1)S(1)} %get-tuple-element.79.qt_ref, ...), custom_call_target="tpu_custom_call" | custom-call | flops 536870912 | bytes 2228224 | tf_op jit(solution)/shard_map/pallas_call | solution.py:378
  49.4 0.1 shard_map.164
  49.5 1.1 %collective-permute-start.11 = (bf16[2,160,128]{2,1,0:T(8,128)(2,1)S(1)}, bf16[2,160,128]{2,1,0:T(8,128)(2,1)S(1)}, u32[]{:S(2)}, u32[]{:S(2)}) collective-permute-start(bf16[2,160,128]{2,1,0:T(8,128)(2,1)S(1)} %get-tuple-element.117), channel_id=1, source_target_pairs={{0,2},{1,3},{2,0},{3,1},{4,6},{5,7},{6,4},{7,5},{8,10},{9,11},{10,... | collective-permute-start | bytes 245768 | tf_op jit(solution)/shard_map/ppermute | solution.py:390
  50.6 2.5 %shard_map.159 = (f32[512,256]{1,0:T(8,128)S(1)}, f32[32,512]{1,0:T(8,128)S(1)}, f32[32,512]{1,0:T(8,128)S(1)}) custom-call(bf16[512,128]{1,0:T(8,128)(2,1)S(1)} %get-tuple-element.77.q_ref, bf16[512,128]{1,0:T(8,128)(2,1)S(1)} %get-tuple-element.78.k_ref, bf16[128,512]{1,0:T(8,128)(2,1)S(1)} %get-tuple-element.79.qt_ref, ...), custom_call_target="tpu_custom_call" | custom-call | flops 536870912 | bytes 2228224 | tf_op jit(solution)/shard_map/pallas_call | solution.py:378
  53.1 0.9 %shard_map.160 = (f32[512,128]{1,0:T(8,128)S(1)}, f32[3,128]{1,0:T(4,128)S(1)}) custom-call(bf16[512,128]{1,0:T(8,128)(2,1)S(1)} %copy-done.3, bf16[16,1280]{1,0:T(8,128)(2,1)S(1)} %collective-permute-done.rim, bf16[128,512]{1,0:T(8,128)(2,1)S(1)} %get-tuple-element.79.qt_ref, bf16[512,512]{1,0:T(8,128)(2,1)S(1)} %get-tuple-element.93.gs_ref.gs_a, ...), custom_call_target="tpu_custom_call" | custom-call | flops 83886080 | bytes 2206720 | tf_op jit(solution)/shard_map/pallas_call | solution.py:378
  54.0 0.1 shard_map.165
  54.1 0.1 collective-permute-start.12
  54.2 1.1 %shard_map.166 = (f32[512,512]{1,0:T(8,128)S(1)}, f32[64,512]{1,0:T(8,128)S(1)}, f32[3,512]{1,0:T(4,128)S(1)}) custom-call(bf16[512,1024]{1,0:T(8,128)(2,1)S(1)} %copy-done, bf16[16,1280]{1,0:T(8,128)(2,1)S(1)} %collective-permute-done.rim, bf16[128,512]{1,0:T(8,128)(2,1)S(1)} %get-tuple-element.80.kt.kt_ref, ...), custom_call_target="tpu_custom_call" | custom-call | flops 167772160 | bytes 4929536 | tf_op jit(solution)/shard_map/pallas_call | solution.py:378
  55.3 0.3 collective-permute-done.12.state
  55.6 1.1 %shard_map.167 = (f32[512,512]{1,0:T(8,128)S(1)}, f32[512,128]{1,0:T(8,128)S(1)}, f32[8,1280]{1,0:T(8,128)S(1)}, f32[4,1280]{1,0:T(4,128)S(1)}) custom-call(bf16[512,128]{1,0:T(8,128)(2,1)S(1)} %copy-done.2, bf16[512,1024]{1,0:T(8,128)(2,1)S(1)} %copy-done, bf16[16,1280]{1,0:T(8,128)(2,1)S(1)} %collective-permute-done.rim, ...), custom_call_target="tpu_custom_call" | custom-call | flops 167772160 | bytes 6700544 | tf_op jit(solution)/shard_map/pallas_call | solution.py:378
  56.7 4.5 %collective-permute-start.16 = (f32[4,1280]{1,0:T(4,128)S(1)}, f32[4,1280]{1,0:T(4,128)S(1)}, u32[]{:S(2)}, u32[]{:S(2)}) collective-permute-start(f32[4,1280]{1,0:T(4,128)S(1)} %get-tuple-element.140), channel_id=1, source_target_pairs={{0,12},{1,13},{2,14},{3,15},{4,8},{5,9},{6,10},{7,11},{8,4},{9,5},... | collective-permute-start | bytes 61448 | tf_op jit(solution)/shard_map/ppermute | solution.py:390
  61.2 0.6 collective-permute-start.14
  61.8 1.3 %collective-permute-start.13 = (f32[8,1280]{1,0:T(8,128)S(1)}, f32[8,1280]{1,0:T(8,128)S(1)}, u32[]{:S(2)}, u32[]{:S(2)}) collective-permute-start(f32[8,1280]{1,0:T(8,128)S(1)} %get-tuple-element.136), channel_id=1, source_target_pairs={{1,0},{2,1},{3,2},{4,3},{5,4},{6,5},{7,6},{8,7},{9,8},{10,9},{11,1... | collective-permute-start | bytes 122888 | tf_op jit(solution)/shard_map/ppermute | solution.py:623
  63.1 2.7 %collective-permute-done.15 = f32[4,1280]{1,0:T(4,128)S(1)} collective-permute-done((f32[4,1280]{1,0:T(4,128)S(1)}, f32[4,1280]{1,0:T(4,128)S(1)}, u32[]{:S(2)}, u32[]{:S(2)}) %collective-permute-start.15) | collective-permute-done | bytes 20512 | tf_op jit(solution)/shard_map/ppermute | solution.py:390
  65.9 0.1 collective-permute-start.17
  65.9 1.1 %collective-permute-start.18 = (f32[4,1280]{1,0:T(4,128)S(1)}, f32[4,1280]{1,0:T(4,128)S(1)}, u32[]{:S(2)}, u32[]{:S(2)}) collective-permute-start(f32[4,1280]{1,0:T(4,128)S(1)} %add_add_fusion.refs_0_), channel_id=1, source_target_pairs={{0,2},{1,3},{2,0},{3,1},{4,6},{5,7},{6,4},{7,5},{8,10},{9,11},{10,... | collective-permute-start | bytes 61448 | tf_op jit(solution)/shard_map/ppermute | solution.py:390
  67.0 0.8 %collective-permute-start.19 = (f32[4,1280]{1,0:T(4,128)S(1)}, f32[4,1280]{1,0:T(4,128)S(1)}, u32[]{:S(2)}, u32[]{:S(2)}) collective-permute-start(f32[4,1280]{1,0:T(4,128)S(1)} %add_add_fusion.refs_0_), channel_id=1, source_target_pairs={{0,3},{1,2},{2,1},{3,0},{4,7},{5,6},{6,5},{7,4},{8,11},{9,10},{10,... | collective-permute-start | bytes 61448 | tf_op jit(solution)/shard_map/ppermute | solution.py:390
  67.8 2.2 %shard_map.168 = (bf16[512,128]{1,0:T(8,128)(2,1)}, bf16[512,128]{1,0:T(8,128)(2,1)}, bf16[512,1024]{1,0:T(8,128)(2,1)}) custom-call(f32[512,128]{1,0:T(8,128)S(1)} %get-tuple-element.104.gq, f32[512,128]{1,0:T(8,128)S(1)} %get-tuple-element.134.gk, f32[512,512]{1,0:T(8,128)S(1)} %get-tuple-element.135.gv_a, f32[512,512]{1,0:T(8,128)S(1)} %get-tuple-element.125.gv_b, ...), custom_call_target="tpu_custom_call" | custom-call | flops 167772160 | bytes 3988480 | tf_op jit(solution)/shard_map/pallas_call | solution.py:378
  70.0 0.2 collective-permute-done.19.refs_3_
  70.2 0.6 shard_map.169
  (36 shorter events, 0.3 us)
Async XLA Ops:
  0.6 4.3 %copy-start.2 = (bf16[512,128]{1,0:T(8,128)(2,1)S(1)}, bf16[512,128]{1,0:T(8,128)(2,1)}, u32[]{:S(2)}) copy-start(bf16[512,128]{1,0:T(8,128)(2,1)} %key.5) | copy-start | bytes 393220
  0.6 4.3 %copy-start = (bf16[512,1024]{1,0:T(8,128)(2,1)S(1)}, bf16[512,1024]{1,0:T(8,128)(2,1)}, u32[]{:S(2)}) copy-start(bf16[512,1024]{1,0:T(8,128)(2,1)} %value.9) | copy-start | bytes 3145732
  0.7 4.3 %copy-start.7 = (f32[3,128]{1,0:T(4,128)S(1)}, f32[3,128]{1,0:T(4,128)}, u32[]{:S(2)}) copy-start(f32[3,128]{1,0:T(4,128)} %taps_k.3) | copy-start | bytes 4612
  0.7 4.3 %copy-start.4 = (f32[3,1024]{1,0:T(4,128)S(1)}, f32[3,1024]{1,0:T(4,128)}, u32[]{:S(2)}) copy-start(f32[3,1024]{1,0:T(4,128)} %taps_v.5) | copy-start | bytes 36868
  1.6 10.9 %copy-start.3 = (bf16[512,128]{1,0:T(8,128)(2,1)S(1)}, bf16[512,128]{1,0:T(8,128)(2,1)}, u32[]{:S(2)}) copy-start(bf16[512,128]{1,0:T(8,128)(2,1)} %query.5) | copy-start | bytes 393220
  1.6 10.9 %copy-start.6 = (f32[3,128]{1,0:T(4,128)S(1)}, f32[3,128]{1,0:T(4,128)}, u32[]{:S(2)}) copy-start(f32[3,128]{1,0:T(4,128)} %taps_q.5) | copy-start | bytes 4612
  1.6 3.3 %collective-permute-start = (bf16[16,1280]{1,0:T(8,128)(2,1)S(1)}, bf16[16,1280]{1,0:T(8,128)(2,1)S(1)}, u32[]{:S(2)}, u32[]{:S(2)}) collective-permute-start(bf16[16,1280]{1,0:T(8,128)(2,1)S(1)} %shard_map.143), channel_id=1, source_target_pairs={{0,1},{1,2},{2,3},{3,4},{4,5},{5,6},{6,7},{7,8},{8,9},{9,10},{10,1... | collective-permute-start | bytes 122888 | tf_op jit(solution)/shard_map/ppermute | solution.py:501
  5.9 4.0 %collective-permute-start.1 = (bf16[4,160,128]{2,1,0:T(8,128)(2,1)S(1)}, bf16[4,160,128]{2,1,0:T(8,128)(2,1)S(1)}, u32[]{:S(2)}, u32[]{:S(2)}) collective-permute-start(bf16[4,160,128]{2,1,0:T(8,128)(2,1)S(1)} %get-tuple-element.84), channel_id=1, source_target_pairs={{0,1},{1,0},{2,3},{3,2},{4,5},{5,4},{6,7},{7,6},{8,9},{9,8},{10,11... | collective-permute-start | bytes 491528 | tf_op jit(solution)/shard_map/ppermute | solution.py:390
  9.9 5.4 %collective-permute-start.2 = (bf16[2,160,128]{2,1,0:T(8,128)(2,1)S(1)}, bf16[2,160,128]{2,1,0:T(8,128)(2,1)S(1)}, u32[]{:S(2)}, u32[]{:S(2)}) collective-permute-start(bf16[2,160,128]{2,1,0:T(8,128)(2,1)S(1)} %get-tuple-element.86), channel_id=1, source_target_pairs={{0,2},{1,3},{2,0},{3,1},{4,6},{5,7},{6,4},{7,5},{8,10},{9,11},{10,... | collective-permute-start | bytes 245768 | tf_op jit(solution)/shard_map/ppermute | solution.py:390
  15.3 5.1 %collective-permute-start.3 = (bf16[2,160,128]{2,1,0:T(8,128)(2,1)S(1)}, bf16[2,160,128]{2,1,0:T(8,128)(2,1)S(1)}, u32[]{:S(2)}, u32[]{:S(2)}) collective-permute-start(bf16[2,160,128]{2,1,0:T(8,128)(2,1)S(1)} %shard_map.149), channel_id=1, source_target_pairs={{0,4},{1,5},{2,6},{3,7},{4,0},{5,1},{6,2},{7,3},{8,12},{9,13},{10,... | collective-permute-start | bytes 245768 | tf_op jit(solution)/shard_map/ppermute | solution.py:390
  18.0 12.7 %copy-start.1 = (bf16[512,1024]{1,0:T(8,128)(2,1)S(1)}, bf16[512,1024]{1,0:T(8,128)(2,1)}, u32[]{:S(2)}) copy-start(bf16[512,1024]{1,0:T(8,128)(2,1)} %grad.3) | copy-start | bytes 3145732
  18.0 12.7 %copy-start.5 = (f32[1024]{0:T(1024)S(1)}, f32[1024]{0:T(1024)}, u32[]{:S(2)}) copy-start(f32[1024]{0:T(1024)} %param.14) | copy-start | bytes 12292
  20.5 5.5 %collective-permute-start.4 = (bf16[2,160,128]{2,1,0:T(8,128)(2,1)S(1)}, bf16[2,160,128]{2,1,0:T(8,128)(2,1)S(1)}, u32[]{:S(2)}, u32[]{:S(2)}) collective-permute-start(bf16[2,160,128]{2,1,0:T(8,128)(2,1)S(1)} %shard_map.150), channel_id=1, source_target_pairs={{0,8},{1,9},{2,10},{3,11},{4,12},{5,13},{6,14},{7,15},{8,0},{9,1},... | collective-permute-start | bytes 245768 | tf_op jit(solution)/shard_map/ppermute | solution.py:390
  26.1 4.5 %collective-permute-start.5 = (bf16[2,160,128]{2,1,0:T(8,128)(2,1)S(1)}, bf16[2,160,128]{2,1,0:T(8,128)(2,1)S(1)}, u32[]{:S(2)}, u32[]{:S(2)}) collective-permute-start(bf16[2,160,128]{2,1,0:T(8,128)(2,1)S(1)} %get-tuple-element.91), channel_id=1, source_target_pairs={{0,2},{1,3},{2,0},{3,1},{4,6},{5,7},{6,4},{7,5},{8,10},{9,11},{10,... | collective-permute-start | bytes 245768 | tf_op jit(solution)/shard_map/ppermute | solution.py:390
  30.7 2.0 %collective-permute-start.6 = (bf16[4,160,128]{2,1,0:T(8,128)(2,1)S(1)}, bf16[4,160,128]{2,1,0:T(8,128)(2,1)S(1)}, u32[]{:S(2)}, u32[]{:S(2)}) collective-permute-start(bf16[4,160,128]{2,1,0:T(8,128)(2,1)S(1)} %get-tuple-element.94), channel_id=1, source_target_pairs={{0,1},{1,0},{2,3},{3,2},{4,5},{5,4},{6,7},{7,6},{8,9},{9,8},{10,11... | collective-permute-start | bytes 491528 | tf_op jit(solution)/shard_map/ppermute | solution.py:390
  32.2 2.0 %collective-permute-start.7 = (bf16[4,160,128]{2,1,0:T(8,128)(2,1)S(1)}, bf16[4,160,128]{2,1,0:T(8,128)(2,1)S(1)}, u32[]{:S(2)}, u32[]{:S(2)}) collective-permute-start(bf16[4,160,128]{2,1,0:T(8,128)(2,1)S(1)} %get-tuple-element.107), channel_id=1, source_target_pairs={{0,1},{1,0},{2,3},{3,2},{4,5},{5,4},{6,7},{7,6},{8,9},{9,8},{10,11... | collective-permute-start | bytes 491528 | tf_op jit(solution)/shard_map/ppermute | solution.py:390
  34.2 4.5 %collective-permute-start.8 = (bf16[2,160,128]{2,1,0:T(8,128)(2,1)S(1)}, bf16[2,160,128]{2,1,0:T(8,128)(2,1)S(1)}, u32[]{:S(2)}, u32[]{:S(2)}) collective-permute-start(bf16[2,160,128]{2,1,0:T(8,128)(2,1)S(1)} %get-tuple-element.109), channel_id=1, source_target_pairs={{0,2},{1,3},{2,0},{3,1},{4,6},{5,7},{6,4},{7,5},{8,10},{9,11},{10,... | collective-permute-start | bytes 245768 | tf_op jit(solution)/shard_map/ppermute | solution.py:390
  38.8 4.5 %collective-permute-start.9 = (bf16[2,160,128]{2,1,0:T(8,128)(2,1)S(1)}, bf16[2,160,128]{2,1,0:T(8,128)(2,1)S(1)}, u32[]{:S(2)}, u32[]{:S(2)}) collective-permute-start(bf16[2,160,128]{2,1,0:T(8,128)(2,1)S(1)} %shard_map.162), channel_id=1, source_target_pairs={{0,4},{1,5},{2,6},{3,7},{4,0},{5,1},{6,2},{7,3},{8,12},{9,13},{10,... | collective-permute-start | bytes 245768 | tf_op jit(solution)/shard_map/ppermute | solution.py:390
  43.3 6.1 %collective-permute-start.10 = (bf16[2,160,128]{2,1,0:T(8,128)(2,1)S(1)}, bf16[2,160,128]{2,1,0:T(8,128)(2,1)S(1)}, u32[]{:S(2)}, u32[]{:S(2)}) collective-permute-start(bf16[2,160,128]{2,1,0:T(8,128)(2,1)S(1)} %shard_map.163), channel_id=1, source_target_pairs={{0,8},{1,9},{2,10},{3,11},{4,12},{5,13},{6,14},{7,15},{8,0},{9,1},... | collective-permute-start | bytes 245768 | tf_op jit(solution)/shard_map/ppermute | solution.py:390
  49.5 4.5 %collective-permute-start.11 = (bf16[2,160,128]{2,1,0:T(8,128)(2,1)S(1)}, bf16[2,160,128]{2,1,0:T(8,128)(2,1)S(1)}, u32[]{:S(2)}, u32[]{:S(2)}) collective-permute-start(bf16[2,160,128]{2,1,0:T(8,128)(2,1)S(1)} %get-tuple-element.117), channel_id=1, source_target_pairs={{0,2},{1,3},{2,0},{3,1},{4,6},{5,7},{6,4},{7,5},{8,10},{9,11},{10,... | collective-permute-start | bytes 245768 | tf_op jit(solution)/shard_map/ppermute | solution.py:390
  54.1 1.5 %collective-permute-start.12 = (bf16[4,160,128]{2,1,0:T(8,128)(2,1)S(1)}, bf16[4,160,128]{2,1,0:T(8,128)(2,1)S(1)}, u32[]{:S(2)}, u32[]{:S(2)}) collective-permute-start(bf16[4,160,128]{2,1,0:T(8,128)(2,1)S(1)} %get-tuple-element.120), channel_id=1, source_target_pairs={{0,1},{1,0},{2,3},{3,2},{4,5},{5,4},{6,7},{7,6},{8,9},{9,8},{10,11... | collective-permute-start | bytes 491528 | tf_op jit(solution)/shard_map/ppermute | solution.py:390
  56.7 6.4 %collective-permute-start.16 = (f32[4,1280]{1,0:T(4,128)S(1)}, f32[4,1280]{1,0:T(4,128)S(1)}, u32[]{:S(2)}, u32[]{:S(2)}) collective-permute-start(f32[4,1280]{1,0:T(4,128)S(1)} %get-tuple-element.140), channel_id=1, source_target_pairs={{0,12},{1,13},{2,14},{3,15},{4,8},{5,9},{6,10},{7,11},{8,4},{9,5},... | collective-permute-start | bytes 61448 | tf_op jit(solution)/shard_map/ppermute | solution.py:390
  61.2 4.7 %collective-permute-start.15 = (f32[4,1280]{1,0:T(4,128)S(1)}, f32[4,1280]{1,0:T(4,128)S(1)}, u32[]{:S(2)}, u32[]{:S(2)}) collective-permute-start(f32[4,1280]{1,0:T(4,128)S(1)} %get-tuple-element.140), channel_id=1, source_target_pairs={{0,8},{1,9},{2,10},{3,11},{4,12},{5,13},{6,14},{7,15},{8,0},{9,1},... | collective-permute-start | bytes 61448 | tf_op jit(solution)/shard_map/ppermute | solution.py:390
  61.2 4.7 %collective-permute-start.14 = (f32[4,1280]{1,0:T(4,128)S(1)}, f32[4,1280]{1,0:T(4,128)S(1)}, u32[]{:S(2)}, u32[]{:S(2)}) collective-permute-start(f32[4,1280]{1,0:T(4,128)S(1)} %get-tuple-element.140), channel_id=1, source_target_pairs={{0,4},{1,5},{2,6},{3,7},{4,0},{5,1},{6,2},{7,3},{8,12},{9,13},{10,... | collective-permute-start | bytes 61448 | tf_op jit(solution)/shard_map/ppermute | solution.py:390
  61.8 6.0 %collective-permute-start.13 = (f32[8,1280]{1,0:T(8,128)S(1)}, f32[8,1280]{1,0:T(8,128)S(1)}, u32[]{:S(2)}, u32[]{:S(2)}) collective-permute-start(f32[8,1280]{1,0:T(8,128)S(1)} %get-tuple-element.136), channel_id=1, source_target_pairs={{1,0},{2,1},{3,2},{4,3},{5,4},{6,5},{7,6},{8,7},{9,8},{10,9},{11,1... | collective-permute-start | bytes 122888 | tf_op jit(solution)/shard_map/ppermute | solution.py:623
  65.9 4.1 %collective-permute-start.17 = (f32[4,1280]{1,0:T(4,128)S(1)}, f32[4,1280]{1,0:T(4,128)S(1)}, u32[]{:S(2)}, u32[]{:S(2)}) collective-permute-start(f32[4,1280]{1,0:T(4,128)S(1)} %add_add_fusion.refs_0_), channel_id=1, source_target_pairs={{0,1},{1,0},{2,3},{3,2},{4,5},{5,4},{6,7},{7,6},{8,9},{9,8},{10,11... | collective-permute-start | bytes 61448 | tf_op jit(solution)/shard_map/ppermute | solution.py:390
  65.9 4.0 %collective-permute-start.18 = (f32[4,1280]{1,0:T(4,128)S(1)}, f32[4,1280]{1,0:T(4,128)S(1)}, u32[]{:S(2)}, u32[]{:S(2)}) collective-permute-start(f32[4,1280]{1,0:T(4,128)S(1)} %add_add_fusion.refs_0_), channel_id=1, source_target_pairs={{0,2},{1,3},{2,0},{3,1},{4,6},{5,7},{6,4},{7,5},{8,10},{9,11},{10,... | collective-permute-start | bytes 61448 | tf_op jit(solution)/shard_map/ppermute | solution.py:390
  67.0 3.2 %collective-permute-start.19 = (f32[4,1280]{1,0:T(4,128)S(1)}, f32[4,1280]{1,0:T(4,128)S(1)}, u32[]{:S(2)}, u32[]{:S(2)}) collective-permute-start(f32[4,1280]{1,0:T(4,128)S(1)} %add_add_fusion.refs_0_), channel_id=1, source_target_pairs={{0,3},{1,2},{2,1},{3,0},{4,7},{5,6},{6,5},{7,4},{8,11},{9,10},{10,... | collective-permute-start | bytes 61448 | tf_op jit(solution)/shard_map/ppermute | solution.py:390

commit v7 on v6

--- a/solution.py
+++ b/solution.py
@@ -21,6 +21,7 @@
 TAIL = 144
 RIM = 16
 STEP = 128
+CUT = 128
 F32 = jnp.float32
 BF16 = jnp.bfloat16
 
@@ -126,28 +127,59 @@
         copy.wait()
 
 
-def value_states(half, kt, value, rim, taps_v, v_out, f_out, state_out, wide):
-    rows = value.shape[0]
-    for g in range(HALF):
-        f_out[g] = features(kt[rows_of(half, g)].astype(F32))
-    for g in range(HALF):
-        fill(wide, rim[:, lanes_of(half, g, 2 * LANES)], value[:, lanes_of(half, g)])
-        v_out[:, head_lanes(g)] = conv(wide, taps_v[:, lanes_of(half, g)], rows).astype(BF16)
-    for g in range(HALF):
-        state_out[g] = dot(f_out[g], v_out[:, head_lanes(g)], NN).astype(BF16)
-
-
-def first_key_kernel(key, value, rim, taps_k, taps_v, k_out, kt_out, v_out, f_out, state_out, wide):
-    rows = key.shape[0]
-    fill(wide, rim[:, LANES : 2 * LANES], key[...])
+def bulk_kernel(
+    key, value, taps_k, taps_v, k_out, kt_out, v_b, f_b, state_b, v_a, f_a, state_a, wide
+):
+    rows = key.shape[0] - CUT
+    fill(wide, key[CUT - RIM : CUT], key[CUT:])
     k = conv(wide, taps_k[...], rows).astype(BF16)
     k_out[...] = k
     kt_out[...] = k.astype(F32).T.astype(BF16)
-    value_states(half_index(False), kt_out, value, rim, taps_v, v_out, f_out, state_out, wide)
-
-
-def second_key_kernel(kt, value, rim, taps_v, v_out, f_out, state_out, wide):
-    value_states(half_index(True), kt, value, rim, taps_v, v_out, f_out, state_out, wide)
+    for own, v_out, f_out, state_out in ((False, v_b, f_b, state_b), (True, v_a, f_a, state_a)):
+        half = half_index(own)
+        for g in range(HALF):
+            f_out[g] = features(kt_out[rows_of(half, g)].astype(F32))
+        for g in range(HALF):
+            lanes = lanes_of(half, g)
+            fill(wide, value[CUT - RIM : CUT, lanes], value[CUT:, lanes])
+            v_out[:, head_lanes(g)] = conv(wide, taps_v[:, lanes], rows).astype(BF16)
+        for g in range(HALF):
+            state_out[g] = dot(f_out[g], v_out[:, head_lanes(g)], NN)
+
+
+def value_states(half, kt, value, rim, taps_v, v_rest, f_rest, state_rest, v_out, f_out, state_out, wide):
+    for g in range(HALF):
+        f_out[g, :, 0:CUT] = features(kt[rows_of(half, g), 0:CUT].astype(F32))
+        f_out[g, :, CUT:] = f_rest[g]
+    v_out[CUT:] = v_rest[...]
+    for g in range(HALF):
+        lanes = lanes_of(half, g)
+        fill(wide, rim[:, lanes_of(half, g, 2 * LANES)], value[0:CUT, lanes])
+        v_out[0:CUT, head_lanes(g)] = conv(wide, taps_v[:, lanes], CUT).astype(BF16)
+    for g in range(HALF):
+        first = dot(f_out[g, :, 0:CUT], v_out[0:CUT, head_lanes(g)], NN)
+        state_out[g] = (state_rest[g] + first).astype(BF16)
+
+
+def first_key_kernel(
+    key, value, rim, taps_k, taps_v, k_rest, kt_rest, v_rest, f_rest, state_rest,
+    k_out, kt_out, v_out, f_out, state_out, wide,
+):
+    fill(wide, rim[:, LANES : 2 * LANES], key[0:CUT])
+    k = conv(wide, taps_k[...], CUT).astype(BF16)
+    k_out[0:CUT] = k
+    k_out[CUT:] = k_rest[...]
+    kt_out[:, 0:CUT] = k.astype(F32).T.astype(BF16)
+    kt_out[:, CUT:] = kt_rest[...]
+    value_states(
+        half_index(False), kt_out, value, rim, taps_v, v_rest, f_rest, state_rest, v_out, f_out, state_out, wide
+    )
+
+
+def second_key_kernel(kt, value, rim, taps_v, v_rest, f_rest, state_rest, v_out, f_out, state_out, wide):
+    value_states(
+        half_index(True), kt, value, rim, taps_v, v_rest, f_rest, state_rest, v_out, f_out, state_out, wide
+    )
 
 
 def query_kernel(query, rim, taps_q, q_out, qt_out, fq_out, wide):
@@ -323,30 +355,39 @@
     count = taps_q.shape[0]
     copies = []
 
-    def one(grad, after, taps):
-        wide[0:rows] = grad
-        wide[rows : rows + 8] = after
-        total = taps[0:1] * wide[count - 1 : count - 1 + rows]
+    def one(grad, place, start, stop, after, taps, part, lanes):
+        last = stop == rows
+        body = stop - start - (RIM if last else 0)
+        total = taps[0:1] * grad[start + count - 1 : start + count - 1 + body, place]
         for o in range(1, count):
-            total = total + taps[o : o + 1] * wide[count - 1 - o : count - 1 - o + rows]
-        return total.astype(BF16)
+            total = total + taps[o : o + 1] * grad[start + count - 1 - o : start + count - 1 - o + body, place]
+        part[start : start + body, lanes] = total.astype(BF16)
+        if last:
+            wide[0:RIM] = grad[rows - RIM :, place]
+            wide[RIM : RIM + 8] = after
+            total = taps[0:1] * wide[count - 1 : count - 1 + RIM]
+            for o in range(1, count):
+                total = total + taps[o : o + 1] * wide[count - 1 - o : count - 1 - o + RIM]
+            part[rows - RIM :, lanes] = total.astype(BF16)
 
     def move(part, out):
         copies.append(pltpu.make_async_copy(part, out, sems.at[len(copies)]))
         copies[-1].start()
 
-    for i, (own, gv) in enumerate(((True, gv_a), (False, gv_b))):
-        half = half_index(own)
-        for g in range(HALF):
-            place = lanes_of(half, g)
-            slot = i * HALF + g
-            after = follow[:, lanes_of(half, g, 2 * LANES)]
-            v_part[slot] = one(gv[:, head_lanes(g)], after, taps_v[:, place])
-            move(v_part.at[slot], v_out.at[:, place])
-    q_part[...] = one(gq[...], follow[:, 0:LANES], taps_q[...])
-    move(q_part, q_out)
-    k_part[...] = one(gk[...], follow[:, LANES : 2 * LANES], taps_k[...])
-    move(k_part, k_out)
+    for start in reversed(range(0, rows, STEP)):
+        stop = start + STEP
+        for own, gv in ((True, gv_a), (False, gv_b)):
+            half = half_index(own)
+            for g in range(HALF):
+                lanes = lanes_of(half, g)
+                after = follow[:, lanes_of(half, g, 2 * LANES)]
+                one(gv, head_lanes(g), start, stop, after, taps_v[:, lanes], v_part, lanes)
+        move(v_part.at[start:stop], v_out.at[start:stop])
+    for grad, place, taps, part, out in (
+        (gq, slice(0, LANES), taps_q, q_part, q_out), (gk, slice(LANES, 2 * LANES), taps_k, k_part, k_out)
+    ):
+        one(grad, slice(0, LANES), 0, rows, follow[:, place], taps[...], part, slice(0, LANES))
+        move(part, out)
     for copy in copies:
         copy.wait()
 
@@ -500,18 +541,27 @@
     )[0]
     rim = lax.ppermute(ends, "seq", [(i, i + 1) for i in range(count - 1)])
 
+    rest = rows - CUT
+    half_rest = [st((rest, half_width), BF16), st((HALF, ROWS, rest), BF16), st((HALF, ROWS, DIM), F32)]
+    k_rest, kt_rest, *rests = call(
+        bulk_kernel,
+        [st((rest, LANES), BF16), st((LANES, rest), BF16), *half_rest, *half_rest],
+        [wide],
+        (key_in, value_in, conv_key, conv_value),
+        2 * state_flops,
+    )
     k, kt, v_b, fk_b, state_b = call(
         first_key_kernel,
         [st((rows, LANES), BF16), turned_flat, half_narrow, half_features, half_state],
         [wide],
-        (key_in, value_in, rim, conv_key, conv_value),
+        (key_in, value_in, rim, conv_key, conv_value, *held(k_rest, kt_rest, *rests[:3])),
         state_flops,
     )
     v_a, fk_a, state_a = call(
         second_key_kernel,
         [half_narrow, half_features, half_state],
         [wide],
-        (*held(kt), value_in, rim, conv_value),
+        (*held(kt), value_in, rim, conv_value, *held(*rests[3:])),
         state_flops,
     )
     made = {}
@@ -631,8 +681,8 @@
     grad_query, grad_key, grad_value = call(
         signal_kernel,
         [flat_narrow, flat_narrow, st((rows, WIDE), BF16)],
-        [pltpu.VMEM((rows + 8, DIM), F32), pltpu.VMEM((rows, LANES), BF16), pltpu.VMEM((rows, LANES), BF16),
-         pltpu.VMEM((HEADS, rows, DIM), BF16), pltpu.SemaphoreType.DMA((HEADS + 2,))],
+        [pltpu.VMEM((RIM + 8, DIM), F32), pltpu.VMEM((rows, LANES), BF16), pltpu.VMEM((rows, LANES), BF16),
+         pltpu.VMEM((rows, WIDE), BF16), pltpu.SemaphoreType.DMA((rows // STEP + 2,))],
         (*held(gq, gk, gv_a, gv_b), follow, conv_query, conv_key, conv_value),
         2 * state_flops,
         loose=(0, 1, 2),
@@ -642,7 +692,7 @@
         functools.partial(finish_kernel, total_rows ** (-0.5)),
         [st((taps, LANES), F32), st((taps, LANES), F32), st((taps, WIDE), F32), st((1, WIDE), F32)],
         [],
-        (tie(sums, grad_value), *[exchange(sums, distance) for distance in (1, 2, 3)]),
+        (tie(sums, grad_value), *[exchange(sums, distance) for distance in (3, 2, 1)]),
         rows,
         loose=(0, 1, 2, 3),
     )

time: 71 us -> 70.1 us (0.987)
    ppermute x1, waiting for transfers between devices: 0.85 us -> 0.01 us  [shards(): rim = lax.ppermute(ends, 'seq', [(i, i + 1) for i in range(count - 1)])]
    pallas_call x27 -> x28, Pallas kernels: 27.7 us -> 27.7 us  [call(): pl.pallas_call(kernel, out_shape=[o if i in loose else pltpu.VMEM(o.shape...]
  transfers between devices with their start and end apart: 20 -> 20, of which waited for: 9 -> 8; matrix products, arithmetic and copies ran while one was open for 0% -> 0% of each run, Pallas kernels for 33% -> 35%
where the time goes in v7:
time: 70.1 us; the launch traced here: 69.9 us
  starting transfers between devices  30.8 us (44%)
  Pallas kernels  27.7 us (40%)
  waiting for transfers between devices  10.3 us (15%)
  between operations  0.95 us (1%)
    pallas_call x28, Pallas kernels, call(): pl.pallas_call(kernel, out_shape=[o if i in loose else pltpu.VMEM(o.shape...  27.7 us
    ppermute x18, starting transfers between devices, exchange(): return lax.ppermute(x, 'seq', [(i, i ^ distance) for i in range(count)])  27.2 us
    ppermute x18, waiting for transfers between devices, exchange(): return lax.ppermute(x, 'seq', [(i, i ^ distance) for i in range(count)])  10.3 us
    ppermute x1, starting transfers between devices, shards(): rim = lax.ppermute(ends, 'seq', [(i, i + 1) for i in range(count - 1)])  2.36 us
  transfers between devices with their start and end apart: 20, of which 8 were waited for; matrix products, arithmetic and copies ran while one was open for 0% of the time, Pallas kernels for 35%

profile of v7, /device:TPU:0, one launch (start us, length us, event | category | flops | bytes accessed | tf_op | source)
XLA Modules:
  0.0 69.9 jit_solution(13663558974857765169)
XLA Ops:
  0.7 0.9 %shard_map.143 = bf16[16,1280]{1,0:T(8,128)(2,1)S(1)} custom-call(bf16[512,128]{1,0:T(8,128)(2,1)} %query.5, bf16[512,128]{1,0:T(8,128)(2,1)} %key.7, bf16[512,1024]{1,0:T(8,128)(2,1)} %value.11), custom_call_target="tpu_custom_call" | custom-call | flops 512 | bytes 1351680 | tf_op jit(solution)/shard_map/pallas_call | solution.py:419
  1.6 2.4 %collective-permute-start = (bf16[16,1280]{1,0:T(8,128)(2,1)S(1)}, bf16[16,1280]{1,0:T(8,128)(2,1)S(1)}, u32[]{:S(2)}, u32[]{:S(2)}) collective-permute-start(bf16[16,1280]{1,0:T(8,128)(2,1)S(1)} %shard_map.143), channel_id=1, source_target_pairs={{0,1},{1,2},{2,3},{3,4},{4,5},{5,6},{6,7},{7,8},{8,9},{9,10},{10,1... | collective-permute-start | bytes 122888 | tf_op jit(solution)/shard_map/ppermute | solution.py:542
  4.0 1.2 %shard_map.145 = (bf16[384,128]{1,0:T(8,128)(2,1)S(1)}, bf16[128,384]{1,0:T(8,128)(2,1)S(1)}, bf16[384,512]{1,0:T(8,128)(2,1)S(1)}, bf16[4,160,384]{2,1,0:T(8,12...) custom-call(bf16[512,128]{1,0:T(8,128)(2,1)S(1)} %copy-done.2, ...), custom_call_target="tpu_custom_call" | custom-call | flops 167772160 | bytes 3814912 | tf_op jit(solution)/shard_map/pallas_call | solution.py:419
  5.2 0.4 shard_map.146
  5.6 2.7 %collective-permute-start.1 = (bf16[4,160,128]{2,1,0:T(8,128)(2,1)S(1)}, bf16[4,160,128]{2,1,0:T(8,128)(2,1)S(1)}, u32[]{:S(2)}, u32[]{:S(2)}) collective-permute-start(bf16[4,160,128]{2,1,0:T(8,128)(2,1)S(1)} %get-tuple-element.100), channel_id=1, source_target_pairs={{0,1},{1,0},{2,3},{3,2},{4,5},{5,4},{6,7},{7,6},{8,9},{9,8},{10,11... | collective-permute-start | bytes 491528 | tf_op jit(solution)/shard_map/ppermute | solution.py:431
  8.3 0.4 shard_map.147
  8.7 0.6 collective-permute-done.1.near
  9.4 2.5 %collective-permute-start.2 = (bf16[2,160,128]{2,1,0:T(8,128)(2,1)S(1)}, bf16[2,160,128]{2,1,0:T(8,128)(2,1)S(1)}, u32[]{:S(2)}, u32[]{:S(2)}) collective-permute-start(bf16[2,160,128]{2,1,0:T(8,128)(2,1)S(1)} %get-tuple-element.102), channel_id=1, source_target_pairs={{0,2},{1,3},{2,0},{3,1},{4,6},{5,7},{6,4},{7,5},{8,10},{9,11},{10,... | collective-permute-start | bytes 245768 | tf_op jit(solution)/shard_map/ppermute | solution.py:431
  11.9 0.5 shard_map.144
  12.3 2.3 %shard_map.148.local = f32[512,512]{1,0:T(8,128)S(1)} custom-call(bf16[512,128]{1,0:T(8,128)(2,1)S(1)} %get-tuple-element.85.q_ref, bf16[512,128]{1,0:T(8,128)(2,1)S(1)} %get-tuple-element.91.k_ref, bf16[512,512]{1,0:T(8,128)(2,1)S(1)} %get-tuple-element.97.v_ref.v), custom_call_target="tpu_custom_call" | custom-call | flops 536870912 | bytes 1835008 | tf_op jit(solution)/shard_map/pallas_call | solution.py:419
  14.7 2.7 %collective-permute-start.3 = (bf16[2,160,128]{2,1,0:T(8,128)(2,1)S(1)}, bf16[2,160,128]{2,1,0:T(8,128)(2,1)S(1)}, u32[]{:S(2)}, u32[]{:S(2)}) collective-permute-start(bf16[2,160,128]{2,1,0:T(8,128)(2,1)S(1)} %shard_map.150), channel_id=1, source_target_pairs={{0,4},{1,5},{2,6},{3,7},{4,0},{5,1},{6,2},{7,3},{8,12},{9,13},{10,... | collective-permute-start | bytes 245768 | tf_op jit(solution)/shard_map/ppermute | solution.py:431
  17.4 2.3 %shard_map.152.local = f32[512,512]{1,0:T(8,128)S(1)} custom-call(bf16[512,128]{1,0:T(8,128)(2,1)S(1)} %get-tuple-element.85.q_ref, bf16[512,128]{1,0:T(8,128)(2,1)S(1)} %get-tuple-element.91.k_ref, bf16[512,512]{1,0:T(8,128)(2,1)S(1)} %get-tuple-element.104.v_ref.v), custom_call_target="tpu_custom_call" | custom-call | flops 536870912 | bytes 1835008 | tf_op jit(solution)/shard_map/pallas_call | solution.py:419
  19.7 0.1 collective-permute-done.3.refs_1_.rest_0_
  19.8 3.1 %collective-permute-start.4 = (bf16[2,160,128]{2,1,0:T(8,128)(2,1)S(1)}, bf16[2,160,128]{2,1,0:T(8,128)(2,1)S(1)}, u32[]{:S(2)}, u32[]{:S(2)}) collective-permute-start(bf16[2,160,128]{2,1,0:T(8,128)(2,1)S(1)} %shard_map.151), channel_id=1, source_target_pairs={{0,8},{1,9},{2,10},{3,11},{4,12},{5,13},{6,14},{7,15},{8,0},{9,1},... | collective-permute-start | bytes 245768 | tf_op jit(solution)/shard_map/ppermute | solution.py:431
  22.9 2.4 %collective-permute-done.4.rest_1_ = bf16[2,160,128]{2,1,0:T(8,128)(2,1)S(1)} collective-permute-done((bf16[2,160,128]{2,1,0:T(8,128)(2,1)S(1)}, bf16[2,160,128]{2,1,0:T(8,128)(2,1)S(1)}, u32[]{:S(2)}, u32[]{:S(2)}) %collective-permute-start.4) | collective-permute-done | bytes 81952 | tf_op jit(solution)/shard_map/ppermute | solution.py:431
  25.4 1.0 %collective-permute-start.5 = (bf16[2,160,128]{2,1,0:T(8,128)(2,1)S(1)}, bf16[2,160,128]{2,1,0:T(8,128)(2,1)S(1)}, u32[]{:S(2)}, u32[]{:S(2)}) collective-permute-start(bf16[2,160,128]{2,1,0:T(8,128)(2,1)S(1)} %get-tuple-element.107), channel_id=1, source_target_pairs={{0,2},{1,3},{2,0},{3,1},{4,6},{5,7},{6,4},{7,5},{8,10},{9,11},{10,... | collective-permute-start | bytes 245768 | tf_op jit(solution)/shard_map/ppermute | solution.py:431
  26.5 3.5 %collective-permute-done.5.other_part = bf16[2,160,128]{2,1,0:T(8,128)(2,1)S(1)} collective-permute-done((bf16[2,160,128]{2,1,0:T(8,128)(2,1)S(1)}, bf16[2,160,128]{2,1,0:T(8,128)(2,1)S(1)}, u32[]{:S(2)}, u32[]{:S(2)}) %collective-permute-start.5) | collective-permute-done | bytes 81952 | tf_op jit(solution)/shard_map/ppermute | solution.py:431
  29.9 0.1 shard_map.154
  30.0 0.1 collective-permute-start.6
  30.1 1.4 %shard_map.155 = (bf16[512,512]{1,0:T(8,128)(2,1)S(1)}, bf16[512,512]{1,0:T(8,128)(2,1)S(1)}, bf16[4,160,128]{2,1,0:T(8,128)(2,1)S(1)}, f32[4,128]{1,0:T(4,128)S(1)}) custom-call(f32[512,512]{1,0:T(8,128)S(1)} %shard_map.148.local, bf16[8,160,512]{2,1,0:T(8,128)(2,1)S(1)} %get-tuple-element.98.fq, bf16[4,160,128]{2,1,0:T(8,128)(2,1)S(1)} %get-tuple-element.108.prefix.pre_a, ...), custom_call_target="tpu_custom_call" | custom-call | flops 167772160 | bytes 4790272 | tf_op jit(solution)/shard_map/pallas_call | solution.py:419
  31.5 0.5 collective-permute-start.7
  32.0 1.5 %shard_map.156 = (bf16[512,1024]{1,0:T(8,128)(2,1)S(1)}, bf16[512,512]{1,0:T(8,128)(2,1)S(1)}, bf16[4,160,128]{2,1,0:T(8,128)(2,1)S(1)}, f32[4,128]{1,0:T(4,128)S(1)}) custom-call(f32[512,512]{1,0:T(8,128)S(1)} %shard_map.152.local, bf16[8,160,512]{2,1,0:T(8,128)(2,1)S(1)} %get-tuple-element.98.fq, ...), custom_call_target="tpu_custom_call" | custom-call | flops 167772160 | bytes 5838848 | tf_op jit(solution)/shard_map/pallas_call | solution.py:419
  33.6 1.0 %collective-permute-start.8 = (bf16[2,160,128]{2,1,0:T(8,128)(2,1)S(1)}, bf16[2,160,128]{2,1,0:T(8,128)(2,1)S(1)}, u32[]{:S(2)}, u32[]{:S(2)}) collective-permute-start(bf16[2,160,128]{2,1,0:T(8,128)(2,1)S(1)} %get-tuple-element.125), channel_id=1, source_target_pairs={{0,2},{1,3},{2,0},{3,1},{4,6},{5,7},{6,4},{7,5},{8,10},{9,11},{10,... | collective-permute-start | bytes 245768 | tf_op jit(solution)/shard_map/ppermute | solution.py:431
  34.6 3.1 %shard_map.157 = (f32[512,256]{1,0:T(8,128)S(1)}, f32[32,512]{1,0:T(8,128)S(1)}, f32[32,512]{1,0:T(8,128)S(1)}, bf16[512,1024]{1,0:T(8,128)(2,1)}) custom-call(bf16[512,128]{1,0:T(8,128)(2,1)S(1)} %get-tuple-element.85.q_ref, bf16[512,128]{1,0:T(8,128)(2,1)S(1)} %get-tuple-element.91.k_ref, bf16[128,512]{1,0:T(8,128)(2,1)S(1)} %get-tuple-element.92.qt_ref, ...), custom_call_target="tpu_custom_call" | custom-call | flops 536870912 | bytes 4325376 | tf_op jit(solution)/shard_map/pallas_call | solution.py:419
  37.7 0.3 collective-permute-done.8.refs_0_.got_y
  38.1 2.0 %collective-permute-start.9 = (bf16[2,160,128]{2,1,0:T(8,128)(2,1)S(1)}, bf16[2,160,128]{2,1,0:T(8,128)(2,1)S(1)}, u32[]{:S(2)}, u32[]{:S(2)}) collective-permute-start(bf16[2,160,128]{2,1,0:T(8,128)(2,1)S(1)} %shard_map.163), channel_id=1, source_target_pairs={{0,4},{1,5},{2,6},{3,7},{4,0},{5,1},{6,2},{7,3},{8,12},{9,13},{10,... | collective-permute-start | bytes 245768 | tf_op jit(solution)/shard_map/ppermute | solution.py:431
  40.1 2.5 %shard_map.158 = (f32[512,256]{1,0:T(8,128)S(1)}, f32[32,512]{1,0:T(8,128)S(1)}, f32[32,512]{1,0:T(8,128)S(1)}) custom-call(bf16[512,128]{1,0:T(8,128)(2,1)S(1)} %get-tuple-element.85.q_ref, bf16[512,128]{1,0:T(8,128)(2,1)S(1)} %get-tuple-element.91.k_ref, bf16[128,512]{1,0:T(8,128)(2,1)S(1)} %get-tuple-element.92.qt_ref, ...), custom_call_target="tpu_custom_call" | custom-call | flops 536870912 | bytes 2228224 | tf_op jit(solution)/shard_map/pallas_call | solution.py:419
  42.6 3.4 %collective-permute-start.10 = (bf16[2,160,128]{2,1,0:T(8,128)(2,1)S(1)}, bf16[2,160,128]{2,1,0:T(8,128)(2,1)S(1)}, u32[]{:S(2)}, u32[]{:S(2)}) collective-permute-start(bf16[2,160,128]{2,1,0:T(8,128)(2,1)S(1)} %shard_map.164), channel_id=1, source_target_pairs={{0,8},{1,9},{2,10},{3,11},{4,12},{5,13},{6,14},{7,15},{8,0},{9,1},... | collective-permute-start | bytes 245768 | tf_op jit(solution)/shard_map/ppermute | solution.py:431
  46.1 2.7 %shard_map.159 = (f32[512,256]{1,0:T(8,128)S(1)}, f32[32,512]{1,0:T(8,128)S(1)}, f32[32,512]{1,0:T(8,128)S(1)}) custom-call(bf16[512,128]{1,0:T(8,128)(2,1)S(1)} %get-tuple-element.85.q_ref, bf16[512,128]{1,0:T(8,128)(2,1)S(1)} %get-tuple-element.91.k_ref, bf16[128,512]{1,0:T(8,128)(2,1)S(1)} %get-tuple-element.92.qt_ref, ...), custom_call_target="tpu_custom_call" | custom-call | flops 536870912 | bytes 2228224 | tf_op jit(solution)/shard_map/pallas_call | solution.py:419
  48.8 0.1 shard_map.165
  48.8 1.1 %collective-permute-start.11 = (bf16[2,160,128]{2,1,0:T(8,128)(2,1)S(1)}, bf16[2,160,128]{2,1,0:T(8,128)(2,1)S(1)}, u32[]{:S(2)}, u32[]{:S(2)}) collective-permute-start(bf16[2,160,128]{2,1,0:T(8,128)(2,1)S(1)} %get-tuple-element.133), channel_id=1, source_target_pairs={{0,2},{1,3},{2,0},{3,1},{4,6},{5,7},{6,4},{7,5},{8,10},{9,11},{10,... | collective-permute-start | bytes 245768 | tf_op jit(solution)/shard_map/ppermute | solution.py:431
  49.9 2.5 %shard_map.160 = (f32[512,256]{1,0:T(8,128)S(1)}, f32[32,512]{1,0:T(8,128)S(1)}, f32[32,512]{1,0:T(8,128)S(1)}) custom-call(bf16[512,128]{1,0:T(8,128)(2,1)S(1)} %get-tuple-element.85.q_ref, bf16[512,128]{1,0:T(8,128)(2,1)S(1)} %get-tuple-element.91.k_ref, bf16[128,512]{1,0:T(8,128)(2,1)S(1)} %get-tuple-element.92.qt_ref, ...), custom_call_target="tpu_custom_call" | custom-call | flops 536870912 | bytes 2228224 | tf_op jit(solution)/shard_map/pallas_call | solution.py:419
  52.4 0.9 %shard_map.161 = (f32[512,128]{1,0:T(8,128)S(1)}, f32[3,128]{1,0:T(4,128)S(1)}) custom-call(bf16[512,128]{1,0:T(8,128)(2,1)S(1)} %copy-done.3, bf16[16,1280]{1,0:T(8,128)(2,1)S(1)} %collective-permute-done.rim, bf16[128,512]{1,0:T(8,128)(2,1)S(1)} %get-tuple-element.92.qt_ref, bf16[512,512]{1,0:T(8,128)(2,1)S(1)} %get-tuple-element.109.gs_ref.gs_a, ...), custom_call_target="tpu_custom_call" | custom-call | flops 83886080 | bytes 2206720 | tf_op jit(solution)/shard_map/pallas_call | solution.py:419
  53.4 0.1 shard_map.166
  53.5 0.1 collective-permute-start.12
  53.5 1.1 %shard_map.167 = (f32[512,512]{1,0:T(8,128)S(1)}, f32[64,512]{1,0:T(8,128)S(1)}, f32[3,512]{1,0:T(4,128)S(1)}) custom-call(bf16[512,1024]{1,0:T(8,128)(2,1)S(1)} %copy-done, bf16[16,1280]{1,0:T(8,128)(2,1)S(1)} %collective-permute-done.rim, bf16[128,512]{1,0:T(8,128)(2,1)S(1)} %get-tuple-element.93.kt.kt_ref, ...), custom_call_target="tpu_custom_call" | custom-call | flops 167772160 | bytes 4929536 | tf_op jit(solution)/shard_map/pallas_call | solution.py:419
  54.6 0.3 collective-permute-done.12.state
  54.9 1.1 %shard_map.168 = (f32[512,512]{1,0:T(8,128)S(1)}, f32[512,128]{1,0:T(8,128)S(1)}, f32[8,1280]{1,0:T(8,128)S(1)}, f32[4,1280]{1,0:T(4,128)S(1)}) custom-call(bf16[512,128]{1,0:T(8,128)(2,1)S(1)} %copy-done.2, bf16[512,1024]{1,0:T(8,128)(2,1)S(1)} %copy-done, bf16[16,1280]{1,0:T(8,128)(2,1)S(1)} %collective-permute-done.rim, ...), custom_call_target="tpu_custom_call" | custom-call | flops 167772160 | bytes 6700544 | tf_op jit(solution)/shard_map/pallas_call | solution.py:419
  56.0 4.5 %collective-permute-start.16 = (f32[4,1280]{1,0:T(4,128)S(1)}, f32[4,1280]{1,0:T(4,128)S(1)}, u32[]{:S(2)}, u32[]{:S(2)}) collective-permute-start(f32[4,1280]{1,0:T(4,128)S(1)} %get-tuple-element.156), channel_id=1, source_target_pairs={{0,12},{1,13},{2,14},{3,15},{4,8},{5,9},{6,10},{7,11},{8,4},{9,5},... | collective-permute-start | bytes 61448 | tf_op jit(solution)/shard_map/ppermute | solution.py:431
  60.5 0.6 collective-permute-start.14
  61.1 1.3 %collective-permute-start.13 = (f32[8,1280]{1,0:T(8,128)S(1)}, f32[8,1280]{1,0:T(8,128)S(1)}, u32[]{:S(2)}, u32[]{:S(2)}) collective-permute-start(f32[8,1280]{1,0:T(8,128)S(1)} %get-tuple-element.152), channel_id=1, source_target_pairs={{1,0},{2,1},{3,2},{4,3},{5,4},{6,5},{7,6},{8,7},{9,8},{10,9},{11,1... | collective-permute-start | bytes 122888 | tf_op jit(solution)/shard_map/ppermute | solution.py:673
  62.4 2.7 %collective-permute-done.15 = f32[4,1280]{1,0:T(4,128)S(1)} collective-permute-done((f32[4,1280]{1,0:T(4,128)S(1)}, f32[4,1280]{1,0:T(4,128)S(1)}, u32[]{:S(2)}, u32[]{:S(2)}) %collective-permute-start.15) | collective-permute-done | bytes 20512 | tf_op jit(solution)/shard_map/ppermute | solution.py:431
  65.2 0.1 collective-permute-start.17
  65.3 1.1 %collective-permute-start.18 = (f32[4,1280]{1,0:T(4,128)S(1)}, f32[4,1280]{1,0:T(4,128)S(1)}, u32[]{:S(2)}, u32[]{:S(2)}) collective-permute-start(f32[4,1280]{1,0:T(4,128)S(1)} %add_add_fusion.refs_0_), channel_id=1, source_target_pairs={{0,2},{1,3},{2,0},{3,1},{4,6},{5,7},{6,4},{7,5},{8,10},{9,11},{10,... | collective-permute-start | bytes 61448 | tf_op jit(solution)/shard_map/ppermute | solution.py:431
  66.4 0.8 %collective-permute-start.19 = (f32[4,1280]{1,0:T(4,128)S(1)}, f32[4,1280]{1,0:T(4,128)S(1)}, u32[]{:S(2)}, u32[]{:S(2)}) collective-permute-start(f32[4,1280]{1,0:T(4,128)S(1)} %add_add_fusion.refs_0_), channel_id=1, source_target_pairs={{0,1},{1,0},{2,3},{3,2},{4,5},{5,4},{6,7},{7,6},{8,9},{9,8},{10,11... | collective-permute-start | bytes 61448 | tf_op jit(solution)/shard_map/ppermute | solution.py:431
  67.1 1.9 %shard_map.169 = (bf16[512,128]{1,0:T(8,128)(2,1)}, bf16[512,128]{1,0:T(8,128)(2,1)}, bf16[512,1024]{1,0:T(8,128)(2,1)}) custom-call(f32[512,128]{1,0:T(8,128)S(1)} %get-tuple-element.120.gq, f32[512,128]{1,0:T(8,128)S(1)} %get-tuple-element.150.gk, f32[512,512]{1,0:T(8,128)S(1)} %get-tuple-element.151.gv_a, f32[512,512]{1,0:T(8,128)S(1)} %get-tuple-element.141.gv_b, ...), custom_call_target="tpu_custom_call" | custom-call | flops 167772160 | bytes 3988480 | tf_op jit(solution)/shard_map/pallas_call | solution.py:419
  69.0 0.2 collective-permute-done.18.refs_2_
  69.3 0.6 shard_map.170
  (37 shorter events, 0.4 us)
Async XLA Ops:
  0.6 3.3 %copy-start.2 = (bf16[512,128]{1,0:T(8,128)(2,1)S(1)}, bf16[512,128]{1,0:T(8,128)(2,1)}, u32[]{:S(2)}) copy-start(bf16[512,128]{1,0:T(8,128)(2,1)} %key.7) | copy-start | bytes 393220
  0.6 3.3 %copy-start = (bf16[512,1024]{1,0:T(8,128)(2,1)S(1)}, bf16[512,1024]{1,0:T(8,128)(2,1)}, u32[]{:S(2)}) copy-start(bf16[512,1024]{1,0:T(8,128)(2,1)} %value.11) | copy-start | bytes 3145732
  0.7 3.3 %copy-start.5 = (f32[3,128]{1,0:T(4,128)S(1)}, f32[3,128]{1,0:T(4,128)}, u32[]{:S(2)}) copy-start(f32[3,128]{1,0:T(4,128)} %taps_k.5) | copy-start | bytes 4612
  0.7 3.3 %copy-start.4 = (f32[3,1024]{1,0:T(4,128)S(1)}, f32[3,1024]{1,0:T(4,128)}, u32[]{:S(2)}) copy-start(f32[3,1024]{1,0:T(4,128)} %taps_v.7) | copy-start | bytes 36868
  1.6 3.6 %collective-permute-start = (bf16[16,1280]{1,0:T(8,128)(2,1)S(1)}, bf16[16,1280]{1,0:T(8,128)(2,1)S(1)}, u32[]{:S(2)}, u32[]{:S(2)}) collective-permute-start(bf16[16,1280]{1,0:T(8,128)(2,1)S(1)} %shard_map.143), channel_id=1, source_target_pairs={{0,1},{1,2},{2,3},{3,4},{4,5},{5,6},{6,7},{7,8},{8,9},{9,10},{10,1... | collective-permute-start | bytes 122888 | tf_op jit(solution)/shard_map/ppermute | solution.py:542
  5.6 3.7 %collective-permute-start.1 = (bf16[4,160,128]{2,1,0:T(8,128)(2,1)S(1)}, bf16[4,160,128]{2,1,0:T(8,128)(2,1)S(1)}, u32[]{:S(2)}, u32[]{:S(2)}) collective-permute-start(bf16[4,160,128]{2,1,0:T(8,128)(2,1)S(1)} %get-tuple-element.100), channel_id=1, source_target_pairs={{0,1},{1,0},{2,3},{3,2},{4,5},{5,4},{6,7},{7,6},{8,9},{9,8},{10,11... | collective-permute-start | bytes 491528 | tf_op jit(solution)/shard_map/ppermute | solution.py:431
  8.3 3.5 %copy-start.3 = (bf16[512,128]{1,0:T(8,128)(2,1)S(1)}, bf16[512,128]{1,0:T(8,128)(2,1)}, u32[]{:S(2)}) copy-start(bf16[512,128]{1,0:T(8,128)(2,1)} %query.5) | copy-start | bytes 393220
  8.3 3.5 %copy-start.7 = (f32[3,128]{1,0:T(4,128)S(1)}, f32[3,128]{1,0:T(4,128)}, u32[]{:S(2)}) copy-start(f32[3,128]{1,0:T(4,128)} %taps_q.5) | copy-start | bytes 4612
  9.4 5.3 %collective-permute-start.2 = (bf16[2,160,128]{2,1,0:T(8,128)(2,1)S(1)}, bf16[2,160,128]{2,1,0:T(8,128)(2,1)S(1)}, u32[]{:S(2)}, u32[]{:S(2)}) collective-permute-start(bf16[2,160,128]{2,1,0:T(8,128)(2,1)S(1)} %get-tuple-element.102), channel_id=1, source_target_pairs={{0,2},{1,3},{2,0},{3,1},{4,6},{5,7},{6,4},{7,5},{8,10},{9,11},{10,... | collective-permute-start | bytes 245768 | tf_op jit(solution)/shard_map/ppermute | solution.py:431
  14.7 5.1 %collective-permute-start.3 = (bf16[2,160,128]{2,1,0:T(8,128)(2,1)S(1)}, bf16[2,160,128]{2,1,0:T(8,128)(2,1)S(1)}, u32[]{:S(2)}, u32[]{:S(2)}) collective-permute-start(bf16[2,160,128]{2,1,0:T(8,128)(2,1)S(1)} %shard_map.150), channel_id=1, source_target_pairs={{0,4},{1,5},{2,6},{3,7},{4,0},{5,1},{6,2},{7,3},{8,12},{9,13},{10,... | collective-permute-start | bytes 245768 | tf_op jit(solution)/shard_map/ppermute | solution.py:431
  17.4 12.7 %copy-start.1 = (bf16[512,1024]{1,0:T(8,128)(2,1)S(1)}, bf16[512,1024]{1,0:T(8,128)(2,1)}, u32[]{:S(2)}) copy-start(bf16[512,1024]{1,0:T(8,128)(2,1)} %grad.3) | copy-start | bytes 3145732
  17.4 12.7 %copy-start.6 = (f32[1024]{0:T(1024)S(1)}, f32[1024]{0:T(1024)}, u32[]{:S(2)}) copy-start(f32[1024]{0:T(1024)} %param.14) | copy-start | bytes 12292
  19.8 5.5 %collective-permute-start.4 = (bf16[2,160,128]{2,1,0:T(8,128)(2,1)S(1)}, bf16[2,160,128]{2,1,0:T(8,128)(2,1)S(1)}, u32[]{:S(2)}, u32[]{:S(2)}) collective-permute-start(bf16[2,160,128]{2,1,0:T(8,128)(2,1)S(1)} %shard_map.151), channel_id=1, source_target_pairs={{0,8},{1,9},{2,10},{3,11},{4,12},{5,13},{6,14},{7,15},{8,0},{9,1},... | collective-permute-start | bytes 245768 | tf_op jit(solution)/shard_map/ppermute | solution.py:431
  25.4 4.5 %collective-permute-start.5 = (bf16[2,160,128]{2,1,0:T(8,128)(2,1)S(1)}, bf16[2,160,128]{2,1,0:T(8,128)(2,1)S(1)}, u32[]{:S(2)}, u32[]{:S(2)}) collective-permute-start(bf16[2,160,128]{2,1,0:T(8,128)(2,1)S(1)} %get-tuple-element.107), channel_id=1, source_target_pairs={{0,2},{1,3},{2,0},{3,1},{4,6},{5,7},{6,4},{7,5},{8,10},{9,11},{10,... | collective-permute-start | bytes 245768 | tf_op jit(solution)/shard_map/ppermute | solution.py:431
  30.0 2.0 %collective-permute-start.6 = (bf16[4,160,128]{2,1,0:T(8,128)(2,1)S(1)}, bf16[4,160,128]{2,1,0:T(8,128)(2,1)S(1)}, u32[]{:S(2)}, u32[]{:S(2)}) collective-permute-start(bf16[4,160,128]{2,1,0:T(8,128)(2,1)S(1)} %get-tuple-element.110), channel_id=1, source_target_pairs={{0,1},{1,0},{2,3},{3,2},{4,5},{5,4},{6,7},{7,6},{8,9},{9,8},{10,11... | collective-permute-start | bytes 491528 | tf_op jit(solution)/shard_map/ppermute | solution.py:431
  31.5 2.0 %collective-permute-start.7 = (bf16[4,160,128]{2,1,0:T(8,128)(2,1)S(1)}, bf16[4,160,128]{2,1,0:T(8,128)(2,1)S(1)}, u32[]{:S(2)}, u32[]{:S(2)}) collective-permute-start(bf16[4,160,128]{2,1,0:T(8,128)(2,1)S(1)} %get-tuple-element.123), channel_id=1, source_target_pairs={{0,1},{1,0},{2,3},{3,2},{4,5},{5,4},{6,7},{7,6},{8,9},{9,8},{10,11... | collective-permute-start | bytes 491528 | tf_op jit(solution)/shard_map/ppermute | solution.py:431
  33.6 4.5 %collective-permute-start.8 = (bf16[2,160,128]{2,1,0:T(8,128)(2,1)S(1)}, bf16[2,160,128]{2,1,0:T(8,128)(2,1)S(1)}, u32[]{:S(2)}, u32[]{:S(2)}) collective-permute-start(bf16[2,160,128]{2,1,0:T(8,128)(2,1)S(1)} %get-tuple-element.125), channel_id=1, source_target_pairs={{0,2},{1,3},{2,0},{3,1},{4,6},{5,7},{6,4},{7,5},{8,10},{9,11},{10,... | collective-permute-start | bytes 245768 | tf_op jit(solution)/shard_map/ppermute | solution.py:431
  38.1 4.5 %collective-permute-start.9 = (bf16[2,160,128]{2,1,0:T(8,128)(2,1)S(1)}, bf16[2,160,128]{2,1,0:T(8,128)(2,1)S(1)}, u32[]{:S(2)}, u32[]{:S(2)}) collective-permute-start(bf16[2,160,128]{2,1,0:T(8,128)(2,1)S(1)} %shard_map.163), channel_id=1, source_target_pairs={{0,4},{1,5},{2,6},{3,7},{4,0},{5,1},{6,2},{7,3},{8,12},{9,13},{10,... | collective-permute-start | bytes 245768 | tf_op jit(solution)/shard_map/ppermute | solution.py:431
  42.6 6.1 %collective-permute-start.10 = (bf16[2,160,128]{2,1,0:T(8,128)(2,1)S(1)}, bf16[2,160,128]{2,1,0:T(8,128)(2,1)S(1)}, u32[]{:S(2)}, u32[]{:S(2)}) collective-permute-start(bf16[2,160,128]{2,1,0:T(8,128)(2,1)S(1)} %shard_map.164), channel_id=1, source_target_pairs={{0,8},{1,9},{2,10},{3,11},{4,12},{5,13},{6,14},{7,15},{8,0},{9,1},... | collective-permute-start | bytes 245768 | tf_op jit(solution)/shard_map/ppermute | solution.py:431
  48.8 4.5 %collective-permute-start.11 = (bf16[2,160,128]{2,1,0:T(8,128)(2,1)S(1)}, bf16[2,160,128]{2,1,0:T(8,128)(2,1)S(1)}, u32[]{:S(2)}, u32[]{:S(2)}) collective-permute-start(bf16[2,160,128]{2,1,0:T(8,128)(2,1)S(1)} %get-tuple-element.133), channel_id=1, source_target_pairs={{0,2},{1,3},{2,0},{3,1},{4,6},{5,7},{6,4},{7,5},{8,10},{9,11},{10,... | collective-permute-start | bytes 245768 | tf_op jit(solution)/shard_map/ppermute | solution.py:431
  53.5 1.5 %collective-permute-start.12 = (bf16[4,160,128]{2,1,0:T(8,128)(2,1)S(1)}, bf16[4,160,128]{2,1,0:T(8,128)(2,1)S(1)}, u32[]{:S(2)}, u32[]{:S(2)}) collective-permute-start(bf16[4,160,128]{2,1,0:T(8,128)(2,1)S(1)} %get-tuple-element.136), channel_id=1, source_target_pairs={{0,1},{1,0},{2,3},{3,2},{4,5},{5,4},{6,7},{7,6},{8,9},{9,8},{10,11... | collective-permute-start | bytes 491528 | tf_op jit(solution)/shard_map/ppermute | solution.py:431
  56.0 6.4 %collective-permute-start.16 = (f32[4,1280]{1,0:T(4,128)S(1)}, f32[4,1280]{1,0:T(4,128)S(1)}, u32[]{:S(2)}, u32[]{:S(2)}) collective-permute-start(f32[4,1280]{1,0:T(4,128)S(1)} %get-tuple-element.156), channel_id=1, source_target_pairs={{0,12},{1,13},{2,14},{3,15},{4,8},{5,9},{6,10},{7,11},{8,4},{9,5},... | collective-permute-start | bytes 61448 | tf_op jit(solution)/shard_map/ppermute | solution.py:431
  60.5 4.7 %collective-permute-start.15 = (f32[4,1280]{1,0:T(4,128)S(1)}, f32[4,1280]{1,0:T(4,128)S(1)}, u32[]{:S(2)}, u32[]{:S(2)}) collective-permute-start(f32[4,1280]{1,0:T(4,128)S(1)} %get-tuple-element.156), channel_id=1, source_target_pairs={{0,8},{1,9},{2,10},{3,11},{4,12},{5,13},{6,14},{7,15},{8,0},{9,1},... | collective-permute-start | bytes 61448 | tf_op jit(solution)/shard_map/ppermute | solution.py:431
  60.5 4.7 %collective-permute-start.14 = (f32[4,1280]{1,0:T(4,128)S(1)}, f32[4,1280]{1,0:T(4,128)S(1)}, u32[]{:S(2)}, u32[]{:S(2)}) collective-permute-start(f32[4,1280]{1,0:T(4,128)S(1)} %get-tuple-element.156), channel_id=1, source_target_pairs={{0,4},{1,5},{2,6},{3,7},{4,0},{5,1},{6,2},{7,3},{8,12},{9,13},{10,... | collective-permute-start | bytes 61448 | tf_op jit(solution)/shard_map/ppermute | solution.py:431
  61.1 6.0 %collective-permute-start.13 = (f32[8,1280]{1,0:T(8,128)S(1)}, f32[8,1280]{1,0:T(8,128)S(1)}, u32[]{:S(2)}, u32[]{:S(2)}) collective-permute-start(f32[8,1280]{1,0:T(8,128)S(1)} %get-tuple-element.152), channel_id=1, source_target_pairs={{1,0},{2,1},{3,2},{4,3},{5,4},{6,5},{7,6},{8,7},{9,8},{10,9},{11,1... | collective-permute-start | bytes 122888 | tf_op jit(solution)/shard_map/ppermute | solution.py:673
  65.2 3.8 %collective-permute-start.17 = (f32[4,1280]{1,0:T(4,128)S(1)}, f32[4,1280]{1,0:T(4,128)S(1)}, u32[]{:S(2)}, u32[]{:S(2)}) collective-permute-start(f32[4,1280]{1,0:T(4,128)S(1)} %add_add_fusion.refs_0_), channel_id=1, source_target_pairs={{0,3},{1,2},{2,1},{3,0},{4,7},{5,6},{6,5},{7,4},{8,11},{9,10},{10,... | collective-permute-start | bytes 61448 | tf_op jit(solution)/shard_map/ppermute | solution.py:431
  65.3 4.0 %collective-permute-start.18 = (f32[4,1280]{1,0:T(4,128)S(1)}, f32[4,1280]{1,0:T(4,128)S(1)}, u32[]{:S(2)}, u32[]{:S(2)}) collective-permute-start(f32[4,1280]{1,0:T(4,128)S(1)} %add_add_fusion.refs_0_), channel_id=1, source_target_pairs={{0,2},{1,3},{2,0},{3,1},{4,6},{5,7},{6,4},{7,5},{8,10},{9,11},{10,... | collective-permute-start | bytes 61448 | tf_op jit(solution)/shard_map/ppermute | solution.py:431
  66.4 2.9 %collective-permute-start.19 = (f32[4,1280]{1,0:T(4,128)S(1)}, f32[4,1280]{1,0:T(4,128)S(1)}, u32[]{:S(2)}, u32[]{:S(2)}) collective-permute-start(f32[4,1280]{1,0:T(4,128)S(1)} %add_add_fusion.refs_0_), channel_id=1, source_target_pairs={{0,1},{1,0},{2,3},{3,2},{4,5},{5,4},{6,7},{7,6},{8,9},{9,8},{10,11... | collective-permute-start | bytes 61448 | tf_op jit(solution)/shard_map/ppermute | solution.py:431

commit v8 on v7

--- a/solution.py
+++ b/solution.py
@@ -673,7 +673,7 @@
     follow = lax.ppermute(heads, "seq", [(i + 1, i) for i in range(count - 1)])
     bit = 4
     while bit < count:
-        group = (bit, 2 * bit, 3 * bit) if 2 * bit < count else (bit,)
+        group = (bit, 3 * bit, 2 * bit) if 2 * bit < count else (bit,)
         for got in [exchange(sums, distance) for distance in group]:
             sums = sums + got
         bit *= len(group) + 1

time: 70.1 us -> 69.5 us (level)
  no operation moved by 1% of the time
where the time goes in v8:
time: 69.5 us; the launch traced here: 69.3 us
  starting transfers between devices  30.8 us (44%)
  Pallas kernels  27.7 us (40%)
  waiting for transfers between devices  9.8 us (14%)
  between operations  0.95 us (1%)
    pallas_call x28, Pallas kernels, call(): pl.pallas_call(kernel, out_shape=[o if i in loose else pltpu.VMEM(o.shape...  27.7 us
    ppermute x18, starting transfers between devices, exchange(): return lax.ppermute(x, 'seq', [(i, i ^ distance) for i in range(count)])  27.1 us
    ppermute x18, waiting for transfers between devices, exchange(): return lax.ppermute(x, 'seq', [(i, i ^ distance) for i in range(count)])  9.8 us
    ppermute x1, starting transfers between devices, shards(): rim = lax.ppermute(ends, 'seq', [(i, i + 1) for i in range(count - 1)])  2.36 us
  transfers between devices with their start and end apart: 20, of which 8 were waited for; matrix products, arithmetic and copies ran while one was open for 0% of the time, Pallas kernels for 35%

profile of v8, /device:TPU:0, one launch (start us, length us, event | category | flops | bytes accessed | tf_op | source)
XLA Modules:
  0.0 69.3 jit_solution(8037769582207442073)
XLA Ops:
  0.7 0.9 %shard_map.143 = bf16[16,1280]{1,0:T(8,128)(2,1)S(1)} custom-call(bf16[512,128]{1,0:T(8,128)(2,1)} %query.5, bf16[512,128]{1,0:T(8,128)(2,1)} %key.7, bf16[512,1024]{1,0:T(8,128)(2,1)} %value.11), custom_call_target="tpu_custom_call" | custom-call | flops 512 | bytes 1351680 | tf_op jit(solution)/shard_map/pallas_call | solution.py:419
  1.6 2.4 %collective-permute-start = (bf16[16,1280]{1,0:T(8,128)(2,1)S(1)}, bf16[16,1280]{1,0:T(8,128)(2,1)S(1)}, u32[]{:S(2)}, u32[]{:S(2)}) collective-permute-start(bf16[16,1280]{1,0:T(8,128)(2,1)S(1)} %shard_map.143), channel_id=1, source_target_pairs={{0,1},{1,2},{2,3},{3,4},{4,5},{5,6},{6,7},{7,8},{8,9},{9,10},{10,1... | collective-permute-start | bytes 122888 | tf_op jit(solution)/shard_map/ppermute | solution.py:542
  4.0 1.2 %shard_map.145 = (bf16[384,128]{1,0:T(8,128)(2,1)S(1)}, bf16[128,384]{1,0:T(8,128)(2,1)S(1)}, bf16[384,512]{1,0:T(8,128)(2,1)S(1)}, bf16[4,160,384]{2,1,0:T(8,12...) custom-call(bf16[512,128]{1,0:T(8,128)(2,1)S(1)} %copy-done.2, ...), custom_call_target="tpu_custom_call" | custom-call | flops 167772160 | bytes 3814912 | tf_op jit(solution)/shard_map/pallas_call | solution.py:419
  5.2 0.4 shard_map.146
  5.6 2.7 %collective-permute-start.1 = (bf16[4,160,128]{2,1,0:T(8,128)(2,1)S(1)}, bf16[4,160,128]{2,1,0:T(8,128)(2,1)S(1)}, u32[]{:S(2)}, u32[]{:S(2)}) collective-permute-start(bf16[4,160,128]{2,1,0:T(8,128)(2,1)S(1)} %get-tuple-element.100), channel_id=1, source_target_pairs={{0,1},{1,0},{2,3},{3,2},{4,5},{5,4},{6,7},{7,6},{8,9},{9,8},{10,11... | collective-permute-start | bytes 491528 | tf_op jit(solution)/shard_map/ppermute | solution.py:431
  8.3 0.4 shard_map.147
  8.7 0.6 collective-permute-done.1.near
  9.4 2.5 %collective-permute-start.2 = (bf16[2,160,128]{2,1,0:T(8,128)(2,1)S(1)}, bf16[2,160,128]{2,1,0:T(8,128)(2,1)S(1)}, u32[]{:S(2)}, u32[]{:S(2)}) collective-permute-start(bf16[2,160,128]{2,1,0:T(8,128)(2,1)S(1)} %get-tuple-element.102), channel_id=1, source_target_pairs={{0,2},{1,3},{2,0},{3,1},{4,6},{5,7},{6,4},{7,5},{8,10},{9,11},{10,... | collective-permute-start | bytes 245768 | tf_op jit(solution)/shard_map/ppermute | solution.py:431
  11.9 0.5 shard_map.144
  12.3 2.3 %shard_map.148.local = f32[512,512]{1,0:T(8,128)S(1)} custom-call(bf16[512,128]{1,0:T(8,128)(2,1)S(1)} %get-tuple-element.85.q_ref, bf16[512,128]{1,0:T(8,128)(2,1)S(1)} %get-tuple-element.91.k_ref, bf16[512,512]{1,0:T(8,128)(2,1)S(1)} %get-tuple-element.97.v_ref.v), custom_call_target="tpu_custom_call" | custom-call | flops 536870912 | bytes 1835008 | tf_op jit(solution)/shard_map/pallas_call | solution.py:419
  14.7 2.7 %collective-permute-start.3 = (bf16[2,160,128]{2,1,0:T(8,128)(2,1)S(1)}, bf16[2,160,128]{2,1,0:T(8,128)(2,1)S(1)}, u32[]{:S(2)}, u32[]{:S(2)}) collective-permute-start(bf16[2,160,128]{2,1,0:T(8,128)(2,1)S(1)} %shard_map.150), channel_id=1, source_target_pairs={{0,4},{1,5},{2,6},{3,7},{4,0},{5,1},{6,2},{7,3},{8,12},{9,13},{10,... | collective-permute-start | bytes 245768 | tf_op jit(solution)/shard_map/ppermute | solution.py:431
  17.4 2.3 %shard_map.152.local = f32[512,512]{1,0:T(8,128)S(1)} custom-call(bf16[512,128]{1,0:T(8,128)(2,1)S(1)} %get-tuple-element.85.q_ref, bf16[512,128]{1,0:T(8,128)(2,1)S(1)} %get-tuple-element.91.k_ref, bf16[512,512]{1,0:T(8,128)(2,1)S(1)} %get-tuple-element.104.v_ref.v), custom_call_target="tpu_custom_call" | custom-call | flops 536870912 | bytes 1835008 | tf_op jit(solution)/shard_map/pallas_call | solution.py:419
  19.7 0.1 collective-permute-done.3.refs_1_.rest_0_
  19.8 3.1 %collective-permute-start.4 = (bf16[2,160,128]{2,1,0:T(8,128)(2,1)S(1)}, bf16[2,160,128]{2,1,0:T(8,128)(2,1)S(1)}, u32[]{:S(2)}, u32[]{:S(2)}) collective-permute-start(bf16[2,160,128]{2,1,0:T(8,128)(2,1)S(1)} %shard_map.151), channel_id=1, source_target_pairs={{0,8},{1,9},{2,10},{3,11},{4,12},{5,13},{6,14},{7,15},{8,0},{9,1},... | collective-permute-start | bytes 245768 | tf_op jit(solution)/shard_map/ppermute | solution.py:431
  22.9 2.4 %collective-permute-done.4.rest_1_ = bf16[2,160,128]{2,1,0:T(8,128)(2,1)S(1)} collective-permute-done((bf16[2,160,128]{2,1,0:T(8,128)(2,1)S(1)}, bf16[2,160,128]{2,1,0:T(8,128)(2,1)S(1)}, u32[]{:S(2)}, u32[]{:S(2)}) %collective-permute-start.4) | collective-permute-done | bytes 81952 | tf_op jit(solution)/shard_map/ppermute | solution.py:431
  25.4 1.0 %collective-permute-start.5 = (bf16[2,160,128]{2,1,0:T(8,128)(2,1)S(1)}, bf16[2,160,128]{2,1,0:T(8,128)(2,1)S(1)}, u32[]{:S(2)}, u32[]{:S(2)}) collective-permute-start(bf16[2,160,128]{2,1,0:T(8,128)(2,1)S(1)} %get-tuple-element.107), channel_id=1, source_target_pairs={{0,2},{1,3},{2,0},{3,1},{4,6},{5,7},{6,4},{7,5},{8,10},{9,11},{10,... | collective-permute-start | bytes 245768 | tf_op jit(solution)/shard_map/ppermute | solution.py:431
  26.5 3.5 %collective-permute-done.5.other_part = bf16[2,160,128]{2,1,0:T(8,128)(2,1)S(1)} collective-permute-done((bf16[2,160,128]{2,1,0:T(8,128)(2,1)S(1)}, bf16[2,160,128]{2,1,0:T(8,128)(2,1)S(1)}, u32[]{:S(2)}, u32[]{:S(2)}) %collective-permute-start.5) | collective-permute-done | bytes 81952 | tf_op jit(solution)/shard_map/ppermute | solution.py:431
  29.9 0.1 shard_map.154
  30.0 0.1 collective-permute-start.6
  30.1 1.4 %shard_map.155 = (bf16[512,512]{1,0:T(8,128)(2,1)S(1)}, bf16[512,512]{1,0:T(8,128)(2,1)S(1)}, bf16[4,160,128]{2,1,0:T(8,128)(2,1)S(1)}, f32[4,128]{1,0:T(4,128)S(1)}) custom-call(f32[512,512]{1,0:T(8,128)S(1)} %shard_map.148.local, bf16[8,160,512]{2,1,0:T(8,128)(2,1)S(1)} %get-tuple-element.98.fq, bf16[4,160,128]{2,1,0:T(8,128)(2,1)S(1)} %get-tuple-element.108.prefix.pre_a, ...), custom_call_target="tpu_custom_call" | custom-call | flops 167772160 | bytes 4790272 | tf_op jit(solution)/shard_map/pallas_call | solution.py:419
  31.5 0.5 collective-permute-start.7
  32.0 1.5 %shard_map.156 = (bf16[512,1024]{1,0:T(8,128)(2,1)S(1)}, bf16[512,512]{1,0:T(8,128)(2,1)S(1)}, bf16[4,160,128]{2,1,0:T(8,128)(2,1)S(1)}, f32[4,128]{1,0:T(4,128)S(1)}) custom-call(f32[512,512]{1,0:T(8,128)S(1)} %shard_map.152.local, bf16[8,160,512]{2,1,0:T(8,128)(2,1)S(1)} %get-tuple-element.98.fq, ...), custom_call_target="tpu_custom_call" | custom-call | flops 167772160 | bytes 5838848 | tf_op jit(solution)/shard_map/pallas_call | solution.py:419
  33.6 1.0 %collective-permute-start.8 = (bf16[2,160,128]{2,1,0:T(8,128)(2,1)S(1)}, bf16[2,160,128]{2,1,0:T(8,128)(2,1)S(1)}, u32[]{:S(2)}, u32[]{:S(2)}) collective-permute-start(bf16[2,160,128]{2,1,0:T(8,128)(2,1)S(1)} %get-tuple-element.125), channel_id=1, source_target_pairs={{0,2},{1,3},{2,0},{3,1},{4,6},{5,7},{6,4},{7,5},{8,10},{9,11},{10,... | collective-permute-start | bytes 245768 | tf_op jit(solution)/shard_map/ppermute | solution.py:431
  34.6 3.1 %shard_map.157 = (f32[512,256]{1,0:T(8,128)S(1)}, f32[32,512]{1,0:T(8,128)S(1)}, f32[32,512]{1,0:T(8,128)S(1)}, bf16[512,1024]{1,0:T(8,128)(2,1)}) custom-call(bf16[512,128]{1,0:T(8,128)(2,1)S(1)} %get-tuple-element.85.q_ref, bf16[512,128]{1,0:T(8,128)(2,1)S(1)} %get-tuple-element.91.k_ref, bf16[128,512]{1,0:T(8,128)(2,1)S(1)} %get-tuple-element.92.qt_ref, ...), custom_call_target="tpu_custom_call" | custom-call | flops 536870912 | bytes 4325376 | tf_op jit(solution)/shard_map/pallas_call | solution.py:419
  37.7 0.3 collective-permute-done.8.refs_0_.got_y
  38.1 2.0 %collective-permute-start.9 = (bf16[2,160,128]{2,1,0:T(8,128)(2,1)S(1)}, bf16[2,160,128]{2,1,0:T(8,128)(2,1)S(1)}, u32[]{:S(2)}, u32[]{:S(2)}) collective-permute-start(bf16[2,160,128]{2,1,0:T(8,128)(2,1)S(1)} %shard_map.163), channel_id=1, source_target_pairs={{0,4},{1,5},{2,6},{3,7},{4,0},{5,1},{6,2},{7,3},{8,12},{9,13},{10,... | collective-permute-start | bytes 245768 | tf_op jit(solution)/shard_map/ppermute | solution.py:431
  40.1 2.5 %shard_map.158 = (f32[512,256]{1,0:T(8,128)S(1)}, f32[32,512]{1,0:T(8,128)S(1)}, f32[32,512]{1,0:T(8,128)S(1)}) custom-call(bf16[512,128]{1,0:T(8,128)(2,1)S(1)} %get-tuple-element.85.q_ref, bf16[512,128]{1,0:T(8,128)(2,1)S(1)} %get-tuple-element.91.k_ref, bf16[128,512]{1,0:T(8,128)(2,1)S(1)} %get-tuple-element.92.qt_ref, ...), custom_call_target="tpu_custom_call" | custom-call | flops 536870912 | bytes 2228224 | tf_op jit(solution)/shard_map/pallas_call | solution.py:419
  42.6 3.4 %collective-permute-start.10 = (bf16[2,160,128]{2,1,0:T(8,128)(2,1)S(1)}, bf16[2,160,128]{2,1,0:T(8,128)(2,1)S(1)}, u32[]{:S(2)}, u32[]{:S(2)}) collective-permute-start(bf16[2,160,128]{2,1,0:T(8,128)(2,1)S(1)} %shard_map.164), channel_id=1, source_target_pairs={{0,8},{1,9},{2,10},{3,11},{4,12},{5,13},{6,14},{7,15},{8,0},{9,1},... | collective-permute-start | bytes 245768 | tf_op jit(solution)/shard_map/ppermute | solution.py:431
  46.1 2.7 %shard_map.159 = (f32[512,256]{1,0:T(8,128)S(1)}, f32[32,512]{1,0:T(8,128)S(1)}, f32[32,512]{1,0:T(8,128)S(1)}) custom-call(bf16[512,128]{1,0:T(8,128)(2,1)S(1)} %get-tuple-element.85.q_ref, bf16[512,128]{1,0:T(8,128)(2,1)S(1)} %get-tuple-element.91.k_ref, bf16[128,512]{1,0:T(8,128)(2,1)S(1)} %get-tuple-element.92.qt_ref, ...), custom_call_target="tpu_custom_call" | custom-call | flops 536870912 | bytes 2228224 | tf_op jit(solution)/shard_map/pallas_call | solution.py:419
  48.8 0.1 shard_map.165
  48.8 1.1 %collective-permute-start.11 = (bf16[2,160,128]{2,1,0:T(8,128)(2,1)S(1)}, bf16[2,160,128]{2,1,0:T(8,128)(2,1)S(1)}, u32[]{:S(2)}, u32[]{:S(2)}) collective-permute-start(bf16[2,160,128]{2,1,0:T(8,128)(2,1)S(1)} %get-tuple-element.133), channel_id=1, source_target_pairs={{0,2},{1,3},{2,0},{3,1},{4,6},{5,7},{6,4},{7,5},{8,10},{9,11},{10,... | collective-permute-start | bytes 245768 | tf_op jit(solution)/shard_map/ppermute | solution.py:431
  49.9 2.5 %shard_map.160 = (f32[512,256]{1,0:T(8,128)S(1)}, f32[32,512]{1,0:T(8,128)S(1)}, f32[32,512]{1,0:T(8,128)S(1)}) custom-call(bf16[512,128]{1,0:T(8,128)(2,1)S(1)} %get-tuple-element.85.q_ref, bf16[512,128]{1,0:T(8,128)(2,1)S(1)} %get-tuple-element.91.k_ref, bf16[128,512]{1,0:T(8,128)(2,1)S(1)} %get-tuple-element.92.qt_ref, ...), custom_call_target="tpu_custom_call" | custom-call | flops 536870912 | bytes 2228224 | tf_op jit(solution)/shard_map/pallas_call | solution.py:419
  52.4 0.9 %shard_map.161 = (f32[512,128]{1,0:T(8,128)S(1)}, f32[3,128]{1,0:T(4,128)S(1)}) custom-call(bf16[512,128]{1,0:T(8,128)(2,1)S(1)} %copy-done.3, bf16[16,1280]{1,0:T(8,128)(2,1)S(1)} %collective-permute-done.rim, bf16[128,512]{1,0:T(8,128)(2,1)S(1)} %get-tuple-element.92.qt_ref, bf16[512,512]{1,0:T(8,128)(2,1)S(1)} %get-tuple-element.109.gs_ref.gs_a, ...), custom_call_target="tpu_custom_call" | custom-call | flops 83886080 | bytes 2206720 | tf_op jit(solution)/shard_map/pallas_call | solution.py:419
  53.4 0.1 shard_map.166
  53.5 0.1 collective-permute-start.12
  53.5 1.1 %shard_map.167 = (f32[512,512]{1,0:T(8,128)S(1)}, f32[64,512]{1,0:T(8,128)S(1)}, f32[3,512]{1,0:T(4,128)S(1)}) custom-call(bf16[512,1024]{1,0:T(8,128)(2,1)S(1)} %copy-done, bf16[16,1280]{1,0:T(8,128)(2,1)S(1)} %collective-permute-done.rim, bf16[128,512]{1,0:T(8,128)(2,1)S(1)} %get-tuple-element.93.kt.kt_ref, ...), custom_call_target="tpu_custom_call" | custom-call | flops 167772160 | bytes 4929536 | tf_op jit(solution)/shard_map/pallas_call | solution.py:419
  54.6 0.3 collective-permute-done.12.state
  54.9 1.1 %shard_map.168 = (f32[512,512]{1,0:T(8,128)S(1)}, f32[512,128]{1,0:T(8,128)S(1)}, f32[8,1280]{1,0:T(8,128)S(1)}, f32[4,1280]{1,0:T(4,128)S(1)}) custom-call(bf16[512,128]{1,0:T(8,128)(2,1)S(1)} %copy-done.2, bf16[512,1024]{1,0:T(8,128)(2,1)S(1)} %copy-done, bf16[16,1280]{1,0:T(8,128)(2,1)S(1)} %collective-permute-done.rim, ...), custom_call_target="tpu_custom_call" | custom-call | flops 167772160 | bytes 6700544 | tf_op jit(solution)/shard_map/pallas_call | solution.py:419
  56.0 2.7 %collective-permute-start.16 = (f32[4,1280]{1,0:T(4,128)S(1)}, f32[4,1280]{1,0:T(4,128)S(1)}, u32[]{:S(2)}, u32[]{:S(2)}) collective-permute-start(f32[4,1280]{1,0:T(4,128)S(1)} %get-tuple-element.156), channel_id=1, source_target_pairs={{0,8},{1,9},{2,10},{3,11},{4,12},{5,13},{6,14},{7,15},{8,0},{9,1},... | collective-permute-start | bytes 61448 | tf_op jit(solution)/shard_map/ppermute | solution.py:431
  58.8 1.8 %collective-permute-start.15 = (f32[4,1280]{1,0:T(4,128)S(1)}, f32[4,1280]{1,0:T(4,128)S(1)}, u32[]{:S(2)}, u32[]{:S(2)}) collective-permute-start(f32[4,1280]{1,0:T(4,128)S(1)} %get-tuple-element.156), channel_id=1, source_target_pairs={{0,12},{1,13},{2,14},{3,15},{4,8},{5,9},{6,10},{7,11},{8,4},{9,5},... | collective-permute-start | bytes 61448 | tf_op jit(solution)/shard_map/ppermute | solution.py:431
  60.6 0.5 collective-permute-start.14
  61.1 1.3 %collective-permute-start.13 = (f32[8,1280]{1,0:T(8,128)S(1)}, f32[8,1280]{1,0:T(8,128)S(1)}, u32[]{:S(2)}, u32[]{:S(2)}) collective-permute-start(f32[8,1280]{1,0:T(8,128)S(1)} %get-tuple-element.152), channel_id=1, source_target_pairs={{1,0},{2,1},{3,2},{4,3},{5,4},{6,5},{7,6},{8,7},{9,8},{10,9},{11,1... | collective-permute-start | bytes 122888 | tf_op jit(solution)/shard_map/ppermute | solution.py:673
  62.4 2.2 %collective-permute-done.15 = f32[4,1280]{1,0:T(4,128)S(1)} collective-permute-done((f32[4,1280]{1,0:T(4,128)S(1)}, f32[4,1280]{1,0:T(4,128)S(1)}, u32[]{:S(2)}, u32[]{:S(2)}) %collective-permute-start.15) | collective-permute-done | bytes 20512 | tf_op jit(solution)/shard_map/ppermute | solution.py:431
  64.7 1.1 %collective-permute-start.18 = (f32[4,1280]{1,0:T(4,128)S(1)}, f32[4,1280]{1,0:T(4,128)S(1)}, u32[]{:S(2)}, u32[]{:S(2)}) collective-permute-start(f32[4,1280]{1,0:T(4,128)S(1)} %add_add_fusion.refs_0_), channel_id=1, source_target_pairs={{0,2},{1,3},{2,0},{3,1},{4,6},{5,7},{6,4},{7,5},{8,10},{9,11},{10,... | collective-permute-start | bytes 61448 | tf_op jit(solution)/shard_map/ppermute | solution.py:431
  65.8 0.8 %collective-permute-start.19 = (f32[4,1280]{1,0:T(4,128)S(1)}, f32[4,1280]{1,0:T(4,128)S(1)}, u32[]{:S(2)}, u32[]{:S(2)}) collective-permute-start(f32[4,1280]{1,0:T(4,128)S(1)} %add_add_fusion.refs_0_), channel_id=1, source_target_pairs={{0,1},{1,0},{2,3},{3,2},{4,5},{5,4},{6,7},{7,6},{8,9},{9,8},{10,11... | collective-permute-start | bytes 61448 | tf_op jit(solution)/shard_map/ppermute | solution.py:431
  66.5 1.9 %shard_map.169 = (bf16[512,128]{1,0:T(8,128)(2,1)}, bf16[512,128]{1,0:T(8,128)(2,1)}, bf16[512,1024]{1,0:T(8,128)(2,1)}) custom-call(f32[512,128]{1,0:T(8,128)S(1)} %get-tuple-element.120.gq, f32[512,128]{1,0:T(8,128)S(1)} %get-tuple-element.150.gk, f32[512,512]{1,0:T(8,128)S(1)} %get-tuple-element.151.gv_a, f32[512,512]{1,0:T(8,128)S(1)} %get-tuple-element.141.gv_b, ...), custom_call_target="tpu_custom_call" | custom-call | flops 167772160 | bytes 3988480 | tf_op jit(solution)/shard_map/pallas_call | solution.py:419
  68.4 0.2 collective-permute-done.18.refs_2_
  68.7 0.6 shard_map.170
  (37 shorter events, 0.4 us)
Async XLA Ops:
  0.6 3.3 %copy-start.2 = (bf16[512,128]{1,0:T(8,128)(2,1)S(1)}, bf16[512,128]{1,0:T(8,128)(2,1)}, u32[]{:S(2)}) copy-start(bf16[512,128]{1,0:T(8,128)(2,1)} %key.7) | copy-start | bytes 393220
  0.6 3.3 %copy-start = (bf16[512,1024]{1,0:T(8,128)(2,1)S(1)}, bf16[512,1024]{1,0:T(8,128)(2,1)}, u32[]{:S(2)}) copy-start(bf16[512,1024]{1,0:T(8,128)(2,1)} %value.11) | copy-start | bytes 3145732
  0.7 3.3 %copy-start.5 = (f32[3,128]{1,0:T(4,128)S(1)}, f32[3,128]{1,0:T(4,128)}, u32[]{:S(2)}) copy-start(f32[3,128]{1,0:T(4,128)} %taps_k.5) | copy-start | bytes 4612
  0.7 3.3 %copy-start.4 = (f32[3,1024]{1,0:T(4,128)S(1)}, f32[3,1024]{1,0:T(4,128)}, u32[]{:S(2)}) copy-start(f32[3,1024]{1,0:T(4,128)} %taps_v.7) | copy-start | bytes 36868
  1.6 3.6 %collective-permute-start = (bf16[16,1280]{1,0:T(8,128)(2,1)S(1)}, bf16[16,1280]{1,0:T(8,128)(2,1)S(1)}, u32[]{:S(2)}, u32[]{:S(2)}) collective-permute-start(bf16[16,1280]{1,0:T(8,128)(2,1)S(1)} %shard_map.143), channel_id=1, source_target_pairs={{0,1},{1,2},{2,3},{3,4},{4,5},{5,6},{6,7},{7,8},{8,9},{9,10},{10,1... | collective-permute-start | bytes 122888 | tf_op jit(solution)/shard_map/ppermute | solution.py:542
  5.6 3.7 %collective-permute-start.1 = (bf16[4,160,128]{2,1,0:T(8,128)(2,1)S(1)}, bf16[4,160,128]{2,1,0:T(8,128)(2,1)S(1)}, u32[]{:S(2)}, u32[]{:S(2)}) collective-permute-start(bf16[4,160,128]{2,1,0:T(8,128)(2,1)S(1)} %get-tuple-element.100), channel_id=1, source_target_pairs={{0,1},{1,0},{2,3},{3,2},{4,5},{5,4},{6,7},{7,6},{8,9},{9,8},{10,11... | collective-permute-start | bytes 491528 | tf_op jit(solution)/shard_map/ppermute | solution.py:431
  8.3 3.5 %copy-start.3 = (bf16[512,128]{1,0:T(8,128)(2,1)S(1)}, bf16[512,128]{1,0:T(8,128)(2,1)}, u32[]{:S(2)}) copy-start(bf16[512,128]{1,0:T(8,128)(2,1)} %query.5) | copy-start | bytes 393220
  8.3 3.5 %copy-start.7 = (f32[3,128]{1,0:T(4,128)S(1)}, f32[3,128]{1,0:T(4,128)}, u32[]{:S(2)}) copy-start(f32[3,128]{1,0:T(4,128)} %taps_q.5) | copy-start | bytes 4612
  9.4 5.3 %collective-permute-start.2 = (bf16[2,160,128]{2,1,0:T(8,128)(2,1)S(1)}, bf16[2,160,128]{2,1,0:T(8,128)(2,1)S(1)}, u32[]{:S(2)}, u32[]{:S(2)}) collective-permute-start(bf16[2,160,128]{2,1,0:T(8,128)(2,1)S(1)} %get-tuple-element.102), channel_id=1, source_target_pairs={{0,2},{1,3},{2,0},{3,1},{4,6},{5,7},{6,4},{7,5},{8,10},{9,11},{10,... | collective-permute-start | bytes 245768 | tf_op jit(solution)/shard_map/ppermute | solution.py:431
  14.7 5.1 %collective-permute-start.3 = (bf16[2,160,128]{2,1,0:T(8,128)(2,1)S(1)}, bf16[2,160,128]{2,1,0:T(8,128)(2,1)S(1)}, u32[]{:S(2)}, u32[]{:S(2)}) collective-permute-start(bf16[2,160,128]{2,1,0:T(8,128)(2,1)S(1)} %shard_map.150), channel_id=1, source_target_pairs={{0,4},{1,5},{2,6},{3,7},{4,0},{5,1},{6,2},{7,3},{8,12},{9,13},{10,... | collective-permute-start | bytes 245768 | tf_op jit(solution)/shard_map/ppermute | solution.py:431
  17.4 12.7 %copy-start.1 = (bf16[512,1024]{1,0:T(8,128)(2,1)S(1)}, bf16[512,1024]{1,0:T(8,128)(2,1)}, u32[]{:S(2)}) copy-start(bf16[512,1024]{1,0:T(8,128)(2,1)} %grad.3) | copy-start | bytes 3145732
  17.4 12.7 %copy-start.6 = (f32[1024]{0:T(1024)S(1)}, f32[1024]{0:T(1024)}, u32[]{:S(2)}) copy-start(f32[1024]{0:T(1024)} %param.14) | copy-start | bytes 12292
  19.8 5.5 %collective-permute-start.4 = (bf16[2,160,128]{2,1,0:T(8,128)(2,1)S(1)}, bf16[2,160,128]{2,1,0:T(8,128)(2,1)S(1)}, u32[]{:S(2)}, u32[]{:S(2)}) collective-permute-start(bf16[2,160,128]{2,1,0:T(8,128)(2,1)S(1)} %shard_map.151), channel_id=1, source_target_pairs={{0,8},{1,9},{2,10},{3,11},{4,12},{5,13},{6,14},{7,15},{8,0},{9,1},... | collective-permute-start | bytes 245768 | tf_op jit(solution)/shard_map/ppermute | solution.py:431
  25.4 4.5 %collective-permute-start.5 = (bf16[2,160,128]{2,1,0:T(8,128)(2,1)S(1)}, bf16[2,160,128]{2,1,0:T(8,128)(2,1)S(1)}, u32[]{:S(2)}, u32[]{:S(2)}) collective-permute-start(bf16[2,160,128]{2,1,0:T(8,128)(2,1)S(1)} %get-tuple-element.107), channel_id=1, source_target_pairs={{0,2},{1,3},{2,0},{3,1},{4,6},{5,7},{6,4},{7,5},{8,10},{9,11},{10,... | collective-permute-start | bytes 245768 | tf_op jit(solution)/shard_map/ppermute | solution.py:431
  30.0 2.0 %collective-permute-start.6 = (bf16[4,160,128]{2,1,0:T(8,128)(2,1)S(1)}, bf16[4,160,128]{2,1,0:T(8,128)(2,1)S(1)}, u32[]{:S(2)}, u32[]{:S(2)}) collective-permute-start(bf16[4,160,128]{2,1,0:T(8,128)(2,1)S(1)} %get-tuple-element.110), channel_id=1, source_target_pairs={{0,1},{1,0},{2,3},{3,2},{4,5},{5,4},{6,7},{7,6},{8,9},{9,8},{10,11... | collective-permute-start | bytes 491528 | tf_op jit(solution)/shard_map/ppermute | solution.py:431
  31.5 2.0 %collective-permute-start.7 = (bf16[4,160,128]{2,1,0:T(8,128)(2,1)S(1)}, bf16[4,160,128]{2,1,0:T(8,128)(2,1)S(1)}, u32[]{:S(2)}, u32[]{:S(2)}) collective-permute-start(bf16[4,160,128]{2,1,0:T(8,128)(2,1)S(1)} %get-tuple-element.123), channel_id=1, source_target_pairs={{0,1},{1,0},{2,3},{3,2},{4,5},{5,4},{6,7},{7,6},{8,9},{9,8},{10,11... | collective-permute-start | bytes 491528 | tf_op jit(solution)/shard_map/ppermute | solution.py:431
  33.6 4.5 %collective-permute-start.8 = (bf16[2,160,128]{2,1,0:T(8,128)(2,1)S(1)}, bf16[2,160,128]{2,1,0:T(8,128)(2,1)S(1)}, u32[]{:S(2)}, u32[]{:S(2)}) collective-permute-start(bf16[2,160,128]{2,1,0:T(8,128)(2,1)S(1)} %get-tuple-element.125), channel_id=1, source_target_pairs={{0,2},{1,3},{2,0},{3,1},{4,6},{5,7},{6,4},{7,5},{8,10},{9,11},{10,... | collective-permute-start | bytes 245768 | tf_op jit(solution)/shard_map/ppermute | solution.py:431
  38.1 4.5 %collective-permute-start.9 = (bf16[2,160,128]{2,1,0:T(8,128)(2,1)S(1)}, bf16[2,160,128]{2,1,0:T(8,128)(2,1)S(1)}, u32[]{:S(2)}, u32[]{:S(2)}) collective-permute-start(bf16[2,160,128]{2,1,0:T(8,128)(2,1)S(1)} %shard_map.163), channel_id=1, source_target_pairs={{0,4},{1,5},{2,6},{3,7},{4,0},{5,1},{6,2},{7,3},{8,12},{9,13},{10,... | collective-permute-start | bytes 245768 | tf_op jit(solution)/shard_map/ppermute | solution.py:431
  42.6 6.1 %collective-permute-start.10 = (bf16[2,160,128]{2,1,0:T(8,128)(2,1)S(1)}, bf16[2,160,128]{2,1,0:T(8,128)(2,1)S(1)}, u32[]{:S(2)}, u32[]{:S(2)}) collective-permute-start(bf16[2,160,128]{2,1,0:T(8,128)(2,1)S(1)} %shard_map.164), channel_id=1, source_target_pairs={{0,8},{1,9},{2,10},{3,11},{4,12},{5,13},{6,14},{7,15},{8,0},{9,1},... | collective-permute-start | bytes 245768 | tf_op jit(solution)/shard_map/ppermute | solution.py:431
  48.8 4.5 %collective-permute-start.11 = (bf16[2,160,128]{2,1,0:T(8,128)(2,1)S(1)}, bf16[2,160,128]{2,1,0:T(8,128)(2,1)S(1)}, u32[]{:S(2)}, u32[]{:S(2)}) collective-permute-start(bf16[2,160,128]{2,1,0:T(8,128)(2,1)S(1)} %get-tuple-element.133), channel_id=1, source_target_pairs={{0,2},{1,3},{2,0},{3,1},{4,6},{5,7},{6,4},{7,5},{8,10},{9,11},{10,... | collective-permute-start | bytes 245768 | tf_op jit(solution)/shard_map/ppermute | solution.py:431
  53.5 1.5 %collective-permute-start.12 = (bf16[4,160,128]{2,1,0:T(8,128)(2,1)S(1)}, bf16[4,160,128]{2,1,0:T(8,128)(2,1)S(1)}, u32[]{:S(2)}, u32[]{:S(2)}) collective-permute-start(bf16[4,160,128]{2,1,0:T(8,128)(2,1)S(1)} %get-tuple-element.136), channel_id=1, source_target_pairs={{0,1},{1,0},{2,3},{3,2},{4,5},{5,4},{6,7},{7,6},{8,9},{9,8},{10,11... | collective-permute-start | bytes 491528 | tf_op jit(solution)/shard_map/ppermute | solution.py:431
  56.0 6.3 %collective-permute-start.16 = (f32[4,1280]{1,0:T(4,128)S(1)}, f32[4,1280]{1,0:T(4,128)S(1)}, u32[]{:S(2)}, u32[]{:S(2)}) collective-permute-start(f32[4,1280]{1,0:T(4,128)S(1)} %get-tuple-element.156), channel_id=1, source_target_pairs={{0,8},{1,9},{2,10},{3,11},{4,12},{5,13},{6,14},{7,15},{8,0},{9,1},... | collective-permute-start | bytes 61448 | tf_op jit(solution)/shard_map/ppermute | solution.py:431
  58.8 5.8 %collective-permute-start.15 = (f32[4,1280]{1,0:T(4,128)S(1)}, f32[4,1280]{1,0:T(4,128)S(1)}, u32[]{:S(2)}, u32[]{:S(2)}) collective-permute-start(f32[4,1280]{1,0:T(4,128)S(1)} %get-tuple-element.156), channel_id=1, source_target_pairs={{0,12},{1,13},{2,14},{3,15},{4,8},{5,9},{6,10},{7,11},{8,4},{9,5},... | collective-permute-start | bytes 61448 | tf_op jit(solution)/shard_map/ppermute | solution.py:431
  60.6 4.0 %collective-permute-start.14 = (f32[4,1280]{1,0:T(4,128)S(1)}, f32[4,1280]{1,0:T(4,128)S(1)}, u32[]{:S(2)}, u32[]{:S(2)}) collective-permute-start(f32[4,1280]{1,0:T(4,128)S(1)} %get-tuple-element.156), channel_id=1, source_target_pairs={{0,4},{1,5},{2,6},{3,7},{4,0},{5,1},{6,2},{7,3},{8,12},{9,13},{10,... | collective-permute-start | bytes 61448 | tf_op jit(solution)/shard_map/ppermute | solution.py:431
  61.1 5.4 %collective-permute-start.13 = (f32[8,1280]{1,0:T(8,128)S(1)}, f32[8,1280]{1,0:T(8,128)S(1)}, u32[]{:S(2)}, u32[]{:S(2)}) collective-permute-start(f32[8,1280]{1,0:T(8,128)S(1)} %get-tuple-element.152), channel_id=1, source_target_pairs={{1,0},{2,1},{3,2},{4,3},{5,4},{6,5},{7,6},{8,7},{9,8},{10,9},{11,1... | collective-permute-start | bytes 122888 | tf_op jit(solution)/shard_map/ppermute | solution.py:673
  64.6 3.8 %collective-permute-start.17 = (f32[4,1280]{1,0:T(4,128)S(1)}, f32[4,1280]{1,0:T(4,128)S(1)}, u32[]{:S(2)}, u32[]{:S(2)}) collective-permute-start(f32[4,1280]{1,0:T(4,128)S(1)} %add_add_fusion.refs_0_), channel_id=1, source_target_pairs={{0,3},{1,2},{2,1},{3,0},{4,7},{5,6},{6,5},{7,4},{8,11},{9,10},{10,... | collective-permute-start | bytes 61448 | tf_op jit(solution)/shard_map/ppermute | solution.py:431
  64.7 4.0 %collective-permute-start.18 = (f32[4,1280]{1,0:T(4,128)S(1)}, f32[4,1280]{1,0:T(4,128)S(1)}, u32[]{:S(2)}, u32[]{:S(2)}) collective-permute-start(f32[4,1280]{1,0:T(4,128)S(1)} %add_add_fusion.refs_0_), channel_id=1, source_target_pairs={{0,2},{1,3},{2,0},{3,1},{4,6},{5,7},{6,4},{7,5},{8,10},{9,11},{10,... | collective-permute-start | bytes 61448 | tf_op jit(solution)/shard_map/ppermute | solution.py:431
  65.8 2.9 %collective-permute-start.19 = (f32[4,1280]{1,0:T(4,128)S(1)}, f32[4,1280]{1,0:T(4,128)S(1)}, u32[]{:S(2)}, u32[]{:S(2)}) collective-permute-start(f32[4,1280]{1,0:T(4,128)S(1)} %add_add_fusion.refs_0_), channel_id=1, source_target_pairs={{0,1},{1,0},{2,3},{3,2},{4,5},{5,4},{6,7},{7,6},{8,9},{9,8},{10,11... | collective-permute-start | bytes 61448 | tf_op jit(solution)/shard_map/ppermute | solution.py:431

commit v9 on v8

--- a/solution.py
+++ b/solution.py
@@ -111,20 +111,21 @@
 
 
 def fill(wide, rim, rest):
-    wide[0:RIM] = rim.astype(F32)
+    wide[RIM - rim.shape[0] : RIM] = rim.astype(F32)
     wide[RIM : RIM + rest.shape[0]] = rest.astype(F32)
 
 
-def end_kernel(query, key, value, out, sems):
+def end_kernel(query, key, value, out, ends, sems):
     start = query.shape[0] - RIM
     copies = [
-        pltpu.make_async_copy(ref.at[pl.ds(start, RIM)], out.at[:, pl.ds(lane, ref.shape[1])], sems.at[i])
+        pltpu.make_async_copy(ref.at[pl.ds(start, RIM)], ends.at[:, pl.ds(lane, ref.shape[1])], sems.at[i])
         for i, (ref, lane) in enumerate(((query, 0), (key, LANES), (value, 2 * LANES)))
     ]
     for copy in copies:
         copy.start()
     for copy in copies:
         copy.wait()
+    out[...] = ends[...].astype(F32)[RIM - out.shape[0] :].astype(BF16)
 
 
 def bulk_kernel(
@@ -339,13 +340,13 @@
         sums[o : o + 1, LANES : 2 * LANES] = row
     sums[0:taps, 0:LANES] = sums_q[...]
     sums[taps : taps + 1, 0 : 2 * LANES] = jnp.zeros((1, 2 * LANES), F32)
-    head_out[:, 0:LANES] = gq[0:8]
-    head_out[:, LANES : 2 * LANES] = grad[0:8]
+    head_out[:, 0:LANES] = gq[0 : taps - 1]
+    head_out[:, LANES : 2 * LANES] = grad[0 : taps - 1]
     for g in range(HALF):
         sums[0:taps, lanes_of(half_b, g, 2 * LANES)] = sums_b[:, head_lanes(g)]
         for half, gain, gv in ((half_a, gain_a, gv_out), (half_b, gain_b, gv_b)):
             sums[taps : taps + 1, lanes_of(half, g, 2 * LANES)] = gain[g : g + 1]
-            head_out[:, lanes_of(half, g, 2 * LANES)] = gv[0:8, head_lanes(g)]
+            head_out[:, lanes_of(half, g, 2 * LANES)] = gv[0 : taps - 1, head_lanes(g)]
 
 
 def signal_kernel(
@@ -364,7 +365,7 @@
         part[start : start + body, lanes] = total.astype(BF16)
         if last:
             wide[0:RIM] = grad[rows - RIM :, place]
-            wide[RIM : RIM + 8] = after
+            wide[RIM : RIM + count - 1] = after
             total = taps[0:1] * wide[count - 1 : count - 1 + RIM]
             for o in range(1, count):
                 total = total + taps[o : o + 1] * wide[count - 1 - o : count - 1 - o + RIM]
@@ -533,8 +534,8 @@
     near = pl.BlockSpec(memory_space=pltpu.VMEM)
     ends = call(
         end_kernel,
-        [st((RIM, ALL), BF16)],
-        [pltpu.SemaphoreType.DMA((3,))],
+        [st((taps - 1, ALL), BF16)],
+        [pltpu.VMEM((RIM, ALL), BF16), pltpu.SemaphoreType.DMA((3,))],
         (far(query_in), far(key_in), far(value_in)),
         rows,
         in_specs=[apart] * 3,
@@ -664,7 +665,7 @@
     gq, sums_q = made["gq"]
     gv_a, gk, heads, sums = call(
         second_later_kernel,
-        [half_wide, flat, st((8, ALL), F32), st((taps + 1, ALL), F32)],
+        [half_wide, flat, st((taps - 1, ALL), F32), st((taps + 1, ALL), F32)],
         [wide, state_scratch, pltpu.VMEM((LANES, rows), F32)],
         (key_in, value_in, rim, *held(kt, fk_a, v_a), post_a,
          *held(back[0][0], back[1][0], back[0][2], back[1][2], gv_b, gk_b, sums_b, gq, sums_q, gain_a, gain_b)),

time: 69.5 us -> 69.2 us (level)
  no operation moved by 1% of the time
where the time goes in v9:
time: 69.2 us; the launch traced here: 69 us
  starting transfers between devices  30.3 us (44%)
  Pallas kernels  28.1 us (41%)
  waiting for transfers between devices  9.65 us (14%)
  between operations  0.94 us (1%)
    pallas_call x28, Pallas kernels, call(): pl.pallas_call(kernel, out_shape=[o if i in loose else pltpu.VMEM(o.shape...  28.1 us
    ppermute x18, starting transfers between devices, exchange(): return lax.ppermute(x, 'seq', [(i, i ^ distance) for i in range(count)])  26.7 us
    ppermute x18, waiting for transfers between devices, exchange(): return lax.ppermute(x, 'seq', [(i, i ^ distance) for i in range(count)])  9.64 us
    ppermute x1, starting transfers between devices, shards(): rim = lax.ppermute(ends, 'seq', [(i, i + 1) for i in range(count - 1)])  2.36 us
  transfers between devices with their start and end apart: 20, of which 8 were waited for; matrix products, arithmetic and copies ran while one was open for 0% of the time, Pallas kernels for 35%

profile of v9, /device:TPU:0, one launch (start us, length us, event | category | flops | bytes accessed | tf_op | source)
XLA Modules:
  0.0 69.0 jit_solution(5220427439461598214)
XLA Ops:
  0.7 0.9 %shard_map.143 = bf16[2,1280]{1,0:T(2,128)(2,1)S(1)} custom-call(bf16[512,128]{1,0:T(8,128)(2,1)} %query.5, bf16[512,128]{1,0:T(8,128)(2,1)} %key.7, bf16[512,1024]{1,0:T(8,128)(2,1)} %value.11), custom_call_target="tpu_custom_call" | custom-call | flops 512 | bytes 1315840 | tf_op jit(solution)/shard_map/pallas_call | solution.py:420
  1.6 2.4 %collective-permute-start = (bf16[2,1280]{1,0:T(2,128)(2,1)S(1)}, bf16[2,1280]{1,0:T(2,128)(2,1)S(1)}, u32[]{:S(2)}, u32[]{:S(2)}) collective-permute-start(bf16[2,1280]{1,0:T(2,128)(2,1)S(1)} %shard_map.143), channel_id=1, source_target_pairs={{0,1},{1,2},{2,3},{3,4},{4,5},{5,6},{6,7},{7,8},{8,9},{9,10},{10,1... | collective-permute-start | bytes 15368 | tf_op jit(solution)/shard_map/ppermute | solution.py:543
  4.0 1.2 %shard_map.145 = (bf16[384,128]{1,0:T(8,128)(2,1)S(1)}, bf16[128,384]{1,0:T(8,128)(2,1)S(1)}, bf16[384,512]{1,0:T(8,128)(2,1)S(1)}, bf16[4,160,384]{2,1,0:T(8,12...) custom-call(bf16[512,128]{1,0:T(8,128)(2,1)S(1)} %copy-done.2, ...), custom_call_target="tpu_custom_call" | custom-call | flops 167772160 | bytes 3814912 | tf_op jit(solution)/shard_map/pallas_call | solution.py:420
  5.2 0.4 shard_map.146
  5.7 2.7 %collective-permute-start.1 = (bf16[4,160,128]{2,1,0:T(8,128)(2,1)S(1)}, bf16[4,160,128]{2,1,0:T(8,128)(2,1)S(1)}, u32[]{:S(2)}, u32[]{:S(2)}) collective-permute-start(bf16[4,160,128]{2,1,0:T(8,128)(2,1)S(1)} %get-tuple-element.100), channel_id=1, source_target_pairs={{0,1},{1,0},{2,3},{3,2},{4,5},{5,4},{6,7},{7,6},{8,9},{9,8},{10,11... | collective-permute-start | bytes 491528 | tf_op jit(solution)/shard_map/ppermute | solution.py:432
  8.3 0.4 shard_map.147
  8.7 0.6 collective-permute-done.1.near
  9.4 2.1 %collective-permute-start.2 = (bf16[2,160,128]{2,1,0:T(8,128)(2,1)S(1)}, bf16[2,160,128]{2,1,0:T(8,128)(2,1)S(1)}, u32[]{:S(2)}, u32[]{:S(2)}) collective-permute-start(bf16[2,160,128]{2,1,0:T(8,128)(2,1)S(1)} %get-tuple-element.102), channel_id=1, source_target_pairs={{0,2},{1,3},{2,0},{3,1},{4,6},{5,7},{6,4},{7,5},{8,10},{9,11},{10,... | collective-permute-start | bytes 245768 | tf_op jit(solution)/shard_map/ppermute | solution.py:432
  11.5 0.5 shard_map.144
  12.0 2.3 %shard_map.148.local = f32[512,512]{1,0:T(8,128)S(1)} custom-call(bf16[512,128]{1,0:T(8,128)(2,1)S(1)} %get-tuple-element.85.q_ref, bf16[512,128]{1,0:T(8,128)(2,1)S(1)} %get-tuple-element.91.k_ref, bf16[512,512]{1,0:T(8,128)(2,1)S(1)} %get-tuple-element.97.v_ref.v), custom_call_target="tpu_custom_call" | custom-call | flops 536870912 | bytes 1835008 | tf_op jit(solution)/shard_map/pallas_call | solution.py:420
  14.3 2.7 %collective-permute-start.3 = (bf16[2,160,128]{2,1,0:T(8,128)(2,1)S(1)}, bf16[2,160,128]{2,1,0:T(8,128)(2,1)S(1)}, u32[]{:S(2)}, u32[]{:S(2)}) collective-permute-start(bf16[2,160,128]{2,1,0:T(8,128)(2,1)S(1)} %shard_map.150), channel_id=1, source_target_pairs={{0,4},{1,5},{2,6},{3,7},{4,0},{5,1},{6,2},{7,3},{8,12},{9,13},{10,... | collective-permute-start | bytes 245768 | tf_op jit(solution)/shard_map/ppermute | solution.py:432
  17.0 2.3 %shard_map.152.local = f32[512,512]{1,0:T(8,128)S(1)} custom-call(bf16[512,128]{1,0:T(8,128)(2,1)S(1)} %get-tuple-element.85.q_ref, bf16[512,128]{1,0:T(8,128)(2,1)S(1)} %get-tuple-element.91.k_ref, bf16[512,512]{1,0:T(8,128)(2,1)S(1)} %get-tuple-element.104.v_ref.v), custom_call_target="tpu_custom_call" | custom-call | flops 536870912 | bytes 1835008 | tf_op jit(solution)/shard_map/pallas_call | solution.py:420
  19.4 0.1 collective-permute-done.3.refs_1_.rest_0_
  19.5 3.1 %collective-permute-start.4 = (bf16[2,160,128]{2,1,0:T(8,128)(2,1)S(1)}, bf16[2,160,128]{2,1,0:T(8,128)(2,1)S(1)}, u32[]{:S(2)}, u32[]{:S(2)}) collective-permute-start(bf16[2,160,128]{2,1,0:T(8,128)(2,1)S(1)} %shard_map.151), channel_id=1, source_target_pairs={{0,8},{1,9},{2,10},{3,11},{4,12},{5,13},{6,14},{7,15},{8,0},{9,1},... | collective-permute-start | bytes 245768 | tf_op jit(solution)/shard_map/ppermute | solution.py:432
  22.6 2.4 %collective-permute-done.4.rest_1_ = bf16[2,160,128]{2,1,0:T(8,128)(2,1)S(1)} collective-permute-done((bf16[2,160,128]{2,1,0:T(8,128)(2,1)S(1)}, bf16[2,160,128]{2,1,0:T(8,128)(2,1)S(1)}, u32[]{:S(2)}, u32[]{:S(2)}) %collective-permute-start.4) | collective-permute-done | bytes 81952 | tf_op jit(solution)/shard_map/ppermute | solution.py:432
  25.1 1.0 %collective-permute-start.5 = (bf16[2,160,128]{2,1,0:T(8,128)(2,1)S(1)}, bf16[2,160,128]{2,1,0:T(8,128)(2,1)S(1)}, u32[]{:S(2)}, u32[]{:S(2)}) collective-permute-start(bf16[2,160,128]{2,1,0:T(8,128)(2,1)S(1)} %get-tuple-element.107), channel_id=1, source_target_pairs={{0,2},{1,3},{2,0},{3,1},{4,6},{5,7},{6,4},{7,5},{8,10},{9,11},{10,... | collective-permute-start | bytes 245768 | tf_op jit(solution)/shard_map/ppermute | solution.py:432
  26.1 3.5 %collective-permute-done.5.other_part = bf16[2,160,128]{2,1,0:T(8,128)(2,1)S(1)} collective-permute-done((bf16[2,160,128]{2,1,0:T(8,128)(2,1)S(1)}, bf16[2,160,128]{2,1,0:T(8,128)(2,1)S(1)}, u32[]{:S(2)}, u32[]{:S(2)}) %collective-permute-start.5) | collective-permute-done | bytes 81952 | tf_op jit(solution)/shard_map/ppermute | solution.py:432
  29.6 0.1 shard_map.154
  29.7 0.1 collective-permute-start.6
  29.8 1.4 %shard_map.155 = (bf16[512,512]{1,0:T(8,128)(2,1)S(1)}, bf16[512,512]{1,0:T(8,128)(2,1)S(1)}, bf16[4,160,128]{2,1,0:T(8,128)(2,1)S(1)}, f32[4,128]{1,0:T(4,128)S(1)}) custom-call(f32[512,512]{1,0:T(8,128)S(1)} %shard_map.148.local, bf16[8,160,512]{2,1,0:T(8,128)(2,1)S(1)} %get-tuple-element.98.fq, bf16[4,160,128]{2,1,0:T(8,128)(2,1)S(1)} %get-tuple-element.108.prefix.pre_a, ...), custom_call_target="tpu_custom_call" | custom-call | flops 167772160 | bytes 4790272 | tf_op jit(solution)/shard_map/pallas_call | solution.py:420
  31.2 0.6 collective-permute-start.7
  31.7 1.5 %shard_map.156 = (bf16[512,1024]{1,0:T(8,128)(2,1)S(1)}, bf16[512,512]{1,0:T(8,128)(2,1)S(1)}, bf16[4,160,128]{2,1,0:T(8,128)(2,1)S(1)}, f32[4,128]{1,0:T(4,128)S(1)}) custom-call(f32[512,512]{1,0:T(8,128)S(1)} %shard_map.152.local, bf16[8,160,512]{2,1,0:T(8,128)(2,1)S(1)} %get-tuple-element.98.fq, ...), custom_call_target="tpu_custom_call" | custom-call | flops 167772160 | bytes 5838848 | tf_op jit(solution)/shard_map/pallas_call | solution.py:420
  33.3 1.0 %collective-permute-start.8 = (bf16[2,160,128]{2,1,0:T(8,128)(2,1)S(1)}, bf16[2,160,128]{2,1,0:T(8,128)(2,1)S(1)}, u32[]{:S(2)}, u32[]{:S(2)}) collective-permute-start(bf16[2,160,128]{2,1,0:T(8,128)(2,1)S(1)} %get-tuple-element.125), channel_id=1, source_target_pairs={{0,2},{1,3},{2,0},{3,1},{4,6},{5,7},{6,4},{7,5},{8,10},{9,11},{10,... | collective-permute-start | bytes 245768 | tf_op jit(solution)/shard_map/ppermute | solution.py:432
  34.3 3.1 %shard_map.157 = (f32[512,256]{1,0:T(8,128)S(1)}, f32[32,512]{1,0:T(8,128)S(1)}, f32[32,512]{1,0:T(8,128)S(1)}, bf16[512,1024]{1,0:T(8,128)(2,1)}) custom-call(bf16[512,128]{1,0:T(8,128)(2,1)S(1)} %get-tuple-element.85.q_ref, bf16[512,128]{1,0:T(8,128)(2,1)S(1)} %get-tuple-element.91.k_ref, bf16[128,512]{1,0:T(8,128)(2,1)S(1)} %get-tuple-element.92.qt_ref, ...), custom_call_target="tpu_custom_call" | custom-call | flops 536870912 | bytes 4325376 | tf_op jit(solution)/shard_map/pallas_call | solution.py:420
  37.5 0.3 collective-permute-done.8.refs_0_.got_y
  37.8 2.0 %collective-permute-start.9 = (bf16[2,160,128]{2,1,0:T(8,128)(2,1)S(1)}, bf16[2,160,128]{2,1,0:T(8,128)(2,1)S(1)}, u32[]{:S(2)}, u32[]{:S(2)}) collective-permute-start(bf16[2,160,128]{2,1,0:T(8,128)(2,1)S(1)} %shard_map.163), channel_id=1, source_target_pairs={{0,4},{1,5},{2,6},{3,7},{4,0},{5,1},{6,2},{7,3},{8,12},{9,13},{10,... | collective-permute-start | bytes 245768 | tf_op jit(solution)/shard_map/ppermute | solution.py:432
  39.8 2.5 %shard_map.158 = (f32[512,256]{1,0:T(8,128)S(1)}, f32[32,512]{1,0:T(8,128)S(1)}, f32[32,512]{1,0:T(8,128)S(1)}) custom-call(bf16[512,128]{1,0:T(8,128)(2,1)S(1)} %get-tuple-element.85.q_ref, bf16[512,128]{1,0:T(8,128)(2,1)S(1)} %get-tuple-element.91.k_ref, bf16[128,512]{1,0:T(8,128)(2,1)S(1)} %get-tuple-element.92.qt_ref, ...), custom_call_target="tpu_custom_call" | custom-call | flops 536870912 | bytes 2228224 | tf_op jit(solution)/shard_map/pallas_call | solution.py:420
  42.4 3.4 %collective-permute-start.10 = (bf16[2,160,128]{2,1,0:T(8,128)(2,1)S(1)}, bf16[2,160,128]{2,1,0:T(8,128)(2,1)S(1)}, u32[]{:S(2)}, u32[]{:S(2)}) collective-permute-start(bf16[2,160,128]{2,1,0:T(8,128)(2,1)S(1)} %shard_map.164), channel_id=1, source_target_pairs={{0,8},{1,9},{2,10},{3,11},{4,12},{5,13},{6,14},{7,15},{8,0},{9,1},... | collective-permute-start | bytes 245768 | tf_op jit(solution)/shard_map/ppermute | solution.py:432
  45.8 2.7 %shard_map.159 = (f32[512,256]{1,0:T(8,128)S(1)}, f32[32,512]{1,0:T(8,128)S(1)}, f32[32,512]{1,0:T(8,128)S(1)}) custom-call(bf16[512,128]{1,0:T(8,128)(2,1)S(1)} %get-tuple-element.85.q_ref, bf16[512,128]{1,0:T(8,128)(2,1)S(1)} %get-tuple-element.91.k_ref, bf16[128,512]{1,0:T(8,128)(2,1)S(1)} %get-tuple-element.92.qt_ref, ...), custom_call_target="tpu_custom_call" | custom-call | flops 536870912 | bytes 2228224 | tf_op jit(solution)/shard_map/pallas_call | solution.py:420
  48.5 0.1 shard_map.165
  48.6 1.0 %collective-permute-start.11 = (bf16[2,160,128]{2,1,0:T(8,128)(2,1)S(1)}, bf16[2,160,128]{2,1,0:T(8,128)(2,1)S(1)}, u32[]{:S(2)}, u32[]{:S(2)}) collective-permute-start(bf16[2,160,128]{2,1,0:T(8,128)(2,1)S(1)} %get-tuple-element.133), channel_id=1, source_target_pairs={{0,2},{1,3},{2,0},{3,1},{4,6},{5,7},{6,4},{7,5},{8,10},{9,11},{10,... | collective-permute-start | bytes 245768 | tf_op jit(solution)/shard_map/ppermute | solution.py:432
  49.6 2.5 %shard_map.160 = (f32[512,256]{1,0:T(8,128)S(1)}, f32[32,512]{1,0:T(8,128)S(1)}, f32[32,512]{1,0:T(8,128)S(1)}) custom-call(bf16[512,128]{1,0:T(8,128)(2,1)S(1)} %get-tuple-element.85.q_ref, bf16[512,128]{1,0:T(8,128)(2,1)S(1)} %get-tuple-element.91.k_ref, bf16[128,512]{1,0:T(8,128)(2,1)S(1)} %get-tuple-element.92.qt_ref, ...), custom_call_target="tpu_custom_call" | custom-call | flops 536870912 | bytes 2228224 | tf_op jit(solution)/shard_map/pallas_call | solution.py:420
  52.2 0.9 %shard_map.161 = (f32[512,128]{1,0:T(8,128)S(1)}, f32[3,128]{1,0:T(4,128)S(1)}) custom-call(bf16[512,128]{1,0:T(8,128)(2,1)S(1)} %copy-done.3, bf16[2,1280]{1,0:T(2,128)(2,1)S(1)} %collective-permute-done.rim, bf16[128,512]{1,0:T(8,128)(2,1)S(1)} %get-tuple-element.92.qt_ref, bf16[512,512]{1,0:T(8,128)(2,1)S(1)} %get-tuple-element.109.gs_ref.gs_a, ...), custom_call_target="tpu_custom_call" | custom-call | flops 83886080 | bytes 2170880 | tf_op jit(solution)/shard_map/pallas_call | solution.py:420
  53.1 0.1 shard_map.166
  53.2 0.1 collective-permute-start.12
  53.3 1.2 %shard_map.167 = (f32[512,512]{1,0:T(8,128)S(1)}, f32[64,512]{1,0:T(8,128)S(1)}, f32[3,512]{1,0:T(4,128)S(1)}) custom-call(bf16[512,1024]{1,0:T(8,128)(2,1)S(1)} %copy-done, bf16[2,1280]{1,0:T(2,128)(2,1)S(1)} %collective-permute-done.rim, bf16[128,512]{1,0:T(8,128)(2,1)S(1)} %get-tuple-element.93.kt.kt_ref, bf16[4,160,512]{2,1,0:T(8,128)(2,1)S(1)} %get-tuple-element.137.fk, ...), custom_call_target="tpu_custom_call" | custom-call | flops 167772160 | bytes 4893696 | tf_op jit(solution)/shard_map/pallas_call | solution.py:420
  54.5 0.2 collective-permute-done.12.state
  54.7 1.1 %shard_map.168 = (f32[512,512]{1,0:T(8,128)S(1)}, f32[512,128]{1,0:T(8,128)S(1)}, f32[2,1280]{1,0:T(2,128)S(1)}, f32[4,1280]{1,0:T(4,128)S(1)}) custom-call(bf16[512,128]{1,0:T(8,128)(2,1)S(1)} %copy-done.2, bf16[512,1024]{1,0:T(8,128)(2,1)S(1)} %copy-done, bf16[2,1280]{1,0:T(2,128)(2,1)S(1)} %collective-permute-done.rim, ...), custom_call_target="tpu_custom_call" | custom-call | flops 167772160 | bytes 6633984 | tf_op jit(solution)/shard_map/pallas_call | solution.py:420
  55.8 2.7 %collective-permute-start.16 = (f32[4,1280]{1,0:T(4,128)S(1)}, f32[4,1280]{1,0:T(4,128)S(1)}, u32[]{:S(2)}, u32[]{:S(2)}) collective-permute-start(f32[4,1280]{1,0:T(4,128)S(1)} %get-tuple-element.156), channel_id=1, source_target_pairs={{0,8},{1,9},{2,10},{3,11},{4,12},{5,13},{6,14},{7,15},{8,0},{9,1},... | collective-permute-start | bytes 61448 | tf_op jit(solution)/shard_map/ppermute | solution.py:432
  58.5 1.8 %collective-permute-start.15 = (f32[4,1280]{1,0:T(4,128)S(1)}, f32[4,1280]{1,0:T(4,128)S(1)}, u32[]{:S(2)}, u32[]{:S(2)}) collective-permute-start(f32[4,1280]{1,0:T(4,128)S(1)} %get-tuple-element.156), channel_id=1, source_target_pairs={{0,12},{1,13},{2,14},{3,15},{4,8},{5,9},{6,10},{7,11},{8,4},{9,5},... | collective-permute-start | bytes 61448 | tf_op jit(solution)/shard_map/ppermute | solution.py:432
  60.4 0.5 collective-permute-start.14
  60.8 1.3 %collective-permute-start.13 = (f32[2,1280]{1,0:T(2,128)S(1)}, f32[2,1280]{1,0:T(2,128)S(1)}, u32[]{:S(2)}, u32[]{:S(2)}) collective-permute-start(f32[2,1280]{1,0:T(2,128)S(1)} %get-tuple-element.152), channel_id=1, source_target_pairs={{1,0},{2,1},{3,2},{4,3},{5,4},{6,5},{7,6},{8,7},{9,8},{10,9},{11,1... | collective-permute-start | bytes 30728 | tf_op jit(solution)/shard_map/ppermute | solution.py:674
  62.1 2.2 %collective-permute-done.15 = f32[4,1280]{1,0:T(4,128)S(1)} collective-permute-done((f32[4,1280]{1,0:T(4,128)S(1)}, f32[4,1280]{1,0:T(4,128)S(1)}, u32[]{:S(2)}, u32[]{:S(2)}) %collective-permute-start.15) | collective-permute-done | bytes 20512 | tf_op jit(solution)/shard_map/ppermute | solution.py:432
  64.4 1.1 %collective-permute-start.18 = (f32[4,1280]{1,0:T(4,128)S(1)}, f32[4,1280]{1,0:T(4,128)S(1)}, u32[]{:S(2)}, u32[]{:S(2)}) collective-permute-start(f32[4,1280]{1,0:T(4,128)S(1)} %add_add_fusion.refs_0_), channel_id=1, source_target_pairs={{0,2},{1,3},{2,0},{3,1},{4,6},{5,7},{6,4},{7,5},{8,10},{9,11},{10,... | collective-permute-start | bytes 61448 | tf_op jit(solution)/shard_map/ppermute | solution.py:432
  65.6 0.7 %collective-permute-start.19 = (f32[4,1280]{1,0:T(4,128)S(1)}, f32[4,1280]{1,0:T(4,128)S(1)}, u32[]{:S(2)}, u32[]{:S(2)}) collective-permute-start(f32[4,1280]{1,0:T(4,128)S(1)} %add_add_fusion.refs_0_), channel_id=1, source_target_pairs={{0,1},{1,0},{2,3},{3,2},{4,5},{5,4},{6,7},{7,6},{8,9},{9,8},{10,11... | collective-permute-start | bytes 61448 | tf_op jit(solution)/shard_map/ppermute | solution.py:432
  66.3 1.9 %shard_map.169 = (bf16[512,128]{1,0:T(8,128)(2,1)}, bf16[512,128]{1,0:T(8,128)(2,1)}, bf16[512,1024]{1,0:T(8,128)(2,1)}) custom-call(f32[512,128]{1,0:T(8,128)S(1)} %get-tuple-element.120.gq, f32[512,128]{1,0:T(8,128)S(1)} %get-tuple-element.150.gk, f32[512,512]{1,0:T(8,128)S(1)} %get-tuple-element.151.gv_a, f32[512,512]{1,0:T(8,128)S(1)} %get-tuple-element.141.gv_b, ...), custom_call_target="tpu_custom_call" | custom-call | flops 167772160 | bytes 3957760 | tf_op jit(solution)/shard_map/pallas_call | solution.py:420
  68.2 0.2 collective-permute-done.18.refs_2_
  68.4 0.6 shard_map.170
  (37 shorter events, 0.4 us)
Async XLA Ops:
  0.6 3.3 %copy-start.2 = (bf16[512,128]{1,0:T(8,128)(2,1)S(1)}, bf16[512,128]{1,0:T(8,128)(2,1)}, u32[]{:S(2)}) copy-start(bf16[512,128]{1,0:T(8,128)(2,1)} %key.7) | copy-start | bytes 393220
  0.6 3.3 %copy-start = (bf16[512,1024]{1,0:T(8,128)(2,1)S(1)}, bf16[512,1024]{1,0:T(8,128)(2,1)}, u32[]{:S(2)}) copy-start(bf16[512,1024]{1,0:T(8,128)(2,1)} %value.11) | copy-start | bytes 3145732
  0.7 3.3 %copy-start.5 = (f32[3,128]{1,0:T(4,128)S(1)}, f32[3,128]{1,0:T(4,128)}, u32[]{:S(2)}) copy-start(f32[3,128]{1,0:T(4,128)} %taps_k.5) | copy-start | bytes 4612
  0.7 3.3 %copy-start.4 = (f32[3,1024]{1,0:T(4,128)S(1)}, f32[3,1024]{1,0:T(4,128)}, u32[]{:S(2)}) copy-start(f32[3,1024]{1,0:T(4,128)} %taps_v.7) | copy-start | bytes 36868
  1.6 3.6 %collective-permute-start = (bf16[2,1280]{1,0:T(2,128)(2,1)S(1)}, bf16[2,1280]{1,0:T(2,128)(2,1)S(1)}, u32[]{:S(2)}, u32[]{:S(2)}) collective-permute-start(bf16[2,1280]{1,0:T(2,128)(2,1)S(1)} %shard_map.143), channel_id=1, source_target_pairs={{0,1},{1,2},{2,3},{3,4},{4,5},{5,6},{6,7},{7,8},{8,9},{9,10},{10,1... | collective-permute-start | bytes 15368 | tf_op jit(solution)/shard_map/ppermute | solution.py:543
  5.7 3.7 %collective-permute-start.1 = (bf16[4,160,128]{2,1,0:T(8,128)(2,1)S(1)}, bf16[4,160,128]{2,1,0:T(8,128)(2,1)S(1)}, u32[]{:S(2)}, u32[]{:S(2)}) collective-permute-start(bf16[4,160,128]{2,1,0:T(8,128)(2,1)S(1)} %get-tuple-element.100), channel_id=1, source_target_pairs={{0,1},{1,0},{2,3},{3,2},{4,5},{5,4},{6,7},{7,6},{8,9},{9,8},{10,11... | collective-permute-start | bytes 491528 | tf_op jit(solution)/shard_map/ppermute | solution.py:432
  8.3 3.2 %copy-start.3 = (bf16[512,128]{1,0:T(8,128)(2,1)S(1)}, bf16[512,128]{1,0:T(8,128)(2,1)}, u32[]{:S(2)}) copy-start(bf16[512,128]{1,0:T(8,128)(2,1)} %query.5) | copy-start | bytes 393220
  8.3 3.2 %copy-start.7 = (f32[3,128]{1,0:T(4,128)S(1)}, f32[3,128]{1,0:T(4,128)}, u32[]{:S(2)}) copy-start(f32[3,128]{1,0:T(4,128)} %taps_q.5) | copy-start | bytes 4612
  9.4 4.9 %collective-permute-start.2 = (bf16[2,160,128]{2,1,0:T(8,128)(2,1)S(1)}, bf16[2,160,128]{2,1,0:T(8,128)(2,1)S(1)}, u32[]{:S(2)}, u32[]{:S(2)}) collective-permute-start(bf16[2,160,128]{2,1,0:T(8,128)(2,1)S(1)} %get-tuple-element.102), channel_id=1, source_target_pairs={{0,2},{1,3},{2,0},{3,1},{4,6},{5,7},{6,4},{7,5},{8,10},{9,11},{10,... | collective-permute-start | bytes 245768 | tf_op jit(solution)/shard_map/ppermute | solution.py:432
  14.3 5.1 %collective-permute-start.3 = (bf16[2,160,128]{2,1,0:T(8,128)(2,1)S(1)}, bf16[2,160,128]{2,1,0:T(8,128)(2,1)S(1)}, u32[]{:S(2)}, u32[]{:S(2)}) collective-permute-start(bf16[2,160,128]{2,1,0:T(8,128)(2,1)S(1)} %shard_map.150), channel_id=1, source_target_pairs={{0,4},{1,5},{2,6},{3,7},{4,0},{5,1},{6,2},{7,3},{8,12},{9,13},{10,... | collective-permute-start | bytes 245768 | tf_op jit(solution)/shard_map/ppermute | solution.py:432
  17.0 12.7 %copy-start.1 = (bf16[512,1024]{1,0:T(8,128)(2,1)S(1)}, bf16[512,1024]{1,0:T(8,128)(2,1)}, u32[]{:S(2)}) copy-start(bf16[512,1024]{1,0:T(8,128)(2,1)} %grad.3) | copy-start | bytes 3145732
  17.0 12.7 %copy-start.6 = (f32[1024]{0:T(1024)S(1)}, f32[1024]{0:T(1024)}, u32[]{:S(2)}) copy-start(f32[1024]{0:T(1024)} %param.14) | copy-start | bytes 12292
  19.5 5.5 %collective-permute-start.4 = (bf16[2,160,128]{2,1,0:T(8,128)(2,1)S(1)}, bf16[2,160,128]{2,1,0:T(8,128)(2,1)S(1)}, u32[]{:S(2)}, u32[]{:S(2)}) collective-permute-start(bf16[2,160,128]{2,1,0:T(8,128)(2,1)S(1)} %shard_map.151), channel_id=1, source_target_pairs={{0,8},{1,9},{2,10},{3,11},{4,12},{5,13},{6,14},{7,15},{8,0},{9,1},... | collective-permute-start | bytes 245768 | tf_op jit(solution)/shard_map/ppermute | solution.py:432
  25.1 4.5 %collective-permute-start.5 = (bf16[2,160,128]{2,1,0:T(8,128)(2,1)S(1)}, bf16[2,160,128]{2,1,0:T(8,128)(2,1)S(1)}, u32[]{:S(2)}, u32[]{:S(2)}) collective-permute-start(bf16[2,160,128]{2,1,0:T(8,128)(2,1)S(1)} %get-tuple-element.107), channel_id=1, source_target_pairs={{0,2},{1,3},{2,0},{3,1},{4,6},{5,7},{6,4},{7,5},{8,10},{9,11},{10,... | collective-permute-start | bytes 245768 | tf_op jit(solution)/shard_map/ppermute | solution.py:432
  29.7 2.0 %collective-permute-start.6 = (bf16[4,160,128]{2,1,0:T(8,128)(2,1)S(1)}, bf16[4,160,128]{2,1,0:T(8,128)(2,1)S(1)}, u32[]{:S(2)}, u32[]{:S(2)}) collective-permute-start(bf16[4,160,128]{2,1,0:T(8,128)(2,1)S(1)} %get-tuple-element.110), channel_id=1, source_target_pairs={{0,1},{1,0},{2,3},{3,2},{4,5},{5,4},{6,7},{7,6},{8,9},{9,8},{10,11... | collective-permute-start | bytes 491528 | tf_op jit(solution)/shard_map/ppermute | solution.py:432
  31.2 2.1 %collective-permute-start.7 = (bf16[4,160,128]{2,1,0:T(8,128)(2,1)S(1)}, bf16[4,160,128]{2,1,0:T(8,128)(2,1)S(1)}, u32[]{:S(2)}, u32[]{:S(2)}) collective-permute-start(bf16[4,160,128]{2,1,0:T(8,128)(2,1)S(1)} %get-tuple-element.123), channel_id=1, source_target_pairs={{0,1},{1,0},{2,3},{3,2},{4,5},{5,4},{6,7},{7,6},{8,9},{9,8},{10,11... | collective-permute-start | bytes 491528 | tf_op jit(solution)/shard_map/ppermute | solution.py:432
  33.3 4.5 %collective-permute-start.8 = (bf16[2,160,128]{2,1,0:T(8,128)(2,1)S(1)}, bf16[2,160,128]{2,1,0:T(8,128)(2,1)S(1)}, u32[]{:S(2)}, u32[]{:S(2)}) collective-permute-start(bf16[2,160,128]{2,1,0:T(8,128)(2,1)S(1)} %get-tuple-element.125), channel_id=1, source_target_pairs={{0,2},{1,3},{2,0},{3,1},{4,6},{5,7},{6,4},{7,5},{8,10},{9,11},{10,... | collective-permute-start | bytes 245768 | tf_op jit(solution)/shard_map/ppermute | solution.py:432
  37.8 4.5 %collective-permute-start.9 = (bf16[2,160,128]{2,1,0:T(8,128)(2,1)S(1)}, bf16[2,160,128]{2,1,0:T(8,128)(2,1)S(1)}, u32[]{:S(2)}, u32[]{:S(2)}) collective-permute-start(bf16[2,160,128]{2,1,0:T(8,128)(2,1)S(1)} %shard_map.163), channel_id=1, source_target_pairs={{0,4},{1,5},{2,6},{3,7},{4,0},{5,1},{6,2},{7,3},{8,12},{9,13},{10,... | collective-permute-start | bytes 245768 | tf_op jit(solution)/shard_map/ppermute | solution.py:432
  42.4 6.1 %collective-permute-start.10 = (bf16[2,160,128]{2,1,0:T(8,128)(2,1)S(1)}, bf16[2,160,128]{2,1,0:T(8,128)(2,1)S(1)}, u32[]{:S(2)}, u32[]{:S(2)}) collective-permute-start(bf16[2,160,128]{2,1,0:T(8,128)(2,1)S(1)} %shard_map.164), channel_id=1, source_target_pairs={{0,8},{1,9},{2,10},{3,11},{4,12},{5,13},{6,14},{7,15},{8,0},{9,1},... | collective-permute-start | bytes 245768 | tf_op jit(solution)/shard_map/ppermute | solution.py:432
  48.6 4.5 %collective-permute-start.11 = (bf16[2,160,128]{2,1,0:T(8,128)(2,1)S(1)}, bf16[2,160,128]{2,1,0:T(8,128)(2,1)S(1)}, u32[]{:S(2)}, u32[]{:S(2)}) collective-permute-start(bf16[2,160,128]{2,1,0:T(8,128)(2,1)S(1)} %get-tuple-element.133), channel_id=1, source_target_pairs={{0,2},{1,3},{2,0},{3,1},{4,6},{5,7},{6,4},{7,5},{8,10},{9,11},{10,... | collective-permute-start | bytes 245768 | tf_op jit(solution)/shard_map/ppermute | solution.py:432
  53.2 1.5 %collective-permute-start.12 = (bf16[4,160,128]{2,1,0:T(8,128)(2,1)S(1)}, bf16[4,160,128]{2,1,0:T(8,128)(2,1)S(1)}, u32[]{:S(2)}, u32[]{:S(2)}) collective-permute-start(bf16[4,160,128]{2,1,0:T(8,128)(2,1)S(1)} %get-tuple-element.136), channel_id=1, source_target_pairs={{0,1},{1,0},{2,3},{3,2},{4,5},{5,4},{6,7},{7,6},{8,9},{9,8},{10,11... | collective-permute-start | bytes 491528 | tf_op jit(solution)/shard_map/ppermute | solution.py:432
  55.8 6.3 %collective-permute-start.16 = (f32[4,1280]{1,0:T(4,128)S(1)}, f32[4,1280]{1,0:T(4,128)S(1)}, u32[]{:S(2)}, u32[]{:S(2)}) collective-permute-start(f32[4,1280]{1,0:T(4,128)S(1)} %get-tuple-element.156), channel_id=1, source_target_pairs={{0,8},{1,9},{2,10},{3,11},{4,12},{5,13},{6,14},{7,15},{8,0},{9,1},... | collective-permute-start | bytes 61448 | tf_op jit(solution)/shard_map/ppermute | solution.py:432
  58.5 5.8 %collective-permute-start.15 = (f32[4,1280]{1,0:T(4,128)S(1)}, f32[4,1280]{1,0:T(4,128)S(1)}, u32[]{:S(2)}, u32[]{:S(2)}) collective-permute-start(f32[4,1280]{1,0:T(4,128)S(1)} %get-tuple-element.156), channel_id=1, source_target_pairs={{0,12},{1,13},{2,14},{3,15},{4,8},{5,9},{6,10},{7,11},{8,4},{9,5},... | collective-permute-start | bytes 61448 | tf_op jit(solution)/shard_map/ppermute | solution.py:432
  60.4 4.0 %collective-permute-start.14 = (f32[4,1280]{1,0:T(4,128)S(1)}, f32[4,1280]{1,0:T(4,128)S(1)}, u32[]{:S(2)}, u32[]{:S(2)}) collective-permute-start(f32[4,1280]{1,0:T(4,128)S(1)} %get-tuple-element.156), channel_id=1, source_target_pairs={{0,4},{1,5},{2,6},{3,7},{4,0},{5,1},{6,2},{7,3},{8,12},{9,13},{10,... | collective-permute-start | bytes 61448 | tf_op jit(solution)/shard_map/ppermute | solution.py:432
  60.8 5.5 %collective-permute-start.13 = (f32[2,1280]{1,0:T(2,128)S(1)}, f32[2,1280]{1,0:T(2,128)S(1)}, u32[]{:S(2)}, u32[]{:S(2)}) collective-permute-start(f32[2,1280]{1,0:T(2,128)S(1)} %get-tuple-element.152), channel_id=1, source_target_pairs={{1,0},{2,1},{3,2},{4,3},{5,4},{6,5},{7,6},{8,7},{9,8},{10,9},{11,1... | collective-permute-start | bytes 30728 | tf_op jit(solution)/shard_map/ppermute | solution.py:674
  64.4 3.8 %collective-permute-start.17 = (f32[4,1280]{1,0:T(4,128)S(1)}, f32[4,1280]{1,0:T(4,128)S(1)}, u32[]{:S(2)}, u32[]{:S(2)}) collective-permute-start(f32[4,1280]{1,0:T(4,128)S(1)} %add_add_fusion.refs_0_), channel_id=1, source_target_pairs={{0,3},{1,2},{2,1},{3,0},{4,7},{5,6},{6,5},{7,4},{8,11},{9,10},{10,... | collective-permute-start | bytes 61448 | tf_op jit(solution)/shard_map/ppermute | solution.py:432
  64.4 3.9 %collective-permute-start.18 = (f32[4,1280]{1,0:T(4,128)S(1)}, f32[4,1280]{1,0:T(4,128)S(1)}, u32[]{:S(2)}, u32[]{:S(2)}) collective-permute-start(f32[4,1280]{1,0:T(4,128)S(1)} %add_add_fusion.refs_0_), channel_id=1, source_target_pairs={{0,2},{1,3},{2,0},{3,1},{4,6},{5,7},{6,4},{7,5},{8,10},{9,11},{10,... | collective-permute-start | bytes 61448 | tf_op jit(solution)/shard_map/ppermute | solution.py:432
  65.6 2.8 %collective-permute-start.19 = (f32[4,1280]{1,0:T(4,128)S(1)}, f32[4,1280]{1,0:T(4,128)S(1)}, u32[]{:S(2)}, u32[]{:S(2)}) collective-permute-start(f32[4,1280]{1,0:T(4,128)S(1)} %add_add_fusion.refs_0_), channel_id=1, source_target_pairs={{0,1},{1,0},{2,3},{3,2},{4,5},{5,4},{6,7},{7,6},{8,9},{9,8},{10,11... | collective-permute-start | bytes 61448 | tf_op jit(solution)/shard_map/ppermute | solution.py:432

commit v10 on v9

--- a/solution.py
+++ b/solution.py
@@ -97,12 +97,10 @@
     return pl.ds(pl.multiple_of(start + (half * HALF + g) * DIM, DIM), DIM)
 
 
-def doubled(state_ref, out_ref):
+def pair_weight():
     rows = lax.broadcasted_iota(jnp.int32, (ROWS, DIM), 0)
     pair = ((rows >= FEAT) & (rows < LIN)) | ((rows >= TAIL) & (rows < TAIL + 8))
-    weight = jnp.where(pair, 2.0, 1.0).astype(F32)
-    for g in range(HALF):
-        out_ref[g] = (state_ref[g].astype(F32) * weight).astype(BF16)
+    return jnp.where(pair, 2.0, 1.0).astype(F32)
 
 
 def head_mask(h):
@@ -212,7 +210,7 @@
 def norm_kernel(own, local, fq, prefix, grad, gain, *refs):
     *others, out, gs_out, state_out, gain_out, pre, summed_ref = refs
     half = half_index(own)
-    doubled(prefix, pre)
+    pre = prefix
     for other in others:
         for g in range(HALF):
             out[:, lanes_of(1 - half, g)] = other[:, head_lanes(g)]
@@ -274,7 +272,7 @@
 ):
     for own, gs, prefix, locals_ in ((True, gs_a, pre_a, (a0, a1)), (False, gs_b, pre_b, (b0, b1))):
         half = half_index(own)
-        doubled(prefix, pre)
+        pre = prefix
         for g in range(HALF):
             x = qt_ref[rows_of(half, g)].astype(F32)
             turned_grad[rows_of(half, g)] = locals_[g // PART][head_rows(g % PART)] + feature_grad(
@@ -288,7 +286,7 @@
 
 
 def later_half(half, value, rim, kt, fk, v, state, locals_v, locals_k, gv_out, gk_put, sums_put, wide, post, taps):
-    doubled(state, post)
+    post = state
     for g in range(HALF):
         local = locals_v[g // PART][:, head_lanes(g % PART)]
         gv_out[:, head_lanes(g)] = local + dot(fk[g], post[g], TN)
@@ -476,11 +474,12 @@
 def merge_kernel(reverse, own_part, other_part, keep, near, own, give):
     upper = lax.rem(lax.div(lax.axis_index("seq"), 2), 2)
     side = on_side(1, reverse)
+    weight = pair_weight()
     for part, which in ((own_part, upper), (other_part, 1 - upper)):
         place = pl.ds(which * PART, PART)
         before = part[...].astype(F32)
-        own[place] = (before + chosen(side, near[place].astype(F32))).astype(BF16)
-        give[place] = (before + chosen(jnp.logical_not(side), keep[place].astype(F32))).astype(BF16)
+        own[place] = ((before + chosen(side, near[place].astype(F32))) * weight).astype(BF16)
+        give[place] = ((before + chosen(jnp.logical_not(side), keep[place].astype(F32))) * weight).astype(BF16)
 
 
 def beyond(keep, send, reverse, works, last):

time: 69.2 us -> 69.2 us (level)
  transfers between devices with their start and end apart: 20 -> 20, of which waited for: 8 -> 9; matrix products, arithmetic and copies ran while one was open for 0% -> 0% of each run, Pallas kernels for 35% -> 35%
where the time goes in v10:
time: 69.2 us; the launch traced here: 69 us
  starting transfers between devices  30.3 us (44%)
  Pallas kernels  27.9 us (40%)
  waiting for transfers between devices  9.79 us (14%)
  between operations  0.94 us (1%)
    pallas_call x28, Pallas kernels, call(): pl.pallas_call(kernel, out_shape=[o if i in loose else pltpu.VMEM(o.shape...  27.9 us
    ppermute x18, starting transfers between devices, exchange(): return lax.ppermute(x, 'seq', [(i, i ^ distance) for i in range(count)])  26.7 us
    ppermute x18, waiting for transfers between devices, exchange(): return lax.ppermute(x, 'seq', [(i, i ^ distance) for i in range(count)])  9.78 us
    ppermute x1, starting transfers between devices, shards(): rim = lax.ppermute(ends, 'seq', [(i, i + 1) for i in range(count - 1)])  2.36 us
  transfers between devices with their start and end apart: 20, of which 9 were waited for; matrix products, arithmetic and copies ran while one was open for 0% of the time, Pallas kernels for 35%

profile of v10, /device:TPU:0, one launch (start us, length us, event | category | flops | bytes accessed | tf_op | source)
XLA Modules:
  0.0 69.0 jit_solution(3642817554914860860)
XLA Ops:
  0.7 0.9 %shard_map.143 = bf16[2,1280]{1,0:T(2,128)(2,1)S(1)} custom-call(bf16[512,128]{1,0:T(8,128)(2,1)} %query.5, bf16[512,128]{1,0:T(8,128)(2,1)} %key.7, bf16[512,1024]{1,0:T(8,128)(2,1)} %value.11), custom_call_target="tpu_custom_call" | custom-call | flops 512 | bytes 1315840 | tf_op jit(solution)/shard_map/pallas_call | solution.py:418
  1.6 2.4 %collective-permute-start = (bf16[2,1280]{1,0:T(2,128)(2,1)S(1)}, bf16[2,1280]{1,0:T(2,128)(2,1)S(1)}, u32[]{:S(2)}, u32[]{:S(2)}) collective-permute-start(bf16[2,1280]{1,0:T(2,128)(2,1)S(1)} %shard_map.143), channel_id=1, source_target_pairs={{0,1},{1,2},{2,3},{3,4},{4,5},{5,6},{6,7},{7,8},{8,9},{9,10},{10,1... | collective-permute-start | bytes 15368 | tf_op jit(solution)/shard_map/ppermute | solution.py:542
  4.0 1.2 %shard_map.145 = (bf16[384,128]{1,0:T(8,128)(2,1)S(1)}, bf16[128,384]{1,0:T(8,128)(2,1)S(1)}, bf16[384,512]{1,0:T(8,128)(2,1)S(1)}, bf16[4,160,384]{2,1,0:T(8,12...) custom-call(bf16[512,128]{1,0:T(8,128)(2,1)S(1)} %copy-done.2, ...), custom_call_target="tpu_custom_call" | custom-call | flops 167772160 | bytes 3814912 | tf_op jit(solution)/shard_map/pallas_call | solution.py:418
  5.2 0.4 shard_map.146
  5.7 2.7 %collective-permute-start.1 = (bf16[4,160,128]{2,1,0:T(8,128)(2,1)S(1)}, bf16[4,160,128]{2,1,0:T(8,128)(2,1)S(1)}, u32[]{:S(2)}, u32[]{:S(2)}) collective-permute-start(bf16[4,160,128]{2,1,0:T(8,128)(2,1)S(1)} %get-tuple-element.100), channel_id=1, source_target_pairs={{0,1},{1,0},{2,3},{3,2},{4,5},{5,4},{6,7},{7,6},{8,9},{9,8},{10,11... | collective-permute-start | bytes 491528 | tf_op jit(solution)/shard_map/ppermute | solution.py:430
  8.3 0.4 shard_map.147
  8.7 0.6 collective-permute-done.1.near
  9.4 2.1 %collective-permute-start.2 = (bf16[2,160,128]{2,1,0:T(8,128)(2,1)S(1)}, bf16[2,160,128]{2,1,0:T(8,128)(2,1)S(1)}, u32[]{:S(2)}, u32[]{:S(2)}) collective-permute-start(bf16[2,160,128]{2,1,0:T(8,128)(2,1)S(1)} %get-tuple-element.102), channel_id=1, source_target_pairs={{0,2},{1,3},{2,0},{3,1},{4,6},{5,7},{6,4},{7,5},{8,10},{9,11},{10,... | collective-permute-start | bytes 245768 | tf_op jit(solution)/shard_map/ppermute | solution.py:430
  11.5 0.5 shard_map.144
  12.0 2.3 %shard_map.148.local = f32[512,512]{1,0:T(8,128)S(1)} custom-call(bf16[512,128]{1,0:T(8,128)(2,1)S(1)} %get-tuple-element.85.q_ref, bf16[512,128]{1,0:T(8,128)(2,1)S(1)} %get-tuple-element.91.k_ref, bf16[512,512]{1,0:T(8,128)(2,1)S(1)} %get-tuple-element.97.v_ref.v), custom_call_target="tpu_custom_call" | custom-call | flops 536870912 | bytes 1835008 | tf_op jit(solution)/shard_map/pallas_call | solution.py:418
  14.3 2.7 %collective-permute-start.3 = (bf16[2,160,128]{2,1,0:T(8,128)(2,1)S(1)}, bf16[2,160,128]{2,1,0:T(8,128)(2,1)S(1)}, u32[]{:S(2)}, u32[]{:S(2)}) collective-permute-start(bf16[2,160,128]{2,1,0:T(8,128)(2,1)S(1)} %shard_map.150), channel_id=1, source_target_pairs={{0,4},{1,5},{2,6},{3,7},{4,0},{5,1},{6,2},{7,3},{8,12},{9,13},{10,... | collective-permute-start | bytes 245768 | tf_op jit(solution)/shard_map/ppermute | solution.py:430
  17.0 2.3 %shard_map.152.local = f32[512,512]{1,0:T(8,128)S(1)} custom-call(bf16[512,128]{1,0:T(8,128)(2,1)S(1)} %get-tuple-element.85.q_ref, bf16[512,128]{1,0:T(8,128)(2,1)S(1)} %get-tuple-element.91.k_ref, bf16[512,512]{1,0:T(8,128)(2,1)S(1)} %get-tuple-element.104.v_ref.v), custom_call_target="tpu_custom_call" | custom-call | flops 536870912 | bytes 1835008 | tf_op jit(solution)/shard_map/pallas_call | solution.py:418
  19.4 0.1 collective-permute-done.3.refs_1_.rest_0_
  19.5 3.1 %collective-permute-start.4 = (bf16[2,160,128]{2,1,0:T(8,128)(2,1)S(1)}, bf16[2,160,128]{2,1,0:T(8,128)(2,1)S(1)}, u32[]{:S(2)}, u32[]{:S(2)}) collective-permute-start(bf16[2,160,128]{2,1,0:T(8,128)(2,1)S(1)} %shard_map.151), channel_id=1, source_target_pairs={{0,8},{1,9},{2,10},{3,11},{4,12},{5,13},{6,14},{7,15},{8,0},{9,1},... | collective-permute-start | bytes 245768 | tf_op jit(solution)/shard_map/ppermute | solution.py:430
  22.6 2.4 %collective-permute-done.4.rest_1_ = bf16[2,160,128]{2,1,0:T(8,128)(2,1)S(1)} collective-permute-done((bf16[2,160,128]{2,1,0:T(8,128)(2,1)S(1)}, bf16[2,160,128]{2,1,0:T(8,128)(2,1)S(1)}, u32[]{:S(2)}, u32[]{:S(2)}) %collective-permute-start.4) | collective-permute-done | bytes 81952 | tf_op jit(solution)/shard_map/ppermute | solution.py:430
  25.1 1.0 %collective-permute-start.5 = (bf16[2,160,128]{2,1,0:T(8,128)(2,1)S(1)}, bf16[2,160,128]{2,1,0:T(8,128)(2,1)S(1)}, u32[]{:S(2)}, u32[]{:S(2)}) collective-permute-start(bf16[2,160,128]{2,1,0:T(8,128)(2,1)S(1)} %get-tuple-element.107), channel_id=1, source_target_pairs={{0,2},{1,3},{2,0},{3,1},{4,6},{5,7},{6,4},{7,5},{8,10},{9,11},{10,... | collective-permute-start | bytes 245768 | tf_op jit(solution)/shard_map/ppermute | solution.py:430
  26.1 3.5 %collective-permute-done.5.other_part = bf16[2,160,128]{2,1,0:T(8,128)(2,1)S(1)} collective-permute-done((bf16[2,160,128]{2,1,0:T(8,128)(2,1)S(1)}, bf16[2,160,128]{2,1,0:T(8,128)(2,1)S(1)}, u32[]{:S(2)}, u32[]{:S(2)}) %collective-permute-start.5) | collective-permute-done | bytes 81952 | tf_op jit(solution)/shard_map/ppermute | solution.py:430
  29.6 0.1 shard_map.154
  29.7 0.1 collective-permute-start.6
  29.8 1.3 %shard_map.155 = (bf16[512,512]{1,0:T(8,128)(2,1)S(1)}, bf16[512,512]{1,0:T(8,128)(2,1)S(1)}, bf16[4,160,128]{2,1,0:T(8,128)(2,1)S(1)}, f32[4,128]{1,0:T(4,128)S(1)}) custom-call(f32[512,512]{1,0:T(8,128)S(1)} %shard_map.148.local, bf16[8,160,512]{2,1,0:T(8,128)(2,1)S(1)} %get-tuple-element.98.fq, bf16[4,160,128]{2,1,0:T(8,128)(2,1)S(1)} %get-tuple-element.108.prefix.pre_a, ...), custom_call_target="tpu_custom_call" | custom-call | flops 167772160 | bytes 4790272 | tf_op jit(solution)/shard_map/pallas_call | solution.py:418
  31.1 0.6 collective-permute-start.7
  31.7 1.5 %shard_map.156 = (bf16[512,1024]{1,0:T(8,128)(2,1)S(1)}, bf16[512,512]{1,0:T(8,128)(2,1)S(1)}, bf16[4,160,128]{2,1,0:T(8,128)(2,1)S(1)}, f32[4,128]{1,0:T(4,128)S(1)}) custom-call(f32[512,512]{1,0:T(8,128)S(1)} %shard_map.152.local, bf16[8,160,512]{2,1,0:T(8,128)(2,1)S(1)} %get-tuple-element.98.fq, ...), custom_call_target="tpu_custom_call" | custom-call | flops 167772160 | bytes 5838848 | tf_op jit(solution)/shard_map/pallas_call | solution.py:418
  33.3 1.0 %collective-permute-start.8 = (bf16[2,160,128]{2,1,0:T(8,128)(2,1)S(1)}, bf16[2,160,128]{2,1,0:T(8,128)(2,1)S(1)}, u32[]{:S(2)}, u32[]{:S(2)}) collective-permute-start(bf16[2,160,128]{2,1,0:T(8,128)(2,1)S(1)} %get-tuple-element.125), channel_id=1, source_target_pairs={{0,2},{1,3},{2,0},{3,1},{4,6},{5,7},{6,4},{7,5},{8,10},{9,11},{10,... | collective-permute-start | bytes 245768 | tf_op jit(solution)/shard_map/ppermute | solution.py:430
  34.3 3.1 %shard_map.157 = (f32[512,256]{1,0:T(8,128)S(1)}, f32[32,512]{1,0:T(8,128)S(1)}, f32[32,512]{1,0:T(8,128)S(1)}, bf16[512,1024]{1,0:T(8,128)(2,1)}) custom-call(bf16[512,128]{1,0:T(8,128)(2,1)S(1)} %get-tuple-element.85.q_ref, bf16[512,128]{1,0:T(8,128)(2,1)S(1)} %get-tuple-element.91.k_ref, bf16[128,512]{1,0:T(8,128)(2,1)S(1)} %get-tuple-element.92.qt_ref, ...), custom_call_target="tpu_custom_call" | custom-call | flops 536870912 | bytes 4325376 | tf_op jit(solution)/shard_map/pallas_call | solution.py:418
  37.4 0.3 collective-permute-done.8.refs_0_.got_y
  37.8 2.0 %collective-permute-start.9 = (bf16[2,160,128]{2,1,0:T(8,128)(2,1)S(1)}, bf16[2,160,128]{2,1,0:T(8,128)(2,1)S(1)}, u32[]{:S(2)}, u32[]{:S(2)}) collective-permute-start(bf16[2,160,128]{2,1,0:T(8,128)(2,1)S(1)} %shard_map.163), channel_id=1, source_target_pairs={{0,4},{1,5},{2,6},{3,7},{4,0},{5,1},{6,2},{7,3},{8,12},{9,13},{10,... | collective-permute-start | bytes 245768 | tf_op jit(solution)/shard_map/ppermute | solution.py:430
  39.8 2.5 %shard_map.158 = (f32[512,256]{1,0:T(8,128)S(1)}, f32[32,512]{1,0:T(8,128)S(1)}, f32[32,512]{1,0:T(8,128)S(1)}) custom-call(bf16[512,128]{1,0:T(8,128)(2,1)S(1)} %get-tuple-element.85.q_ref, bf16[512,128]{1,0:T(8,128)(2,1)S(1)} %get-tuple-element.91.k_ref, bf16[128,512]{1,0:T(8,128)(2,1)S(1)} %get-tuple-element.92.qt_ref, ...), custom_call_target="tpu_custom_call" | custom-call | flops 536870912 | bytes 2228224 | tf_op jit(solution)/shard_map/pallas_call | solution.py:418
  42.3 3.4 %collective-permute-start.10 = (bf16[2,160,128]{2,1,0:T(8,128)(2,1)S(1)}, bf16[2,160,128]{2,1,0:T(8,128)(2,1)S(1)}, u32[]{:S(2)}, u32[]{:S(2)}) collective-permute-start(bf16[2,160,128]{2,1,0:T(8,128)(2,1)S(1)} %shard_map.164), channel_id=1, source_target_pairs={{0,8},{1,9},{2,10},{3,11},{4,12},{5,13},{6,14},{7,15},{8,0},{9,1},... | collective-permute-start | bytes 245768 | tf_op jit(solution)/shard_map/ppermute | solution.py:430
  45.8 2.7 %shard_map.159 = (f32[512,256]{1,0:T(8,128)S(1)}, f32[32,512]{1,0:T(8,128)S(1)}, f32[32,512]{1,0:T(8,128)S(1)}) custom-call(bf16[512,128]{1,0:T(8,128)(2,1)S(1)} %get-tuple-element.85.q_ref, bf16[512,128]{1,0:T(8,128)(2,1)S(1)} %get-tuple-element.91.k_ref, bf16[128,512]{1,0:T(8,128)(2,1)S(1)} %get-tuple-element.92.qt_ref, ...), custom_call_target="tpu_custom_call" | custom-call | flops 536870912 | bytes 2228224 | tf_op jit(solution)/shard_map/pallas_call | solution.py:418
  48.5 0.1 shard_map.165
  48.6 1.0 %collective-permute-start.11 = (bf16[2,160,128]{2,1,0:T(8,128)(2,1)S(1)}, bf16[2,160,128]{2,1,0:T(8,128)(2,1)S(1)}, u32[]{:S(2)}, u32[]{:S(2)}) collective-permute-start(bf16[2,160,128]{2,1,0:T(8,128)(2,1)S(1)} %get-tuple-element.133), channel_id=1, source_target_pairs={{0,2},{1,3},{2,0},{3,1},{4,6},{5,7},{6,4},{7,5},{8,10},{9,11},{10,... | collective-permute-start | bytes 245768 | tf_op jit(solution)/shard_map/ppermute | solution.py:430
  49.6 2.5 %shard_map.160 = (f32[512,256]{1,0:T(8,128)S(1)}, f32[32,512]{1,0:T(8,128)S(1)}, f32[32,512]{1,0:T(8,128)S(1)}) custom-call(bf16[512,128]{1,0:T(8,128)(2,1)S(1)} %get-tuple-element.85.q_ref, bf16[512,128]{1,0:T(8,128)(2,1)S(1)} %get-tuple-element.91.k_ref, bf16[128,512]{1,0:T(8,128)(2,1)S(1)} %get-tuple-element.92.qt_ref, ...), custom_call_target="tpu_custom_call" | custom-call | flops 536870912 | bytes 2228224 | tf_op jit(solution)/shard_map/pallas_call | solution.py:418
  52.1 0.9 %shard_map.161 = (f32[512,128]{1,0:T(8,128)S(1)}, f32[3,128]{1,0:T(4,128)S(1)}) custom-call(bf16[512,128]{1,0:T(8,128)(2,1)S(1)} %copy-done.3, bf16[2,1280]{1,0:T(2,128)(2,1)S(1)} %collective-permute-done.rim, bf16[128,512]{1,0:T(8,128)(2,1)S(1)} %get-tuple-element.92.qt_ref, bf16[512,512]{1,0:T(8,128)(2,1)S(1)} %get-tuple-element.109.gs_ref.gs_a, ...), custom_call_target="tpu_custom_call" | custom-call | flops 83886080 | bytes 2170880 | tf_op jit(solution)/shard_map/pallas_call | solution.py:418
  53.0 0.1 collective-permute-done.11.other_part
  53.1 0.1 shard_map.166
  53.3 1.1 %shard_map.167 = (f32[512,512]{1,0:T(8,128)S(1)}, f32[64,512]{1,0:T(8,128)S(1)}, f32[3,512]{1,0:T(4,128)S(1)}) custom-call(bf16[512,1024]{1,0:T(8,128)(2,1)S(1)} %copy-done, bf16[2,1280]{1,0:T(2,128)(2,1)S(1)} %collective-permute-done.rim, bf16[128,512]{1,0:T(8,128)(2,1)S(1)} %get-tuple-element.93.kt.kt_ref, bf16[4,160,512]{2,1,0:T(8,128)(2,1)S(1)} %get-tuple-element.137.fk, ...), custom_call_target="tpu_custom_call" | custom-call | flops 167772160 | bytes 4893696 | tf_op jit(solution)/shard_map/pallas_call | solution.py:418
  54.4 0.3 collective-permute-done.12.state
  54.6 1.1 %shard_map.168 = (f32[512,512]{1,0:T(8,128)S(1)}, f32[512,128]{1,0:T(8,128)S(1)}, f32[2,1280]{1,0:T(2,128)S(1)}, f32[4,1280]{1,0:T(4,128)S(1)}) custom-call(bf16[512,128]{1,0:T(8,128)(2,1)S(1)} %copy-done.2, bf16[512,1024]{1,0:T(8,128)(2,1)S(1)} %copy-done, bf16[2,1280]{1,0:T(2,128)(2,1)S(1)} %collective-permute-done.rim, ...), custom_call_target="tpu_custom_call" | custom-call | flops 167772160 | bytes 6633984 | tf_op jit(solution)/shard_map/pallas_call | solution.py:418
  55.8 2.7 %collective-permute-start.16 = (f32[4,1280]{1,0:T(4,128)S(1)}, f32[4,1280]{1,0:T(4,128)S(1)}, u32[]{:S(2)}, u32[]{:S(2)}) collective-permute-start(f32[4,1280]{1,0:T(4,128)S(1)} %get-tuple-element.156), channel_id=1, source_target_pairs={{0,8},{1,9},{2,10},{3,11},{4,12},{5,13},{6,14},{7,15},{8,0},{9,1},... | collective-permute-start | bytes 61448 | tf_op jit(solution)/shard_map/ppermute | solution.py:430
  58.5 1.8 %collective-permute-start.15 = (f32[4,1280]{1,0:T(4,128)S(1)}, f32[4,1280]{1,0:T(4,128)S(1)}, u32[]{:S(2)}, u32[]{:S(2)}) collective-permute-start(f32[4,1280]{1,0:T(4,128)S(1)} %get-tuple-element.156), channel_id=1, source_target_pairs={{0,12},{1,13},{2,14},{3,15},{4,8},{5,9},{6,10},{7,11},{8,4},{9,5},... | collective-permute-start | bytes 61448 | tf_op jit(solution)/shard_map/ppermute | solution.py:430
  60.3 0.5 collective-permute-start.14
  60.8 1.3 %collective-permute-start.13 = (f32[2,1280]{1,0:T(2,128)S(1)}, f32[2,1280]{1,0:T(2,128)S(1)}, u32[]{:S(2)}, u32[]{:S(2)}) collective-permute-start(f32[2,1280]{1,0:T(2,128)S(1)} %get-tuple-element.152), channel_id=1, source_target_pairs={{1,0},{2,1},{3,2},{4,3},{5,4},{6,5},{7,6},{8,7},{9,8},{10,9},{11,1... | collective-permute-start | bytes 30728 | tf_op jit(solution)/shard_map/ppermute | solution.py:673
  62.1 2.2 %collective-permute-done.15 = f32[4,1280]{1,0:T(4,128)S(1)} collective-permute-done((f32[4,1280]{1,0:T(4,128)S(1)}, f32[4,1280]{1,0:T(4,128)S(1)}, u32[]{:S(2)}, u32[]{:S(2)}) %collective-permute-start.15) | collective-permute-done | bytes 20512 | tf_op jit(solution)/shard_map/ppermute | solution.py:430
  64.4 1.1 %collective-permute-start.18 = (f32[4,1280]{1,0:T(4,128)S(1)}, f32[4,1280]{1,0:T(4,128)S(1)}, u32[]{:S(2)}, u32[]{:S(2)}) collective-permute-start(f32[4,1280]{1,0:T(4,128)S(1)} %add_add_fusion.refs_0_), channel_id=1, source_target_pairs={{0,2},{1,3},{2,0},{3,1},{4,6},{5,7},{6,4},{7,5},{8,10},{9,11},{10,... | collective-permute-start | bytes 61448 | tf_op jit(solution)/shard_map/ppermute | solution.py:430
  65.5 0.8 %collective-permute-start.19 = (f32[4,1280]{1,0:T(4,128)S(1)}, f32[4,1280]{1,0:T(4,128)S(1)}, u32[]{:S(2)}, u32[]{:S(2)}) collective-permute-start(f32[4,1280]{1,0:T(4,128)S(1)} %add_add_fusion.refs_0_), channel_id=1, source_target_pairs={{0,1},{1,0},{2,3},{3,2},{4,5},{5,4},{6,7},{7,6},{8,9},{9,8},{10,11... | collective-permute-start | bytes 61448 | tf_op jit(solution)/shard_map/ppermute | solution.py:430
  66.2 1.9 %shard_map.169 = (bf16[512,128]{1,0:T(8,128)(2,1)}, bf16[512,128]{1,0:T(8,128)(2,1)}, bf16[512,1024]{1,0:T(8,128)(2,1)}) custom-call(f32[512,128]{1,0:T(8,128)S(1)} %get-tuple-element.120.gq, f32[512,128]{1,0:T(8,128)S(1)} %get-tuple-element.150.gk, f32[512,512]{1,0:T(8,128)S(1)} %get-tuple-element.151.gv_a, f32[512,512]{1,0:T(8,128)S(1)} %get-tuple-element.141.gv_b, ...), custom_call_target="tpu_custom_call" | custom-call | flops 167772160 | bytes 3957760 | tf_op jit(solution)/shard_map/pallas_call | solution.py:418
  68.2 0.2 collective-permute-done.18.refs_2_
  68.4 0.6 shard_map.170
  (37 shorter events, 0.5 us)
Async XLA Ops:
  0.6 3.3 %copy-start.2 = (bf16[512,128]{1,0:T(8,128)(2,1)S(1)}, bf16[512,128]{1,0:T(8,128)(2,1)}, u32[]{:S(2)}) copy-start(bf16[512,128]{1,0:T(8,128)(2,1)} %key.7) | copy-start | bytes 393220
  0.6 3.3 %copy-start = (bf16[512,1024]{1,0:T(8,128)(2,1)S(1)}, bf16[512,1024]{1,0:T(8,128)(2,1)}, u32[]{:S(2)}) copy-start(bf16[512,1024]{1,0:T(8,128)(2,1)} %value.11) | copy-start | bytes 3145732
  0.7 3.3 %copy-start.5 = (f32[3,128]{1,0:T(4,128)S(1)}, f32[3,128]{1,0:T(4,128)}, u32[]{:S(2)}) copy-start(f32[3,128]{1,0:T(4,128)} %taps_k.5) | copy-start | bytes 4612
  0.7 3.3 %copy-start.4 = (f32[3,1024]{1,0:T(4,128)S(1)}, f32[3,1024]{1,0:T(4,128)}, u32[]{:S(2)}) copy-start(f32[3,1024]{1,0:T(4,128)} %taps_v.7) | copy-start | bytes 36868
  1.6 3.6 %collective-permute-start = (bf16[2,1280]{1,0:T(2,128)(2,1)S(1)}, bf16[2,1280]{1,0:T(2,128)(2,1)S(1)}, u32[]{:S(2)}, u32[]{:S(2)}) collective-permute-start(bf16[2,1280]{1,0:T(2,128)(2,1)S(1)} %shard_map.143), channel_id=1, source_target_pairs={{0,1},{1,2},{2,3},{3,4},{4,5},{5,6},{6,7},{7,8},{8,9},{9,10},{10,1... | collective-permute-start | bytes 15368 | tf_op jit(solution)/shard_map/ppermute | solution.py:542
  5.7 3.7 %collective-permute-start.1 = (bf16[4,160,128]{2,1,0:T(8,128)(2,1)S(1)}, bf16[4,160,128]{2,1,0:T(8,128)(2,1)S(1)}, u32[]{:S(2)}, u32[]{:S(2)}) collective-permute-start(bf16[4,160,128]{2,1,0:T(8,128)(2,1)S(1)} %get-tuple-element.100), channel_id=1, source_target_pairs={{0,1},{1,0},{2,3},{3,2},{4,5},{5,4},{6,7},{7,6},{8,9},{9,8},{10,11... | collective-permute-start | bytes 491528 | tf_op jit(solution)/shard_map/ppermute | solution.py:430
  8.3 3.2 %copy-start.3 = (bf16[512,128]{1,0:T(8,128)(2,1)S(1)}, bf16[512,128]{1,0:T(8,128)(2,1)}, u32[]{:S(2)}) copy-start(bf16[512,128]{1,0:T(8,128)(2,1)} %query.5) | copy-start | bytes 393220
  8.3 3.2 %copy-start.7 = (f32[3,128]{1,0:T(4,128)S(1)}, f32[3,128]{1,0:T(4,128)}, u32[]{:S(2)}) copy-start(f32[3,128]{1,0:T(4,128)} %taps_q.5) | copy-start | bytes 4612
  9.4 4.9 %collective-permute-start.2 = (bf16[2,160,128]{2,1,0:T(8,128)(2,1)S(1)}, bf16[2,160,128]{2,1,0:T(8,128)(2,1)S(1)}, u32[]{:S(2)}, u32[]{:S(2)}) collective-permute-start(bf16[2,160,128]{2,1,0:T(8,128)(2,1)S(1)} %get-tuple-element.102), channel_id=1, source_target_pairs={{0,2},{1,3},{2,0},{3,1},{4,6},{5,7},{6,4},{7,5},{8,10},{9,11},{10,... | collective-permute-start | bytes 245768 | tf_op jit(solution)/shard_map/ppermute | solution.py:430
  14.3 5.1 %collective-permute-start.3 = (bf16[2,160,128]{2,1,0:T(8,128)(2,1)S(1)}, bf16[2,160,128]{2,1,0:T(8,128)(2,1)S(1)}, u32[]{:S(2)}, u32[]{:S(2)}) collective-permute-start(bf16[2,160,128]{2,1,0:T(8,128)(2,1)S(1)} %shard_map.150), channel_id=1, source_target_pairs={{0,4},{1,5},{2,6},{3,7},{4,0},{5,1},{6,2},{7,3},{8,12},{9,13},{10,... | collective-permute-start | bytes 245768 | tf_op jit(solution)/shard_map/ppermute | solution.py:430
  17.0 12.8 %copy-start.1 = (bf16[512,1024]{1,0:T(8,128)(2,1)S(1)}, bf16[512,1024]{1,0:T(8,128)(2,1)}, u32[]{:S(2)}) copy-start(bf16[512,1024]{1,0:T(8,128)(2,1)} %grad.3) | copy-start | bytes 3145732
  17.0 12.8 %copy-start.6 = (f32[1024]{0:T(1024)S(1)}, f32[1024]{0:T(1024)}, u32[]{:S(2)}) copy-start(f32[1024]{0:T(1024)} %param.14) | copy-start | bytes 12292
  19.5 5.5 %collective-permute-start.4 = (bf16[2,160,128]{2,1,0:T(8,128)(2,1)S(1)}, bf16[2,160,128]{2,1,0:T(8,128)(2,1)S(1)}, u32[]{:S(2)}, u32[]{:S(2)}) collective-permute-start(bf16[2,160,128]{2,1,0:T(8,128)(2,1)S(1)} %shard_map.151), channel_id=1, source_target_pairs={{0,8},{1,9},{2,10},{3,11},{4,12},{5,13},{6,14},{7,15},{8,0},{9,1},... | collective-permute-start | bytes 245768 | tf_op jit(solution)/shard_map/ppermute | solution.py:430
  25.1 4.5 %collective-permute-start.5 = (bf16[2,160,128]{2,1,0:T(8,128)(2,1)S(1)}, bf16[2,160,128]{2,1,0:T(8,128)(2,1)S(1)}, u32[]{:S(2)}, u32[]{:S(2)}) collective-permute-start(bf16[2,160,128]{2,1,0:T(8,128)(2,1)S(1)} %get-tuple-element.107), channel_id=1, source_target_pairs={{0,2},{1,3},{2,0},{3,1},{4,6},{5,7},{6,4},{7,5},{8,10},{9,11},{10,... | collective-permute-start | bytes 245768 | tf_op jit(solution)/shard_map/ppermute | solution.py:430
  29.7 2.0 %collective-permute-start.6 = (bf16[4,160,128]{2,1,0:T(8,128)(2,1)S(1)}, bf16[4,160,128]{2,1,0:T(8,128)(2,1)S(1)}, u32[]{:S(2)}, u32[]{:S(2)}) collective-permute-start(bf16[4,160,128]{2,1,0:T(8,128)(2,1)S(1)} %get-tuple-element.110), channel_id=1, source_target_pairs={{0,1},{1,0},{2,3},{3,2},{4,5},{5,4},{6,7},{7,6},{8,9},{9,8},{10,11... | collective-permute-start | bytes 491528 | tf_op jit(solution)/shard_map/ppermute | solution.py:430
  31.1 2.0 %collective-permute-start.7 = (bf16[4,160,128]{2,1,0:T(8,128)(2,1)S(1)}, bf16[4,160,128]{2,1,0:T(8,128)(2,1)S(1)}, u32[]{:S(2)}, u32[]{:S(2)}) collective-permute-start(bf16[4,160,128]{2,1,0:T(8,128)(2,1)S(1)} %get-tuple-element.123), channel_id=1, source_target_pairs={{0,1},{1,0},{2,3},{3,2},{4,5},{5,4},{6,7},{7,6},{8,9},{9,8},{10,11... | collective-permute-start | bytes 491528 | tf_op jit(solution)/shard_map/ppermute | solution.py:430
  33.3 4.5 %collective-permute-start.8 = (bf16[2,160,128]{2,1,0:T(8,128)(2,1)S(1)}, bf16[2,160,128]{2,1,0:T(8,128)(2,1)S(1)}, u32[]{:S(2)}, u32[]{:S(2)}) collective-permute-start(bf16[2,160,128]{2,1,0:T(8,128)(2,1)S(1)} %get-tuple-element.125), channel_id=1, source_target_pairs={{0,2},{1,3},{2,0},{3,1},{4,6},{5,7},{6,4},{7,5},{8,10},{9,11},{10,... | collective-permute-start | bytes 245768 | tf_op jit(solution)/shard_map/ppermute | solution.py:430
  37.8 4.5 %collective-permute-start.9 = (bf16[2,160,128]{2,1,0:T(8,128)(2,1)S(1)}, bf16[2,160,128]{2,1,0:T(8,128)(2,1)S(1)}, u32[]{:S(2)}, u32[]{:S(2)}) collective-permute-start(bf16[2,160,128]{2,1,0:T(8,128)(2,1)S(1)} %shard_map.163), channel_id=1, source_target_pairs={{0,4},{1,5},{2,6},{3,7},{4,0},{5,1},{6,2},{7,3},{8,12},{9,13},{10,... | collective-permute-start | bytes 245768 | tf_op jit(solution)/shard_map/ppermute | solution.py:430
  42.3 6.1 %collective-permute-start.10 = (bf16[2,160,128]{2,1,0:T(8,128)(2,1)S(1)}, bf16[2,160,128]{2,1,0:T(8,128)(2,1)S(1)}, u32[]{:S(2)}, u32[]{:S(2)}) collective-permute-start(bf16[2,160,128]{2,1,0:T(8,128)(2,1)S(1)} %shard_map.164), channel_id=1, source_target_pairs={{0,8},{1,9},{2,10},{3,11},{4,12},{5,13},{6,14},{7,15},{8,0},{9,1},... | collective-permute-start | bytes 245768 | tf_op jit(solution)/shard_map/ppermute | solution.py:430
  48.6 4.5 %collective-permute-start.11 = (bf16[2,160,128]{2,1,0:T(8,128)(2,1)S(1)}, bf16[2,160,128]{2,1,0:T(8,128)(2,1)S(1)}, u32[]{:S(2)}, u32[]{:S(2)}) collective-permute-start(bf16[2,160,128]{2,1,0:T(8,128)(2,1)S(1)} %get-tuple-element.133), channel_id=1, source_target_pairs={{0,2},{1,3},{2,0},{3,1},{4,6},{5,7},{6,4},{7,5},{8,10},{9,11},{10,... | collective-permute-start | bytes 245768 | tf_op jit(solution)/shard_map/ppermute | solution.py:430
  53.2 1.5 %collective-permute-start.12 = (bf16[4,160,128]{2,1,0:T(8,128)(2,1)S(1)}, bf16[4,160,128]{2,1,0:T(8,128)(2,1)S(1)}, u32[]{:S(2)}, u32[]{:S(2)}) collective-permute-start(bf16[4,160,128]{2,1,0:T(8,128)(2,1)S(1)} %get-tuple-element.136), channel_id=1, source_target_pairs={{0,1},{1,0},{2,3},{3,2},{4,5},{5,4},{6,7},{7,6},{8,9},{9,8},{10,11... | collective-permute-start | bytes 491528 | tf_op jit(solution)/shard_map/ppermute | solution.py:430
  55.8 6.3 %collective-permute-start.16 = (f32[4,1280]{1,0:T(4,128)S(1)}, f32[4,1280]{1,0:T(4,128)S(1)}, u32[]{:S(2)}, u32[]{:S(2)}) collective-permute-start(f32[4,1280]{1,0:T(4,128)S(1)} %get-tuple-element.156), channel_id=1, source_target_pairs={{0,8},{1,9},{2,10},{3,11},{4,12},{5,13},{6,14},{7,15},{8,0},{9,1},... | collective-permute-start | bytes 61448 | tf_op jit(solution)/shard_map/ppermute | solution.py:430
  58.5 5.8 %collective-permute-start.15 = (f32[4,1280]{1,0:T(4,128)S(1)}, f32[4,1280]{1,0:T(4,128)S(1)}, u32[]{:S(2)}, u32[]{:S(2)}) collective-permute-start(f32[4,1280]{1,0:T(4,128)S(1)} %get-tuple-element.156), channel_id=1, source_target_pairs={{0,12},{1,13},{2,14},{3,15},{4,8},{5,9},{6,10},{7,11},{8,4},{9,5},... | collective-permute-start | bytes 61448 | tf_op jit(solution)/shard_map/ppermute | solution.py:430
  60.3 4.0 %collective-permute-start.14 = (f32[4,1280]{1,0:T(4,128)S(1)}, f32[4,1280]{1,0:T(4,128)S(1)}, u32[]{:S(2)}, u32[]{:S(2)}) collective-permute-start(f32[4,1280]{1,0:T(4,128)S(1)} %get-tuple-element.156), channel_id=1, source_target_pairs={{0,4},{1,5},{2,6},{3,7},{4,0},{5,1},{6,2},{7,3},{8,12},{9,13},{10,... | collective-permute-start | bytes 61448 | tf_op jit(solution)/shard_map/ppermute | solution.py:430
  60.8 5.4 %collective-permute-start.13 = (f32[2,1280]{1,0:T(2,128)S(1)}, f32[2,1280]{1,0:T(2,128)S(1)}, u32[]{:S(2)}, u32[]{:S(2)}) collective-permute-start(f32[2,1280]{1,0:T(2,128)S(1)} %get-tuple-element.152), channel_id=1, source_target_pairs={{1,0},{2,1},{3,2},{4,3},{5,4},{6,5},{7,6},{8,7},{9,8},{10,9},{11,1... | collective-permute-start | bytes 30728 | tf_op jit(solution)/shard_map/ppermute | solution.py:673
  64.3 3.8 %collective-permute-start.17 = (f32[4,1280]{1,0:T(4,128)S(1)}, f32[4,1280]{1,0:T(4,128)S(1)}, u32[]{:S(2)}, u32[]{:S(2)}) collective-permute-start(f32[4,1280]{1,0:T(4,128)S(1)} %add_add_fusion.refs_0_), channel_id=1, source_target_pairs={{0,3},{1,2},{2,1},{3,0},{4,7},{5,6},{6,5},{7,4},{8,11},{9,10},{10,... | collective-permute-start | bytes 61448 | tf_op jit(solution)/shard_map/ppermute | solution.py:430
  64.4 4.0 %collective-permute-start.18 = (f32[4,1280]{1,0:T(4,128)S(1)}, f32[4,1280]{1,0:T(4,128)S(1)}, u32[]{:S(2)}, u32[]{:S(2)}) collective-permute-start(f32[4,1280]{1,0:T(4,128)S(1)} %add_add_fusion.refs_0_), channel_id=1, source_target_pairs={{0,2},{1,3},{2,0},{3,1},{4,6},{5,7},{6,4},{7,5},{8,10},{9,11},{10,... | collective-permute-start | bytes 61448 | tf_op jit(solution)/shard_map/ppermute | solution.py:430
  65.5 2.9 %collective-permute-start.19 = (f32[4,1280]{1,0:T(4,128)S(1)}, f32[4,1280]{1,0:T(4,128)S(1)}, u32[]{:S(2)}, u32[]{:S(2)}) collective-permute-start(f32[4,1280]{1,0:T(4,128)S(1)} %add_add_fusion.refs_0_), channel_id=1, source_target_pairs={{0,1},{1,0},{2,3},{3,2},{4,5},{5,4},{6,7},{7,6},{8,9},{9,8},{10,11... | collective-permute-start | bytes 61448 | tf_op jit(solution)/shard_map/ppermute | solution.py:430
